TPU v7x, 32 devices: a whole 2x2x4 slice. The times are simulated.
32 devices in a mesh: samp: 16 (over z, y, x), mark: 2 (over core).
Axes of the slice: x: 2, y: 2, z: 4, core: 2. Of those that a mesh axis runs over, the one named last changes fastest.
Arguments:
- genotypes: bfloat16 [16000, 12288], P('mark', 'samp'), may hold values from -6 to 6
- variants: bfloat16 [2048, 12288], P('mark', 'samp'), may hold values from -6 to 6
- weights: float32 [12288], P('samp'), may hold values from 0.05 to 0.25
- variance_ratio: float32 [1], replicated, may hold values from 1 to 4
- panel: float32 [24, 12288], P(None, 'samp'), may hold values from -24 to 24
- gene_sizes: int32 [2, 24], P('mark'), may hold values from 1 to 400, 1024 in all within a row
Outputs:
- solution: float32 [24, 12288], P(None, 'samp')
- residual: float32 [24, 12288], P(None, 'samp')
- direction: float32 [24, 12288], P(None, 'samp')
- gene_gram: float32 [2, 1024, 1024], P('mark', 'samp')
Inputs may be any that keep to these rules, and one draw needn't show every extreme that they name: `gene_sizes`: row j lists in order the sizes of the genes that partition the 1024 test variants of block j, and sums to 1024.
All inputs are finite; a program needn't handle non-finite values.
Results may differ from a plain program's by a relative error of at most 0.0044.
Values sent between devices are 32-bit elements; how exact they have to be, the bound alone decides.
No kernel may reach another device: no remote copies, remote signals or barrier semaphores. Data moves between devices by JAX's collectives and lax.ppermute only.
A program may use at most 64 MiB of HBM per device.

v0:
```python
import jax
import jax.numpy as jnp
from jax import lax
from jax.sharding import PartitionSpec as P

MARKERS = 16000


def body(genotypes, variants, weights, variance_ratio, panel, gene_sizes):
    ratio = variance_ratio[0]
    diag = 1.0 / weights + ratio
    start_dir = panel / diag
    partial_scores = lax.dot_general(
        start_dir.astype(jnp.bfloat16),
        genotypes,
        (((1,), (1,)), ((), ())),
        preferred_element_type=jnp.float32,
    )
    summed_scores = lax.psum(partial_scores, "samp")
    scores = ratio / MARKERS * summed_scores
    partial_terms = jnp.dot(
        scores.astype(jnp.bfloat16), genotypes, preferred_element_type=jnp.float32
    )
    share_terms = lax.psum_scatter(partial_terms, "mark", scatter_dimension=1, tiled=True)
    share_width = share_terms.shape[1]
    offset = lax.axis_index("mark") * share_width
    share_dir = lax.dynamic_slice_in_dim(start_dir, offset, share_width, 1)
    share_panel = lax.dynamic_slice_in_dim(panel, offset, share_width, 1)
    share_weights = lax.dynamic_slice_in_dim(weights, offset, share_width, 0)
    share_image = share_dir / share_weights + share_terms
    start_norm, curvature = lax.psum(
        (jnp.sum(share_panel * share_dir, axis=1), jnp.sum(share_dir * share_image, axis=1)),
        ("samp", "mark"),
    )
    alpha = (start_norm / curvature)[:, None]
    share_solution = alpha * share_dir
    share_residual = share_panel - alpha * share_image
    solution, residual = (
        lax.all_gather(share_solution, "mark", axis=1, tiled=True),
        lax.all_gather(share_residual, "mark", axis=1, tiled=True),
    )
    precond = residual / diag
    weighted = (weights * solution).astype(jnp.bfloat16)
    partial_var = lax.dot_general(
        weighted, variants, (((1,), (1,)), ((), ())), preferred_element_type=jnp.float32
    )
    new_norm, var_scores = lax.psum((jnp.sum(residual * precond, axis=1), partial_var), "samp")
    direction = precond + (new_norm / start_norm)[:, None] * start_dir
    scaled = (variants * weights).astype(jnp.bfloat16)
    num_variants = variants.shape[0]
    row_count = num_variants // lax.axis_size("samp")
    first_row = lax.axis_index("samp") * row_count
    positions = jnp.arange(num_variants, dtype=jnp.int32)
    sizes_row = gene_sizes[0]
    ends = jnp.cumsum(sizes_row, dtype=jnp.int32)
    gene_index = jnp.sum((ends[None, :] <= positions[:, None]).astype(jnp.int32), axis=1)
    row_genes = lax.dynamic_slice_in_dim(gene_index, first_row, row_count, 0)
    same_gene = row_genes[:, None] == gene_index[None, :]
    cross = lax.psum_scatter(
        lax.dot_general(
            scaled, variants, (((1,), (1,)), ((), ())), preferred_element_type=jnp.float32
        ),
        "samp",
        scatter_dimension=0,
        tiled=True,
    )
    row_scores = lax.dynamic_slice_in_dim(var_scores, first_row, row_count, 1)
    correction = jnp.dot(row_scores.T, var_scores, precision=lax.Precision.HIGHEST)
    total_samples = panel.shape[1] * lax.axis_size("samp")
    gram_rows = jnp.where(same_gene, (cross - correction) / total_samples, jnp.zeros_like(cross))
    return (solution, residual, direction, gram_rows[None])


def solution(mesh):
    return jax.shard_map(
        body,
        mesh=mesh,
        in_specs=(
            P("mark", "samp"),
            P("mark", "samp"),
            P("samp"),
            P(),
            P(None, "samp"),
            P("mark", None),
        ),
        out_specs=(P(None, "samp"), P(None, "samp"), P(None, "samp"), P("mark", "samp", None)),
        check_vma=False,
    )
```

profile of v0, /device:TPU:0, one launch (start us, length us, event | category | flops | bytes accessed | tf_op | source)
XLA Modules:
  0.0 402.5 jit_solution(8407566228730937837)
XLA Ops:
  7.2 0.0 all-reduce.4.cloned.1.call-start
  7.9 0.7 divide_add_fusion.1
  8.5 0.9 broadcast_divide_fusion
  9.5 8.7 %fusion.9 = f32[24,8000]{1,0:T(8,128)} fusion(bf16[8000,768]{1,0:T(8,128)(2,1)} %param.6, f32[24,768]{1,0:T(8,128)S(1)} %broadcast_divide_fusion), kind=kOutput, calls=%fused_computation.19 | convolution fusion | flops 294930432 | bytes 13129728 | tf_op jit(solution)/shard_map/dot_general | solution.py:13
  18.2 0.0 reduce-scatter.3.cloned.1.call-start
  18.3 113.3 %all-reduce.4.cloned.1.call-done = f32[24,8000]{1,0:T(8,128)} async-done(((f32[24,8000]{1,0:T(8,128)}), f32[24,8000]{1,0:T(8,128)}) %all-reduce.4.cloned.1.call-update) | async-done | bytes 768016 | tf_op jit(solution)/shard_map/psum | solution.py:19
  131.6 7.1 %fusion.5 = f32[24,768]{1,0:T(8,128)} fusion(bf16[8000,768]{1,0:T(8,128)(2,1)} %param.6, f32[24,8000]{1,0:T(8,128)} %all-reduce.4.cloned.1.call-done, f32[]{:T(128)S(6)} %div.49), kind=kOutput, calls=%fused_computation.8 | convolution fusion | flops 295296000 | bytes 13129732 | tf_op jit(solution)/shard_map/dot_general | solution.py:21
  138.7 0.0 reduce-scatter.3.cloned.1.call-update
  138.7 0.0 all-reduce.6.cloned.1.call-start
  138.8 0.1 dynamic_slice.17
  138.9 6.5 %reduce-scatter.3.cloned.1.call-done = f32[24,384]{1,0:T(8,128)} async-done(((f32[24,768]{1,0:T(8,128)}), f32[24,384]{1,0:T(8,128)}) %reduce-scatter.3.cloned.1.call-update) | async-done | bytes 36880 | tf_op jit(solution)/shard_map/reduce_scatter | solution.py:24
  145.4 0.9 multiply_reduce_fusion.1
  146.3 40.4 %all-reduce = (f32[24]{0:T(128)S(1)}, f32[24]{0:T(128)S(1)}) all-reduce(f32[24]{0:T(128)S(1)} %get-tuple-element.5, f32[24]{0:T(128)S(1)} %get-tuple-element.4), channel_id=1, replica_groups=mesh['samp'=16,'mark'=2] {'samp','mark'}, use_global_device_ids=true, to_apply=%region_1.0 | all-reduce | flops 48 | bytes 384 | tf_op jit(solution)/shard_map/psum | solution.py:31
  186.8 0.8 multiply_subtract_fusion
  187.6 1.8 all_gather.6
  189.5 1.2 fusion.7
  190.6 0.0 reduce-scatter.5.cloned.1.call-start
  190.7 3.8 fusion
  194.5 0.6 copy-done.3
  195.1 0.1 copy.12
  195.2 0.1 reduce
  195.4 0.1 convert_reduce_fusion
  195.5 0.1 dynamic_slice.18
  195.5 1.8 all_gather.7
  197.4 0.1 multiply_reduce_fusion
  197.5 40.5 %psum.38 = f32[24]{0:T(128)S(1)} all-reduce(f32[24]{0:T(128)S(1)} %multiply_reduce_fusion), channel_id=1, replica_groups=mesh['samp'=16,'mark'=2] {'samp'}, use_global_device_ids=true, to_apply=%region_7.0 | all-reduce | flops 24 | bytes 192 | tf_op jit(solution)/shard_map/psum | solution.py:47
  238.0 0.7 multiply_add_fusion
  238.8 56.3 %all-reduce.6.cloned.1.call-done = f32[24,1024]{1,0:T(8,128)} async-done(((f32[24,1024]{1,0:T(8,128)}), f32[24,1024]{1,0:T(8,128)}) %all-reduce.6.cloned.1.call-update) | async-done | bytes 98320 | tf_op jit(solution)/shard_map/psum | solution.py:47
  295.1 97.4 %reduce-scatter.5.cloned.1.call-done = f32[64,1024]{1,0:T(8,128)} async-done(((f32[1024,1024]{1,0:T(8,128)}), f32[64,1024]{1,0:T(8,128)}) %reduce-scatter.5.cloned.1.call-update) | async-done | bytes 262160 | tf_op jit(solution)/shard_map/reduce_scatter | solution.py:59
  392.4 2.2 fusion.4
  394.7 0.6 copy.18
  395.3 0.6 copy.19
  (13 shorter events, 0.1 us)
Async XLA Ops:
  7.2 124.4 %all-reduce.4.cloned.1.call-start = ((), (), s32[]{:S(2)}) async-start(), calls=%async_computation.2 | async-start | bytes 1548288 | tf_op jit(solution)/shard_map/psum | solution.py:19
  18.2 127.2 %reduce-scatter.3.cloned.1.call-start = ((), (), s32[]{:S(2)}) async-start(), calls=%async_computation.3 | async-start | bytes 110592 | tf_op jit(solution)/shard_map/reduce_scatter | solution.py:24
  18.2 120.6 %copy-start.2 = (f32[768]{0:T(1024)S(1)}, f32[768]{0:T(1024)}, u32[]{:S(2)}) copy-start(f32[768]{0:T(1024)} %param.8) | copy-start | bytes 9220
  18.2 127.2 %copy-start.1 = (f32[24,768]{1,0:T(8,128)S(1)}, f32[24,768]{1,0:T(8,128)}, u32[]{:S(2)}) copy-start(f32[24,768]{1,0:T(8,128)} %param.10) | copy-start | bytes 221188
  18.2 171.2 %copy-start = (bf16[1024,768]{1,0:T(8,128)(2,1)S(1)}, bf16[1024,768]{1,0:T(8,128)(2,1)}, u32[]{:S(2)}) copy-start(bf16[1024,768]{1,0:T(8,128)(2,1)} %param.7) | copy-start | bytes 4718596
  138.7 156.3 %all-reduce.6.cloned.1.call-start = ((), (), s32[]{:S(2)}) async-start(), calls=%async_computation.5 | async-start | bytes 196608 | tf_op jit(solution)/shard_map/psum | solution.py:47
  190.6 201.8 %reduce-scatter.5.cloned.1.call-start = ((), (), s32[]{:S(2)}) async-start(), calls=%async_computation.4 | async-start | bytes 4456448 | tf_op jit(solution)/shard_map/reduce_scatter | solution.py:59
  194.4 0.7 copy-start.3
Sparse Core Ops, SparseCore 0:
  18.3 113.2 all-reduce.3
  138.8 6.5 reduce-scatter.2
  190.8 104.2 all-reduce.5
  297.2 95.1 reduce-scatter.4
where the time goes:
time: 403 us; the launch traced here: 402 us
  waiting for transfers between devices  274 us (68%)
  blocking collectives  84.7 us (21%)
  matrix products  23 us (6%)
  between operations  14.5 us (4%)
  other arithmetic  4.43 us (1%)
    psum x1, waiting for transfers between devices, body(): summed_scores = lax.psum(partial_scores, 'samp')  113 us
    reduce_scatter x1, waiting for transfers between devices, body(): lax.psum_scatter(lax.dot_general(scaled, variants, (((1,), (1,)), ((), ()...  97.4 us
    psum x1, waiting for transfers between devices, body(): lax.psum((jnp.sum(residual * precond, axis=1), partial_var), 'samp')  56.3 us
    psum x1, blocking collectives, body(): lax.psum((jnp.sum(residual * precond, axis=1), partial_var), 'samp')  40.5 us
    psum x1, blocking collectives, body(): lax.psum((jnp.sum(share_panel * share_dir, axis=1), jnp.sum(share_dir * s...  40.4 us
    dot_general x1, matrix products, body(): lax.dot_general(start_dir.astype(jnp.bfloat16), genotypes, (((1,), (1,)),...  8.69 us
  transfers between devices with their start and end apart: 4, of which 4 were waited for; matrix products, arithmetic and copies ran while one was open for 1% of the time, Pallas kernels for 0%

commit v1 on v0

v1 whole, which is shorter than its diff:
```python
import functools

import jax
import jax.numpy as jnp
from jax import lax
from jax.experimental import pallas as pl
from jax.experimental.pallas import tpu as pltpu
from jax.sharding import PartitionSpec as P

GENE_MAX = 400
LANES = 128
F32 = jnp.float32
BF16 = jnp.bfloat16
VMEM = pltpu.VMEM
NT = (((1,), (1,)), ((), ()))


def up(value, step):
    return -(-value // step) * step


def stages_of(count):
    found, stride = [], 1
    while stride < count:
        radix = 4 if count // stride % 4 == 0 else 2
        found.append((radix, stride))
        stride *= radix
    return found


def offsets_of(stages):
    found = [0]
    for radix, stride in stages:
        found = [base ^ (digit * stride) for base in found for digit in range(radix)]
    return found


def swap(array, count, offset, axis="samp"):
    return lax.ppermute(array, axis, [(i, i ^ offset) for i in range(count)])


def start_dir_of(ratio_ref, weights_ref, panel_ref):
    diag = 1.0 / weights_ref[...] + ratio_ref[0]
    return diag, panel_ref[...] / diag


def chunk_start(chunk, width, total):
    return pl.multiple_of(jnp.minimum(chunk * width, total - width), 16)


def fresh_lanes(chunk, width, total, rows):
    lane = lax.broadcasted_iota(jnp.int32, (rows, width), 1)
    return lane + jnp.minimum(chunk * width, total - width) >= chunk * width


def scores_kernel(width, total, count, ids, quarter, ratio, weights, panel, geno, variants, out, dir_bf):
    step = pl.program_id(0)
    steps = pl.num_programs(0)

    @pl.when(step == 0)
    def _():
        _, start_dir = start_dir_of(ratio, weights, panel)
        dir_bf[...] = start_dir.astype(BF16)
        weighted = (weights[...] * start_dir).astype(BF16)
        out[:, ids.shape[0] * width :] = lax.dot_general(
            weighted, variants[...], NT, preferred_element_type=F32
        )

    chunk = ids[step]
    part = lax.dot_general(dir_bf[...], geno[...], NT, preferred_element_type=F32)
    part = jnp.where(fresh_lanes(chunk, width, total, part.shape[0]), part, 0.0)
    at = pl.multiple_of(step * width, LANES)
    out[:, pl.ds(at, width)] = part

    @pl.when(chunk == count - 1)
    def _():
        _, start_dir = start_dir_of(ratio, weights, panel)
        norm = jnp.sum(panel[...] * start_dir, axis=1, keepdims=True)
        own = jnp.sum(start_dir * (start_dir / weights[...]), axis=1, keepdims=True)
        lane = lax.broadcasted_iota(jnp.int32, (part.shape[0], LANES), 1)
        head = part[:, :LANES]
        head = jnp.where(lane == 0, norm, jnp.where(lane == 1, own, head))
        out[:, pl.ds(at, LANES)] = head


def scores_call(ids, quarter, ratio, weights, panel, geno, variants, width, count, share):
    total, samples = geno.shape
    rows = panel.shape[0]
    chunks = ids.shape[0]
    return pl.pallas_call(
        functools.partial(scores_kernel, width, total, count),
        out_shape=jax.ShapeDtypeStruct((rows, chunks * width + share), F32),
        grid_spec=pltpu.PrefetchScalarGridSpec(
            num_scalar_prefetch=2,
            grid=(chunks,),
            in_specs=[
                pl.BlockSpec(memory_space=pltpu.SMEM),
                pl.BlockSpec((1, samples), lambda j, ids, q: (0, 0)),
                pl.BlockSpec((rows, samples), lambda j, ids, q: (0, 0)),
                pl.BlockSpec(
                    (pl.Element(width), pl.Element(samples)),
                    lambda j, ids, q: (chunk_start(ids[j], width, total), 0),
                ),
                pl.BlockSpec((share, samples), lambda j, ids, q: (q[0], 0)),
            ],
            out_specs=pl.BlockSpec(memory_space=VMEM),
            scratch_shapes=[VMEM((rows, samples), BF16)],
        ),
        name="scores",
    )(ids, quarter, ratio, weights, panel, geno, variants)


def terms_kernel(width, total, count, markers, ids, ratio, scores, geno, before, out):
    step = pl.program_id(0)
    samples = geno.shape[1]

    @pl.when(step == 0)
    def _():
        out[...] = before[...]

    chunk = ids[step]
    raw = scores[:, pl.ds(pl.multiple_of(step * width, LANES), width)]
    fresh = fresh_lanes(chunk, width, total, raw.shape[0])
    scaled = jnp.where(fresh, (ratio[0] / markers) * raw, 0.0)
    out[:, :samples] += jnp.dot(scaled.astype(BF16), geno[...], preferred_element_type=F32)
    square = jnp.sum(scaled * raw, axis=1, keepdims=True)
    lane = lax.broadcasted_iota(jnp.int32, (raw.shape[0], LANES), 1)
    stats = jnp.where((lane < 2) & (chunk == count - 1), raw[:, :LANES], 0.0)
    out[:, samples:] += jnp.where(lane == 2, square, stats)


def terms_call(ids, ratio, scores, geno, before, width, count, markers):
    total, samples = geno.shape
    rows = scores.shape[0]
    chunks = ids.shape[0]
    return pl.pallas_call(
        functools.partial(terms_kernel, width, total, count, markers),
        out_shape=jax.ShapeDtypeStruct((rows, samples + LANES), F32),
        grid_spec=pltpu.PrefetchScalarGridSpec(
            num_scalar_prefetch=1,
            grid=(chunks,),
            in_specs=[
                pl.BlockSpec(memory_space=pltpu.SMEM),
                pl.BlockSpec(memory_space=VMEM),
                pl.BlockSpec(
                    (pl.Element(width), pl.Element(samples)),
                    lambda j, ids: (chunk_start(ids[j], width, total), 0),
                ),
                pl.BlockSpec(memory_space=VMEM),
            ],
            out_specs=pl.BlockSpec(memory_space=VMEM),
        ),
        name="terms",
    )(ids, ratio, scores, geno, before)


def update_kernel(ratio, weights, panel, own, other, solution, residual, norm, alpha_out):
    samples = panel.shape[1]
    diag, start_dir = start_dir_of(ratio, weights, panel)
    total = own[...] + other[...]
    terms = total[:, :samples]
    start_norm = own[:, samples : samples + 1]
    curvature = own[:, samples + 1 : samples + 2] + total[:, samples + 2 : samples + 3]
    alpha = start_norm / curvature
    image = start_dir / weights[...] + terms
    left = panel[...] - alpha * image
    solution[...] = alpha * start_dir
    residual[...] = left
    norm[...] = jnp.broadcast_to(jnp.sum(left * (left / diag), axis=1, keepdims=True), norm.shape)
    alpha_out[...] = jnp.broadcast_to(alpha, alpha_out.shape)


def direction_kernel(ratio, weights, panel, own, residual, norm, out):
    samples = panel.shape[1]
    diag, start_dir = start_dir_of(ratio, weights, panel)
    start_norm = own[:, samples : samples + 1]
    out[...] = residual[...] / diag + (norm[:, :1] / start_norm) * start_dir


def genes_of(sizes, index):
    gene = jnp.zeros(index.shape, jnp.int32)
    end = jnp.int32(0)
    for g in range(sizes.shape[1]):
        end = end + sizes[0, g]
        gene = gene + (end <= index).astype(jnp.int32)
    return gene


def cross_kernel(block, span, ids, sizes, weights, variants, *outs):
    count = variants.shape[0]
    cols = genes_of(sizes, lax.broadcasted_iota(jnp.int32, (1, count), 1))
    per = ids.shape[0] // len(outs)
    row = lax.broadcasted_iota(jnp.int32, (block, LANES), 0)
    for at, out in enumerate(outs):
        for j in range(per):
            first = pl.multiple_of(ids[at * per + j] * block, block)
            mine = variants[pl.ds(first, block), :]
            scaled = (mine.astype(F32) * weights[...]).astype(BF16)
            cross = lax.dot_general(scaled, variants[...], NT, preferred_element_type=F32)
            rows = genes_of(sizes, first + row)[:, :1]
            cross = jnp.where(rows == cols, cross, 0.0)
            folded = cross[:, :span]
            for low in range(span, count, span):
                folded = folded + cross[:, low : low + span]
            out[j * block : (j + 1) * block, :] = folded


def gram_kernel(samples, where, sizes, alpha, *refs):
    *parts, out, full = refs
    shares, sums = parts[: where.shape[0] - 1], parts[where.shape[0] - 1 :]
    count = out.shape[2]
    block = out.shape[1]
    share = shares[0].shape[1]
    for at, ref in enumerate(shares):
        place = pl.multiple_of(where[1 + at] * share, LANES)
        full[:, pl.ds(place, share)] = ref[...] * alpha[:, :1]
    cross = sums[0][...]
    for ref in sums[1:]:
        cross = cross + ref[...]
    first = where[0] * block
    window = max(block, LANES)
    base = pl.multiple_of(first // window * window, window)
    wide = lax.dot_general(
        full[:, pl.ds(base, window)],
        full[...],
        (((0,), (0,)), ((), ())),
        precision=lax.Precision.HIGHEST,
        preferred_element_type=F32,
    )
    correction = wide[:block]
    for step in range(1, window // block):
        correction = jnp.where(first - base == step * block, wide[step * block : (step + 1) * block], correction)
    cols = genes_of(sizes, lax.broadcasted_iota(jnp.int32, (1, count), 1))
    rows = genes_of(sizes, first + lax.broadcasted_iota(jnp.int32, (block, LANES), 0))[:, :1]
    span = cross.shape[1]
    for low in range(0, count, span):
        piece = (cross - correction[:, low : low + span]) / samples
        out[0, :, low : low + span] = jnp.where(rows == cols[:, low : low + span], piece, 0.0)


def body(genotypes, variants, weights, variance_ratio, panel, gene_sizes):
    count = lax.axis_size("samp")
    marks = lax.axis_size("mark")
    me = lax.axis_index("samp").astype(jnp.int32)
    stages = stages_of(count)
    (radix, stride), later = stages[0], stages[1:]
    firsts = [digit * stride for digit in range(radix)]
    rest = offsets_of(later)
    ids = [me ^ jnp.array([first ^ r for r in rest], jnp.int32) for first in firsts]
    quarters = [(me // stride % radix ^ d).reshape(1).astype(jnp.int32) for d in range(radix)]

    local, samples = genotypes.shape
    markers = local * marks
    width = up(-(-local // count), LANES)
    if count * width - local < 2:
        width += LANES
    num_variants = variants.shape[0]
    share = num_variants // radix
    row_weights = weights.reshape(1, samples)
    rows = panel.shape[0]

    sent = {}
    for d in (*range(radix - 1, 0, -1), 0):
        sent[d] = scores_call(
            ids[d], quarters[d], variance_ratio, row_weights, panel, genotypes, variants, width, count, share
        )
    got = sent[0]
    for d in range(1, radix):
        got = got + swap(sent[d], count, firsts[d])
    shared, got = got[:, -share:], got[:, :-share]
    for r, s in later:
        wide = got.shape[1] // r
        pieces = [jnp.concatenate([got[:, d * wide : (d + 1) * wide], shared], axis=1) for d in range(r)]
        total = pieces[0]
        for d in range(1, r):
            total = total + swap(pieces[d], count, d * s)
        got, shared = total[:, :wide], total[:, wide:]
    for r, s in reversed(later):
        got = jnp.concatenate([got] + [swap(got, count, d * s) for d in range(1, r)], axis=1)
    everything = jnp.concatenate([got, shared], axis=1)
    arrays = [everything] + [swap(everything, count, first) for first in firsts[1:]]

    block = num_variants // count
    span = up(GENE_MAX, LANES)
    if num_variants % span or num_variants <= span:
        span = num_variants
    crosses = pl.pallas_call(
        functools.partial(cross_kernel, block, span),
        out_shape=[jax.ShapeDtypeStruct((block * len(rest), span), F32)] * radix,
        in_specs=[pl.BlockSpec(memory_space=pltpu.SMEM)] * 2 + [pl.BlockSpec(memory_space=VMEM)] * 2,
        out_specs=[pl.BlockSpec(memory_space=VMEM)] * radix,
        name="cross",
    )(jnp.concatenate(ids), gene_sizes, row_weights, variants)
    held = crosses[0]
    for d in range(1, radix):
        held = held + swap(crosses[d], count, firsts[d])
    sums = [held]
    for r, s in later:
        held = sums[0]
        for other in sums[1:]:
            held = held + other
        tall = held.shape[0] // r
        sums = [held[:tall]] + [swap(held[d * tall : (d + 1) * tall], count, d * s) for d in range(1, r)]

    own = jnp.zeros((rows, samples + LANES), F32)
    for d in range(radix):
        own = terms_call(ids[d], variance_ratio, arrays[d], genotypes, own, width, count, markers)
    assert marks & (marks - 1) == 0
    other = None
    held = own
    offset = 1
    while offset < marks:
        other = swap(held, marks, offset, "mark")
        offset *= 2
        if offset < marks:
            stats = held[:, samples : samples + 2]
            held = held + other
            held = jnp.concatenate([held[:, :samples], stats, held[:, samples + 2 :]], axis=1)
    vmem = pl.BlockSpec(memory_space=VMEM)
    smem = pl.BlockSpec(memory_space=pltpu.SMEM)
    wide = jax.ShapeDtypeStruct((rows, LANES), F32)
    full = jax.ShapeDtypeStruct((rows, samples), F32)
    solution, residual, norm, alpha = pl.pallas_call(
        update_kernel,
        out_shape=[full, full, wide, wide],
        in_specs=[smem] + [vmem] * 4,
        out_specs=[vmem] * 4,
        name="update",
    )(variance_ratio, row_weights, panel, held, other)
    for r, s in stages:
        total = norm
        for d in range(1, r):
            total = total + swap(norm, count, d * s)
        norm = total
    direction = pl.pallas_call(
        direction_kernel,
        out_shape=full,
        in_specs=[smem] + [vmem] * 5,
        out_specs=vmem,
        name="direction",
    )(variance_ratio, row_weights, panel, held, residual, norm)

    shares = [array[:, -share:] for array in arrays]
    gram = pl.pallas_call(
        functools.partial(gram_kernel, samples * count),
        out_shape=jax.ShapeDtypeStruct((1, block, num_variants), F32),
        in_specs=[smem] * 2 + [vmem] * (1 + len(shares) + len(sums)),
        out_specs=vmem,
        scratch_shapes=[VMEM((rows, num_variants), F32)],
        name="gram",
    )(jnp.concatenate([me.reshape(1)] + quarters), gene_sizes, alpha, *shares, *sums)
    return solution, residual, direction, gram


def solution(mesh):
    return jax.shard_map(
        body,
        mesh=mesh,
        in_specs=(
            P("mark", "samp"),
            P("mark", "samp"),
            P("samp"),
            P(),
            P(None, "samp"),
            P("mark", None),
        ),
        out_specs=(P(None, "samp"), P(None, "samp"), P(None, "samp"), P("mark", "samp", None)),
        check_vma=False,
    )
```

time: 403 us -> 136 us (0.34)
  waiting for transfers between devices: 274 us -> 27.2 us
  blocking collectives: 84.7 us -> 0 us
  Pallas kernels: 0 us -> 55.1 us
  starting transfers between devices: 0.16 us -> 34.1 us
  matrix products: 23 us -> 0 us
  between operations: 14.5 us -> 1.52 us
  local copies, waits for them, and re-layouts: 2.15 us -> 10.7 us
    psum x2 -> x0, waiting for transfers between devices: 170 us -> none  [the longest x1 113 us: body(): summed_scores = lax.psum(partial_scores, 'samp')]
    reduce_scatter x2 -> x0, waiting for transfers between devices: 104 us -> none  [the longest x1 97.4 us: body(): lax.psum_scatter(lax.dot_general(scaled, variants, (((1,), (1,)), ((), ()...]
    psum x2 -> x0, blocking collectives: 81 us -> none  [the longest x1 40.5 us: body(): lax.psum((jnp.sum(residual * precond, axis=1), partial_var), 'samp')]
    pallas_call x0 -> x12, Pallas kernels: none -> 55.1 us  [the longest x4 20.9 us: scores_call(): pl.pallas_call(functools.partial(scores_kernel, width, total, count), out...]
    ppermute x0 -> x25, starting transfers between devices: none -> 34.1 us  [swap(): return lax.ppermute(array, axis, [(i, i ^ offset) for i in range(count)])]
    ppermute x0 -> x25, waiting for transfers between devices: none -> 27.2 us  [swap(): return lax.ppermute(array, axis, [(i, i ^ offset) for i in range(count)])]
    dot_general x5 -> x0, matrix products: 23 us -> none  [the longest x1 8.69 us: body(): lax.dot_general(start_dir.astype(jnp.bfloat16), genotypes, (((1,), (1,)),...]
    slice x0 -> x8, local copies, waits for them, and re-layouts: none -> 5.34 us  [the longest x3 4.02 us: body(): shares = [array[:, -share:] for array in arrays]]
  transfers between devices with their start and end apart: 4 -> 25, of which waited for: 4 -> 8; matrix products, arithmetic and copies ran while one was open for 1% -> 7% of each run, Pallas kernels for 0% -> 34%
where the time goes in v1:
time: 136 us; the launch traced here: 135 us
  Pallas kernels  55.1 us (41%)
  starting transfers between devices  34.1 us (25%)
  waiting for transfers between devices  27.2 us (20%)
  local copies, waits for them, and re-layouts  10.7 us (8%)
  other arithmetic  5.94 us (4%)
  between operations  1.52 us (1%)
    ppermute x25, starting transfers between devices, swap(): return lax.ppermute(array, axis, [(i, i ^ offset) for i in range(count)])  34.1 us
    ppermute x25, waiting for transfers between devices, swap(): return lax.ppermute(array, axis, [(i, i ^ offset) for i in range(count)])  27.2 us
    pallas_call x4, Pallas kernels, scores_call(): pl.pallas_call(functools.partial(scores_kernel, width, total, count), out...  20.9 us
    pallas_call x4, Pallas kernels, terms_call(): pl.pallas_call(functools.partial(terms_kernel, width, total, count, marke...  17.9 us
    pallas_call x1, Pallas kernels, body(): pl.pallas_call(functools.partial(cross_kernel, block, span), out_shape=[j...  10.1 us
    slice x3, local copies, waits for them, and re-layouts, body(): shares = [array[:, -share:] for array in arrays]  4.02 us
    xor x4, other arithmetic, body(): me ^ jnp.array([first ^ r for r in rest], jnp.int32)  2.79 us
    unnamed x33, local copies, waits for them, and re-layouts  2.76 us
  transfers between devices with their start and end apart: 25, of which 8 were waited for; matrix products, arithmetic and copies ran while one was open for 7% of the time, Pallas kernels for 34%

profile of v1, /device:TPU:0, one launch (start us, length us, event | category | flops | bytes accessed | tf_op | source)
XLA Modules:
  0.0 134.6 jit_solution(509955579594485373)
XLA Ops:
  3.8 5.2 %scores.5 = f32[24,2304]{1,0:T(8,128)} custom-call(s32[4]{0:T(128)} %broadcast_xor_fusion.1.ids, s32[1]{0:T(128)} %bitcast.1.quarter, f32[1]{0:T(128)S(6)} %copy.18.ratio, f32[1,768]{1,0:T(1,128)} %reshape.26.weights, f32[24,768]{1,0:T(8,128)} %panel.11, bf16[8000,768]{1,0:T(8,128)(2,1)} %geno.15, bf16[1024,768]{1,0:T(8,128)(2,1)} %variants.9), custom_call_target="tpu_custom_call" | custom-call | tf_op jit(solution)/shard_map/scores/pallas_call | solution.py:90
  9.0 3.0 %collective-permute-start = (f32[24,2304]{1,0:T(8,128)}, f32[24,2304]{1,0:T(8,128)S(1)}, u32[]{:S(2)}, u32[]{:S(2)}) collective-permute-start(f32[24,2304]{1,0:T(8,128)} %scores.5), channel_id=1, source_target_pairs={{0,2},{2,0},{4,6},{6,4},{8,10},{10,8},{12,14},{14,12},{16,18},{18,... | collective-permute-start | bytes 663560 | tf_op jit(solution)/shard_map/ppermute | solution.py:39
  12.5 5.1 %scores.6 = f32[24,2304]{1,0:T(8,128)} custom-call(s32[4]{0:T(128)} %broadcast_xor_fusion.ids, s32[1]{0:T(128)} %bitcast.2.quarter, f32[1]{0:T(128)S(6)} %copy.18.ratio, f32[1,768]{1,0:T(1,128)} %reshape.26.weights, f32[24,768]{1,0:T(8,128)} %panel.11, bf16[8000,768]{1,0:T(8,128)(2,1)} %geno.15, bf16[1024,768]{1,0:T(8,128)(2,1)} %variants.9), custom_call_target="tpu_custom_call" | custom-call | tf_op jit(solution)/shard_map/scores/pallas_call | solution.py:90
  17.6 1.5 %collective-permute-start.1 = (f32[24,2304]{1,0:T(8,128)}, f32[24,2304]{1,0:T(8,128)S(1)}, u32[]{:S(2)}, u32[]{:S(2)}) collective-permute-start(f32[24,2304]{1,0:T(8,128)} %scores.6), channel_id=1, source_target_pairs={{0,4},{2,6},{4,0},{6,2},{8,12},{10,14},{12,8},{14,10},{16,20},{18,... | collective-permute-start | bytes 663560 | tf_op jit(solution)/shard_map/ppermute | solution.py:39
  19.7 5.3 %scores.7 = f32[24,2304]{1,0:T(8,128)} custom-call(s32[4]{0:T(128)} %broadcast_xor_fusion.2.ids, s32[1]{0:T(128)} %bitcast.3.quarter, f32[1]{0:T(128)S(6)} %copy.18.ratio, f32[1,768]{1,0:T(1,128)} %reshape.26.weights, f32[24,768]{1,0:T(8,128)} %panel.11, bf16[8000,768]{1,0:T(8,128)(2,1)} %geno.15, bf16[1024,768]{1,0:T(8,128)(2,1)} %variants.9), custom_call_target="tpu_custom_call" | custom-call | tf_op jit(solution)/shard_map/scores/pallas_call | solution.py:90
  25.6 5.2 %scores.4 = f32[24,2304]{1,0:T(8,128)} custom-call(s32[4]{0:T(128)} %multiply_xor_fusion.ids, s32[1]{0:T(128)} %bitcast.quarter, f32[1]{0:T(128)S(6)} %copy.18.ratio, f32[1,768]{1,0:T(1,128)} %reshape.26.weights, f32[24,768]{1,0:T(8,128)} %panel.11, bf16[8000,768]{1,0:T(8,128)(2,1)} %geno.15, bf16[1024,768]{1,0:T(8,128)(2,1)} %variants.9), custom_call_target="tpu_custom_call" | custom-call | tf_op jit(solution)/shard_map/scores/pallas_call | solution.py:90
  30.8 1.9 %collective-permute-done.2 = f32[24,2304]{1,0:T(8,128)S(1)} collective-permute-done((f32[24,2304]{1,0:T(8,128)}, f32[24,2304]{1,0:T(8,128)S(1)}, u32[]{:S(2)}, u32[]{:S(2)}) %collective-permute-start.2) | collective-permute-done | bytes 221216 | tf_op jit(solution)/shard_map/ppermute | solution.py:39
  33.8 1.6 %collective-permute-start.3 = (f32[24,768]{1,0:T(8,128)S(1)}, f32[24,768]{1,0:T(8,128)S(1)}, u32[]{:S(2)}, u32[]{:S(2)}) collective-permute-start(f32[24,768]{1,0:T(8,128)S(1)} %get-tuple-element.31), channel_id=1, source_target_pairs={{0,8},{2,10},{4,12},{6,14},{8,0},{10,2},{12,4},{14,6},{16,24},{18,... | collective-permute-start | bytes 221192 | tf_op jit(solution)/shard_map/ppermute | solution.py:39
  35.4 2.7 %collective-permute-start.4 = (f32[24,768]{1,0:T(8,128)S(1)}, f32[24,768]{1,0:T(8,128)S(1)}, u32[]{:S(2)}, u32[]{:S(2)}) collective-permute-start(f32[24,768]{1,0:T(8,128)S(1)} %get-tuple-element.32), channel_id=1, source_target_pairs={{0,16},{2,18},{4,20},{6,22},{8,24},{10,26},{12,28},{14,30},{16,0},... | collective-permute-start | bytes 221192 | tf_op jit(solution)/shard_map/ppermute | solution.py:39
  38.6 3.6 %collective-permute-done.4 = f32[24,768]{1,0:T(8,128)S(1)} collective-permute-done((f32[24,768]{1,0:T(8,128)S(1)}, f32[24,768]{1,0:T(8,128)S(1)}, u32[]{:S(2)}, u32[]{:S(2)}) %collective-permute-start.4) | collective-permute-done | bytes 73760 | tf_op jit(solution)/shard_map/ppermute | solution.py:39
  42.2 2.4 %collective-permute-done.5 = f32[24,768]{1,0:T(8,128)S(1)} collective-permute-done((f32[24,768]{1,0:T(8,128)S(1)}, f32[24,768]{1,0:T(8,128)S(1)}, u32[]{:S(2)}, u32[]{:S(2)}) %collective-permute-start.5) | collective-permute-done | bytes 73760 | tf_op jit(solution)/shard_map/ppermute | solution.py:39
  45.4 10.1 %cross.1 = (f32[256,512]{1,0:T(8,128)}, f32[256,512]{1,0:T(8,128)}, f32[256,512]{1,0:T(8,128)}, f32[256,512]{1,0:T(8,128)}) custom-call(s32[16]{0:T(128)} %pad_add_fusion.ids, s32[1,24]{1,0:T(1,128)} %sizes.3, f32[1,768]{1,0:T(1,128)} %reshape.26.weights, bf16[1024,768]{1,0:T(8,128)(2,1)} %variants.9), custom_call_target="tpu_custom_call" | custom-call | tf_op jit(solution)/shard_map/cross/pallas_call | solution.py:287
  56.8 2.3 %collective-permute-start.21 = (f32[256,512]{1,0:T(8,128)}, f32[256,512]{1,0:T(8,128)S(1)}, u32[]{:S(2)}, u32[]{:S(2)}) collective-permute-start(f32[256,512]{1,0:T(8,128)} %get-tuple-element.19), channel_id=1, source_target_pairs={{0,6},{2,4},{4,2},{6,0},{8,14},{10,12},{12,10},{14,8},{16,22},{18,... | collective-permute-start | bytes 1572872 | tf_op jit(solution)/shard_map/ppermute | solution.py:39
  60.2 3.2 %collective-permute-start.8 = (f32[24,512]{1,0:T(8,128)S(1)}, f32[24,512]{1,0:T(8,128)S(1)}, u32[]{:S(2)}, u32[]{:S(2)}) collective-permute-start(f32[24,512]{1,0:T(8,128)S(1)} %get-tuple-element.29), channel_id=1, source_target_pairs={{0,24},{2,26},{4,28},{6,30},{8,16},{10,18},{12,20},{14,22},{16,8},... | collective-permute-start | bytes 147464 | tf_op jit(solution)/shard_map/ppermute | solution.py:39
  64.0 2.1 %collective-permute-done.8 = f32[24,512]{1,0:T(8,128)S(1)} collective-permute-done((f32[24,512]{1,0:T(8,128)S(1)}, f32[24,512]{1,0:T(8,128)S(1)}, u32[]{:S(2)}, u32[]{:S(2)}) %collective-permute-start.8) | collective-permute-done | bytes 49184 | tf_op jit(solution)/shard_map/ppermute | solution.py:39
  67.3 1.5 %collective-permute-start.10 = (f32[24,2304]{1,0:T(8,128)S(1)}, f32[24,2304]{1,0:T(8,128)S(1)}, u32[]{:S(2)}, u32[]{:S(2)}) collective-permute-start(f32[24,2304]{1,0:T(8,128)S(1)} %get-tuple-element.28.scores), channel_id=1, source_target_pairs={{0,4},{2,6},{4,0},{6,2},{8,12},{10,14},{12,8},{14,10},{16,20},{18,... | collective-permute-start | bytes 663560 | tf_op jit(solution)/shard_map/ppermute | solution.py:39
  68.8 14.9 %collective-permute-done.11.scores = f32[24,2304]{1,0:T(8,128)S(1)} collective-permute-done((f32[24,2304]{1,0:T(8,128)S(1)}, f32[24,2304]{1,0:T(8,128)S(1)}, u32[]{:S(2)}, u32[]{:S(2)}) %collective-permute-start.11) | collective-permute-done | bytes 221216 | tf_op jit(solution)/shard_map/ppermute | solution.py:39
  85.3 4.5 %terms.4.before = f32[24,896]{1,0:T(8,128)} custom-call(s32[4]{0:T(128)} %multiply_xor_fusion.ids, f32[1]{0:T(128)S(6)} %copy.18.ratio, f32[24,2304]{1,0:T(8,128)} %copy-done.1, bf16[8000,768]{1,0:T(8,128)(2,1)} %geno.15, f32[24,896]{1,0:T(8,128)} %broadcast_in_dim.3.before), custom_call_target="tpu_custom_call" | custom-call | tf_op jit(solution)/shard_map/terms/pallas_call | solution.py:136
  89.8 4.5 %terms.5.before = f32[24,896]{1,0:T(8,128)} custom-call(s32[4]{0:T(128)} %broadcast_xor_fusion.1.ids, f32[1]{0:T(128)S(6)} %copy.18.ratio, f32[24,2304]{1,0:T(8,128)} %copy-done.2, bf16[8000,768]{1,0:T(8,128)(2,1)} %geno.15, f32[24,896]{1,0:T(8,128)} %terms.4.before), custom_call_target="tpu_custom_call" | custom-call | tf_op jit(solution)/shard_map/terms/pallas_call | solution.py:136
  94.9 4.5 %terms.6.before = f32[24,896]{1,0:T(8,128)} custom-call(s32[4]{0:T(128)} %broadcast_xor_fusion.ids, f32[1]{0:T(128)S(6)} %copy.18.ratio, f32[24,2304]{1,0:T(8,128)} %copy-done.3, bf16[8000,768]{1,0:T(8,128)(2,1)} %geno.15, f32[24,896]{1,0:T(8,128)} %terms.5.before), custom_call_target="tpu_custom_call" | custom-call | tf_op jit(solution)/shard_map/terms/pallas_call | solution.py:136
  100.1 4.5 %terms.7.own = f32[24,896]{1,0:T(8,128)} custom-call(s32[4]{0:T(128)} %broadcast_xor_fusion.2.ids, f32[1]{0:T(128)S(6)} %copy.18.ratio, f32[24,2304]{1,0:T(8,128)} %copy-done.4, bf16[8000,768]{1,0:T(8,128)(2,1)} %geno.15, f32[24,896]{1,0:T(8,128)} %terms.6.before), custom_call_target="tpu_custom_call" | custom-call | tf_op jit(solution)/shard_map/terms/pallas_call | solution.py:136
  106.7 1.9 %update.1 = (f32[24,768]{1,0:T(8,128)}, f32[24,768]{1,0:T(8,128)}, f32[24,128]{1,0:T(8,128)}, f32[24,128]{1,0:T(8,128)}) custom-call(f32[1]{0:T(128)S(6)} %copy.18.ratio, f32[1,768]{1,0:T(1,128)} %reshape.26.weights, f32[24,768]{1,0:T(8,128)} %panel.11, f32[24,896]{1,0:T(8,128)} %terms.7.own, f32[24,896]{1,0:T(8,128)} %copy-done.8), custom_call_target="tpu_custom_call" | custom-call | tf_op jit(solution)/shard_map/update/pallas_call | solution.py:323
  108.6 2.5 %collective-permute-start.14 = (f32[24,128]{1,0:T(8,128)}, f32[24,128]{1,0:T(8,128)S(1)}, u32[]{:S(2)}, u32[]{:S(2)}) collective-permute-start(f32[24,128]{1,0:T(8,128)} %get-tuple-element.14), channel_id=1, source_target_pairs={{0,4},{2,6},{4,0},{6,2},{8,12},{10,14},{12,8},{14,10},{16,20},{18,... | collective-permute-start | bytes 36872 | tf_op jit(solution)/shard_map/ppermute | solution.py:39
  112.7 2.0 %collective-permute-start.22 = (f32[64,512]{1,0:T(8,128)S(1)}, f32[64,512]{1,0:T(8,128)S(1)}, u32[]{:S(2)}, u32[]{:S(2)}) collective-permute-start(f32[64,512]{1,0:T(8,128)S(1)} %get-tuple-element.22), channel_id=1, source_target_pairs={{0,8},{2,10},{4,12},{6,14},{8,0},{10,2},{12,4},{14,6},{16,24},{18,... | collective-permute-start | bytes 393224 | tf_op jit(solution)/shard_map/ppermute | solution.py:39
  114.7 3.1 %collective-permute-start.23 = (f32[64,512]{1,0:T(8,128)S(1)}, f32[64,512]{1,0:T(8,128)S(1)}, u32[]{:S(2)}, u32[]{:S(2)}) collective-permute-start(f32[64,512]{1,0:T(8,128)S(1)} %get-tuple-element.21), channel_id=1, source_target_pairs={{0,16},{2,18},{4,20},{6,22},{8,24},{10,26},{12,28},{14,30},{16,0},... | collective-permute-start | bytes 393224 | tf_op jit(solution)/shard_map/ppermute | solution.py:39
  119.0 3.8 %collective-permute-start.17 = (f32[24,128]{1,0:T(8,128)S(1)}, f32[24,128]{1,0:T(8,128)S(1)}, u32[]{:S(2)}, u32[]{:S(2)}) collective-permute-start(f32[24,128]{1,0:T(8,128)S(1)} %add_add_fusion.3), channel_id=1, source_target_pairs={{0,16},{2,18},{4,20},{6,22},{8,24},{10,26},{12,28},{14,30},{16,0},... | collective-permute-start | bytes 36872 | tf_op jit(solution)/shard_map/ppermute | solution.py:39
  122.9 1.4 %collective-permute-start.18 = (f32[24,128]{1,0:T(8,128)S(1)}, f32[24,128]{1,0:T(8,128)S(1)}, u32[]{:S(2)}, u32[]{:S(2)}) collective-permute-start(f32[24,128]{1,0:T(8,128)S(1)} %add_add_fusion.3), channel_id=1, source_target_pairs={{0,24},{2,26},{4,28},{6,30},{8,16},{10,18},{12,20},{14,22},{16,8},... | collective-permute-start | bytes 36872 | tf_op jit(solution)/shard_map/ppermute | solution.py:39
  124.9 1.3 slice.65.refs_1_
  126.3 1.3 slice.66.refs_2_
  127.6 1.3 %slice.67.refs_3_ = f32[24,256]{1,0:T(8,128)} slice(f32[24,2304]{1,0:T(8,128)} %copy-done.4), slice={[0:24], [2048:2304]} | slice | bytes 49152 | tf_op jit(solution)/shard_map/slice | solution.py:343
  129.7 2.6 %gram.1 = f32[1,64,1024]{2,1,0:T(8,128)} custom-call(s32[5]{0:T(128)} %concatenate.26.where, s32[1,24]{1,0:T(1,128)} %sizes.3, f32[24,128]{1,0:T(8,128)} %get-tuple-element.15.alpha, f32[24,256]{1,0:T(8,128)} %get-tuple-element.27.refs_0_, f32[24,256]{1,0:T(8,128)} %slice.65.refs_1_, f32[24,256]{1,0:T(8,128)} %slice.66.refs_2_, f32[24,256]{1,0:T(8,128)} %slice.67.refs_3_, ...), custom_call_target="tpu_custom_call" | custom-call | tf_op jit(solution)/shard_map/gram/pallas_call | solution.py:344
  132.9 1.7 %direction.1 = f32[24,768]{1,0:T(8,128)} custom-call(f32[1]{0:T(128)S(6)} %copy.18.ratio, f32[1,768]{1,0:T(1,128)} %reshape.26.weights, f32[24,768]{1,0:T(8,128)} %panel.11, f32[24,896]{1,0:T(8,128)} %terms.7.own, f32[24,768]{1,0:T(8,128)} %get-tuple-element.9.residual, f32[24,128]{1,0:T(8,128)} %add_add_fusion.2.norm), custom_call_target="tpu_custom_call" | custom-call | tf_op jit(solution)/shard_map/direction/pallas_call | solution.py:335
  (86 shorter events, 20.7 us)
Async XLA Ops:
  0.6 11.4 %copy-start.14 = (s32[4]{0:T(128)S(1)}, s32[4]{0:T(128)}, u32[]{:S(2)}) copy-start(s32[4]{0:T(128)} %constant.59.clone) | copy-start | bytes 52
  3.8 15.4 %copy-start.13 = (s32[4]{0:T(128)S(1)}, s32[4]{0:T(128)}, u32[]{:S(2)}) copy-start(s32[4]{0:T(128)} %constant.60.clone) | copy-start | bytes 52
  9.0 21.8 %collective-permute-start = (f32[24,2304]{1,0:T(8,128)}, f32[24,2304]{1,0:T(8,128)S(1)}, u32[]{:S(2)}, u32[]{:S(2)}) collective-permute-start(f32[24,2304]{1,0:T(8,128)} %scores.5), channel_id=1, source_target_pairs={{0,2},{2,0},{4,6},{6,4},{8,10},{10,8},{12,14},{14,12},{16,18},{18,... | collective-permute-start | bytes 663560 | tf_op jit(solution)/shard_map/ppermute | solution.py:39
  17.6 13.2 %collective-permute-start.1 = (f32[24,2304]{1,0:T(8,128)}, f32[24,2304]{1,0:T(8,128)S(1)}, u32[]{:S(2)}, u32[]{:S(2)}) collective-permute-start(f32[24,2304]{1,0:T(8,128)} %scores.6), channel_id=1, source_target_pairs={{0,4},{2,6},{4,0},{6,2},{8,12},{10,14},{12,8},{14,10},{16,20},{18,... | collective-permute-start | bytes 663560 | tf_op jit(solution)/shard_map/ppermute | solution.py:39
  19.7 25.1 %copy-start.9 = (s32[4]{0:T(128)S(1)}, s32[4]{0:T(128)}, u32[]{:S(2)}) copy-start(s32[4]{0:T(128)} %broadcast_xor_fusion.1.ids) | copy-start | bytes 52
  19.7 25.1 %copy-start.10 = (s32[4]{0:T(128)S(1)}, s32[4]{0:T(128)}, u32[]{:S(2)}) copy-start(s32[4]{0:T(128)} %broadcast_xor_fusion.ids) | copy-start | bytes 52
  19.7 25.1 %copy-start.11 = (s32[4]{0:T(128)S(1)}, s32[4]{0:T(128)}, u32[]{:S(2)}) copy-start(s32[4]{0:T(128)} %broadcast_xor_fusion.2.ids) | copy-start | bytes 52
  25.0 7.7 %collective-permute-start.2 = (f32[24,2304]{1,0:T(8,128)}, f32[24,2304]{1,0:T(8,128)S(1)}, u32[]{:S(2)}, u32[]{:S(2)}) collective-permute-start(f32[24,2304]{1,0:T(8,128)} %scores.7), channel_id=1, source_target_pairs={{0,6},{2,4},{4,2},{6,0},{8,14},{10,12},{12,10},{14,8},{16,22},{18,... | collective-permute-start | bytes 663560 | tf_op jit(solution)/shard_map/ppermute | solution.py:39
  25.6 19.2 %copy-start.12 = (s32[4]{0:T(128)S(1)}, s32[4]{0:T(128)}, u32[]{:S(2)}) copy-start(s32[4]{0:T(128)} %multiply_xor_fusion.ids) | copy-start | bytes 52
  33.8 4.8 %collective-permute-start.3 = (f32[24,768]{1,0:T(8,128)S(1)}, f32[24,768]{1,0:T(8,128)S(1)}, u32[]{:S(2)}, u32[]{:S(2)}) collective-permute-start(f32[24,768]{1,0:T(8,128)S(1)} %get-tuple-element.31), channel_id=1, source_target_pairs={{0,8},{2,10},{4,12},{6,14},{8,0},{10,2},{12,4},{14,6},{16,24},{18,... | collective-permute-start | bytes 221192 | tf_op jit(solution)/shard_map/ppermute | solution.py:39
  35.4 6.8 %collective-permute-start.4 = (f32[24,768]{1,0:T(8,128)S(1)}, f32[24,768]{1,0:T(8,128)S(1)}, u32[]{:S(2)}, u32[]{:S(2)}) collective-permute-start(f32[24,768]{1,0:T(8,128)S(1)} %get-tuple-element.32), channel_id=1, source_target_pairs={{0,16},{2,18},{4,20},{6,22},{8,24},{10,26},{12,28},{14,30},{16,0},... | collective-permute-start | bytes 221192 | tf_op jit(solution)/shard_map/ppermute | solution.py:39
  38.0 6.6 %collective-permute-start.5 = (f32[24,768]{1,0:T(8,128)S(1)}, f32[24,768]{1,0:T(8,128)S(1)}, u32[]{:S(2)}, u32[]{:S(2)}) collective-permute-start(f32[24,768]{1,0:T(8,128)S(1)} %concatenate.28), channel_id=1, source_target_pairs={{0,24},{2,26},{4,28},{6,30},{8,16},{10,18},{12,20},{14,22},{16,8},... | collective-permute-start | bytes 221192 | tf_op jit(solution)/shard_map/ppermute | solution.py:39
  44.7 15.5 %collective-permute-start.6 = (f32[24,512]{1,0:T(8,128)S(1)}, f32[24,512]{1,0:T(8,128)S(1)}, u32[]{:S(2)}, u32[]{:S(2)}) collective-permute-start(f32[24,512]{1,0:T(8,128)S(1)} %get-tuple-element.29), channel_id=1, source_target_pairs={{0,8},{2,10},{4,12},{6,14},{8,0},{10,2},{12,4},{14,6},{16,24},{18,... | collective-permute-start | bytes 147464 | tf_op jit(solution)/shard_map/ppermute | solution.py:39
  55.5 49.0 %collective-permute-start.19 = (f32[256,512]{1,0:T(8,128)}, f32[256,512]{1,0:T(8,128)S(1)}, u32[]{:S(2)}, u32[]{:S(2)}) collective-permute-start(f32[256,512]{1,0:T(8,128)} %get-tuple-element.17), channel_id=1, source_target_pairs={{0,2},{2,0},{4,6},{6,4},{8,10},{10,8},{12,14},{14,12},{16,18},{18,... | collective-permute-start | bytes 1572872 | tf_op jit(solution)/shard_map/ppermute | solution.py:39
  56.0 48.5 %collective-permute-start.20 = (f32[256,512]{1,0:T(8,128)}, f32[256,512]{1,0:T(8,128)S(1)}, u32[]{:S(2)}, u32[]{:S(2)}) collective-permute-start(f32[256,512]{1,0:T(8,128)} %get-tuple-element.18), channel_id=1, source_target_pairs={{0,4},{2,6},{4,0},{6,2},{8,12},{10,14},{12,8},{14,10},{16,20},{18,... | collective-permute-start | bytes 1572872 | tf_op jit(solution)/shard_map/ppermute | solution.py:39
  56.8 47.8 %collective-permute-start.21 = (f32[256,512]{1,0:T(8,128)}, f32[256,512]{1,0:T(8,128)S(1)}, u32[]{:S(2)}, u32[]{:S(2)}) collective-permute-start(f32[256,512]{1,0:T(8,128)} %get-tuple-element.19), channel_id=1, source_target_pairs={{0,6},{2,4},{4,2},{6,0},{8,14},{10,12},{12,10},{14,8},{16,22},{18,... | collective-permute-start | bytes 1572872 | tf_op jit(solution)/shard_map/ppermute | solution.py:39
  59.0 5.0 %collective-permute-start.7 = (f32[24,512]{1,0:T(8,128)S(1)}, f32[24,512]{1,0:T(8,128)S(1)}, u32[]{:S(2)}, u32[]{:S(2)}) collective-permute-start(f32[24,512]{1,0:T(8,128)S(1)} %get-tuple-element.29), channel_id=1, source_target_pairs={{0,16},{2,18},{4,20},{6,22},{8,24},{10,26},{12,28},{14,30},{16,0},... | collective-permute-start | bytes 147464 | tf_op jit(solution)/shard_map/ppermute | solution.py:39
  60.2 5.9 %collective-permute-start.8 = (f32[24,512]{1,0:T(8,128)S(1)}, f32[24,512]{1,0:T(8,128)S(1)}, u32[]{:S(2)}, u32[]{:S(2)}) collective-permute-start(f32[24,512]{1,0:T(8,128)S(1)} %get-tuple-element.29), channel_id=1, source_target_pairs={{0,24},{2,26},{4,28},{6,30},{8,16},{10,18},{12,20},{14,22},{16,8},... | collective-permute-start | bytes 147464 | tf_op jit(solution)/shard_map/ppermute | solution.py:39
  66.7 18.6 %copy-start.1 = (f32[24,2304]{1,0:T(8,128)}, f32[24,2304]{1,0:T(8,128)S(1)}, u32[]{:S(2)}) copy-start(f32[24,2304]{1,0:T(8,128)S(1)} %get-tuple-element.28.scores) | copy-start | bytes 663556
  66.7 17.0 %collective-permute-start.11 = (f32[24,2304]{1,0:T(8,128)S(1)}, f32[24,2304]{1,0:T(8,128)S(1)}, u32[]{:S(2)}, u32[]{:S(2)}) collective-permute-start(f32[24,2304]{1,0:T(8,128)S(1)} %get-tuple-element.28.scores), channel_id=1, source_target_pairs={{0,2},{2,0},{4,6},{6,4},{8,10},{10,8},{12,14},{14,12},{16,18},{18,... | collective-permute-start | bytes 663560 | tf_op jit(solution)/shard_map/ppermute | solution.py:39
  67.3 26.9 %collective-permute-start.10 = (f32[24,2304]{1,0:T(8,128)S(1)}, f32[24,2304]{1,0:T(8,128)S(1)}, u32[]{:S(2)}, u32[]{:S(2)}) collective-permute-start(f32[24,2304]{1,0:T(8,128)S(1)} %get-tuple-element.28.scores), channel_id=1, source_target_pairs={{0,4},{2,6},{4,0},{6,2},{8,12},{10,14},{12,8},{14,10},{16,20},{18,... | collective-permute-start | bytes 663560 | tf_op jit(solution)/shard_map/ppermute | solution.py:39
  83.7 15.7 %collective-permute-start.9 = (f32[24,2304]{1,0:T(8,128)S(1)}, f32[24,2304]{1,0:T(8,128)S(1)}, u32[]{:S(2)}, u32[]{:S(2)}) collective-permute-start(f32[24,2304]{1,0:T(8,128)S(1)} %get-tuple-element.28.scores), channel_id=1, source_target_pairs={{0,6},{2,4},{4,2},{6,0},{8,14},{10,12},{12,10},{14,8},{16,22},{18,... | collective-permute-start | bytes 663560 | tf_op jit(solution)/shard_map/ppermute | solution.py:39
  104.5 1.5 %collective-permute-start.12 = (f32[24,896]{1,0:T(8,128)}, f32[24,896]{1,0:T(8,128)S(1)}, u32[]{:S(2)}, u32[]{:S(2)}) collective-permute-start(f32[24,896]{1,0:T(8,128)} %terms.7.own), channel_id=1, source_target_pairs={{0,1},{1,0},{2,3},{3,2},{4,5},{5,4},{6,7},{7,6},{8,9},{9,8},{10,11... | collective-permute-start | bytes 258056 | tf_op jit(solution)/shard_map/ppermute | solution.py:39
  108.5 9.2 %collective-permute-start.13 = (f32[24,128]{1,0:T(8,128)}, f32[24,128]{1,0:T(8,128)S(1)}, u32[]{:S(2)}, u32[]{:S(2)}) collective-permute-start(f32[24,128]{1,0:T(8,128)} %get-tuple-element.14), channel_id=1, source_target_pairs={{0,2},{2,0},{4,6},{6,4},{8,10},{10,8},{12,14},{14,12},{16,18},{18,... | collective-permute-start | bytes 36872 | tf_op jit(solution)/shard_map/ppermute | solution.py:39
  108.6 9.2 %collective-permute-start.14 = (f32[24,128]{1,0:T(8,128)}, f32[24,128]{1,0:T(8,128)S(1)}, u32[]{:S(2)}, u32[]{:S(2)}) collective-permute-start(f32[24,128]{1,0:T(8,128)} %get-tuple-element.14), channel_id=1, source_target_pairs={{0,4},{2,6},{4,0},{6,2},{8,12},{10,14},{12,8},{14,10},{16,20},{18,... | collective-permute-start | bytes 36872 | tf_op jit(solution)/shard_map/ppermute | solution.py:39
  111.1 6.7 %collective-permute-start.15 = (f32[24,128]{1,0:T(8,128)}, f32[24,128]{1,0:T(8,128)S(1)}, u32[]{:S(2)}, u32[]{:S(2)}) collective-permute-start(f32[24,128]{1,0:T(8,128)} %get-tuple-element.14), channel_id=1, source_target_pairs={{0,6},{2,4},{4,2},{6,0},{8,14},{10,12},{12,10},{14,8},{16,22},{18,... | collective-permute-start | bytes 36872 | tf_op jit(solution)/shard_map/ppermute | solution.py:39
  112.7 10.1 %collective-permute-start.22 = (f32[64,512]{1,0:T(8,128)S(1)}, f32[64,512]{1,0:T(8,128)S(1)}, u32[]{:S(2)}, u32[]{:S(2)}) collective-permute-start(f32[64,512]{1,0:T(8,128)S(1)} %get-tuple-element.22), channel_id=1, source_target_pairs={{0,8},{2,10},{4,12},{6,14},{8,0},{10,2},{12,4},{14,6},{16,24},{18,... | collective-permute-start | bytes 393224 | tf_op jit(solution)/shard_map/ppermute | solution.py:39
  114.7 14.2 %collective-permute-start.23 = (f32[64,512]{1,0:T(8,128)S(1)}, f32[64,512]{1,0:T(8,128)S(1)}, u32[]{:S(2)}, u32[]{:S(2)}) collective-permute-start(f32[64,512]{1,0:T(8,128)S(1)} %get-tuple-element.21), channel_id=1, source_target_pairs={{0,16},{2,18},{4,20},{6,22},{8,24},{10,26},{12,28},{14,30},{16,0},... | collective-permute-start | bytes 393224 | tf_op jit(solution)/shard_map/ppermute | solution.py:39
  117.8 11.2 %collective-permute-start.24 = (f32[64,512]{1,0:T(8,128)S(1)}, f32[64,512]{1,0:T(8,128)S(1)}, u32[]{:S(2)}, u32[]{:S(2)}) collective-permute-start(f32[64,512]{1,0:T(8,128)S(1)} %get-tuple-element.20), channel_id=1, source_target_pairs={{0,24},{2,26},{4,28},{6,30},{8,16},{10,18},{12,20},{14,22},{16,8},... | collective-permute-start | bytes 393224 | tf_op jit(solution)/shard_map/ppermute | solution.py:39
  118.5 13.8 %collective-permute-start.16 = (f32[24,128]{1,0:T(8,128)S(1)}, f32[24,128]{1,0:T(8,128)S(1)}, u32[]{:S(2)}, u32[]{:S(2)}) collective-permute-start(f32[24,128]{1,0:T(8,128)S(1)} %add_add_fusion.3), channel_id=1, source_target_pairs={{0,8},{2,10},{4,12},{6,14},{8,0},{10,2},{12,4},{14,6},{16,24},{18,... | collective-permute-start | bytes 36872 | tf_op jit(solution)/shard_map/ppermute | solution.py:39
  119.0 13.2 %collective-permute-start.17 = (f32[24,128]{1,0:T(8,128)S(1)}, f32[24,128]{1,0:T(8,128)S(1)}, u32[]{:S(2)}, u32[]{:S(2)}) collective-permute-start(f32[24,128]{1,0:T(8,128)S(1)} %add_add_fusion.3), channel_id=1, source_target_pairs={{0,16},{2,18},{4,20},{6,22},{8,24},{10,26},{12,28},{14,30},{16,0},... | collective-permute-start | bytes 36872 | tf_op jit(solution)/shard_map/ppermute | solution.py:39
  122.9 9.4 %collective-permute-start.18 = (f32[24,128]{1,0:T(8,128)S(1)}, f32[24,128]{1,0:T(8,128)S(1)}, u32[]{:S(2)}, u32[]{:S(2)}) collective-permute-start(f32[24,128]{1,0:T(8,128)S(1)} %add_add_fusion.3), channel_id=1, source_target_pairs={{0,24},{2,26},{4,28},{6,30},{8,16},{10,18},{12,20},{14,22},{16,8},... | collective-permute-start | bytes 36872 | tf_op jit(solution)/shard_map/ppermute | solution.py:39
  (8 other events, 25.9 us)

commit v2 on v1

v2 whole, which is shorter than its diff:
```python
import dataclasses
import functools

import jax
import jax.numpy as jnp
from jax import lax
from jax.experimental import pallas as pl
from jax.experimental.pallas import tpu as pltpu
from jax.sharding import PartitionSpec as P


GENE_MAX = 400
LANES = 128
F32 = jnp.float32
BF16 = jnp.bfloat16
VMEM = pltpu.VMEM
NT = (((1,), (1,)), ((), ()))


def up(value, step):
    return -(-value // step) * step


def stages_of(count):
    found, stride = [], 1
    while stride < count:
        radix = 4 if count // stride % 4 == 0 else 2
        found.append((radix, stride))
        stride *= radix
    return found


def offsets_of(stages):
    found = [0]
    for radix, stride in stages:
        found = [base ^ (digit * stride) for base in found for digit in range(radix)]
    return found


def swap(array, count, offset, axis="samp"):
    return lax.ppermute(array, axis, [(i, i ^ offset) for i in range(count)])


def chunk_start(chunk, width, total):
    return pl.multiple_of(jnp.minimum(chunk * width, total - width), 16)


def fresh_lanes(chunk, width, total, rows):
    lane = lax.broadcasted_iota(jnp.int32, (rows, width), 1)
    return lane + jnp.minimum(chunk * width, total - width) >= chunk * width


def in_vmem(array):
    return pltpu.with_memory_space_constraint(array, pltpu.VMEM)


def fetch(copies):
    for copy in copies:
        copy.start()
    return copies


def geno_copies(plan, chunks, geno, held, sems):
    width, total = plan.width, plan.total
    return [
        pltpu.make_async_copy(
            geno.at[pl.ds(chunk_start(chunk, width, total), width), :],
            held.at[pl.ds(j * width, width), :],
            sems.at[j],
        )
        for j, chunk in enumerate(chunks)
    ]


def scores_body(plan, digit, me, ready, geno, variants, out, held, rows_held, sems):
    width, total = plan.width, plan.total
    chunks = [me ^ (digit * plan.stride) ^ r for r in plan.rest]
    copies = fetch(geno_copies(plan, chunks, geno, held, sems))
    share = rows_held.shape[0]
    quarter = (me // plan.stride % plan.radix) ^ digit
    rows_copy = pltpu.make_async_copy(
        variants.at[pl.ds(pl.multiple_of(quarter * share, 16), share), :], rows_held, sems.at[len(chunks)]
    )
    rows_copy.start()
    start_bf, weighted, stats = ready()
    for j, copy in enumerate(copies):
        copy.wait()
        part = lax.dot_general(
            start_bf, held[j * width : (j + 1) * width, :], NT, preferred_element_type=F32
        )
        part = jnp.where(fresh_lanes(chunks[j], width, total, part.shape[0]), part, 0.0)
        out[:, j * width : (j + 1) * width] = part
        lane = lax.broadcasted_iota(jnp.int32, stats.shape, 1)
        head = jnp.where((lane < 2) & (chunks[j] == plan.count - 1), stats, part[:, :LANES])
        out[:, j * width : j * width + LANES] = head
    rows_copy.wait()
    both = lax.dot_general(weighted, rows_held[...], NT, preferred_element_type=F32)
    high = both.shape[0] // 2
    out[:, len(chunks) * width :] = both[:high] + both[high:]


def lead_kernel(plan, digit, ratio, weights, panel, geno, variants, out, diag, start, start_bf, weighted, stats, *scratch):
    held, rows_held, panel_held, weights_held, sems, small = scratch
    first = fetch(
        [
            pltpu.make_async_copy(panel, panel_held, small.at[0]),
            pltpu.make_async_copy(weights, weights_held, small.at[1]),
        ]
    )

    def ready():
        for copy in first:
            copy.wait()
        mu = weights_held[...].reshape(1, weights_held.shape[0])
        whole = 1.0 / mu + ratio[0]
        right = panel_held[...]
        way = right / whole
        diag[0:1, :] = whole
        diag[1:2, :] = mu
        start[...] = way
        start_bf[...] = way.astype(BF16)
        exact = mu * way
        high = exact.astype(BF16)
        weighted[...] = jnp.concatenate([high, (exact - high.astype(F32)).astype(BF16)], axis=0)
        norm = jnp.sum(right * way, axis=1, keepdims=True)
        own = jnp.sum(way * (way / mu), axis=1, keepdims=True)
        lane = lax.broadcasted_iota(jnp.int32, stats.shape, 1)
        stats[...] = jnp.where(lane == 0, norm, jnp.where(lane == 1, own, 0.0))
        return start_bf[...], weighted[...], stats[...]

    scores_body(plan, digit, lax.axis_index("samp"), ready, geno, variants, out, held, rows_held, sems)


def scores_kernel(plan, digit, start_bf, weighted, stats, geno, variants, out, held, rows_held, sems):
    scores_body(
        plan,
        digit,
        lax.axis_index("samp"),
        lambda: (start_bf[...], weighted[...], stats[...]),
        geno,
        variants,
        out,
        held,
        rows_held,
        sems,
    )


def terms_kernel(plan, digit, ratio, scores, *refs):
    *before, geno, out, held, sems = refs
    width, total = plan.width, plan.total
    me = lax.axis_index("samp")
    samples = geno.shape[1]
    chunks = [me ^ (digit * plan.stride) ^ r for r in plan.rest]
    copies = fetch(geno_copies(plan, chunks, geno, held, sems))
    scale = ratio[0] / plan.markers
    terms = before[0][:, :samples] if before else jnp.zeros((out.shape[0], samples), F32)
    stats = before[0][:, samples:] if before else jnp.zeros((out.shape[0], LANES), F32)
    lane = lax.broadcasted_iota(jnp.int32, stats.shape, 1)
    for j, copy in enumerate(copies):
        raw = scores[:, j * width : (j + 1) * width]
        fresh = fresh_lanes(chunks[j], width, total, raw.shape[0])
        scaled = jnp.where(fresh, scale * raw, 0.0)
        square = jnp.sum(scaled * raw, axis=1, keepdims=True)
        stats = stats + jnp.where(lane == 2, square, jnp.where((lane < 2) & (chunks[j] == plan.count - 1), raw[:, :LANES], 0.0))
        copy.wait()
        terms = terms + jnp.dot(
            scaled.astype(BF16), held[j * width : (j + 1) * width, :], preferred_element_type=F32
        )
    out[:, :samples] = terms
    out[:, samples:] = stats


def update_kernel(diag, start, panel, own, other, solution, residual, norm, alpha_out):
    samples = start.shape[1]
    total = own[...] + other[...]
    start_norm = own[:, samples : samples + 1]
    curvature = own[:, samples + 1 : samples + 2] + total[:, samples + 2 : samples + 3]
    alpha = start_norm / curvature
    image = start[...] / diag[1:2, :] + total[:, :samples]
    left = panel[...] - alpha * image
    solution[...] = alpha * start[...]
    residual[...] = left
    norm[...] = jnp.broadcast_to(jnp.sum(left * (left / diag[0:1, :]), axis=1, keepdims=True), norm.shape)
    alpha_out[...] = jnp.broadcast_to(alpha, alpha_out.shape)


def direction_kernel(diag, start, own, residual, *refs):
    *norms, out = refs
    samples = start.shape[1]
    total = norms[0][:, :1]
    for ref in norms[1:]:
        total = total + ref[:, :1]
    start_norm = own[:, samples : samples + 1]
    out[...] = residual[...] / diag[0:1, :] + (total / start_norm) * start[...]


def genes_of(sizes, index):
    gene = jnp.zeros(index.shape, jnp.int32)
    end = jnp.int32(0)
    for g in range(sizes.shape[1]):
        end = end + sizes[0, g]
        gene = gene + (end <= index).astype(jnp.int32)
    return gene


def cross_kernel(plan, block, span, sizes, weights, variants, *refs):
    *outs, scaled = refs
    me = lax.axis_index("samp")
    count = variants.shape[0]
    mu = weights[...].reshape(1, weights.shape[0])
    cols = genes_of(sizes, lax.broadcasted_iota(jnp.int32, (1, count), 1))
    row = lax.broadcasted_iota(jnp.int32, (block, LANES), 0)
    for digit, out in enumerate(outs):
        places = []
        for j, r in enumerate(plan.rest):
            first = pl.multiple_of((me ^ (digit * plan.stride) ^ r) * block, block)
            mine = variants[pl.ds(first, block), :]
            scaled[j * block : (j + 1) * block, :] = (mine.astype(F32) * mu).astype(BF16)
            places.append(first + row)
        cross = lax.dot_general(scaled[...], variants[...], NT, preferred_element_type=F32)
        rows = genes_of(sizes, jnp.concatenate(places, axis=0))[:, :1]
        cross = jnp.where(rows == cols, cross, 0.0)
        folded = cross[:, :span]
        for low in range(span, count, span):
            folded = folded + cross[:, low : low + span]
        out[...] = folded


def gram_kernel(plan, samples, sizes, alpha, *refs):
    *parts, out, full = refs
    arrays, sums = parts[: plan.radix], parts[plan.radix :]
    me = lax.axis_index("samp")
    count = out.shape[2]
    block = out.shape[1]
    share = count // plan.radix
    for digit, ref in enumerate(arrays):
        quarter = (me // plan.stride % plan.radix) ^ digit
        full[:, pl.ds(pl.multiple_of(quarter * share, LANES), share)] = ref[:, -share:] * alpha[:, :1]
    cross = sums[0][...]
    for ref in sums[1:]:
        cross = cross + ref[...]
    first = me * block
    window = max(block, LANES)
    base = pl.multiple_of(first // window * window, window)
    wide = lax.dot_general(
        full[:, pl.ds(base, window)],
        full[...],
        (((0,), (0,)), ((), ())),
        precision=lax.Precision.HIGHEST,
        preferred_element_type=F32,
    )
    correction = wide[:block]
    for step in range(1, window // block):
        correction = jnp.where(first - base == step * block, wide[step * block : (step + 1) * block], correction)
    cols = genes_of(sizes, lax.broadcasted_iota(jnp.int32, (1, count), 1))
    rows = genes_of(sizes, first + lax.broadcasted_iota(jnp.int32, (block, LANES), 0))[:, :1]
    span = cross.shape[1]
    for low in range(0, count, span):
        piece = (cross - correction[:, low : low + span]) / samples
        out[0, :, low : low + span] = jnp.where(rows == cols[:, low : low + span], piece, 0.0)


@dataclasses.dataclass(frozen=True)
class Plan:
    count: int
    radix: int
    stride: int
    rest: tuple
    width: int
    total: int
    markers: int


def tied(array, *others):
    return lax.optimization_barrier((array, *others))[0]


def body(genotypes, variants, weights, variance_ratio, panel, gene_sizes):
    count = lax.axis_size("samp")
    marks = lax.axis_size("mark")
    stages = stages_of(count)
    (radix, stride), later = stages[0], stages[1:]
    firsts = [digit * stride for digit in range(radix)]
    rest = offsets_of(later)
    local, samples = genotypes.shape
    width = up(-(-local // count), LANES)
    if count * width - local < 2:
        width += LANES
    plan = Plan(count, radix, stride, tuple(rest), width, local, local * marks)
    num_variants = variants.shape[0]
    share = num_variants // radix
    rows = panel.shape[0]
    vmem = pl.BlockSpec(memory_space=VMEM)
    smem = pl.BlockSpec(memory_space=pltpu.SMEM)
    hbm = pl.BlockSpec(memory_space=pl.ANY)
    columns = len(rest) * width
    window = VMEM((columns, samples), BF16)
    sems = pltpu.SemaphoreType.DMA((len(rest) + 1,))
    rows_held = VMEM((share, samples), BF16)
    payload = VMEM((rows, columns + share), F32)

    lead = radix - 1
    sent = {}
    sent[lead], diag, start, start_bf, weighted, stats = pl.pallas_call(
        functools.partial(lead_kernel, plan, lead),
        out_shape=[
            payload,
            VMEM((8, samples), F32),
            VMEM((rows, samples), F32),
            VMEM((rows, samples), BF16),
            VMEM((2 * rows, samples), BF16),
            VMEM((rows, LANES), F32),
        ],
        in_specs=[smem] + [hbm] * 4,
        out_specs=[vmem] * 6,
        scratch_shapes=[
            window,
            rows_held,
            VMEM((rows, samples), F32),
            VMEM((samples,), F32),
            sems,
            pltpu.SemaphoreType.DMA((2,)),
        ],
        name="scores_lead",
    )(variance_ratio, weights, panel, genotypes, variants)
    diag, start = in_vmem(diag), in_vmem(start)
    after = sent[lead]
    for d in (*range(1, lead), 0):
        start_bf, after = lax.optimization_barrier((start_bf, after))
        sent[d] = pl.pallas_call(
            functools.partial(scores_kernel, plan, d),
            out_shape=payload,
            in_specs=[vmem] * 3 + [hbm] * 2,
            out_specs=vmem,
            scratch_shapes=[window, rows_held, sems],
            name="scores",
        )(in_vmem(start_bf), in_vmem(weighted), in_vmem(stats), genotypes, variants)
        after = sent[d]

    block = num_variants // count
    span = up(GENE_MAX, LANES)
    if num_variants % span or num_variants <= span:
        span = num_variants
    crosses = list(
        pl.pallas_call(
            functools.partial(cross_kernel, plan, block, span),
            out_shape=[jax.ShapeDtypeStruct((block * len(rest), span), F32)] * radix,
            in_specs=[smem] + [vmem] * 2,
            out_specs=[vmem] * radix,
            scratch_shapes=[VMEM((block * len(rest), samples), BF16)],
            name="cross",
        )(gene_sizes, weights, tied(variants, sent[0]))
    )

    got = sent[0]
    for d in range(1, radix):
        got = got + swap(sent[d], count, firsts[d])
    got, crosses[0] = lax.optimization_barrier((got, crosses[0]))
    near = [swap(tied(crosses[d], got), count, firsts[d]) for d in range(1, lead)]
    shared, got = got[:, -share:], got[:, :-share]
    for r, s in later:
        wide = got.shape[1] // r
        pieces = [jnp.concatenate([got[:, d * wide : (d + 1) * wide], shared], axis=1) for d in range(r)]
        total = pieces[0]
        for d in range(1, r):
            total = total + swap(pieces[d], count, d * s)
        got, shared = total[:, :wide], total[:, wide:]
    for r, s in reversed(later):
        got = jnp.concatenate([got] + [swap(got, count, d * s) for d in range(1, r)], axis=1)
    everything = jnp.concatenate([got, shared], axis=1)
    arrays = [in_vmem(everything)] + [in_vmem(swap(everything, count, firsts[d])) for d in range(1, radix)]

    own = ()
    for d in range(radix):
        whole = pl.pallas_call(
            functools.partial(terms_kernel, plan, d),
            out_shape=VMEM((rows, samples + LANES), F32),
            in_specs=[smem, vmem] + [vmem] * len(own) + [hbm],
            out_specs=vmem,
            scratch_shapes=[window, sems],
            name="terms",
        )(variance_ratio, arrays[d], *map(in_vmem, own), genotypes)
        own = (whole,)
    (held,) = own
    assert marks & (marks - 1) == 0
    other = None
    offset = 1
    while offset < marks:
        other = swap(held, marks, offset, "mark")
        offset *= 2
        if offset < marks:
            kept = held[:, samples : samples + 2]
            held = held + other
            held = jnp.concatenate([held[:, :samples], kept, held[:, samples + 2 :]], axis=1)
    held = in_vmem(held)
    flat = VMEM((rows, LANES), F32)
    full = jax.ShapeDtypeStruct((rows, samples), F32)
    solution, residual, norm, alpha = pl.pallas_call(
        update_kernel,
        out_shape=[VMEM((rows, samples), F32)] * 2 + [flat] * 2,
        in_specs=[vmem] * 5,
        out_specs=[vmem] * 4,
        name="update",
    )(diag, start, panel, held, in_vmem(other))
    norms = [norm]
    for r, s in stages:
        total = norms[0]
        for one in norms[1:]:
            total = total + one
        norms = [total] + [swap(total, count, d * s) for d in range(1, r)]
    direction = pl.pallas_call(
        direction_kernel,
        out_shape=full,
        in_specs=[vmem] * (4 + len(norms)),
        out_specs=vmem,
        name="direction",
    )(diag, start, held, in_vmem(residual), *map(in_vmem, norms))

    far = swap(crosses[lead], count, firsts[lead])
    sums = [crosses[0], *near, far]
    for r, s in later:
        total = sums[0]
        for one in sums[1:]:
            total = total + one
        tall = total.shape[0] // r
        sums = [total[:tall]] + [swap(total[d * tall : (d + 1) * tall], count, d * s) for d in range(1, r)]
    gram = pl.pallas_call(
        functools.partial(gram_kernel, plan, samples * count),
        out_shape=jax.ShapeDtypeStruct((1, block, num_variants), F32),
        in_specs=[smem] + [vmem] * (1 + radix + len(sums)),
        out_specs=vmem,
        scratch_shapes=[VMEM((rows, num_variants), F32)],
        name="gram",
    )(gene_sizes, in_vmem(alpha), *arrays, *map(in_vmem, sums))
    return solution, residual, direction, gram


def solution(mesh):
    return jax.shard_map(
        body,
        mesh=mesh,
        in_specs=(
            P("mark", "samp"),
            P("mark", "samp"),
            P("samp"),
            P(),
            P(None, "samp"),
            P("mark", None),
        ),
        out_specs=(P(None, "samp"), P(None, "samp"), P(None, "samp"), P("mark", "samp", None)),
        check_vma=False,
    )
```

time: 136 us -> 108 us (0.79)
  Pallas kernels: 55.1 us -> 29.7 us
  waiting for transfers between devices: 27.2 us -> 36.6 us
  local copies, waits for them, and re-layouts: 10.7 us -> 1.35 us
  other arithmetic: 5.94 us -> 1.54 us
  starting transfers between devices: 34.1 us -> 36.8 us
    pallas_call x12, Pallas kernels: 55.1 us -> 29.7 us  [the longest x3 9.02 us: body(): pl.pallas_call(functools.partial(scores_kernel, plan, d), out_shape=paylo...]
    ppermute x25, waiting for transfers between devices: 27.2 us -> 36.6 us  [swap(): return lax.ppermute(array, axis, [(i, i ^ offset) for i in range(count)])]
    slice x4 -> x1, local copies, waits for them, and re-layouts: 4.7 us -> 0.04 us  [body(): total[d * tall:(d + 1) * tall]]
    xor x4 -> x0, other arithmetic: 2.79 us -> none  [body(): me ^ jnp.array([first ^ r for r in rest], jnp.int32)]
    ppermute x25, starting transfers between devices: 34.1 us -> 36.8 us  [swap(): return lax.ppermute(array, axis, [(i, i ^ offset) for i in range(count)])]
    unnamed x33 -> x7, local copies, waits for them, and re-layouts: 2.76 us -> 1.28 us
  transfers between devices with their start and end apart: 25 -> 25, of which waited for: 8 -> 11; matrix products, arithmetic and copies ran while one was open for 7% -> 3% of each run, Pallas kernels for 34% -> 17%
where the time goes in v2:
time: 108 us; the launch traced here: 107 us
  starting transfers between devices  36.8 us (34%)
  waiting for transfers between devices  36.6 us (34%)
  Pallas kernels  29.7 us (28%)
  other arithmetic  1.54 us (1%)
  between operations  1.48 us (1%)
  local copies, waits for them, and re-layouts  1.35 us (1%)
    ppermute x25, starting transfers between devices, swap(): return lax.ppermute(array, axis, [(i, i ^ offset) for i in range(count)])  36.8 us
    ppermute x25, waiting for transfers between devices, swap(): return lax.ppermute(array, axis, [(i, i ^ offset) for i in range(count)])  36.6 us
    pallas_call x3, Pallas kernels, body(): pl.pallas_call(functools.partial(scores_kernel, plan, d), out_shape=paylo...  9.02 us
    pallas_call x4, Pallas kernels, body(): pl.pallas_call(functools.partial(terms_kernel, plan, d), out_shape=VMEM((...  8.69 us
    pallas_call x1, Pallas kernels, body(): pl.pallas_call(functools.partial(cross_kernel, plan, block, span), out_sh...  4.94 us
    pallas_call x1, Pallas kernels, body(): pl.pallas_call(functools.partial(lead_kernel, plan, lead), out_shape=[pay...  3.08 us
  transfers between devices with their start and end apart: 25, of which 11 were waited for; matrix products, arithmetic and copies ran while one was open for 3% of the time, Pallas kernels for 17%

profile of v2, /device:TPU:0, one launch (start us, length us, event | category | flops | bytes accessed | tf_op | source)
XLA Modules:
  0.0 107.4 jit_solution(15033666649129138618)
XLA Ops:
  1.3 3.1 %scores_lead.1 = (f32[24,2304]{1,0:T(8,128)S(1)}, f32[8,768]{1,0:T(8,128)S(1)}, f32[24,768]{1,0:T(8,128)S(1)}, bf16[24,768]{1,0:T(8,128)(2,1)S(1)}, bf16[48,768]{1,0:T(8,128)(2,1)S(1)}, /*index=5*/f32[24,128]{1,0:T(8,128)S(1)}) custom-call(f32[1]{0:T(128)S(6)} %copy.16.ratio, f32[768]{0:T(1024)} %weights.3, f32[24,768]{1,0:T(8,128)} %panel.3, ...), custom_call_target="tpu_custom_call" | custom-call | tf_op jit(solution)/shard_map/scores_lead/pallas_call | solution.py:305
  4.4 3.0 %scores.3 = f32[24,2304]{1,0:T(8,128)S(1)} custom-call(bf16[24,768]{1,0:T(8,128)(2,1)S(1)} %get-tuple-element.34.start_bf, bf16[48,768]{1,0:T(8,128)(2,1)S(1)} %get-tuple-element.31.weighted, f32[24,128]{1,0:T(8,128)S(1)} %get-tuple-element.32.stats, bf16[8000,768]{1,0:T(8,128)(2,1)} %refs_1_.5, bf16[1024,768]{1,0:T(8,128)(2,1)} %variants.8), custom_call_target="tpu_custom_call" | custom-call | tf_op jit(solution)/shard_map/scores/pallas_call | solution.py:331
  7.4 3.0 %scores.4 = f32[24,2304]{1,0:T(8,128)S(1)} custom-call(bf16[24,768]{1,0:T(8,128)(2,1)S(1)} %get-tuple-element.34.start_bf, bf16[48,768]{1,0:T(8,128)(2,1)S(1)} %get-tuple-element.31.weighted, f32[24,128]{1,0:T(8,128)S(1)} %get-tuple-element.32.stats, bf16[8000,768]{1,0:T(8,128)(2,1)} %refs_1_.5, bf16[1024,768]{1,0:T(8,128)(2,1)} %variants.8), custom_call_target="tpu_custom_call" | custom-call | tf_op jit(solution)/shard_map/scores/pallas_call | solution.py:331
  10.4 3.1 %collective-permute-start.1 = (f32[24,2304]{1,0:T(8,128)S(1)}, f32[24,2304]{1,0:T(8,128)S(1)}, u32[]{:S(2)}, u32[]{:S(2)}) collective-permute-start(f32[24,2304]{1,0:T(8,128)S(1)} %scores.4), channel_id=1, source_target_pairs={{0,4},{2,6},{4,0},{6,2},{8,12},{10,14},{12,8},{14,10},{16,20},{18,... | collective-permute-start | bytes 663560 | tf_op jit(solution)/shard_map/ppermute | solution.py:41
  13.5 1.5 %collective-permute-start = (f32[24,2304]{1,0:T(8,128)S(1)}, f32[24,2304]{1,0:T(8,128)S(1)}, u32[]{:S(2)}, u32[]{:S(2)}) collective-permute-start(f32[24,2304]{1,0:T(8,128)S(1)} %scores.3), channel_id=1, source_target_pairs={{0,2},{2,0},{4,6},{6,4},{8,10},{10,8},{12,14},{14,12},{16,18},{18,... | collective-permute-start | bytes 663560 | tf_op jit(solution)/shard_map/ppermute | solution.py:41
  15.0 3.0 %scores.5 = f32[24,2304]{1,0:T(8,128)S(1)} custom-call(bf16[24,768]{1,0:T(8,128)(2,1)S(1)} %get-tuple-element.34.start_bf, bf16[48,768]{1,0:T(8,128)(2,1)S(1)} %get-tuple-element.31.weighted, f32[24,128]{1,0:T(8,128)S(1)} %get-tuple-element.32.stats, bf16[8000,768]{1,0:T(8,128)(2,1)} %refs_1_.5, bf16[1024,768]{1,0:T(8,128)(2,1)} %variants.8), custom_call_target="tpu_custom_call" | custom-call | tf_op jit(solution)/shard_map/scores/pallas_call | solution.py:331
  18.0 4.9 %cross.1 = (f32[256,512]{1,0:T(8,128)}, f32[256,512]{1,0:T(8,128)}, f32[256,512]{1,0:T(8,128)}, f32[256,512]{1,0:T(8,128)}) custom-call(s32[1,24]{1,0:T(1,128)} %sizes.3, f32[768]{0:T(1024)} %weights.3, bf16[1024,768]{1,0:T(8,128)(2,1)} %variants.8), custom_call_target="tpu_custom_call" | custom-call | tf_op jit(solution)/shard_map/cross/pallas_call | solution.py:346
  23.0 1.9 %collective-permute-done.2 = f32[24,2304]{1,0:T(8,128)S(1)} collective-permute-done((f32[24,2304]{1,0:T(8,128)S(1)}, f32[24,2304]{1,0:T(8,128)S(1)}, u32[]{:S(2)}, u32[]{:S(2)}) %collective-permute-start.2) | collective-permute-done | bytes 221216 | tf_op jit(solution)/shard_map/ppermute | solution.py:41
  25.0 1.8 %collective-permute-start.3 = (f32[24,768]{1,0:T(8,128)S(1)}, f32[24,768]{1,0:T(8,128)S(1)}, u32[]{:S(2)}, u32[]{:S(2)}) collective-permute-start(f32[24,768]{1,0:T(8,128)S(1)} %get-tuple-element.57), channel_id=1, source_target_pairs={{0,8},{2,10},{4,12},{6,14},{8,0},{10,2},{12,4},{14,6},{16,24},{18,... | collective-permute-start | bytes 221192 | tf_op jit(solution)/shard_map/ppermute | solution.py:41
  26.8 2.6 %collective-permute-start.4 = (f32[24,768]{1,0:T(8,128)S(1)}, f32[24,768]{1,0:T(8,128)S(1)}, u32[]{:S(2)}, u32[]{:S(2)}) collective-permute-start(f32[24,768]{1,0:T(8,128)S(1)} %get-tuple-element.58), channel_id=1, source_target_pairs={{0,16},{2,18},{4,20},{6,22},{8,24},{10,26},{12,28},{14,30},{16,0},... | collective-permute-start | bytes 221192 | tf_op jit(solution)/shard_map/ppermute | solution.py:41
  30.2 3.5 %collective-permute-done.4 = f32[24,768]{1,0:T(8,128)S(1)} collective-permute-done((f32[24,768]{1,0:T(8,128)S(1)}, f32[24,768]{1,0:T(8,128)S(1)}, u32[]{:S(2)}, u32[]{:S(2)}) %collective-permute-start.4) | collective-permute-done | bytes 73760 | tf_op jit(solution)/shard_map/ppermute | solution.py:41
  33.6 2.1 %collective-permute-done.5 = f32[24,768]{1,0:T(8,128)S(1)} collective-permute-done((f32[24,768]{1,0:T(8,128)S(1)}, f32[24,768]{1,0:T(8,128)S(1)}, u32[]{:S(2)}, u32[]{:S(2)}) %collective-permute-start.5) | collective-permute-done | bytes 73760 | tf_op jit(solution)/shard_map/ppermute | solution.py:41
  35.8 1.8 %collective-permute-start.7 = (f32[24,512]{1,0:T(8,128)S(1)}, f32[24,512]{1,0:T(8,128)S(1)}, u32[]{:S(2)}, u32[]{:S(2)}) collective-permute-start(f32[24,512]{1,0:T(8,128)S(1)} %get-tuple-element.55), channel_id=1, source_target_pairs={{0,16},{2,18},{4,20},{6,22},{8,24},{10,26},{12,28},{14,30},{16,0},... | collective-permute-start | bytes 147464 | tf_op jit(solution)/shard_map/ppermute | solution.py:41
  37.6 2.6 %collective-permute-start.8 = (f32[24,512]{1,0:T(8,128)S(1)}, f32[24,512]{1,0:T(8,128)S(1)}, u32[]{:S(2)}, u32[]{:S(2)}) collective-permute-start(f32[24,512]{1,0:T(8,128)S(1)} %get-tuple-element.55), channel_id=1, source_target_pairs={{0,24},{2,26},{4,28},{6,30},{8,16},{10,18},{12,20},{14,22},{16,8},... | collective-permute-start | bytes 147464 | tf_op jit(solution)/shard_map/ppermute | solution.py:41
  40.9 2.6 %collective-permute-done.8 = f32[24,512]{1,0:T(8,128)S(1)} collective-permute-done((f32[24,512]{1,0:T(8,128)S(1)}, f32[24,512]{1,0:T(8,128)S(1)}, u32[]{:S(2)}, u32[]{:S(2)}) %collective-permute-start.8) | collective-permute-done | bytes 49184 | tf_op jit(solution)/shard_map/ppermute | solution.py:41
  43.5 1.6 %collective-permute-start.11 = (f32[24,2304]{1,0:T(8,128)S(1)}, f32[24,2304]{1,0:T(8,128)S(1)}, u32[]{:S(2)}, u32[]{:S(2)}) collective-permute-start(f32[24,2304]{1,0:T(8,128)S(1)} %slice_dynamic-update-slice_fusion.scores.refs_0_), channel_id=1, source_target_pairs={{0,2},{2,0},{4,6},{6,4},{8,10},{10,8},{12,14},{14,12},{16,18},{18,... | collective-permute-start | bytes 663560 | tf_op jit(solution)/shard_map/ppermute | solution.py:41
  45.0 1.5 %collective-permute-start.21 = (f32[256,512]{1,0:T(8,128)}, f32[256,512]{1,0:T(8,128)S(1)}, u32[]{:S(2)}, u32[]{:S(2)}) collective-permute-start(f32[256,512]{1,0:T(8,128)} %get-tuple-element.47), channel_id=1, source_target_pairs={{0,6},{2,4},{4,2},{6,0},{8,14},{10,12},{12,10},{14,8},{16,22},{18,... | collective-permute-start | bytes 1572872 | tf_op jit(solution)/shard_map/ppermute | solution.py:41
  46.5 1.5 %collective-permute-start.19 = (f32[256,512]{1,0:T(8,128)}, f32[256,512]{1,0:T(8,128)}, u32[]{:S(2)}, u32[]{:S(2)}) collective-permute-start(f32[256,512]{1,0:T(8,128)} %get-tuple-element.44), channel_id=1, source_target_pairs={{0,2},{2,0},{4,6},{6,4},{8,10},{10,8},{12,14},{14,12},{16,18},{18,... | collective-permute-start | bytes 1572872 | tf_op jit(solution)/shard_map/ppermute | solution.py:41
  48.5 1.5 %collective-permute-start.10 = (f32[24,2304]{1,0:T(8,128)S(1)}, f32[24,2304]{1,0:T(8,128)S(1)}, u32[]{:S(2)}, u32[]{:S(2)}) collective-permute-start(f32[24,2304]{1,0:T(8,128)S(1)} %slice_dynamic-update-slice_fusion.scores.refs_0_), channel_id=1, source_target_pairs={{0,4},{2,6},{4,0},{6,2},{8,12},{10,14},{12,8},{14,10},{16,20},{18,... | collective-permute-start | bytes 663560 | tf_op jit(solution)/shard_map/ppermute | solution.py:41
  50.1 1.8 %collective-permute-done.11.scores.refs_1_ = f32[24,2304]{1,0:T(8,128)S(1)} collective-permute-done((f32[24,2304]{1,0:T(8,128)S(1)}, f32[24,2304]{1,0:T(8,128)S(1)}, u32[]{:S(2)}, u32[]{:S(2)}) %collective-permute-start.11) | collective-permute-done | bytes 221216 | tf_op jit(solution)/shard_map/ppermute | solution.py:41
  51.9 2.4 %collective-permute-start.9 = (f32[24,2304]{1,0:T(8,128)S(1)}, f32[24,2304]{1,0:T(8,128)S(1)}, u32[]{:S(2)}, u32[]{:S(2)}) collective-permute-start(f32[24,2304]{1,0:T(8,128)S(1)} %slice_dynamic-update-slice_fusion.scores.refs_0_), channel_id=1, source_target_pairs={{0,6},{2,4},{4,2},{6,0},{8,14},{10,12},{12,10},{14,8},{16,22},{18,... | collective-permute-start | bytes 663560 | tf_op jit(solution)/shard_map/ppermute | solution.py:41
  54.3 2.2 %terms.4.refs_0_ = f32[24,896]{1,0:T(8,128)S(1)} custom-call(f32[1]{0:T(128)S(6)} %copy.16.ratio, f32[24,2304]{1,0:T(8,128)S(1)} %slice_dynamic-update-slice_fusion.scores.refs_0_, bf16[8000,768]{1,0:T(8,128)(2,1)} %refs_1_.5), custom_call_target="tpu_custom_call" | custom-call | tf_op jit(solution)/shard_map/terms/pallas_call | solution.py:376
  56.5 2.2 %terms.5.refs_0_ = f32[24,896]{1,0:T(8,128)S(1)} custom-call(f32[1]{0:T(128)S(6)} %copy.16.ratio, f32[24,2304]{1,0:T(8,128)S(1)} %collective-permute-done.11.scores.refs_1_, f32[24,896]{1,0:T(8,128)S(1)} %terms.4.refs_0_, bf16[8000,768]{1,0:T(8,128)(2,1)} %refs_1_.5), custom_call_target="tpu_custom_call" | custom-call | tf_op jit(solution)/shard_map/terms/pallas_call | solution.py:376
  58.7 18.6 %collective-permute-done.10.scores.refs_2_ = f32[24,2304]{1,0:T(8,128)S(1)} collective-permute-done((f32[24,2304]{1,0:T(8,128)S(1)}, f32[24,2304]{1,0:T(8,128)S(1)}, u32[]{:S(2)}, u32[]{:S(2)}) %collective-permute-start.10) | collective-permute-done | bytes 221216 | tf_op jit(solution)/shard_map/ppermute | solution.py:41
  77.2 2.2 %terms.6.refs_0_ = f32[24,896]{1,0:T(8,128)S(1)} custom-call(f32[1]{0:T(128)S(6)} %copy.16.ratio, f32[24,2304]{1,0:T(8,128)S(1)} %collective-permute-done.10.scores.refs_2_, f32[24,896]{1,0:T(8,128)S(1)} %terms.5.refs_0_, bf16[8000,768]{1,0:T(8,128)(2,1)} %refs_1_.5), custom_call_target="tpu_custom_call" | custom-call | tf_op jit(solution)/shard_map/terms/pallas_call | solution.py:376
  79.4 2.2 %terms.7.own = f32[24,896]{1,0:T(8,128)S(1)} custom-call(f32[1]{0:T(128)S(6)} %copy.16.ratio, f32[24,2304]{1,0:T(8,128)S(1)} %collective-permute-done.9.scores.refs_3_, f32[24,896]{1,0:T(8,128)S(1)} %terms.6.refs_0_, bf16[8000,768]{1,0:T(8,128)(2,1)} %refs_1_.5), custom_call_target="tpu_custom_call" | custom-call | tf_op jit(solution)/shard_map/terms/pallas_call | solution.py:376
  85.7 1.9 %collective-permute-start.15 = (f32[24,128]{1,0:T(8,128)S(1)}, f32[24,128]{1,0:T(8,128)S(1)}, u32[]{:S(2)}, u32[]{:S(2)}) collective-permute-start(f32[24,128]{1,0:T(8,128)S(1)} %get-tuple-element.40), channel_id=1, source_target_pairs={{0,6},{2,4},{4,2},{6,0},{8,14},{10,12},{12,10},{14,8},{16,22},{18,... | collective-permute-start | bytes 36872 | tf_op jit(solution)/shard_map/ppermute | solution.py:41
  89.2 3.3 %collective-permute-start.23 = (f32[64,512]{1,0:T(8,128)S(1)}, f32[64,512]{1,0:T(8,128)S(1)}, u32[]{:S(2)}, u32[]{:S(2)}) collective-permute-start(f32[64,512]{1,0:T(8,128)S(1)} %get-tuple-element.49), channel_id=1, source_target_pairs={{0,16},{2,18},{4,20},{6,22},{8,24},{10,26},{12,28},{14,30},{16,0},... | collective-permute-start | bytes 393224 | tf_op jit(solution)/shard_map/ppermute | solution.py:41
  93.7 3.3 %collective-permute-start.17 = (f32[24,128]{1,0:T(8,128)S(1)}, f32[24,128]{1,0:T(8,128)S(1)}, u32[]{:S(2)}, u32[]{:S(2)}) collective-permute-start(f32[24,128]{1,0:T(8,128)S(1)} %add_add_fusion.2.refs_0_), channel_id=1, source_target_pairs={{0,16},{2,18},{4,20},{6,22},{8,24},{10,26},{12,28},{14,30},{16,0},... | collective-permute-start | bytes 36872 | tf_op jit(solution)/shard_map/ppermute | solution.py:41
  97.8 2.9 %collective-permute-start.18 = (f32[24,128]{1,0:T(8,128)S(1)}, f32[24,128]{1,0:T(8,128)S(1)}, u32[]{:S(2)}, u32[]{:S(2)}) collective-permute-start(f32[24,128]{1,0:T(8,128)S(1)} %add_add_fusion.2.refs_0_), channel_id=1, source_target_pairs={{0,24},{2,26},{4,28},{6,30},{8,16},{10,18},{12,20},{14,22},{16,8},... | collective-permute-start | bytes 36872 | tf_op jit(solution)/shard_map/ppermute | solution.py:41
  101.9 2.7 %collective-permute-done.17.refs_2_ = f32[24,128]{1,0:T(8,128)S(1)} collective-permute-done((f32[24,128]{1,0:T(8,128)S(1)}, f32[24,128]{1,0:T(8,128)S(1)}, u32[]{:S(2)}, u32[]{:S(2)}) %collective-permute-start.17) | collective-permute-done | bytes 12320 | tf_op jit(solution)/shard_map/ppermute | solution.py:41
  105.3 2.1 %gram.1 = f32[1,64,1024]{2,1,0:T(8,128)} custom-call(s32[1,24]{1,0:T(1,128)} %sizes.3, f32[24,128]{1,0:T(8,128)S(1)} %get-tuple-element.41.alpha, f32[24,2304]{1,0:T(8,128)S(1)} %slice_dynamic-update-slice_fusion.scores.refs_0_, f32[24,2304]{1,0:T(8,128)S(1)} %collective-permute-done.11.scores.refs_1_, ...), custom_call_target="tpu_custom_call" | custom-call | tf_op jit(solution)/shard_map/gram/pallas_call | solution.py:428
  (48 shorter events, 11.8 us)
Async XLA Ops:
  10.4 12.6 %collective-permute-start.1 = (f32[24,2304]{1,0:T(8,128)S(1)}, f32[24,2304]{1,0:T(8,128)S(1)}, u32[]{:S(2)}, u32[]{:S(2)}) collective-permute-start(f32[24,2304]{1,0:T(8,128)S(1)} %scores.4), channel_id=1, source_target_pairs={{0,4},{2,6},{4,0},{6,2},{8,12},{10,14},{12,8},{14,10},{16,20},{18,... | collective-permute-start | bytes 663560 | tf_op jit(solution)/shard_map/ppermute | solution.py:41
  13.5 9.5 %collective-permute-start = (f32[24,2304]{1,0:T(8,128)S(1)}, f32[24,2304]{1,0:T(8,128)S(1)}, u32[]{:S(2)}, u32[]{:S(2)}) collective-permute-start(f32[24,2304]{1,0:T(8,128)S(1)} %scores.3), channel_id=1, source_target_pairs={{0,2},{2,0},{4,6},{6,4},{8,10},{10,8},{12,14},{14,12},{16,18},{18,... | collective-permute-start | bytes 663560 | tf_op jit(solution)/shard_map/ppermute | solution.py:41
  15.0 9.9 %collective-permute-start.2 = (f32[24,2304]{1,0:T(8,128)S(1)}, f32[24,2304]{1,0:T(8,128)S(1)}, u32[]{:S(2)}, u32[]{:S(2)}) collective-permute-start(f32[24,2304]{1,0:T(8,128)S(1)} %get-tuple-element.29), channel_id=1, source_target_pairs={{0,6},{2,4},{4,2},{6,0},{8,14},{10,12},{12,10},{14,8},{16,22},{18,... | collective-permute-start | bytes 663560 | tf_op jit(solution)/shard_map/ppermute | solution.py:41
  25.0 5.1 %collective-permute-start.3 = (f32[24,768]{1,0:T(8,128)S(1)}, f32[24,768]{1,0:T(8,128)S(1)}, u32[]{:S(2)}, u32[]{:S(2)}) collective-permute-start(f32[24,768]{1,0:T(8,128)S(1)} %get-tuple-element.57), channel_id=1, source_target_pairs={{0,8},{2,10},{4,12},{6,14},{8,0},{10,2},{12,4},{14,6},{16,24},{18,... | collective-permute-start | bytes 221192 | tf_op jit(solution)/shard_map/ppermute | solution.py:41
  26.8 6.8 %collective-permute-start.4 = (f32[24,768]{1,0:T(8,128)S(1)}, f32[24,768]{1,0:T(8,128)S(1)}, u32[]{:S(2)}, u32[]{:S(2)}) collective-permute-start(f32[24,768]{1,0:T(8,128)S(1)} %get-tuple-element.58), channel_id=1, source_target_pairs={{0,16},{2,18},{4,20},{6,22},{8,24},{10,26},{12,28},{14,30},{16,0},... | collective-permute-start | bytes 221192 | tf_op jit(solution)/shard_map/ppermute | solution.py:41
  29.4 6.3 %collective-permute-start.5 = (f32[24,768]{1,0:T(8,128)S(1)}, f32[24,768]{1,0:T(8,128)S(1)}, u32[]{:S(2)}, u32[]{:S(2)}) collective-permute-start(f32[24,768]{1,0:T(8,128)S(1)} %concatenate.18), channel_id=1, source_target_pairs={{0,24},{2,26},{4,28},{6,30},{8,16},{10,18},{12,20},{14,22},{16,8},... | collective-permute-start | bytes 221192 | tf_op jit(solution)/shard_map/ppermute | solution.py:41
  35.7 4.5 %collective-permute-start.6 = (f32[24,512]{1,0:T(8,128)S(1)}, f32[24,512]{1,0:T(8,128)S(1)}, u32[]{:S(2)}, u32[]{:S(2)}) collective-permute-start(f32[24,512]{1,0:T(8,128)S(1)} %get-tuple-element.55), channel_id=1, source_target_pairs={{0,8},{2,10},{4,12},{6,14},{8,0},{10,2},{12,4},{14,6},{16,24},{18,... | collective-permute-start | bytes 147464 | tf_op jit(solution)/shard_map/ppermute | solution.py:41
  35.8 5.1 %collective-permute-start.7 = (f32[24,512]{1,0:T(8,128)S(1)}, f32[24,512]{1,0:T(8,128)S(1)}, u32[]{:S(2)}, u32[]{:S(2)}) collective-permute-start(f32[24,512]{1,0:T(8,128)S(1)} %get-tuple-element.55), channel_id=1, source_target_pairs={{0,16},{2,18},{4,20},{6,22},{8,24},{10,26},{12,28},{14,30},{16,0},... | collective-permute-start | bytes 147464 | tf_op jit(solution)/shard_map/ppermute | solution.py:41
  37.6 5.9 %collective-permute-start.8 = (f32[24,512]{1,0:T(8,128)S(1)}, f32[24,512]{1,0:T(8,128)S(1)}, u32[]{:S(2)}, u32[]{:S(2)}) collective-permute-start(f32[24,512]{1,0:T(8,128)S(1)} %get-tuple-element.55), channel_id=1, source_target_pairs={{0,24},{2,26},{4,28},{6,30},{8,16},{10,18},{12,20},{14,22},{16,8},... | collective-permute-start | bytes 147464 | tf_op jit(solution)/shard_map/ppermute | solution.py:41
  43.5 8.4 %collective-permute-start.11 = (f32[24,2304]{1,0:T(8,128)S(1)}, f32[24,2304]{1,0:T(8,128)S(1)}, u32[]{:S(2)}, u32[]{:S(2)}) collective-permute-start(f32[24,2304]{1,0:T(8,128)S(1)} %slice_dynamic-update-slice_fusion.scores.refs_0_), channel_id=1, source_target_pairs={{0,2},{2,0},{4,6},{6,4},{8,10},{10,8},{12,14},{14,12},{16,18},{18,... | collective-permute-start | bytes 663560 | tf_op jit(solution)/shard_map/ppermute | solution.py:41
  45.0 40.7 %collective-permute-start.21 = (f32[256,512]{1,0:T(8,128)}, f32[256,512]{1,0:T(8,128)S(1)}, u32[]{:S(2)}, u32[]{:S(2)}) collective-permute-start(f32[256,512]{1,0:T(8,128)} %get-tuple-element.47), channel_id=1, source_target_pairs={{0,6},{2,4},{4,2},{6,0},{8,14},{10,12},{12,10},{14,8},{16,22},{18,... | collective-permute-start | bytes 1572872 | tf_op jit(solution)/shard_map/ppermute | solution.py:41
  46.5 41.1 %collective-permute-start.19 = (f32[256,512]{1,0:T(8,128)}, f32[256,512]{1,0:T(8,128)}, u32[]{:S(2)}, u32[]{:S(2)}) collective-permute-start(f32[256,512]{1,0:T(8,128)} %get-tuple-element.44), channel_id=1, source_target_pairs={{0,2},{2,0},{4,6},{6,4},{8,10},{10,8},{12,14},{14,12},{16,18},{18,... | collective-permute-start | bytes 1572872 | tf_op jit(solution)/shard_map/ppermute | solution.py:41
  48.0 39.6 %collective-permute-start.20 = (f32[256,512]{1,0:T(8,128)}, f32[256,512]{1,0:T(8,128)}, u32[]{:S(2)}, u32[]{:S(2)}) collective-permute-start(f32[256,512]{1,0:T(8,128)} %get-tuple-element.46), channel_id=1, source_target_pairs={{0,4},{2,6},{4,0},{6,2},{8,12},{10,14},{12,8},{14,10},{16,20},{18,... | collective-permute-start | bytes 1572872 | tf_op jit(solution)/shard_map/ppermute | solution.py:41
  48.5 28.7 %collective-permute-start.10 = (f32[24,2304]{1,0:T(8,128)S(1)}, f32[24,2304]{1,0:T(8,128)S(1)}, u32[]{:S(2)}, u32[]{:S(2)}) collective-permute-start(f32[24,2304]{1,0:T(8,128)S(1)} %slice_dynamic-update-slice_fusion.scores.refs_0_), channel_id=1, source_target_pairs={{0,4},{2,6},{4,0},{6,2},{8,12},{10,14},{12,8},{14,10},{16,20},{18,... | collective-permute-start | bytes 663560 | tf_op jit(solution)/shard_map/ppermute | solution.py:41
  51.9 27.6 %collective-permute-start.9 = (f32[24,2304]{1,0:T(8,128)S(1)}, f32[24,2304]{1,0:T(8,128)S(1)}, u32[]{:S(2)}, u32[]{:S(2)}) collective-permute-start(f32[24,2304]{1,0:T(8,128)S(1)} %slice_dynamic-update-slice_fusion.scores.refs_0_), channel_id=1, source_target_pairs={{0,6},{2,4},{4,2},{6,0},{8,14},{10,12},{12,10},{14,8},{16,22},{18,... | collective-permute-start | bytes 663560 | tf_op jit(solution)/shard_map/ppermute | solution.py:41
  58.7 29.0 %copy-start = (f32[256,512]{1,0:T(8,128)S(1)}, f32[256,512]{1,0:T(8,128)}, u32[]{:S(2)}) copy-start(f32[256,512]{1,0:T(8,128)} %get-tuple-element.42) | copy-start | bytes 1572868
  81.6 1.3 %collective-permute-start.12 = (f32[24,896]{1,0:T(8,128)S(1)}, f32[24,896]{1,0:T(8,128)S(1)}, u32[]{:S(2)}, u32[]{:S(2)}) collective-permute-start(f32[24,896]{1,0:T(8,128)S(1)} %terms.7.own), channel_id=1, source_target_pairs={{0,1},{1,0},{2,3},{3,2},{4,5},{5,4},{6,7},{7,6},{8,9},{9,8},{10,11... | collective-permute-start | bytes 258056 | tf_op jit(solution)/shard_map/ppermute | solution.py:41
  84.2 8.4 %collective-permute-start.13 = (f32[24,128]{1,0:T(8,128)S(1)}, f32[24,128]{1,0:T(8,128)S(1)}, u32[]{:S(2)}, u32[]{:S(2)}) collective-permute-start(f32[24,128]{1,0:T(8,128)S(1)} %get-tuple-element.40), channel_id=1, source_target_pairs={{0,2},{2,0},{4,6},{6,4},{8,10},{10,8},{12,14},{14,12},{16,18},{18,... | collective-permute-start | bytes 36872 | tf_op jit(solution)/shard_map/ppermute | solution.py:41
  85.2 8.4 %collective-permute-start.14 = (f32[24,128]{1,0:T(8,128)S(1)}, f32[24,128]{1,0:T(8,128)S(1)}, u32[]{:S(2)}, u32[]{:S(2)}) collective-permute-start(f32[24,128]{1,0:T(8,128)S(1)} %get-tuple-element.40), channel_id=1, source_target_pairs={{0,4},{2,6},{4,0},{6,2},{8,12},{10,14},{12,8},{14,10},{16,20},{18,... | collective-permute-start | bytes 36872 | tf_op jit(solution)/shard_map/ppermute | solution.py:41
  85.7 7.9 %collective-permute-start.15 = (f32[24,128]{1,0:T(8,128)S(1)}, f32[24,128]{1,0:T(8,128)S(1)}, u32[]{:S(2)}, u32[]{:S(2)}) collective-permute-start(f32[24,128]{1,0:T(8,128)S(1)} %get-tuple-element.40), channel_id=1, source_target_pairs={{0,6},{2,4},{4,2},{6,0},{8,14},{10,12},{12,10},{14,8},{16,22},{18,... | collective-permute-start | bytes 36872 | tf_op jit(solution)/shard_map/ppermute | solution.py:41
  89.1 16.2 %collective-permute-start.22 = (f32[64,512]{1,0:T(8,128)S(1)}, f32[64,512]{1,0:T(8,128)S(1)}, u32[]{:S(2)}, u32[]{:S(2)}) collective-permute-start(f32[64,512]{1,0:T(8,128)S(1)} %get-tuple-element.50), channel_id=1, source_target_pairs={{0,8},{2,10},{4,12},{6,14},{8,0},{10,2},{12,4},{14,6},{16,24},{18,... | collective-permute-start | bytes 393224 | tf_op jit(solution)/shard_map/ppermute | solution.py:41
  89.2 16.1 %collective-permute-start.23 = (f32[64,512]{1,0:T(8,128)S(1)}, f32[64,512]{1,0:T(8,128)S(1)}, u32[]{:S(2)}, u32[]{:S(2)}) collective-permute-start(f32[64,512]{1,0:T(8,128)S(1)} %get-tuple-element.49), channel_id=1, source_target_pairs={{0,16},{2,18},{4,20},{6,22},{8,24},{10,26},{12,28},{14,30},{16,0},... | collective-permute-start | bytes 393224 | tf_op jit(solution)/shard_map/ppermute | solution.py:41
  92.5 12.8 %collective-permute-start.24 = (f32[64,512]{1,0:T(8,128)S(1)}, f32[64,512]{1,0:T(8,128)S(1)}, u32[]{:S(2)}, u32[]{:S(2)}) collective-permute-start(f32[64,512]{1,0:T(8,128)S(1)} %get-tuple-element.48), channel_id=1, source_target_pairs={{0,24},{2,26},{4,28},{6,30},{8,16},{10,18},{12,20},{14,22},{16,8},... | collective-permute-start | bytes 393224 | tf_op jit(solution)/shard_map/ppermute | solution.py:41
  93.6 4.2 %collective-permute-start.16 = (f32[24,128]{1,0:T(8,128)S(1)}, f32[24,128]{1,0:T(8,128)S(1)}, u32[]{:S(2)}, u32[]{:S(2)}) collective-permute-start(f32[24,128]{1,0:T(8,128)S(1)} %add_add_fusion.2.refs_0_), channel_id=1, source_target_pairs={{0,8},{2,10},{4,12},{6,14},{8,0},{10,2},{12,4},{14,6},{16,24},{18,... | collective-permute-start | bytes 36872 | tf_op jit(solution)/shard_map/ppermute | solution.py:41
  93.7 10.9 %collective-permute-start.17 = (f32[24,128]{1,0:T(8,128)S(1)}, f32[24,128]{1,0:T(8,128)S(1)}, u32[]{:S(2)}, u32[]{:S(2)}) collective-permute-start(f32[24,128]{1,0:T(8,128)S(1)} %add_add_fusion.2.refs_0_), channel_id=1, source_target_pairs={{0,16},{2,18},{4,20},{6,22},{8,24},{10,26},{12,28},{14,30},{16,0},... | collective-permute-start | bytes 36872 | tf_op jit(solution)/shard_map/ppermute | solution.py:41
  97.8 6.8 %collective-permute-start.18 = (f32[24,128]{1,0:T(8,128)S(1)}, f32[24,128]{1,0:T(8,128)S(1)}, u32[]{:S(2)}, u32[]{:S(2)}) collective-permute-start(f32[24,128]{1,0:T(8,128)S(1)} %add_add_fusion.2.refs_0_), channel_id=1, source_target_pairs={{0,24},{2,26},{4,28},{6,30},{8,16},{10,18},{12,20},{14,22},{16,8},... | collective-permute-start | bytes 36872 | tf_op jit(solution)/shard_map/ppermute | solution.py:41

commit v3 on v2

--- a/solution.py
+++ b/solution.py
@@ -60,43 +60,55 @@
     return copies
 
 
-def geno_copies(plan, chunks, geno, held, sems):
+def geno_copies(plan, chunks, geno, held, sems, base=0):
     width, total = plan.width, plan.total
     return [
         pltpu.make_async_copy(
             geno.at[pl.ds(chunk_start(chunk, width, total), width), :],
             held.at[pl.ds(j * width, width), :],
-            sems.at[j],
+            sems.at[base + j],
         )
         for j, chunk in enumerate(chunks)
     ]
 
 
-def scores_body(plan, digit, me, ready, geno, variants, out, held, rows_held, sems):
+def scores_begin(plan, digits, me, geno, variants, held, rows_held, sems):
+    begun, per = [], len(plan.rest) + 1
+    share = rows_held.shape[0] // len(digits)
+    columns = held.shape[0] // len(digits)
+    for at, digit in enumerate(digits):
+        chunks = [me ^ (digit * plan.stride) ^ r for r in plan.rest]
+        window = held.at[pl.ds(at * columns, columns), :]
+        copies = geno_copies(plan, chunks, geno, window, sems, at * per)
+        quarter = (me // plan.stride % plan.radix) ^ digit
+        rows_copy = pltpu.make_async_copy(
+            variants.at[pl.ds(pl.multiple_of(quarter * share, 16), share), :],
+            rows_held.at[pl.ds(at * share, share), :],
+            sems.at[at * per + len(chunks)],
+        )
+        begun.append((chunks, fetch([*copies, rows_copy])))
+    return begun
+
+
+def scores_finish(plan, begun, start_bf, weighted, stats, held, rows_held, outs):
     width, total = plan.width, plan.total
-    chunks = [me ^ (digit * plan.stride) ^ r for r in plan.rest]
-    copies = fetch(geno_copies(plan, chunks, geno, held, sems))
-    share = rows_held.shape[0]
-    quarter = (me // plan.stride % plan.radix) ^ digit
-    rows_copy = pltpu.make_async_copy(
-        variants.at[pl.ds(pl.multiple_of(quarter * share, 16), share), :], rows_held, sems.at[len(chunks)]
-    )
-    rows_copy.start()
-    start_bf, weighted, stats = ready()
-    for j, copy in enumerate(copies):
-        copy.wait()
-        part = lax.dot_general(
-            start_bf, held[j * width : (j + 1) * width, :], NT, preferred_element_type=F32
+    share = rows_held.shape[0] // len(outs)
+    for at, ((chunks, (*copies, rows_copy)), out) in enumerate(zip(begun, outs)):
+        for j, copy in enumerate(copies):
+            copy.wait()
+            low = (at * len(chunks) + j) * width
+            part = lax.dot_general(start_bf, held[low : low + width, :], NT, preferred_element_type=F32)
+            part = jnp.where(fresh_lanes(chunks[j], width, total, part.shape[0]), part, 0.0)
+            out[:, j * width : (j + 1) * width] = part
+            lane = lax.broadcasted_iota(jnp.int32, stats.shape, 1)
+            head = jnp.where((lane < 2) & (chunks[j] == plan.count - 1), stats, part[:, :LANES])
+            out[:, j * width : j * width + LANES] = head
+        rows_copy.wait()
+        both = lax.dot_general(
+            weighted, rows_held[at * share : (at + 1) * share, :], NT, preferred_element_type=F32
         )
-        part = jnp.where(fresh_lanes(chunks[j], width, total, part.shape[0]), part, 0.0)
-        out[:, j * width : (j + 1) * width] = part
-        lane = lax.broadcasted_iota(jnp.int32, stats.shape, 1)
-        head = jnp.where((lane < 2) & (chunks[j] == plan.count - 1), stats, part[:, :LANES])
-        out[:, j * width : j * width + LANES] = head
-    rows_copy.wait()
-    both = lax.dot_general(weighted, rows_held[...], NT, preferred_element_type=F32)
-    high = both.shape[0] // 2
-    out[:, len(chunks) * width :] = both[:high] + both[high:]
+        high = both.shape[0] // 2
+        out[:, len(chunks) * width :] = both[:high] + both[high:]
 
 
 def lead_kernel(plan, digit, ratio, weights, panel, geno, variants, out, diag, start, start_bf, weighted, stats, *scratch):
@@ -107,43 +119,31 @@
             pltpu.make_async_copy(weights, weights_held, small.at[1]),
         ]
     )
-
-    def ready():
-        for copy in first:
-            copy.wait()
-        mu = weights_held[...].reshape(1, weights_held.shape[0])
-        whole = 1.0 / mu + ratio[0]
-        right = panel_held[...]
-        way = right / whole
-        diag[0:1, :] = whole
-        diag[1:2, :] = mu
-        start[...] = way
-        start_bf[...] = way.astype(BF16)
-        exact = mu * way
-        high = exact.astype(BF16)
-        weighted[...] = jnp.concatenate([high, (exact - high.astype(F32)).astype(BF16)], axis=0)
-        norm = jnp.sum(right * way, axis=1, keepdims=True)
-        own = jnp.sum(way * (way / mu), axis=1, keepdims=True)
-        lane = lax.broadcasted_iota(jnp.int32, stats.shape, 1)
-        stats[...] = jnp.where(lane == 0, norm, jnp.where(lane == 1, own, 0.0))
-        return start_bf[...], weighted[...], stats[...]
-
-    scores_body(plan, digit, lax.axis_index("samp"), ready, geno, variants, out, held, rows_held, sems)
-
-
-def scores_kernel(plan, digit, start_bf, weighted, stats, geno, variants, out, held, rows_held, sems):
-    scores_body(
-        plan,
-        digit,
-        lax.axis_index("samp"),
-        lambda: (start_bf[...], weighted[...], stats[...]),
-        geno,
-        variants,
-        out,
-        held,
-        rows_held,
-        sems,
-    )
+    begun = scores_begin(plan, (digit,), lax.axis_index("samp"), geno, variants, held, rows_held, sems)
+    for copy in first:
+        copy.wait()
+    mu = weights_held[...].reshape(1, weights_held.shape[0])
+    whole = 1.0 / mu + ratio[0]
+    right = panel_held[...]
+    way = right / whole
+    diag[0:1, :] = whole
+    diag[1:2, :] = mu
+    start[...] = way
+    start_bf[...] = way.astype(BF16)
+    exact = mu * way
+    high = exact.astype(BF16)
+    weighted[...] = jnp.concatenate([high, (exact - high.astype(F32)).astype(BF16)], axis=0)
+    norm = jnp.sum(right * way, axis=1, keepdims=True)
+    own = jnp.sum(way * (way / mu), axis=1, keepdims=True)
+    lane = lax.broadcasted_iota(jnp.int32, stats.shape, 1)
+    stats[...] = jnp.where(lane == 0, norm, jnp.where(lane == 1, own, 0.0))
+    scores_finish(plan, begun, start_bf[...], weighted[...], stats[...], held, rows_held, (out,))
+
+
+def scores_kernel(plan, digits, start_bf, weighted, stats, geno, variants, *refs):
+    *outs, held, rows_held, sems = refs
+    begun = scores_begin(plan, digits, lax.axis_index("samp"), geno, variants, held, rows_held, sems)
+    scores_finish(plan, begun, start_bf[...], weighted[...], stats[...], held, rows_held, outs)
 
 
 def terms_kernel(plan, digit, ratio, scores, *refs):
@@ -195,36 +195,75 @@
     out[...] = residual[...] / diag[0:1, :] + (total / start_norm) * start[...]
 
 
-def genes_of(sizes, index):
-    gene = jnp.zeros(index.shape, jnp.int32)
+def gene_bounds(sizes, index, count):
+    low = jnp.zeros(index.shape, jnp.int32)
+    high = jnp.full(index.shape, count, jnp.int32)
     end = jnp.int32(0)
     for g in range(sizes.shape[1]):
         end = end + sizes[0, g]
-        gene = gene + (end <= index).astype(jnp.int32)
-    return gene
-
-
-def cross_kernel(plan, block, span, sizes, weights, variants, *refs):
+        low = jnp.where(end <= index, end, low)
+        high = jnp.where((end > index) & (end < high), end, high)
+    return low, high
+
+
+def cross_kernel(plan, block, sizes, weights, variants, *refs):
     *outs, scaled = refs
+    keep_x, keep_y, send_x, send_y = outs
     me = lax.axis_index("samp")
     count = variants.shape[0]
+    half = GENE_MAX // 2
+    quarter = block * len(plan.rest)
     mu = weights[...].reshape(1, weights.shape[0])
-    cols = genes_of(sizes, lax.broadcasted_iota(jnp.int32, (1, count), 1))
-    row = lax.broadcasted_iota(jnp.int32, (block, LANES), 0)
-    for digit, out in enumerate(outs):
-        places = []
+    lane = lax.broadcasted_iota(jnp.int32, (1, quarter), 1)
+    column = lax.broadcasted_iota(jnp.int32, (count, quarter), 0)
+    places = (
+        ((keep_x, 0), (keep_y, 0)),
+        ((send_x, 0), (keep_y, 1)),
+        ((keep_x, 1), (send_y, 0)),
+        ((send_x, 1), (send_y, 1)),
+    )
+    for digit in range(plan.radix):
+        index = lane
         for j, r in enumerate(plan.rest):
             first = pl.multiple_of((me ^ (digit * plan.stride) ^ r) * block, block)
             mine = variants[pl.ds(first, block), :]
             scaled[j * block : (j + 1) * block, :] = (mine.astype(F32) * mu).astype(BF16)
-            places.append(first + row)
-        cross = lax.dot_general(scaled[...], variants[...], NT, preferred_element_type=F32)
-        rows = genes_of(sizes, jnp.concatenate(places, axis=0))[:, :1]
-        cross = jnp.where(rows == cols, cross, 0.0)
-        folded = cross[:, :span]
-        for low in range(span, count, span):
-            folded = folded + cross[:, low : low + span]
-        out[...] = folded
+            index = jnp.where(lane // block == j, first + lane - j * block, index)
+        cross = lax.dot_general(variants[...], scaled[...], NT, preferred_element_type=F32)
+        low, high = gene_bounds(sizes, index, count)
+        cross = jnp.where((column >= low) & (column < high), cross, 0.0)
+        for part, (out, at) in enumerate(places[digit]):
+            folded = None
+            for base in range(part * half, count, GENE_MAX):
+                piece = cross[base : min(base + half, count)]
+                if piece.shape[0] < half:
+                    piece = jnp.concatenate([piece, jnp.zeros((half - piece.shape[0], quarter), F32)], axis=0)
+                folded = piece if folded is None else folded + piece
+            out[:, at * quarter : (at + 1) * quarter] = folded
+
+
+def halves_kernel(keep_x, keep_y, got_x, got_y, own_x, own_y, pass_x, pass_y):
+    quarter = own_x.shape[1]
+    own_x[...] = keep_x[:, :quarter] + got_x[:, :quarter]
+    own_y[...] = keep_y[:, :quarter] + got_y[:, :quarter]
+    pass_x[...] = keep_x[:, quarter:] + got_x[:, quarter:]
+    pass_y[...] = keep_y[:, quarter:] + got_y[:, quarter:]
+
+
+def split_kernel(terms, *refs):
+    ins, outs = refs[: -len(terms[1])], refs[-len(terms[1]) :]
+    if terms[0]:
+        low, high = ins[0][...] + ins[2][...], ins[1][...] + ins[3][...]
+    else:
+        total = ins[0][...]
+        for ref in ins[1:]:
+            total = total + ref[...]
+        low, high = total[:, : total.shape[1] // 2], total[:, total.shape[1] // 2 :]
+    wide = low.shape[1] // len(outs)
+    for j, out in enumerate(outs):
+        out[...] = jnp.concatenate(
+            [low[:, j * wide : (j + 1) * wide], high[:, j * wide : (j + 1) * wide]], axis=1
+        )
 
 
 def gram_kernel(plan, samples, sizes, alpha, *refs):
@@ -240,6 +279,8 @@
     cross = sums[0][...]
     for ref in sums[1:]:
         cross = cross + ref[...]
+    cross = jnp.concatenate([cross[:, :block], cross[:, block:]], axis=0).T
+    cross = jnp.concatenate([cross] * (-(-count // GENE_MAX)), axis=1)[:, :count]
     first = me * block
     window = max(block, LANES)
     base = pl.multiple_of(first // window * window, window)
@@ -253,12 +294,10 @@
     correction = wide[:block]
     for step in range(1, window // block):
         correction = jnp.where(first - base == step * block, wide[step * block : (step + 1) * block], correction)
-    cols = genes_of(sizes, lax.broadcasted_iota(jnp.int32, (1, count), 1))
-    rows = genes_of(sizes, first + lax.broadcasted_iota(jnp.int32, (block, LANES), 0))[:, :1]
-    span = cross.shape[1]
-    for low in range(0, count, span):
-        piece = (cross - correction[:, low : low + span]) / samples
-        out[0, :, low : low + span] = jnp.where(rows == cols[:, low : low + span], piece, 0.0)
+    low, high = gene_bounds(sizes, first + lax.broadcasted_iota(jnp.int32, (block, LANES), 0), count)
+    column = lax.broadcasted_iota(jnp.int32, (block, count), 1)
+    same = (column >= low[:, :1]) & (column < high[:, :1])
+    out[0] = jnp.where(same, (cross - correction) / samples, 0.0)
 
 
 @dataclasses.dataclass(frozen=True)
@@ -297,7 +336,6 @@
     columns = len(rest) * width
     window = VMEM((columns, samples), BF16)
     sems = pltpu.SemaphoreType.DMA((len(rest) + 1,))
-    rows_held = VMEM((share, samples), BF16)
     payload = VMEM((rows, columns + share), F32)
 
     lead = radix - 1
@@ -315,8 +353,8 @@
         in_specs=[smem] + [hbm] * 4,
         out_specs=[vmem] * 6,
         scratch_shapes=[
-            window,
-            rows_held,
+            VMEM((columns, samples), BF16),
+            VMEM((share, samples), BF16),
             VMEM((rows, samples), F32),
             VMEM((samples,), F32),
             sems,
@@ -326,38 +364,60 @@
     )(variance_ratio, weights, panel, genotypes, variants)
     diag, start = in_vmem(diag), in_vmem(start)
     after = sent[lead]
-    for d in (*range(1, lead), 0):
+    for digits in (tuple(range(1, lead)), (0,)):
         start_bf, after = lax.optimization_barrier((start_bf, after))
-        sent[d] = pl.pallas_call(
-            functools.partial(scores_kernel, plan, d),
-            out_shape=payload,
+        found = pl.pallas_call(
+            functools.partial(scores_kernel, plan, digits),
+            out_shape=[payload] * len(digits),
             in_specs=[vmem] * 3 + [hbm] * 2,
-            out_specs=vmem,
-            scratch_shapes=[window, rows_held, sems],
+            out_specs=[vmem] * len(digits),
+            scratch_shapes=[
+                VMEM((len(digits) * columns, samples), BF16),
+                VMEM((len(digits) * share, samples), BF16),
+                pltpu.SemaphoreType.DMA((len(digits) * (len(rest) + 1),)),
+            ],
             name="scores",
         )(in_vmem(start_bf), in_vmem(weighted), in_vmem(stats), genotypes, variants)
-        after = sent[d]
-
+        sent.update(zip(digits, found))
+        after = found[0]
+
+    assert radix == 4
     block = num_variants // count
-    span = up(GENE_MAX, LANES)
-    if num_variants % span or num_variants <= span:
-        span = num_variants
-    crosses = list(
-        pl.pallas_call(
-            functools.partial(cross_kernel, plan, block, span),
-            out_shape=[jax.ShapeDtypeStruct((block * len(rest), span), F32)] * radix,
-            in_specs=[smem] + [vmem] * 2,
-            out_specs=[vmem] * radix,
-            scratch_shapes=[VMEM((block * len(rest), samples), BF16)],
-            name="cross",
-        )(gene_sizes, weights, tied(variants, sent[0]))
-    )
+    quarter = block * len(rest)
+    half = GENE_MAX // 2
+    keep_x, keep_y, send_x, send_y = pl.pallas_call(
+        functools.partial(cross_kernel, plan, block),
+        out_shape=[VMEM((half, 2 * quarter), F32)] * radix,
+        in_specs=[smem] + [vmem] * 2,
+        out_specs=[vmem] * radix,
+        scratch_shapes=[VMEM((quarter, samples), BF16)],
+        name="cross",
+    )(gene_sizes, weights, tied(variants, sent[0]))
 
     got = sent[0]
     for d in range(1, radix):
         got = got + swap(sent[d], count, firsts[d])
-    got, crosses[0] = lax.optimization_barrier((got, crosses[0]))
-    near = [swap(tied(crosses[d], got), count, firsts[d]) for d in range(1, lead)]
+    got, send_x, send_y = lax.optimization_barrier((got, send_x, send_y))
+    got_x = swap(send_x, count, firsts[1])
+    got_y = swap(send_y, count, firsts[2])
+    piece = VMEM((half, quarter), F32)
+    own_x, own_y, pass_x, pass_y = pl.pallas_call(
+        halves_kernel, out_shape=[piece] * 4, in_specs=[vmem] * 4, out_specs=[vmem] * 4, name="halves"
+    )(*map(in_vmem, (keep_x, keep_y, got_x, got_y)))
+    sums = [own_x, own_y, swap(pass_x, count, firsts[2]), swap(pass_y, count, firsts[1])]
+    paired, wide = True, quarter
+    for r, s in later:
+        wide //= r
+        pieces = pl.pallas_call(
+            functools.partial(split_kernel, (paired, range(r))),
+            out_shape=[VMEM((half, 2 * wide), F32)] * r,
+            in_specs=[vmem] * len(sums),
+            out_specs=[vmem] * r,
+            name="split",
+        )(*map(in_vmem, sums))
+        paired = False
+        sums = [pieces[0]] + [swap(pieces[d], count, d * s) for d in range(1, r)]
+
     shared, got = got[:, -share:], got[:, :-share]
     for r, s in later:
         wide = got.shape[1] // r
@@ -372,7 +432,7 @@
     arrays = [in_vmem(everything)] + [in_vmem(swap(everything, count, firsts[d])) for d in range(1, radix)]
 
     own = ()
-    for d in range(radix):
+    for d in (0, 1, 3, 2):
         whole = pl.pallas_call(
             functools.partial(terms_kernel, plan, d),
             out_shape=VMEM((rows, samples + LANES), F32),
@@ -417,14 +477,6 @@
         name="direction",
     )(diag, start, held, in_vmem(residual), *map(in_vmem, norms))
 
-    far = swap(crosses[lead], count, firsts[lead])
-    sums = [crosses[0], *near, far]
-    for r, s in later:
-        total = sums[0]
-        for one in sums[1:]:
-            total = total + one
-        tall = total.shape[0] // r
-        sums = [total[:tall]] + [swap(total[d * tall : (d + 1) * tall], count, d * s) for d in range(1, r)]
     gram = pl.pallas_call(
         functools.partial(gram_kernel, plan, samples * count),
         out_shape=jax.ShapeDtypeStruct((1, block, num_variants), F32),

time: 108 us -> 87.4 us (0.81)
  waiting for transfers between devices: 36.6 us -> 21.9 us
  starting transfers between devices: 36.8 us -> 32.9 us
  Pallas kernels: 29.7 us -> 28.2 us
  other arithmetic: 1.54 us -> 0.1 us
  local copies, waits for them, and re-layouts: 1.35 us -> 2.66 us
    ppermute x25 -> x26, waiting for transfers between devices: 36.6 us -> 21.9 us  [swap(): return lax.ppermute(array, axis, [(i, i ^ offset) for i in range(count)])]
    ppermute x25 -> x26, starting transfers between devices: 36.8 us -> 32.9 us  [swap(): return lax.ppermute(array, axis, [(i, i ^ offset) for i in range(count)])]
    pallas_call x4 -> x5, Pallas kernels: 14 us -> 12.4 us  [the longest x2 7.62 us: body(): pl.pallas_call(functools.partial(scores_kernel, plan, digits), out_shape=...]
    add x2 -> x1, other arithmetic: 1.43 us -> 0.01 us  [body(): total = total + one]
    unnamed x7 -> x11, local copies, waits for them, and re-layouts: 1.28 us -> 2.63 us
  transfers between devices with their start and end apart: 25 -> 26, of which waited for: 11 -> 11; matrix products, arithmetic and copies ran while one was open for 3% -> 1% of each run, Pallas kernels for 17% -> 21%
where the time goes in v3:
time: 87.4 us; the launch traced here: 87.1 us
  starting transfers between devices  32.9 us (38%)
  Pallas kernels  28.2 us (32%)
  waiting for transfers between devices  21.9 us (25%)
  local copies, waits for them, and re-layouts  2.66 us (3%)
  between operations  1.48 us (2%)
    ppermute x26, starting transfers between devices, swap(): return lax.ppermute(array, axis, [(i, i ^ offset) for i in range(count)])  32.9 us
    ppermute x26, waiting for transfers between devices, swap(): return lax.ppermute(array, axis, [(i, i ^ offset) for i in range(count)])  21.9 us
    pallas_call x4, Pallas kernels, body(): pl.pallas_call(functools.partial(terms_kernel, plan, d), out_shape=VMEM((...  8.69 us
    pallas_call x2, Pallas kernels, body(): pl.pallas_call(functools.partial(scores_kernel, plan, digits), out_shape=...  7.62 us
    pallas_call x1, Pallas kernels, body(): pl.pallas_call(functools.partial(cross_kernel, plan, block), out_shape=[V...  4.46 us
    pallas_call x1, Pallas kernels, body(): pl.pallas_call(functools.partial(lead_kernel, plan, lead), out_shape=[pay...  3.08 us
    unnamed x11, local copies, waits for them, and re-layouts  2.63 us
    pallas_call x1, Pallas kernels, body(): pl.pallas_call(functools.partial(gram_kernel, plan, samples * count), out...  2.12 us
  transfers between devices with their start and end apart: 26, of which 11 were waited for; matrix products, arithmetic and copies ran while one was open for 1% of the time, Pallas kernels for 21%

profile of v3, /device:TPU:0, one launch (start us, length us, event | category | flops | bytes accessed | tf_op | source)
XLA Modules:
  0.0 87.1 jit_solution(1125005687145077759)
XLA Ops:
  1.3 3.1 %scores_lead.1 = (f32[24,2304]{1,0:T(8,128)S(1)}, f32[8,768]{1,0:T(8,128)S(1)}, f32[24,768]{1,0:T(8,128)S(1)}, bf16[24,768]{1,0:T(8,128)(2,1)S(1)}, bf16[48,768]{1,0:T(8,128)(2,1)S(1)}, /*index=5*/f32[24,128]{1,0:T(8,128)S(1)}) custom-call(f32[1]{0:T(128)S(6)} %copy.16.ratio, f32[768]{0:T(1024)} %weights.3, f32[24,768]{1,0:T(8,128)} %panel.3, ...), custom_call_target="tpu_custom_call" | custom-call | tf_op jit(solution)/shard_map/scores_lead/pallas_call | solution.py:343
  4.4 4.6 %scores.2 = (f32[24,2304]{1,0:T(8,128)S(1)}, f32[24,2304]{1,0:T(8,128)S(1)}) custom-call(bf16[24,768]{1,0:T(8,128)(2,1)S(1)} %get-tuple-element.42.start_bf, bf16[48,768]{1,0:T(8,128)(2,1)S(1)} %get-tuple-element.39.weighted, f32[24,128]{1,0:T(8,128)S(1)} %get-tuple-element.40.stats, bf16[8000,768]{1,0:T(8,128)(2,1)} %refs_1_.5, bf16[1024,768]{1,0:T(8,128)(2,1)} %variants.6), custom_call_target="tpu_custom_call" | custom-call | tf_op jit(solution)/shard_map/scores/pallas_call | solution.py:369
  9.0 3.0 %collective-permute-start = (f32[24,2304]{1,0:T(8,128)S(1)}, f32[24,2304]{1,0:T(8,128)S(1)}, u32[]{:S(2)}, u32[]{:S(2)}) collective-permute-start(f32[24,2304]{1,0:T(8,128)S(1)} %get-tuple-element.41), channel_id=1, source_target_pairs={{0,2},{2,0},{4,6},{6,4},{8,10},{10,8},{12,14},{14,12},{16,18},{18,... | collective-permute-start | bytes 663560 | tf_op jit(solution)/shard_map/ppermute | solution.py:41
  12.0 1.5 %collective-permute-start.1 = (f32[24,2304]{1,0:T(8,128)S(1)}, f32[24,2304]{1,0:T(8,128)S(1)}, u32[]{:S(2)}, u32[]{:S(2)}) collective-permute-start(f32[24,2304]{1,0:T(8,128)S(1)} %get-tuple-element.43), channel_id=1, source_target_pairs={{0,4},{2,6},{4,0},{6,2},{8,12},{10,14},{12,8},{14,10},{16,20},{18,... | collective-permute-start | bytes 663560 | tf_op jit(solution)/shard_map/ppermute | solution.py:41
  13.6 3.0 %scores.3 = f32[24,2304]{1,0:T(8,128)S(1)} custom-call(bf16[24,768]{1,0:T(8,128)(2,1)S(1)} %get-tuple-element.42.start_bf, bf16[48,768]{1,0:T(8,128)(2,1)S(1)} %get-tuple-element.39.weighted, f32[24,128]{1,0:T(8,128)S(1)} %get-tuple-element.40.stats, bf16[8000,768]{1,0:T(8,128)(2,1)} %refs_1_.5, bf16[1024,768]{1,0:T(8,128)(2,1)} %variants.6), custom_call_target="tpu_custom_call" | custom-call | tf_op jit(solution)/shard_map/scores/pallas_call | solution.py:369
  16.6 4.5 %cross.1 = (f32[200,512]{1,0:T(8,128)S(1)}, f32[200,512]{1,0:T(8,128)S(1)}, f32[200,512]{1,0:T(8,128)}, f32[200,512]{1,0:T(8,128)S(1)}) custom-call(s32[1,24]{1,0:T(1,128)} %sizes.3, f32[768]{0:T(1024)} %weights.3, bf16[1024,768]{1,0:T(8,128)(2,1)} %variants.6), custom_call_target="tpu_custom_call" | custom-call | tf_op jit(solution)/shard_map/cross/pallas_call | solution.py:388
  21.0 2.6 %collective-permute-done.1 = f32[24,2304]{1,0:T(8,128)S(1)} collective-permute-done((f32[24,2304]{1,0:T(8,128)S(1)}, f32[24,2304]{1,0:T(8,128)S(1)}, u32[]{:S(2)}, u32[]{:S(2)}) %collective-permute-start.1) | collective-permute-done | bytes 221216 | tf_op jit(solution)/shard_map/ppermute | solution.py:41
  23.8 1.6 %collective-permute-start.3 = (f32[24,768]{1,0:T(8,128)S(1)}, f32[24,768]{1,0:T(8,128)S(1)}, u32[]{:S(2)}, u32[]{:S(2)}) collective-permute-start(f32[24,768]{1,0:T(8,128)S(1)} %get-tuple-element.69), channel_id=1, source_target_pairs={{0,8},{2,10},{4,12},{6,14},{8,0},{10,2},{12,4},{14,6},{16,24},{18,... | collective-permute-start | bytes 221192 | tf_op jit(solution)/shard_map/ppermute | solution.py:41
  25.4 2.6 %collective-permute-start.4 = (f32[24,768]{1,0:T(8,128)S(1)}, f32[24,768]{1,0:T(8,128)S(1)}, u32[]{:S(2)}, u32[]{:S(2)}) collective-permute-start(f32[24,768]{1,0:T(8,128)S(1)} %get-tuple-element.70), channel_id=1, source_target_pairs={{0,16},{2,18},{4,20},{6,22},{8,24},{10,26},{12,28},{14,30},{16,0},... | collective-permute-start | bytes 221192 | tf_op jit(solution)/shard_map/ppermute | solution.py:41
  28.9 3.3 %collective-permute-done.4 = f32[24,768]{1,0:T(8,128)S(1)} collective-permute-done((f32[24,768]{1,0:T(8,128)S(1)}, f32[24,768]{1,0:T(8,128)S(1)}, u32[]{:S(2)}, u32[]{:S(2)}) %collective-permute-start.4) | collective-permute-done | bytes 73760 | tf_op jit(solution)/shard_map/ppermute | solution.py:41
  32.3 2.0 %collective-permute-done.5 = f32[24,768]{1,0:T(8,128)S(1)} collective-permute-done((f32[24,768]{1,0:T(8,128)S(1)}, f32[24,768]{1,0:T(8,128)S(1)}, u32[]{:S(2)}, u32[]{:S(2)}) %collective-permute-start.5) | collective-permute-done | bytes 73760 | tf_op jit(solution)/shard_map/ppermute | solution.py:41
  34.4 1.3 %collective-permute-start.19 = (f32[200,512]{1,0:T(8,128)}, f32[200,512]{1,0:T(8,128)S(1)}, u32[]{:S(2)}, u32[]{:S(2)}) collective-permute-start(f32[200,512]{1,0:T(8,128)} %get-tuple-element.54), channel_id=1, source_target_pairs={{0,2},{2,0},{4,6},{6,4},{8,10},{10,8},{12,14},{14,12},{16,18},{18,... | collective-permute-start | bytes 1228808 | tf_op jit(solution)/shard_map/ppermute | solution.py:41
  36.6 1.7 %collective-permute-start.7 = (f32[24,512]{1,0:T(8,128)S(1)}, f32[24,512]{1,0:T(8,128)S(1)}, u32[]{:S(2)}, u32[]{:S(2)}) collective-permute-start(f32[24,512]{1,0:T(8,128)S(1)} %get-tuple-element.67), channel_id=1, source_target_pairs={{0,16},{2,18},{4,20},{6,22},{8,24},{10,26},{12,28},{14,30},{16,0},... | collective-permute-start | bytes 147464 | tf_op jit(solution)/shard_map/ppermute | solution.py:41
  38.3 2.6 %collective-permute-start.8 = (f32[24,512]{1,0:T(8,128)S(1)}, f32[24,512]{1,0:T(8,128)S(1)}, u32[]{:S(2)}, u32[]{:S(2)}) collective-permute-start(f32[24,512]{1,0:T(8,128)S(1)} %get-tuple-element.67), channel_id=1, source_target_pairs={{0,24},{2,26},{4,28},{6,30},{8,16},{10,18},{12,20},{14,22},{16,8},... | collective-permute-start | bytes 147464 | tf_op jit(solution)/shard_map/ppermute | solution.py:41
  41.5 2.6 %collective-permute-done.8 = f32[24,512]{1,0:T(8,128)S(1)} collective-permute-done((f32[24,512]{1,0:T(8,128)S(1)}, f32[24,512]{1,0:T(8,128)S(1)}, u32[]{:S(2)}, u32[]{:S(2)}) %collective-permute-start.8) | collective-permute-done | bytes 49184 | tf_op jit(solution)/shard_map/ppermute | solution.py:41
  44.2 1.2 %collective-permute-start.11 = (f32[24,2304]{1,0:T(8,128)S(1)}, f32[24,2304]{1,0:T(8,128)S(1)}, u32[]{:S(2)}, u32[]{:S(2)}) collective-permute-start(f32[24,2304]{1,0:T(8,128)S(1)} %slice_dynamic-update-slice_fusion.scores.refs_0_), channel_id=1, source_target_pairs={{0,2},{2,0},{4,6},{6,4},{8,10},{10,8},{12,14},{14,12},{16,18},{18,... | collective-permute-start | bytes 663560 | tf_op jit(solution)/shard_map/ppermute | solution.py:41
  45.4 1.6 %collective-permute-start.10 = (f32[24,2304]{1,0:T(8,128)S(1)}, f32[24,2304]{1,0:T(8,128)S(1)}, u32[]{:S(2)}, u32[]{:S(2)}) collective-permute-start(f32[24,2304]{1,0:T(8,128)S(1)} %slice_dynamic-update-slice_fusion.scores.refs_0_), channel_id=1, source_target_pairs={{0,6},{2,4},{4,2},{6,0},{8,14},{10,12},{12,10},{14,8},{16,22},{18,... | collective-permute-start | bytes 663560 | tf_op jit(solution)/shard_map/ppermute | solution.py:41
  49.2 1.3 %collective-permute-start.21 = (f32[200,256]{1,0:T(8,128)S(1)}, f32[200,256]{1,0:T(8,128)S(1)}, u32[]{:S(2)}, u32[]{:S(2)}) collective-permute-start(f32[200,256]{1,0:T(8,128)S(1)} %get-tuple-element.58), channel_id=1, source_target_pairs={{0,4},{2,6},{4,0},{6,2},{8,12},{10,14},{12,8},{14,10},{16,20},{18,... | collective-permute-start | bytes 614408 | tf_op jit(solution)/shard_map/ppermute | solution.py:41
  51.2 2.2 %terms.4.refs_0_ = f32[24,896]{1,0:T(8,128)S(1)} custom-call(f32[1]{0:T(128)S(6)} %copy.16.ratio, f32[24,2304]{1,0:T(8,128)S(1)} %slice_dynamic-update-slice_fusion.scores.refs_0_, bf16[8000,768]{1,0:T(8,128)(2,1)} %refs_1_.5), custom_call_target="tpu_custom_call" | custom-call | tf_op jit(solution)/shard_map/terms/pallas_call | solution.py:436
  53.4 2.2 %terms.5.refs_0_ = f32[24,896]{1,0:T(8,128)S(1)} custom-call(f32[1]{0:T(128)S(6)} %copy.16.ratio, f32[24,2304]{1,0:T(8,128)S(1)} %collective-permute-done.11.scores.refs_1_, f32[24,896]{1,0:T(8,128)S(1)} %terms.4.refs_0_, bf16[8000,768]{1,0:T(8,128)(2,1)} %refs_1_.5), custom_call_target="tpu_custom_call" | custom-call | tf_op jit(solution)/shard_map/terms/pallas_call | solution.py:436
  55.8 2.2 %terms.6.refs_0_ = f32[24,896]{1,0:T(8,128)S(1)} custom-call(f32[1]{0:T(128)S(6)} %copy.16.ratio, f32[24,2304]{1,0:T(8,128)S(1)} %collective-permute-done.10.scores.refs_3_, f32[24,896]{1,0:T(8,128)S(1)} %terms.5.refs_0_, bf16[8000,768]{1,0:T(8,128)(2,1)} %refs_1_.5), custom_call_target="tpu_custom_call" | custom-call | tf_op jit(solution)/shard_map/terms/pallas_call | solution.py:436
  58.0 2.2 %terms.7.own = f32[24,896]{1,0:T(8,128)S(1)} custom-call(f32[1]{0:T(128)S(6)} %copy.16.ratio, f32[24,2304]{1,0:T(8,128)S(1)} %collective-permute-done.9.scores.refs_2_, f32[24,896]{1,0:T(8,128)S(1)} %terms.6.refs_0_, bf16[8000,768]{1,0:T(8,128)(2,1)} %refs_1_.5), custom_call_target="tpu_custom_call" | custom-call | tf_op jit(solution)/shard_map/terms/pallas_call | solution.py:436
  60.3 1.3 %collective-permute-done.12.other = f32[24,896]{1,0:T(8,128)S(1)} collective-permute-done((f32[24,896]{1,0:T(8,128)S(1)}, f32[24,896]{1,0:T(8,128)S(1)}, u32[]{:S(2)}, u32[]{:S(2)}) %collective-permute-start.12) | collective-permute-done | bytes 86048 | tf_op jit(solution)/shard_map/ppermute | solution.py:41
  61.5 1.2 %update.1 = (f32[24,768]{1,0:T(8,128)S(1)}, f32[24,768]{1,0:T(8,128)S(1)}, f32[24,128]{1,0:T(8,128)S(1)}, f32[24,128]{1,0:T(8,128)S(1)}) custom-call(f32[8,768]{1,0:T(8,128)S(1)} %get-tuple-element.34.diag, f32[24,768]{1,0:T(8,128)S(1)} %get-tuple-element.35.start, f32[24,768]{1,0:T(8,128)} %panel.3, f32[24,896]{1,0:T(8,128)S(1)} %terms.7.own, ...), custom_call_target="tpu_custom_call" | custom-call | tf_op jit(solution)/shard_map/update/pallas_call | solution.py:459
  62.7 1.2 %collective-permute-start.13 = (f32[24,128]{1,0:T(8,128)S(1)}, f32[24,128]{1,0:T(8,128)S(1)}, u32[]{:S(2)}, u32[]{:S(2)}) collective-permute-start(f32[24,128]{1,0:T(8,128)S(1)} %get-tuple-element.50), channel_id=1, source_target_pairs={{0,2},{2,0},{4,6},{6,4},{8,10},{10,8},{12,14},{14,12},{16,18},{18,... | collective-permute-start | bytes 36872 | tf_op jit(solution)/shard_map/ppermute | solution.py:41
  64.9 1.3 %collective-permute-start.15 = (f32[24,128]{1,0:T(8,128)S(1)}, f32[24,128]{1,0:T(8,128)S(1)}, u32[]{:S(2)}, u32[]{:S(2)}) collective-permute-start(f32[24,128]{1,0:T(8,128)S(1)} %get-tuple-element.50), channel_id=1, source_target_pairs={{0,6},{2,4},{4,2},{6,0},{8,14},{10,12},{12,10},{14,8},{16,22},{18,... | collective-permute-start | bytes 36872 | tf_op jit(solution)/shard_map/ppermute | solution.py:41
  66.4 3.8 %collective-permute-start.23 = (f32[200,128]{1,0:T(8,128)S(1)}, f32[200,128]{1,0:T(8,128)S(1)}, u32[]{:S(2)}, u32[]{:S(2)}) collective-permute-start(f32[200,128]{1,0:T(8,128)S(1)} %get-tuple-element.61), channel_id=1, source_target_pairs={{0,8},{2,10},{4,12},{6,14},{8,0},{10,2},{12,4},{14,6},{16,24},{18,... | collective-permute-start | bytes 307208 | tf_op jit(solution)/shard_map/ppermute | solution.py:41
  70.2 2.4 %collective-permute-start.25 = (f32[200,128]{1,0:T(8,128)S(1)}, f32[200,128]{1,0:T(8,128)S(1)}, u32[]{:S(2)}, u32[]{:S(2)}) collective-permute-start(f32[200,128]{1,0:T(8,128)S(1)} %get-tuple-element.63), channel_id=1, source_target_pairs={{0,24},{2,26},{4,28},{6,30},{8,16},{10,18},{12,20},{14,22},{16,8},... | collective-permute-start | bytes 307208 | tf_op jit(solution)/shard_map/ppermute | solution.py:41
  74.7 4.1 %collective-permute-done.16.refs_1_ = f32[24,128]{1,0:T(8,128)S(1)} collective-permute-done((f32[24,128]{1,0:T(8,128)S(1)}, f32[24,128]{1,0:T(8,128)S(1)}, u32[]{:S(2)}, u32[]{:S(2)}) %collective-permute-start.16) | collective-permute-done | bytes 12320 | tf_op jit(solution)/shard_map/ppermute | solution.py:41
  80.1 2.0 %collective-permute-done.17.refs_2_ = f32[24,128]{1,0:T(8,128)S(1)} collective-permute-done((f32[24,128]{1,0:T(8,128)S(1)}, f32[24,128]{1,0:T(8,128)S(1)}, u32[]{:S(2)}, u32[]{:S(2)}) %collective-permute-start.17) | collective-permute-done | bytes 12320 | tf_op jit(solution)/shard_map/ppermute | solution.py:41
  82.0 2.3 %collective-permute-done.18.refs_3_ = f32[24,128]{1,0:T(8,128)S(1)} collective-permute-done((f32[24,128]{1,0:T(8,128)S(1)}, f32[24,128]{1,0:T(8,128)S(1)}, u32[]{:S(2)}, u32[]{:S(2)}) %collective-permute-start.18) | collective-permute-done | bytes 12320 | tf_op jit(solution)/shard_map/ppermute | solution.py:41
  85.0 2.1 %gram.1 = f32[1,64,1024]{2,1,0:T(8,128)} custom-call(s32[1,24]{1,0:T(1,128)} %sizes.3, f32[24,128]{1,0:T(8,128)S(1)} %get-tuple-element.51.alpha, f32[24,2304]{1,0:T(8,128)S(1)} %slice_dynamic-update-slice_fusion.scores.refs_0_, f32[24,2304]{1,0:T(8,128)S(1)} %collective-permute-done.11.scores.refs_1_, f32[24,2304]{1,0:T(8,128)S(1)} %collective-permute-done.9.scores.refs_2_, ...), custom_call_target="tpu_custom_call" | custom-call | tf_op jit(solution)/shard_map/gram/pallas_call | solution.py:480
  (53 shorter events, 11.1 us)
Async XLA Ops:
  9.0 12.0 %collective-permute-start = (f32[24,2304]{1,0:T(8,128)S(1)}, f32[24,2304]{1,0:T(8,128)S(1)}, u32[]{:S(2)}, u32[]{:S(2)}) collective-permute-start(f32[24,2304]{1,0:T(8,128)S(1)} %get-tuple-element.41), channel_id=1, source_target_pairs={{0,2},{2,0},{4,6},{6,4},{8,10},{10,8},{12,14},{14,12},{16,18},{18,... | collective-permute-start | bytes 663560 | tf_op jit(solution)/shard_map/ppermute | solution.py:41
  12.0 11.6 %collective-permute-start.1 = (f32[24,2304]{1,0:T(8,128)S(1)}, f32[24,2304]{1,0:T(8,128)S(1)}, u32[]{:S(2)}, u32[]{:S(2)}) collective-permute-start(f32[24,2304]{1,0:T(8,128)S(1)} %get-tuple-element.43), channel_id=1, source_target_pairs={{0,4},{2,6},{4,0},{6,2},{8,12},{10,14},{12,8},{14,10},{16,20},{18,... | collective-permute-start | bytes 663560 | tf_op jit(solution)/shard_map/ppermute | solution.py:41
  13.5 10.1 %collective-permute-start.2 = (f32[24,2304]{1,0:T(8,128)S(1)}, f32[24,2304]{1,0:T(8,128)S(1)}, u32[]{:S(2)}, u32[]{:S(2)}) collective-permute-start(f32[24,2304]{1,0:T(8,128)S(1)} %get-tuple-element.37), channel_id=1, source_target_pairs={{0,6},{2,4},{4,2},{6,0},{8,14},{10,12},{12,10},{14,8},{16,22},{18,... | collective-permute-start | bytes 663560 | tf_op jit(solution)/shard_map/ppermute | solution.py:41
  23.8 5.1 %collective-permute-start.3 = (f32[24,768]{1,0:T(8,128)S(1)}, f32[24,768]{1,0:T(8,128)S(1)}, u32[]{:S(2)}, u32[]{:S(2)}) collective-permute-start(f32[24,768]{1,0:T(8,128)S(1)} %get-tuple-element.69), channel_id=1, source_target_pairs={{0,8},{2,10},{4,12},{6,14},{8,0},{10,2},{12,4},{14,6},{16,24},{18,... | collective-permute-start | bytes 221192 | tf_op jit(solution)/shard_map/ppermute | solution.py:41
  25.4 6.8 %collective-permute-start.4 = (f32[24,768]{1,0:T(8,128)S(1)}, f32[24,768]{1,0:T(8,128)S(1)}, u32[]{:S(2)}, u32[]{:S(2)}) collective-permute-start(f32[24,768]{1,0:T(8,128)S(1)} %get-tuple-element.70), channel_id=1, source_target_pairs={{0,16},{2,18},{4,20},{6,22},{8,24},{10,26},{12,28},{14,30},{16,0},... | collective-permute-start | bytes 221192 | tf_op jit(solution)/shard_map/ppermute | solution.py:41
  28.0 6.3 %collective-permute-start.5 = (f32[24,768]{1,0:T(8,128)S(1)}, f32[24,768]{1,0:T(8,128)S(1)}, u32[]{:S(2)}, u32[]{:S(2)}) collective-permute-start(f32[24,768]{1,0:T(8,128)S(1)} %concatenate.18), channel_id=1, source_target_pairs={{0,24},{2,26},{4,28},{6,30},{8,16},{10,18},{12,20},{14,22},{16,8},... | collective-permute-start | bytes 221192 | tf_op jit(solution)/shard_map/ppermute | solution.py:41
  34.4 6.5 %collective-permute-start.6 = (f32[24,512]{1,0:T(8,128)S(1)}, f32[24,512]{1,0:T(8,128)S(1)}, u32[]{:S(2)}, u32[]{:S(2)}) collective-permute-start(f32[24,512]{1,0:T(8,128)S(1)} %get-tuple-element.67), channel_id=1, source_target_pairs={{0,8},{2,10},{4,12},{6,14},{8,0},{10,2},{12,4},{14,6},{16,24},{18,... | collective-permute-start | bytes 147464 | tf_op jit(solution)/shard_map/ppermute | solution.py:41
  34.4 13.3 %collective-permute-start.19 = (f32[200,512]{1,0:T(8,128)}, f32[200,512]{1,0:T(8,128)S(1)}, u32[]{:S(2)}, u32[]{:S(2)}) collective-permute-start(f32[200,512]{1,0:T(8,128)} %get-tuple-element.54), channel_id=1, source_target_pairs={{0,2},{2,0},{4,6},{6,4},{8,10},{10,8},{12,14},{14,12},{16,18},{18,... | collective-permute-start | bytes 1228808 | tf_op jit(solution)/shard_map/ppermute | solution.py:41
  35.7 12.0 %collective-permute-start.20 = (f32[200,512]{1,0:T(8,128)S(1)}, f32[200,512]{1,0:T(8,128)S(1)}, u32[]{:S(2)}, u32[]{:S(2)}) collective-permute-start(f32[200,512]{1,0:T(8,128)S(1)} %get-tuple-element.55), channel_id=1, source_target_pairs={{0,4},{2,6},{4,0},{6,2},{8,12},{10,14},{12,8},{14,10},{16,20},{18,... | collective-permute-start | bytes 1228808 | tf_op jit(solution)/shard_map/ppermute | solution.py:41
  36.6 5.0 %collective-permute-start.7 = (f32[24,512]{1,0:T(8,128)S(1)}, f32[24,512]{1,0:T(8,128)S(1)}, u32[]{:S(2)}, u32[]{:S(2)}) collective-permute-start(f32[24,512]{1,0:T(8,128)S(1)} %get-tuple-element.67), channel_id=1, source_target_pairs={{0,16},{2,18},{4,20},{6,22},{8,24},{10,26},{12,28},{14,30},{16,0},... | collective-permute-start | bytes 147464 | tf_op jit(solution)/shard_map/ppermute | solution.py:41
  38.3 5.9 %collective-permute-start.8 = (f32[24,512]{1,0:T(8,128)S(1)}, f32[24,512]{1,0:T(8,128)S(1)}, u32[]{:S(2)}, u32[]{:S(2)}) collective-permute-start(f32[24,512]{1,0:T(8,128)S(1)} %get-tuple-element.67), channel_id=1, source_target_pairs={{0,24},{2,26},{4,28},{6,30},{8,16},{10,18},{12,20},{14,22},{16,8},... | collective-permute-start | bytes 147464 | tf_op jit(solution)/shard_map/ppermute | solution.py:41
  44.2 9.2 %collective-permute-start.11 = (f32[24,2304]{1,0:T(8,128)S(1)}, f32[24,2304]{1,0:T(8,128)S(1)}, u32[]{:S(2)}, u32[]{:S(2)}) collective-permute-start(f32[24,2304]{1,0:T(8,128)S(1)} %slice_dynamic-update-slice_fusion.scores.refs_0_), channel_id=1, source_target_pairs={{0,2},{2,0},{4,6},{6,4},{8,10},{10,8},{12,14},{14,12},{16,18},{18,... | collective-permute-start | bytes 663560 | tf_op jit(solution)/shard_map/ppermute | solution.py:41
  45.4 10.4 %collective-permute-start.10 = (f32[24,2304]{1,0:T(8,128)S(1)}, f32[24,2304]{1,0:T(8,128)S(1)}, u32[]{:S(2)}, u32[]{:S(2)}) collective-permute-start(f32[24,2304]{1,0:T(8,128)S(1)} %slice_dynamic-update-slice_fusion.scores.refs_0_), channel_id=1, source_target_pairs={{0,6},{2,4},{4,2},{6,0},{8,14},{10,12},{12,10},{14,8},{16,22},{18,... | collective-permute-start | bytes 663560 | tf_op jit(solution)/shard_map/ppermute | solution.py:41
  47.0 11.0 %collective-permute-start.9 = (f32[24,2304]{1,0:T(8,128)S(1)}, f32[24,2304]{1,0:T(8,128)S(1)}, u32[]{:S(2)}, u32[]{:S(2)}) collective-permute-start(f32[24,2304]{1,0:T(8,128)S(1)} %slice_dynamic-update-slice_fusion.scores.refs_0_), channel_id=1, source_target_pairs={{0,4},{2,6},{4,0},{6,2},{8,12},{10,14},{12,8},{14,10},{16,20},{18,... | collective-permute-start | bytes 663560 | tf_op jit(solution)/shard_map/ppermute | solution.py:41
  47.8 0.7 copy-start
  48.5 0.7 copy-start.2
  49.2 17.0 %collective-permute-start.21 = (f32[200,256]{1,0:T(8,128)S(1)}, f32[200,256]{1,0:T(8,128)S(1)}, u32[]{:S(2)}, u32[]{:S(2)}) collective-permute-start(f32[200,256]{1,0:T(8,128)S(1)} %get-tuple-element.58), channel_id=1, source_target_pairs={{0,4},{2,6},{4,0},{6,2},{8,12},{10,14},{12,8},{14,10},{16,20},{18,... | collective-permute-start | bytes 614408 | tf_op jit(solution)/shard_map/ppermute | solution.py:41
  50.5 15.7 %collective-permute-start.22 = (f32[200,256]{1,0:T(8,128)}, f32[200,256]{1,0:T(8,128)S(1)}, u32[]{:S(2)}, u32[]{:S(2)}) collective-permute-start(f32[200,256]{1,0:T(8,128)} %copy-done.2), channel_id=1, source_target_pairs={{0,2},{2,0},{4,6},{6,4},{8,10},{10,8},{12,14},{14,12},{16,18},{18,... | collective-permute-start | bytes 614408 | tf_op jit(solution)/shard_map/ppermute | solution.py:41
  55.6 10.7 %copy-start.1 = (f32[200,256]{1,0:T(8,128)S(1)}, f32[200,256]{1,0:T(8,128)}, u32[]{:S(2)}) copy-start(f32[200,256]{1,0:T(8,128)} %copy-done) | copy-start | bytes 614404
  60.2 1.3 %collective-permute-start.12 = (f32[24,896]{1,0:T(8,128)S(1)}, f32[24,896]{1,0:T(8,128)S(1)}, u32[]{:S(2)}, u32[]{:S(2)}) collective-permute-start(f32[24,896]{1,0:T(8,128)S(1)} %terms.7.own), channel_id=1, source_target_pairs={{0,1},{1,0},{2,3},{3,2},{4,5},{5,4},{6,7},{7,6},{8,9},{9,8},{10,11... | collective-permute-start | bytes 258056 | tf_op jit(solution)/shard_map/ppermute | solution.py:41
  62.7 7.5 %collective-permute-start.13 = (f32[24,128]{1,0:T(8,128)S(1)}, f32[24,128]{1,0:T(8,128)S(1)}, u32[]{:S(2)}, u32[]{:S(2)}) collective-permute-start(f32[24,128]{1,0:T(8,128)S(1)} %get-tuple-element.50), channel_id=1, source_target_pairs={{0,2},{2,0},{4,6},{6,4},{8,10},{10,8},{12,14},{14,12},{16,18},{18,... | collective-permute-start | bytes 36872 | tf_op jit(solution)/shard_map/ppermute | solution.py:41
  63.9 8.7 %collective-permute-start.14 = (f32[24,128]{1,0:T(8,128)S(1)}, f32[24,128]{1,0:T(8,128)S(1)}, u32[]{:S(2)}, u32[]{:S(2)}) collective-permute-start(f32[24,128]{1,0:T(8,128)S(1)} %get-tuple-element.50), channel_id=1, source_target_pairs={{0,4},{2,6},{4,0},{6,2},{8,12},{10,14},{12,8},{14,10},{16,20},{18,... | collective-permute-start | bytes 36872 | tf_op jit(solution)/shard_map/ppermute | solution.py:41
  64.9 7.7 %collective-permute-start.15 = (f32[24,128]{1,0:T(8,128)S(1)}, f32[24,128]{1,0:T(8,128)S(1)}, u32[]{:S(2)}, u32[]{:S(2)}) collective-permute-start(f32[24,128]{1,0:T(8,128)S(1)} %get-tuple-element.50), channel_id=1, source_target_pairs={{0,6},{2,4},{4,2},{6,0},{8,14},{10,12},{12,10},{14,8},{16,22},{18,... | collective-permute-start | bytes 36872 | tf_op jit(solution)/shard_map/ppermute | solution.py:41
  66.4 18.6 %collective-permute-start.23 = (f32[200,128]{1,0:T(8,128)S(1)}, f32[200,128]{1,0:T(8,128)S(1)}, u32[]{:S(2)}, u32[]{:S(2)}) collective-permute-start(f32[200,128]{1,0:T(8,128)S(1)} %get-tuple-element.61), channel_id=1, source_target_pairs={{0,8},{2,10},{4,12},{6,14},{8,0},{10,2},{12,4},{14,6},{16,24},{18,... | collective-permute-start | bytes 307208 | tf_op jit(solution)/shard_map/ppermute | solution.py:41
  70.2 14.8 %collective-permute-start.24 = (f32[200,128]{1,0:T(8,128)S(1)}, f32[200,128]{1,0:T(8,128)S(1)}, u32[]{:S(2)}, u32[]{:S(2)}) collective-permute-start(f32[200,128]{1,0:T(8,128)S(1)} %get-tuple-element.62), channel_id=1, source_target_pairs={{0,16},{2,18},{4,20},{6,22},{8,24},{10,26},{12,28},{14,30},{16,0},... | collective-permute-start | bytes 307208 | tf_op jit(solution)/shard_map/ppermute | solution.py:41
  70.2 14.8 %collective-permute-start.25 = (f32[200,128]{1,0:T(8,128)S(1)}, f32[200,128]{1,0:T(8,128)S(1)}, u32[]{:S(2)}, u32[]{:S(2)}) collective-permute-start(f32[200,128]{1,0:T(8,128)S(1)} %get-tuple-element.63), channel_id=1, source_target_pairs={{0,24},{2,26},{4,28},{6,30},{8,16},{10,18},{12,20},{14,22},{16,8},... | collective-permute-start | bytes 307208 | tf_op jit(solution)/shard_map/ppermute | solution.py:41
  72.6 6.2 %collective-permute-start.16 = (f32[24,128]{1,0:T(8,128)S(1)}, f32[24,128]{1,0:T(8,128)S(1)}, u32[]{:S(2)}, u32[]{:S(2)}) collective-permute-start(f32[24,128]{1,0:T(8,128)S(1)} %add_add_fusion.1.refs_0_), channel_id=1, source_target_pairs={{0,8},{2,10},{4,12},{6,14},{8,0},{10,2},{12,4},{14,6},{16,24},{18,... | collective-permute-start | bytes 36872 | tf_op jit(solution)/shard_map/ppermute | solution.py:41
  73.8 8.3 %collective-permute-start.17 = (f32[24,128]{1,0:T(8,128)S(1)}, f32[24,128]{1,0:T(8,128)S(1)}, u32[]{:S(2)}, u32[]{:S(2)}) collective-permute-start(f32[24,128]{1,0:T(8,128)S(1)} %add_add_fusion.1.refs_0_), channel_id=1, source_target_pairs={{0,16},{2,18},{4,20},{6,22},{8,24},{10,26},{12,28},{14,30},{16,0},... | collective-permute-start | bytes 36872 | tf_op jit(solution)/shard_map/ppermute | solution.py:41
  78.8 5.5 %collective-permute-start.18 = (f32[24,128]{1,0:T(8,128)S(1)}, f32[24,128]{1,0:T(8,128)S(1)}, u32[]{:S(2)}, u32[]{:S(2)}) collective-permute-start(f32[24,128]{1,0:T(8,128)S(1)} %add_add_fusion.1.refs_0_), channel_id=1, source_target_pairs={{0,24},{2,26},{4,28},{6,30},{8,16},{10,18},{12,20},{14,22},{16,8},... | collective-permute-start | bytes 36872 | tf_op jit(solution)/shard_map/ppermute | solution.py:41

commit v4 on v3

--- a/solution.py
+++ b/solution.py
@@ -208,7 +208,7 @@
 
 def cross_kernel(plan, block, sizes, weights, variants, *refs):
     *outs, scaled = refs
-    keep_x, keep_y, send_x, send_y = outs
+    own_x, own_y, pass_x, pass_y, send_x, send_y = outs
     me = lax.axis_index("samp")
     count = variants.shape[0]
     half = GENE_MAX // 2
@@ -217,9 +217,9 @@
     lane = lax.broadcasted_iota(jnp.int32, (1, quarter), 1)
     column = lax.broadcasted_iota(jnp.int32, (count, quarter), 0)
     places = (
-        ((keep_x, 0), (keep_y, 0)),
-        ((send_x, 0), (keep_y, 1)),
-        ((keep_x, 1), (send_y, 0)),
+        ((own_x, 0), (own_y, 0)),
+        ((send_x, 0), (pass_y, 0)),
+        ((pass_x, 0), (send_y, 0)),
         ((send_x, 1), (send_y, 1)),
     )
     for digit in range(plan.radix):
@@ -242,28 +242,42 @@
             out[:, at * quarter : (at + 1) * quarter] = folded
 
 
-def halves_kernel(keep_x, keep_y, got_x, got_y, own_x, own_y, pass_x, pass_y):
-    quarter = own_x.shape[1]
-    own_x[...] = keep_x[:, :quarter] + got_x[:, :quarter]
-    own_y[...] = keep_y[:, :quarter] + got_y[:, :quarter]
-    pass_x[...] = keep_x[:, quarter:] + got_x[:, quarter:]
-    pass_y[...] = keep_y[:, quarter:] + got_y[:, quarter:]
-
-
-def split_kernel(terms, *refs):
-    ins, outs = refs[: -len(terms[1])], refs[-len(terms[1]) :]
-    if terms[0]:
-        low, high = ins[0][...] + ins[2][...], ins[1][...] + ins[3][...]
+def halves_kernel(got_x, got_y, *refs):
+    before, after = refs[:4], refs[4:]
+    quarter = before[0].shape[1]
+    for at, (old, new) in enumerate(zip(before, after)):
+        got = (got_x, got_y)[at % 2]
+        low = at // 2 * quarter
+        new[...] = old[...] + got[:, low : low + quarter]
+
+
+def split_kernel(paired, keep, *refs):
+    *terms, kept, sent = refs
+    if paired:
+        low, high = keep[...] + terms[1][...], terms[0][...] + terms[2][...]
     else:
-        total = ins[0][...]
-        for ref in ins[1:]:
+        total = keep[...]
+        for ref in terms:
             total = total + ref[...]
         low, high = total[:, : total.shape[1] // 2], total[:, total.shape[1] // 2 :]
-    wide = low.shape[1] // len(outs)
-    for j, out in enumerate(outs):
-        out[...] = jnp.concatenate(
-            [low[:, j * wide : (j + 1) * wide], high[:, j * wide : (j + 1) * wide]], axis=1
-        )
+    wide = low.shape[1] // 4
+    cut = [part[:, j * wide : (j + 1) * wide] for j in range(4) for part in (low, high)]
+    kept[...] = jnp.concatenate(cut[0:2] + cut[4:6], axis=1)
+    sent[...] = jnp.concatenate(cut[2:4] + cut[6:8], axis=1)
+
+
+def merge_kernel(wide, *refs):
+    terms, outs = refs[:-4], refs[-4:]
+    tail = slice(4 * wide, terms[0].shape[1])
+    for place in [slice(j * wide, (j + 1) * wide) for j in range(4)] + [tail]:
+        total = terms[0][:, place]
+        for ref in terms[1:]:
+            total = total + ref[:, place]
+        if place is tail:
+            for out in outs:
+                out[:, wide:] = total
+        else:
+            outs[place.start // wide][:, :wide] = total
 
 
 def gram_kernel(plan, samples, sizes, alpha, *refs):
@@ -385,54 +399,67 @@
     block = num_variants // count
     quarter = block * len(rest)
     half = GENE_MAX // 2
-    keep_x, keep_y, send_x, send_y = pl.pallas_call(
+    *parts, send_x, send_y = pl.pallas_call(
         functools.partial(cross_kernel, plan, block),
-        out_shape=[VMEM((half, 2 * quarter), F32)] * radix,
+        out_shape=[VMEM((half, quarter), F32)] * 4 + [VMEM((half, 2 * quarter), F32)] * 2,
         in_specs=[smem] + [vmem] * 2,
-        out_specs=[vmem] * radix,
+        out_specs=[vmem] * 6,
         scratch_shapes=[VMEM((quarter, samples), BF16)],
         name="cross",
     )(gene_sizes, weights, tied(variants, sent[0]))
 
-    got = sent[0]
-    for d in range(1, radix):
-        got = got + swap(sent[d], count, firsts[d])
-    got, send_x, send_y = lax.optimization_barrier((got, send_x, send_y))
+    terms = [sent[0]] + [swap(sent[d], count, firsts[d]) for d in range(1, radix)]
+    wide = columns
+    assert all(r == 4 for r, _ in later)
+    for level, (r, s) in enumerate(later):
+        wide //= r
+        pieces = pl.pallas_call(
+            functools.partial(merge_kernel, wide),
+            out_shape=[VMEM((rows, wide + share), F32)] * r,
+            in_specs=[vmem] * len(terms),
+            out_specs=[vmem] * r,
+            name="merge",
+        )(*map(in_vmem, terms))
+        if level == 0:
+            piece, send_x, send_y = lax.optimization_barrier((pieces[0], send_x, send_y))
+        else:
+            piece = pieces[0]
+        terms = [piece] + [swap(pieces[d], count, d * s) for d in range(1, r)]
+    total = terms[0]
+    for one in terms[1:]:
+        total = total + one
+    got, shared = total[:, :wide], total[:, wide:]
     got_x = swap(send_x, count, firsts[1])
     got_y = swap(send_y, count, firsts[2])
-    piece = VMEM((half, quarter), F32)
     own_x, own_y, pass_x, pass_y = pl.pallas_call(
-        halves_kernel, out_shape=[piece] * 4, in_specs=[vmem] * 4, out_specs=[vmem] * 4, name="halves"
-    )(*map(in_vmem, (keep_x, keep_y, got_x, got_y)))
+        halves_kernel,
+        out_shape=[VMEM((half, quarter), F32)] * 4,
+        in_specs=[vmem] * 6,
+        out_specs=[vmem] * 4,
+        input_output_aliases={2 + i: i for i in range(4)},
+        name="halves",
+    )(*map(in_vmem, (got_x, got_y, *parts)))
     sums = [own_x, own_y, swap(pass_x, count, firsts[2]), swap(pass_y, count, firsts[1])]
-    paired, wide = True, quarter
-    for r, s in later:
+    wide = quarter
+    for level, (r, s) in enumerate(later):
         wide //= r
-        pieces = pl.pallas_call(
-            functools.partial(split_kernel, (paired, range(r))),
-            out_shape=[VMEM((half, 2 * wide), F32)] * r,
+        kept, moved = pl.pallas_call(
+            functools.partial(split_kernel, level == 0),
+            out_shape=[VMEM((half, 4 * wide), F32)] * 2,
             in_specs=[vmem] * len(sums),
-            out_specs=[vmem] * r,
+            out_specs=[vmem] * 2,
             name="split",
         )(*map(in_vmem, sums))
-        paired = False
-        sums = [pieces[0]] + [swap(pieces[d], count, d * s) for d in range(1, r)]
-
-    shared, got = got[:, -share:], got[:, :-share]
-    for r, s in later:
-        wide = got.shape[1] // r
-        pieces = [jnp.concatenate([got[:, d * wide : (d + 1) * wide], shared], axis=1) for d in range(r)]
-        total = pieces[0]
-        for d in range(1, r):
-            total = total + swap(pieces[d], count, d * s)
-        got, shared = total[:, :wide], total[:, wide:]
+        both = kept + swap(moved, count, s)
+        sums = [both[:, : 2 * wide], swap(both[:, 2 * wide :], count, 2 * s)]
+
     for r, s in reversed(later):
         got = jnp.concatenate([got] + [swap(got, count, d * s) for d in range(1, r)], axis=1)
     everything = jnp.concatenate([got, shared], axis=1)
     arrays = [in_vmem(everything)] + [in_vmem(swap(everything, count, firsts[d])) for d in range(1, radix)]
 
     own = ()
-    for d in (0, 1, 3, 2):
+    for d in range(radix):
         whole = pl.pallas_call(
             functools.partial(terms_kernel, plan, d),
             out_shape=VMEM((rows, samples + LANES), F32),

time: 87.4 us -> 82.5 us (0.944)
  waiting for transfers between devices: 21.9 us -> 20.2 us
  local copies, waits for them, and re-layouts: 2.66 us -> 1.3 us
  starting transfers between devices: 32.9 us -> 31.7 us
    ppermute x26 -> x25, waiting for transfers between devices: 21.9 us -> 20.2 us  [swap(): return lax.ppermute(array, axis, [(i, i ^ offset) for i in range(count)])]
    unnamed x11 -> x5, local copies, waits for them, and re-layouts: 2.63 us -> 1.28 us
    ppermute x26 -> x25, starting transfers between devices: 32.9 us -> 31.7 us  [swap(): return lax.ppermute(array, axis, [(i, i ^ offset) for i in range(count)])]
  transfers between devices with their start and end apart: 26 -> 25, of which waited for: 11 -> 10; matrix products, arithmetic and copies ran while one was open for 1% -> 2% of each run, Pallas kernels for 21% -> 21%
where the time goes in v4:
time: 82.5 us; the launch traced here: 82.3 us
  starting transfers between devices  31.7 us (38%)
  Pallas kernels  27.5 us (33%)
  waiting for transfers between devices  20.2 us (24%)
  between operations  1.46 us (2%)
  local copies, waits for them, and re-layouts  1.3 us (2%)
    ppermute x25, starting transfers between devices, swap(): return lax.ppermute(array, axis, [(i, i ^ offset) for i in range(count)])  31.7 us
    ppermute x25, waiting for transfers between devices, swap(): return lax.ppermute(array, axis, [(i, i ^ offset) for i in range(count)])  20.2 us
    pallas_call x4, Pallas kernels, body(): pl.pallas_call(functools.partial(terms_kernel, plan, d), out_shape=VMEM((...  8.71 us
    pallas_call x2, Pallas kernels, body(): pl.pallas_call(functools.partial(scores_kernel, plan, digits), out_shape=...  7.62 us
    pallas_call x1, Pallas kernels, body(): pl.pallas_call(functools.partial(cross_kernel, plan, block), out_shape=[V...  3.7 us
    pallas_call x1, Pallas kernels, body(): pl.pallas_call(functools.partial(lead_kernel, plan, lead), out_shape=[pay...  3.08 us
    pallas_call x1, Pallas kernels, body(): pl.pallas_call(functools.partial(gram_kernel, plan, samples * count), out...  2.12 us
  transfers between devices with their start and end apart: 25, of which 10 were waited for; matrix products, arithmetic and copies ran while one was open for 2% of the time, Pallas kernels for 21%

profile of v4, /device:TPU:0, one launch (start us, length us, event | category | flops | bytes accessed | tf_op | source)
XLA Modules:
  0.0 82.3 jit_solution(9886831264741560376)
XLA Ops:
  1.3 3.1 %scores_lead.1 = (f32[24,2304]{1,0:T(8,128)S(1)}, f32[8,768]{1,0:T(8,128)S(1)}, f32[24,768]{1,0:T(8,128)S(1)}, bf16[24,768]{1,0:T(8,128)(2,1)S(1)}, bf16[48,768]{1,0:T(8,128)(2,1)S(1)}, /*index=5*/f32[24,128]{1,0:T(8,128)S(1)}) custom-call(f32[1]{0:T(128)S(6)} %copy.24.ratio, f32[768]{0:T(1024)} %weights.3, f32[24,768]{1,0:T(8,128)} %panel.3, ...), custom_call_target="tpu_custom_call" | custom-call | tf_op jit(solution)/shard_map/scores_lead/pallas_call | solution.py:357
  4.4 4.6 %scores.2 = (f32[24,2304]{1,0:T(8,128)S(1)}, f32[24,2304]{1,0:T(8,128)S(1)}) custom-call(bf16[24,768]{1,0:T(8,128)(2,1)S(1)} %get-tuple-element.46.start_bf, bf16[48,768]{1,0:T(8,128)(2,1)S(1)} %get-tuple-element.43.weighted, f32[24,128]{1,0:T(8,128)S(1)} %get-tuple-element.44.stats, bf16[8000,768]{1,0:T(8,128)(2,1)} %refs_1_.5, bf16[1024,768]{1,0:T(8,128)(2,1)} %variants.6), custom_call_target="tpu_custom_call" | custom-call | tf_op jit(solution)/shard_map/scores/pallas_call | solution.py:383
  9.0 3.0 %collective-permute-start = (f32[24,2304]{1,0:T(8,128)S(1)}, f32[24,2304]{1,0:T(8,128)S(1)}, u32[]{:S(2)}, u32[]{:S(2)}) collective-permute-start(f32[24,2304]{1,0:T(8,128)S(1)} %get-tuple-element.45), channel_id=1, source_target_pairs={{0,2},{2,0},{4,6},{6,4},{8,10},{10,8},{12,14},{14,12},{16,18},{18,... | collective-permute-start | bytes 663560 | tf_op jit(solution)/shard_map/ppermute | solution.py:41
  12.0 1.5 %collective-permute-start.1 = (f32[24,2304]{1,0:T(8,128)S(1)}, f32[24,2304]{1,0:T(8,128)S(1)}, u32[]{:S(2)}, u32[]{:S(2)}) collective-permute-start(f32[24,2304]{1,0:T(8,128)S(1)} %get-tuple-element.47), channel_id=1, source_target_pairs={{0,4},{2,6},{4,0},{6,2},{8,12},{10,14},{12,8},{14,10},{16,20},{18,... | collective-permute-start | bytes 663560 | tf_op jit(solution)/shard_map/ppermute | solution.py:41
  13.6 3.0 %scores.3.refs_0_ = f32[24,2304]{1,0:T(8,128)S(1)} custom-call(bf16[24,768]{1,0:T(8,128)(2,1)S(1)} %get-tuple-element.46.start_bf, bf16[48,768]{1,0:T(8,128)(2,1)S(1)} %get-tuple-element.43.weighted, f32[24,128]{1,0:T(8,128)S(1)} %get-tuple-element.44.stats, bf16[8000,768]{1,0:T(8,128)(2,1)} %refs_1_.5, bf16[1024,768]{1,0:T(8,128)(2,1)} %variants.6), custom_call_target="tpu_custom_call" | custom-call | tf_op jit(solution)/shard_map/scores/pallas_call | solution.py:383
  16.6 1.7 %collective-permute-done.refs_1_ = f32[24,2304]{1,0:T(8,128)S(1)} collective-permute-done((f32[24,2304]{1,0:T(8,128)S(1)}, f32[24,2304]{1,0:T(8,128)S(1)}, u32[]{:S(2)}, u32[]{:S(2)}) %collective-permute-start) | collective-permute-done | bytes 221216 | tf_op jit(solution)/shard_map/ppermute | solution.py:41
  18.3 5.3 %collective-permute-done.1.refs_2_ = f32[24,2304]{1,0:T(8,128)S(1)} collective-permute-done((f32[24,2304]{1,0:T(8,128)S(1)}, f32[24,2304]{1,0:T(8,128)S(1)}, u32[]{:S(2)}, u32[]{:S(2)}) %collective-permute-start.1) | collective-permute-done | bytes 221216 | tf_op jit(solution)/shard_map/ppermute | solution.py:41
  23.7 1.6 %collective-permute-start.3 = (f32[24,768]{1,0:T(8,128)S(1)}, f32[24,768]{1,0:T(8,128)S(1)}, u32[]{:S(2)}, u32[]{:S(2)}) collective-permute-start(f32[24,768]{1,0:T(8,128)S(1)} %get-tuple-element.53), channel_id=1, source_target_pairs={{0,8},{2,10},{4,12},{6,14},{8,0},{10,2},{12,4},{14,6},{16,24},{18,... | collective-permute-start | bytes 221192 | tf_op jit(solution)/shard_map/ppermute | solution.py:41
  25.4 2.6 %collective-permute-start.4 = (f32[24,768]{1,0:T(8,128)S(1)}, f32[24,768]{1,0:T(8,128)S(1)}, u32[]{:S(2)}, u32[]{:S(2)}) collective-permute-start(f32[24,768]{1,0:T(8,128)S(1)} %get-tuple-element.54), channel_id=1, source_target_pairs={{0,16},{2,18},{4,20},{6,22},{8,24},{10,26},{12,28},{14,30},{16,0},... | collective-permute-start | bytes 221192 | tf_op jit(solution)/shard_map/ppermute | solution.py:41
  28.2 3.7 %cross.1 = (f32[200,256]{1,0:T(8,128)S(1)}, f32[200,256]{1,0:T(8,128)S(1)}, f32[200,256]{1,0:T(8,128)S(1)}, f32[200,256]{1,0:T(8,128)S(1)}, f32[200,512]{1,0:T(8,128)S(1)}, /*index=5*/f32[200,512]{1,0:T(8,128)S(1)}) custom-call(s32[1,24]{1,0:T(1,128)} %sizes.3, f32[768]{0:T(1024)} %weights.3, bf16[1024,768]{1,0:T(8,128)(2,1)} %variants.6), custom_call_target="tpu_custom_call" | custom-call | tf_op jit(solution)/shard_map/cross/pallas_call | solution.py:402
  31.9 1.3 %collective-permute-start.19 = (f32[200,512]{1,0:T(8,128)S(1)}, f32[200,512]{1,0:T(8,128)S(1)}, u32[]{:S(2)}, u32[]{:S(2)}) collective-permute-start(f32[200,512]{1,0:T(8,128)S(1)} %get-tuple-element.60), channel_id=1, source_target_pairs={{0,2},{2,0},{4,6},{6,4},{8,10},{10,8},{12,14},{14,12},{16,18},{18,... | collective-permute-start | bytes 1228808 | tf_op jit(solution)/shard_map/ppermute | solution.py:41
  34.8 3.5 %collective-permute-start.7 = (f32[24,512]{1,0:T(8,128)S(1)}, f32[24,512]{1,0:T(8,128)S(1)}, u32[]{:S(2)}, u32[]{:S(2)}) collective-permute-start(f32[24,512]{1,0:T(8,128)S(1)} %get-tuple-element.74), channel_id=1, source_target_pairs={{0,16},{2,18},{4,20},{6,22},{8,24},{10,26},{12,28},{14,30},{16,0},... | collective-permute-start | bytes 147464 | tf_op jit(solution)/shard_map/ppermute | solution.py:41
  38.6 2.6 %collective-permute-done.7 = f32[24,512]{1,0:T(8,128)S(1)} collective-permute-done((f32[24,512]{1,0:T(8,128)S(1)}, f32[24,512]{1,0:T(8,128)S(1)}, u32[]{:S(2)}, u32[]{:S(2)}) %collective-permute-start.7) | collective-permute-done | bytes 49184 | tf_op jit(solution)/shard_map/ppermute | solution.py:41
  41.2 3.0 %collective-permute-done.8 = f32[24,512]{1,0:T(8,128)S(1)} collective-permute-done((f32[24,512]{1,0:T(8,128)S(1)}, f32[24,512]{1,0:T(8,128)S(1)}, u32[]{:S(2)}, u32[]{:S(2)}) %collective-permute-start.8) | collective-permute-done | bytes 49184 | tf_op jit(solution)/shard_map/ppermute | solution.py:41
  44.4 1.3 %collective-permute-start.21 = (f32[200,256]{1,0:T(8,128)S(1)}, f32[200,256]{1,0:T(8,128)S(1)}, u32[]{:S(2)}, u32[]{:S(2)}) collective-permute-start(f32[200,256]{1,0:T(8,128)S(1)} %get-tuple-element.68), channel_id=1, source_target_pairs={{0,4},{2,6},{4,0},{6,2},{8,12},{10,14},{12,8},{14,10},{16,20},{18,... | collective-permute-start | bytes 614408 | tf_op jit(solution)/shard_map/ppermute | solution.py:41
  46.4 1.2 %collective-permute-start.11 = (f32[24,2304]{1,0:T(8,128)S(1)}, f32[24,2304]{1,0:T(8,128)S(1)}, u32[]{:S(2)}, u32[]{:S(2)}) collective-permute-start(f32[24,2304]{1,0:T(8,128)S(1)} %slice_dynamic-update-slice_fusion.scores.refs_0_), channel_id=1, source_target_pairs={{0,2},{2,0},{4,6},{6,4},{8,10},{10,8},{12,14},{14,12},{16,18},{18,... | collective-permute-start | bytes 663560 | tf_op jit(solution)/shard_map/ppermute | solution.py:41
  48.5 1.4 %collective-permute-start.9 = (f32[24,2304]{1,0:T(8,128)S(1)}, f32[24,2304]{1,0:T(8,128)S(1)}, u32[]{:S(2)}, u32[]{:S(2)}) collective-permute-start(f32[24,2304]{1,0:T(8,128)S(1)} %slice_dynamic-update-slice_fusion.scores.refs_0_), channel_id=1, source_target_pairs={{0,6},{2,4},{4,2},{6,0},{8,14},{10,12},{12,10},{14,8},{16,22},{18,... | collective-permute-start | bytes 663560 | tf_op jit(solution)/shard_map/ppermute | solution.py:41
  49.9 1.9 %collective-permute-done.21.refs_1_ = f32[200,256]{1,0:T(8,128)S(1)} collective-permute-done((f32[200,256]{1,0:T(8,128)S(1)}, f32[200,256]{1,0:T(8,128)S(1)}, u32[]{:S(2)}, u32[]{:S(2)}) %collective-permute-start.21) | collective-permute-done | bytes 204832 | tf_op jit(solution)/shard_map/ppermute | solution.py:41
  51.8 1.3 %collective-permute-done.22.refs_2_ = f32[200,256]{1,0:T(8,128)S(1)} collective-permute-done((f32[200,256]{1,0:T(8,128)S(1)}, f32[200,256]{1,0:T(8,128)S(1)}, u32[]{:S(2)}, u32[]{:S(2)}) %collective-permute-start.22) | collective-permute-done | bytes 204832 | tf_op jit(solution)/shard_map/ppermute | solution.py:41
  53.4 2.2 %terms.4.refs_0_ = f32[24,896]{1,0:T(8,128)S(1)} custom-call(f32[1]{0:T(128)S(6)} %copy.24.ratio, f32[24,2304]{1,0:T(8,128)S(1)} %slice_dynamic-update-slice_fusion.scores.refs_0_, bf16[8000,768]{1,0:T(8,128)(2,1)} %refs_1_.5), custom_call_target="tpu_custom_call" | custom-call | tf_op jit(solution)/shard_map/terms/pallas_call | solution.py:463
  55.6 2.2 %terms.5.refs_0_ = f32[24,896]{1,0:T(8,128)S(1)} custom-call(f32[1]{0:T(128)S(6)} %copy.24.ratio, f32[24,2304]{1,0:T(8,128)S(1)} %collective-permute-done.11.scores.refs_1_, f32[24,896]{1,0:T(8,128)S(1)} %terms.4.refs_0_, bf16[8000,768]{1,0:T(8,128)(2,1)} %refs_1_.5), custom_call_target="tpu_custom_call" | custom-call | tf_op jit(solution)/shard_map/terms/pallas_call | solution.py:463
  57.8 2.2 %terms.6.refs_0_ = f32[24,896]{1,0:T(8,128)S(1)} custom-call(f32[1]{0:T(128)S(6)} %copy.24.ratio, f32[24,2304]{1,0:T(8,128)S(1)} %collective-permute-done.10.scores.refs_2_, f32[24,896]{1,0:T(8,128)S(1)} %terms.5.refs_0_, bf16[8000,768]{1,0:T(8,128)(2,1)} %refs_1_.5), custom_call_target="tpu_custom_call" | custom-call | tf_op jit(solution)/shard_map/terms/pallas_call | solution.py:463
  60.0 2.2 %terms.7.own = f32[24,896]{1,0:T(8,128)S(1)} custom-call(f32[1]{0:T(128)S(6)} %copy.24.ratio, f32[24,2304]{1,0:T(8,128)S(1)} %collective-permute-done.9.scores.refs_3_, f32[24,896]{1,0:T(8,128)S(1)} %terms.6.refs_0_, bf16[8000,768]{1,0:T(8,128)(2,1)} %refs_1_.5), custom_call_target="tpu_custom_call" | custom-call | tf_op jit(solution)/shard_map/terms/pallas_call | solution.py:463
  62.2 1.3 %collective-permute-done.12.other = f32[24,896]{1,0:T(8,128)S(1)} collective-permute-done((f32[24,896]{1,0:T(8,128)S(1)}, f32[24,896]{1,0:T(8,128)S(1)}, u32[]{:S(2)}, u32[]{:S(2)}) %collective-permute-start.12) | collective-permute-done | bytes 86048 | tf_op jit(solution)/shard_map/ppermute | solution.py:41
  63.5 1.2 %update.1 = (f32[24,768]{1,0:T(8,128)S(1)}, f32[24,768]{1,0:T(8,128)S(1)}, f32[24,128]{1,0:T(8,128)S(1)}, f32[24,128]{1,0:T(8,128)S(1)}) custom-call(f32[8,768]{1,0:T(8,128)S(1)} %get-tuple-element.38.diag, f32[24,768]{1,0:T(8,128)S(1)} %get-tuple-element.39.start, f32[24,768]{1,0:T(8,128)} %panel.3, f32[24,896]{1,0:T(8,128)S(1)} %terms.7.own, ...), custom_call_target="tpu_custom_call" | custom-call | tf_op jit(solution)/shard_map/update/pallas_call | solution.py:486
  66.0 2.2 %collective-permute-start.15 = (f32[24,128]{1,0:T(8,128)S(1)}, f32[24,128]{1,0:T(8,128)S(1)}, u32[]{:S(2)}, u32[]{:S(2)}) collective-permute-start(f32[24,128]{1,0:T(8,128)S(1)} %get-tuple-element.58), channel_id=1, source_target_pairs={{0,6},{2,4},{4,2},{6,0},{8,14},{10,12},{12,10},{14,8},{16,22},{18,... | collective-permute-start | bytes 36872 | tf_op jit(solution)/shard_map/ppermute | solution.py:41
  68.3 2.5 %collective-permute-start.24 = (f32[200,128]{1,0:T(8,128)S(1)}, f32[200,128]{1,0:T(8,128)S(1)}, u32[]{:S(2)}, u32[]{:S(2)}) collective-permute-start(f32[200,128]{1,0:T(8,128)S(1)} %get-tuple-element.72), channel_id=1, source_target_pairs={{0,16},{2,18},{4,20},{6,22},{8,24},{10,26},{12,28},{14,30},{16,0},... | collective-permute-start | bytes 307208 | tf_op jit(solution)/shard_map/ppermute | solution.py:41
  70.8 1.8 %collective-permute-start.16 = (f32[24,128]{1,0:T(8,128)S(1)}, f32[24,128]{1,0:T(8,128)S(1)}, u32[]{:S(2)}, u32[]{:S(2)}) collective-permute-start(f32[24,128]{1,0:T(8,128)S(1)} %add_add_fusion.1.refs_0_), channel_id=1, source_target_pairs={{0,8},{2,10},{4,12},{6,14},{8,0},{10,2},{12,4},{14,6},{16,24},{18,... | collective-permute-start | bytes 36872 | tf_op jit(solution)/shard_map/ppermute | solution.py:41
  72.6 1.3 %collective-permute-start.17 = (f32[24,128]{1,0:T(8,128)S(1)}, f32[24,128]{1,0:T(8,128)S(1)}, u32[]{:S(2)}, u32[]{:S(2)}) collective-permute-start(f32[24,128]{1,0:T(8,128)S(1)} %add_add_fusion.1.refs_0_), channel_id=1, source_target_pairs={{0,16},{2,18},{4,20},{6,22},{8,24},{10,26},{12,28},{14,30},{16,0},... | collective-permute-start | bytes 36872 | tf_op jit(solution)/shard_map/ppermute | solution.py:41
  73.9 1.3 %collective-permute-start.18 = (f32[24,128]{1,0:T(8,128)S(1)}, f32[24,128]{1,0:T(8,128)S(1)}, u32[]{:S(2)}, u32[]{:S(2)}) collective-permute-start(f32[24,128]{1,0:T(8,128)S(1)} %add_add_fusion.1.refs_0_), channel_id=1, source_target_pairs={{0,24},{2,26},{4,28},{6,30},{8,16},{10,18},{12,20},{14,22},{16,8},... | collective-permute-start | bytes 36872 | tf_op jit(solution)/shard_map/ppermute | solution.py:41
  77.2 2.2 %collective-permute-done.18.refs_3_ = f32[24,128]{1,0:T(8,128)S(1)} collective-permute-done((f32[24,128]{1,0:T(8,128)S(1)}, f32[24,128]{1,0:T(8,128)S(1)}, u32[]{:S(2)}, u32[]{:S(2)}) %collective-permute-start.18) | collective-permute-done | bytes 12320 | tf_op jit(solution)/shard_map/ppermute | solution.py:41
  80.1 2.1 %gram.1 = f32[1,64,1024]{2,1,0:T(8,128)} custom-call(s32[1,24]{1,0:T(1,128)} %sizes.3, f32[24,128]{1,0:T(8,128)S(1)} %get-tuple-element.59.alpha, f32[24,2304]{1,0:T(8,128)S(1)} %slice_dynamic-update-slice_fusion.scores.refs_0_, f32[24,2304]{1,0:T(8,128)S(1)} %collective-permute-done.11.scores.refs_1_, ...), custom_call_target="tpu_custom_call" | custom-call | tf_op jit(solution)/shard_map/gram/pallas_call | solution.py:507
  (43 shorter events, 8.3 us)
Async XLA Ops:
  9.0 9.3 %collective-permute-start = (f32[24,2304]{1,0:T(8,128)S(1)}, f32[24,2304]{1,0:T(8,128)S(1)}, u32[]{:S(2)}, u32[]{:S(2)}) collective-permute-start(f32[24,2304]{1,0:T(8,128)S(1)} %get-tuple-element.45), channel_id=1, source_target_pairs={{0,2},{2,0},{4,6},{6,4},{8,10},{10,8},{12,14},{14,12},{16,18},{18,... | collective-permute-start | bytes 663560 | tf_op jit(solution)/shard_map/ppermute | solution.py:41
  12.0 11.6 %collective-permute-start.1 = (f32[24,2304]{1,0:T(8,128)S(1)}, f32[24,2304]{1,0:T(8,128)S(1)}, u32[]{:S(2)}, u32[]{:S(2)}) collective-permute-start(f32[24,2304]{1,0:T(8,128)S(1)} %get-tuple-element.47), channel_id=1, source_target_pairs={{0,4},{2,6},{4,0},{6,2},{8,12},{10,14},{12,8},{14,10},{16,20},{18,... | collective-permute-start | bytes 663560 | tf_op jit(solution)/shard_map/ppermute | solution.py:41
  13.5 10.1 %collective-permute-start.2 = (f32[24,2304]{1,0:T(8,128)S(1)}, f32[24,2304]{1,0:T(8,128)S(1)}, u32[]{:S(2)}, u32[]{:S(2)}) collective-permute-start(f32[24,2304]{1,0:T(8,128)S(1)} %get-tuple-element.41), channel_id=1, source_target_pairs={{0,6},{2,4},{4,2},{6,0},{8,14},{10,12},{12,10},{14,8},{16,22},{18,... | collective-permute-start | bytes 663560 | tf_op jit(solution)/shard_map/ppermute | solution.py:41
  23.7 10.3 %collective-permute-start.3 = (f32[24,768]{1,0:T(8,128)S(1)}, f32[24,768]{1,0:T(8,128)S(1)}, u32[]{:S(2)}, u32[]{:S(2)}) collective-permute-start(f32[24,768]{1,0:T(8,128)S(1)} %get-tuple-element.53), channel_id=1, source_target_pairs={{0,8},{2,10},{4,12},{6,14},{8,0},{10,2},{12,4},{14,6},{16,24},{18,... | collective-permute-start | bytes 221192 | tf_op jit(solution)/shard_map/ppermute | solution.py:41
  25.4 8.6 %collective-permute-start.4 = (f32[24,768]{1,0:T(8,128)S(1)}, f32[24,768]{1,0:T(8,128)S(1)}, u32[]{:S(2)}, u32[]{:S(2)}) collective-permute-start(f32[24,768]{1,0:T(8,128)S(1)} %get-tuple-element.54), channel_id=1, source_target_pairs={{0,16},{2,18},{4,20},{6,22},{8,24},{10,26},{12,28},{14,30},{16,0},... | collective-permute-start | bytes 221192 | tf_op jit(solution)/shard_map/ppermute | solution.py:41
  28.0 6.2 %collective-permute-start.5 = (f32[24,768]{1,0:T(8,128)S(1)}, f32[24,768]{1,0:T(8,128)S(1)}, u32[]{:S(2)}, u32[]{:S(2)}) collective-permute-start(f32[24,768]{1,0:T(8,128)S(1)} %get-tuple-element.55), channel_id=1, source_target_pairs={{0,24},{2,26},{4,28},{6,30},{8,16},{10,18},{12,20},{14,22},{16,8},... | collective-permute-start | bytes 221192 | tf_op jit(solution)/shard_map/ppermute | solution.py:41
  31.9 12.3 %collective-permute-start.19 = (f32[200,512]{1,0:T(8,128)S(1)}, f32[200,512]{1,0:T(8,128)S(1)}, u32[]{:S(2)}, u32[]{:S(2)}) collective-permute-start(f32[200,512]{1,0:T(8,128)S(1)} %get-tuple-element.60), channel_id=1, source_target_pairs={{0,2},{2,0},{4,6},{6,4},{8,10},{10,8},{12,14},{14,12},{16,18},{18,... | collective-permute-start | bytes 1228808 | tf_op jit(solution)/shard_map/ppermute | solution.py:41
  33.2 11.0 %collective-permute-start.20 = (f32[200,512]{1,0:T(8,128)S(1)}, f32[200,512]{1,0:T(8,128)S(1)}, u32[]{:S(2)}, u32[]{:S(2)}) collective-permute-start(f32[200,512]{1,0:T(8,128)S(1)} %get-tuple-element.61), channel_id=1, source_target_pairs={{0,4},{2,6},{4,0},{6,2},{8,12},{10,14},{12,8},{14,10},{16,20},{18,... | collective-permute-start | bytes 1228808 | tf_op jit(solution)/shard_map/ppermute | solution.py:41
  34.1 4.5 %collective-permute-start.6 = (f32[24,512]{1,0:T(8,128)S(1)}, f32[24,512]{1,0:T(8,128)S(1)}, u32[]{:S(2)}, u32[]{:S(2)}) collective-permute-start(f32[24,512]{1,0:T(8,128)S(1)} %get-tuple-element.74), channel_id=1, source_target_pairs={{0,8},{2,10},{4,12},{6,14},{8,0},{10,2},{12,4},{14,6},{16,24},{18,... | collective-permute-start | bytes 147464 | tf_op jit(solution)/shard_map/ppermute | solution.py:41
  34.8 6.4 %collective-permute-start.7 = (f32[24,512]{1,0:T(8,128)S(1)}, f32[24,512]{1,0:T(8,128)S(1)}, u32[]{:S(2)}, u32[]{:S(2)}) collective-permute-start(f32[24,512]{1,0:T(8,128)S(1)} %get-tuple-element.74), channel_id=1, source_target_pairs={{0,16},{2,18},{4,20},{6,22},{8,24},{10,26},{12,28},{14,30},{16,0},... | collective-permute-start | bytes 147464 | tf_op jit(solution)/shard_map/ppermute | solution.py:41
  38.3 5.9 %collective-permute-start.8 = (f32[24,512]{1,0:T(8,128)S(1)}, f32[24,512]{1,0:T(8,128)S(1)}, u32[]{:S(2)}, u32[]{:S(2)}) collective-permute-start(f32[24,512]{1,0:T(8,128)S(1)} %get-tuple-element.74), channel_id=1, source_target_pairs={{0,24},{2,26},{4,28},{6,30},{8,16},{10,18},{12,20},{14,22},{16,8},... | collective-permute-start | bytes 147464 | tf_op jit(solution)/shard_map/ppermute | solution.py:41
  44.4 7.5 %collective-permute-start.21 = (f32[200,256]{1,0:T(8,128)S(1)}, f32[200,256]{1,0:T(8,128)S(1)}, u32[]{:S(2)}, u32[]{:S(2)}) collective-permute-start(f32[200,256]{1,0:T(8,128)S(1)} %get-tuple-element.68), channel_id=1, source_target_pairs={{0,4},{2,6},{4,0},{6,2},{8,12},{10,14},{12,8},{14,10},{16,20},{18,... | collective-permute-start | bytes 614408 | tf_op jit(solution)/shard_map/ppermute | solution.py:41
  45.6 7.5 %collective-permute-start.22 = (f32[200,256]{1,0:T(8,128)S(1)}, f32[200,256]{1,0:T(8,128)S(1)}, u32[]{:S(2)}, u32[]{:S(2)}) collective-permute-start(f32[200,256]{1,0:T(8,128)S(1)} %get-tuple-element.69), channel_id=1, source_target_pairs={{0,2},{2,0},{4,6},{6,4},{8,10},{10,8},{12,14},{14,12},{16,18},{18,... | collective-permute-start | bytes 614408 | tf_op jit(solution)/shard_map/ppermute | solution.py:41
  46.4 9.2 %collective-permute-start.11 = (f32[24,2304]{1,0:T(8,128)S(1)}, f32[24,2304]{1,0:T(8,128)S(1)}, u32[]{:S(2)}, u32[]{:S(2)}) collective-permute-start(f32[24,2304]{1,0:T(8,128)S(1)} %slice_dynamic-update-slice_fusion.scores.refs_0_), channel_id=1, source_target_pairs={{0,2},{2,0},{4,6},{6,4},{8,10},{10,8},{12,14},{14,12},{16,18},{18,... | collective-permute-start | bytes 663560 | tf_op jit(solution)/shard_map/ppermute | solution.py:41
  47.7 10.1 %collective-permute-start.10 = (f32[24,2304]{1,0:T(8,128)S(1)}, f32[24,2304]{1,0:T(8,128)S(1)}, u32[]{:S(2)}, u32[]{:S(2)}) collective-permute-start(f32[24,2304]{1,0:T(8,128)S(1)} %slice_dynamic-update-slice_fusion.scores.refs_0_), channel_id=1, source_target_pairs={{0,4},{2,6},{4,0},{6,2},{8,12},{10,14},{12,8},{14,10},{16,20},{18,... | collective-permute-start | bytes 663560 | tf_op jit(solution)/shard_map/ppermute | solution.py:41
  48.5 11.5 %collective-permute-start.9 = (f32[24,2304]{1,0:T(8,128)S(1)}, f32[24,2304]{1,0:T(8,128)S(1)}, u32[]{:S(2)}, u32[]{:S(2)}) collective-permute-start(f32[24,2304]{1,0:T(8,128)S(1)} %slice_dynamic-update-slice_fusion.scores.refs_0_), channel_id=1, source_target_pairs={{0,6},{2,4},{4,2},{6,0},{8,14},{10,12},{12,10},{14,8},{16,22},{18,... | collective-permute-start | bytes 663560 | tf_op jit(solution)/shard_map/ppermute | solution.py:41
  53.3 14.9 %collective-permute-start.23 = (f32[200,256]{1,0:T(8,128)S(1)}, f32[200,256]{1,0:T(8,128)S(1)}, u32[]{:S(2)}, u32[]{:S(2)}) collective-permute-start(f32[200,256]{1,0:T(8,128)S(1)} %get-tuple-element.71), channel_id=1, source_target_pairs={{0,8},{2,10},{4,12},{6,14},{8,0},{10,2},{12,4},{14,6},{16,24},{18,... | collective-permute-start | bytes 614408 | tf_op jit(solution)/shard_map/ppermute | solution.py:41
  62.2 1.3 %collective-permute-start.12 = (f32[24,896]{1,0:T(8,128)S(1)}, f32[24,896]{1,0:T(8,128)S(1)}, u32[]{:S(2)}, u32[]{:S(2)}) collective-permute-start(f32[24,896]{1,0:T(8,128)S(1)} %terms.7.own), channel_id=1, source_target_pairs={{0,1},{1,0},{2,3},{3,2},{4,5},{5,4},{6,7},{7,6},{8,9},{9,8},{10,11... | collective-permute-start | bytes 258056 | tf_op jit(solution)/shard_map/ppermute | solution.py:41
  64.7 6.1 %collective-permute-start.13 = (f32[24,128]{1,0:T(8,128)S(1)}, f32[24,128]{1,0:T(8,128)S(1)}, u32[]{:S(2)}, u32[]{:S(2)}) collective-permute-start(f32[24,128]{1,0:T(8,128)S(1)} %get-tuple-element.58), channel_id=1, source_target_pairs={{0,2},{2,0},{4,6},{6,4},{8,10},{10,8},{12,14},{14,12},{16,18},{18,... | collective-permute-start | bytes 36872 | tf_op jit(solution)/shard_map/ppermute | solution.py:41
  65.6 5.2 %collective-permute-start.14 = (f32[24,128]{1,0:T(8,128)S(1)}, f32[24,128]{1,0:T(8,128)S(1)}, u32[]{:S(2)}, u32[]{:S(2)}) collective-permute-start(f32[24,128]{1,0:T(8,128)S(1)} %get-tuple-element.58), channel_id=1, source_target_pairs={{0,4},{2,6},{4,0},{6,2},{8,12},{10,14},{12,8},{14,10},{16,20},{18,... | collective-permute-start | bytes 36872 | tf_op jit(solution)/shard_map/ppermute | solution.py:41
  66.0 4.8 %collective-permute-start.15 = (f32[24,128]{1,0:T(8,128)S(1)}, f32[24,128]{1,0:T(8,128)S(1)}, u32[]{:S(2)}, u32[]{:S(2)}) collective-permute-start(f32[24,128]{1,0:T(8,128)S(1)} %get-tuple-element.58), channel_id=1, source_target_pairs={{0,6},{2,4},{4,2},{6,0},{8,14},{10,12},{12,10},{14,8},{16,22},{18,... | collective-permute-start | bytes 36872 | tf_op jit(solution)/shard_map/ppermute | solution.py:41
  68.3 11.9 %collective-permute-start.24 = (f32[200,128]{1,0:T(8,128)S(1)}, f32[200,128]{1,0:T(8,128)S(1)}, u32[]{:S(2)}, u32[]{:S(2)}) collective-permute-start(f32[200,128]{1,0:T(8,128)S(1)} %get-tuple-element.72), channel_id=1, source_target_pairs={{0,16},{2,18},{4,20},{6,22},{8,24},{10,26},{12,28},{14,30},{16,0},... | collective-permute-start | bytes 307208 | tf_op jit(solution)/shard_map/ppermute | solution.py:41
  70.8 5.7 %collective-permute-start.16 = (f32[24,128]{1,0:T(8,128)S(1)}, f32[24,128]{1,0:T(8,128)S(1)}, u32[]{:S(2)}, u32[]{:S(2)}) collective-permute-start(f32[24,128]{1,0:T(8,128)S(1)} %add_add_fusion.1.refs_0_), channel_id=1, source_target_pairs={{0,8},{2,10},{4,12},{6,14},{8,0},{10,2},{12,4},{14,6},{16,24},{18,... | collective-permute-start | bytes 36872 | tf_op jit(solution)/shard_map/ppermute | solution.py:41
  72.6 4.6 %collective-permute-start.17 = (f32[24,128]{1,0:T(8,128)S(1)}, f32[24,128]{1,0:T(8,128)S(1)}, u32[]{:S(2)}, u32[]{:S(2)}) collective-permute-start(f32[24,128]{1,0:T(8,128)S(1)} %add_add_fusion.1.refs_0_), channel_id=1, source_target_pairs={{0,16},{2,18},{4,20},{6,22},{8,24},{10,26},{12,28},{14,30},{16,0},... | collective-permute-start | bytes 36872 | tf_op jit(solution)/shard_map/ppermute | solution.py:41
  73.9 5.5 %collective-permute-start.18 = (f32[24,128]{1,0:T(8,128)S(1)}, f32[24,128]{1,0:T(8,128)S(1)}, u32[]{:S(2)}, u32[]{:S(2)}) collective-permute-start(f32[24,128]{1,0:T(8,128)S(1)} %add_add_fusion.1.refs_0_), channel_id=1, source_target_pairs={{0,24},{2,26},{4,28},{6,30},{8,16},{10,18},{12,20},{14,22},{16,8},... | collective-permute-start | bytes 36872 | tf_op jit(solution)/shard_map/ppermute | solution.py:41

commit v5 on v4

v5 whole, which is shorter than its diff:
```python
import dataclasses
import functools

import jax
import jax.numpy as jnp
from jax import lax
from jax.experimental import pallas as pl
from jax.experimental.pallas import tpu as pltpu
from jax.sharding import PartitionSpec as P


GENE_MAX = 400
LANES = 128
F32 = jnp.float32
BF16 = jnp.bfloat16
VMEM = pltpu.VMEM
NT = (((1,), (1,)), ((), ()))


def up(value, step):
    return -(-value // step) * step


def stages_of(count):
    found, stride = [], 1
    while stride < count:
        radix = 4 if count // stride % 4 == 0 else 2
        found.append((radix, stride))
        stride *= radix
    return found


def offsets_of(stages):
    found = [0]
    for radix, stride in stages:
        found = [base ^ (digit * stride) for base in found for digit in range(radix)]
    return found


def swap(array, count, offset, axis="samp"):
    return lax.ppermute(array, axis, [(i, i ^ offset) for i in range(count)])


def chunk_start(chunk, width, total):
    return pl.multiple_of(jnp.minimum(chunk * width, total - width), 16)


def fresh_lanes(chunk, width, total, rows):
    lane = lax.broadcasted_iota(jnp.int32, (rows, width), 1)
    return lane + jnp.minimum(chunk * width, total - width) >= chunk * width


def in_vmem(array):
    return pltpu.with_memory_space_constraint(array, pltpu.VMEM)


def fetch(copies):
    for copy in copies:
        copy.start()
    return copies


def geno_copies(plan, chunks, geno, held, sems, base=0):
    width, total = plan.width, plan.total
    return [
        pltpu.make_async_copy(
            geno.at[pl.ds(chunk_start(chunk, width, total), width), :],
            held.at[pl.ds(j * width, width), :],
            sems.at[base + j],
        )
        for j, chunk in enumerate(chunks)
    ]


def scores_begin(plan, digits, me, geno, held, sems):
    begun, per = [], len(plan.rest)
    columns = held.shape[0] // len(digits)
    for at, digit in enumerate(digits):
        chunks = [me ^ (digit * plan.stride) ^ r for r in plan.rest]
        window = held.at[pl.ds(at * columns, columns), :]
        begun.append((chunks, fetch(geno_copies(plan, chunks, geno, window, sems, at * per))))
    return begun


def scores_finish(plan, begun, start_bf, stats, held, outs):
    width, total = plan.width, plan.total
    for at, ((chunks, copies), out) in enumerate(zip(begun, outs)):
        for j, copy in enumerate(copies):
            copy.wait()
            low = (at * len(chunks) + j) * width
            part = lax.dot_general(start_bf, held[low : low + width, :], NT, preferred_element_type=F32)
            part = jnp.where(fresh_lanes(chunks[j], width, total, part.shape[0]), part, 0.0)
            out[:, j * width : (j + 1) * width] = part
            lane = lax.broadcasted_iota(jnp.int32, stats.shape, 1)
            head = jnp.where((lane < 2) & (chunks[j] == plan.count - 1), stats, part[:, :LANES])
            out[:, j * width : j * width + LANES] = head


def lead_kernel(plan, digit, ratio, weights, panel, geno, out, diag, right, start, start_bf, weighted, stats, *scratch):
    held, weights_held, ratio_held, sems, small = scratch
    first = fetch(
        [
            pltpu.make_async_copy(panel, right, small.at[0]),
            pltpu.make_async_copy(weights, weights_held, small.at[1]),
            pltpu.make_async_copy(ratio, ratio_held, small.at[2]),
        ]
    )
    begun = scores_begin(plan, (digit,), lax.axis_index("samp"), geno, held, sems)
    for copy in first:
        copy.wait()
    mu = weights_held[...].reshape(1, weights_held.shape[0])
    whole = 1.0 / mu + ratio_held[0]
    way = right[...] / whole
    diag[0:1, :] = whole
    diag[1:2, :] = mu
    diag[2:3, :] = jnp.full(mu.shape, ratio_held[0], F32)
    start[...] = way
    start_bf[...] = way.astype(BF16)
    exact = mu * way
    high = exact.astype(BF16)
    weighted[...] = jnp.concatenate([high, (exact - high.astype(F32)).astype(BF16)], axis=0)
    norm = jnp.sum(right[...] * way, axis=1, keepdims=True)
    own = jnp.sum(way * (way / mu), axis=1, keepdims=True)
    lane = lax.broadcasted_iota(jnp.int32, stats.shape, 1)
    stats[...] = jnp.where(lane == 0, norm, jnp.where(lane == 1, own, 0.0))
    scores_finish(plan, begun, start_bf[...], stats[...], held, (out,))


def scores_kernel(plan, digits, start_bf, stats, geno, *refs):
    *outs, held, sems = refs
    begun = scores_begin(plan, digits, lax.axis_index("samp"), geno, held, sems)
    scores_finish(plan, begun, start_bf[...], stats[...], held, outs)


def terms_kernel(plan, digit, diag, scores, *refs):
    *before, geno, out, held, sems = refs
    width, total = plan.width, plan.total
    me = lax.axis_index("samp")
    samples = geno.shape[1]
    chunks = [me ^ (digit * plan.stride) ^ r for r in plan.rest]
    copies = fetch(geno_copies(plan, chunks, geno, held, sems))
    scale = diag[2:3, 0:1] / plan.markers
    terms = before[0][:, :samples] if before else jnp.zeros((out.shape[0], samples), F32)
    stats = before[0][:, samples:] if before else jnp.zeros((out.shape[0], LANES), F32)
    lane = lax.broadcasted_iota(jnp.int32, stats.shape, 1)
    for j, copy in enumerate(copies):
        raw = scores[:, j * width : (j + 1) * width]
        fresh = fresh_lanes(chunks[j], width, total, raw.shape[0])
        scaled = jnp.where(fresh, scale * raw, 0.0)
        square = jnp.sum(scaled * raw, axis=1, keepdims=True)
        stats = stats + jnp.where(lane == 2, square, jnp.where((lane < 2) & (chunks[j] == plan.count - 1), raw[:, :LANES], 0.0))
        copy.wait()
        terms = terms + jnp.dot(
            scaled.astype(BF16), held[j * width : (j + 1) * width, :], preferred_element_type=F32
        )
    out[:, :samples] = terms
    out[:, samples:] = stats


def update_kernel(diag, start, right, own, other, solution, residual, norm, alpha_out):
    samples = start.shape[1]
    total = own[...] + other[...]
    start_norm = own[:, samples : samples + 1]
    curvature = own[:, samples + 1 : samples + 2] + total[:, samples + 2 : samples + 3]
    alpha = start_norm / curvature
    image = start[...] / diag[1:2, :] + total[:, :samples]
    left = right[...] - alpha * image
    solution[...] = alpha * start[...]
    residual[...] = left
    norm[...] = jnp.broadcast_to(jnp.sum(left * (left / diag[0:1, :]), axis=1, keepdims=True), norm.shape)
    alpha_out[...] = jnp.broadcast_to(alpha, alpha_out.shape)


def direction_kernel(diag, start, own, residual, *refs):
    *norms, out = refs
    samples = start.shape[1]
    total = norms[0][:, :1]
    for ref in norms[1:]:
        total = total + ref[:, :1]
    start_norm = own[:, samples : samples + 1]
    out[...] = residual[...] / diag[0:1, :] + (total / start_norm) * start[...]


def gene_bounds(sizes, index, count):
    low = jnp.zeros(index.shape, jnp.int32)
    high = jnp.full(index.shape, count, jnp.int32)
    end = jnp.int32(0)
    for g in range(sizes.shape[1]):
        end = end + sizes[0, g]
        low = jnp.where(end <= index, end, low)
        high = jnp.where((end > index) & (end < high), end, high)
    return low, high


def cross_kernel(plan, block, sizes, weights, variants, weighted, *refs):
    *outs, scaled = refs
    own_x, own_y, pass_x, pass_y, send_x, send_y = outs
    me = lax.axis_index("samp")
    count = variants.shape[0]
    half = GENE_MAX // 2
    quarter = block * len(plan.rest)
    both = lax.dot_general(weighted[...], variants[...], NT, preferred_element_type=F32)
    rows = both.shape[0] // 2
    beta = both[:rows] + both[rows:]
    for at, (sent, kept) in enumerate(((send_x, pass_x), (send_y, pass_y))):
        sent[half:, :] = beta[:, 2 * at * quarter : 2 * (at + 1) * quarter]
        for j in range(2):
            low = (2 * at + j) * quarter
            kept[half + j * rows : half + (j + 1) * rows, :] = beta[:, low : low + quarter]
    mu = weights[...].reshape(1, weights.shape[0])
    lane = lax.broadcasted_iota(jnp.int32, (1, quarter), 1)
    column = lax.broadcasted_iota(jnp.int32, (count, quarter), 0)
    places = (
        ((own_x, 0), (own_y, 0)),
        ((send_x, 0), (pass_y, 0)),
        ((pass_x, 0), (send_y, 0)),
        ((send_x, 1), (send_y, 1)),
    )
    for digit in range(plan.radix):
        index = lane
        for j, r in enumerate(plan.rest):
            first = pl.multiple_of((me ^ (digit * plan.stride) ^ r) * block, block)
            mine = variants[pl.ds(first, block), :]
            scaled[j * block : (j + 1) * block, :] = (mine.astype(F32) * mu).astype(BF16)
            index = jnp.where(lane // block == j, first + lane - j * block, index)
        cross = lax.dot_general(variants[...], scaled[...], NT, preferred_element_type=F32)
        low, high = gene_bounds(sizes, index, count)
        cross = jnp.where((column >= low) & (column < high), cross, 0.0)
        for part, (out, at) in enumerate(places[digit]):
            folded = None
            for base in range(part * half, count, GENE_MAX):
                piece = cross[base : min(base + half, count)]
                if piece.shape[0] < half:
                    piece = jnp.concatenate([piece, jnp.zeros((half - piece.shape[0], quarter), F32)], axis=0)
                folded = piece if folded is None else folded + piece
            out[:half, at * quarter : (at + 1) * quarter] = folded


def halves_kernel(got_x, got_y, *refs):
    before, after = refs[:4], refs[4:]
    half, quarter = before[0].shape
    rows = got_x.shape[0] - half
    for at, (old, new) in enumerate(zip(before, after)):
        got = (got_x, got_y)[at % 2]
        low = at // 2 * quarter
        new[:half, :] = old[:half, :] + got[:half, low : low + quarter]
        if at >= 2:
            for j in range(2):
                to = slice(half + j * rows, half + (j + 1) * rows)
                new[to, :] = old[to, :] + got[half:, j * quarter : (j + 1) * quarter]


def split_kernel(own_x, own_y, pass_x, pass_y, got_x, got_y, kept, sent):
    half, quarter = own_x.shape
    low, high = own_x[...] + got_x[:half, :], own_y[...] + got_y[:half, :]
    wide = quarter // 4
    cut = [part[:, j * wide : (j + 1) * wide] for j in range(4) for part in (low, high)]
    kept[:half, :] = jnp.concatenate(cut[0:2] + cut[4:6], axis=1)
    sent[:half, :] = jnp.concatenate(cut[2:4] + cut[6:8], axis=1)
    tall = pass_x.shape[0] - half
    for at, (mine, got) in enumerate(((pass_x, got_x), (pass_y, got_y))):
        beta = mine[half:, :] + got[half:, :]
        for out in (kept, sent):
            out[half + at * tall : half + (at + 1) * tall, :] = beta


def pair_kernel(half, kept, got, stay, sent):
    wide = kept.shape[1] // 2
    tall = kept.shape[0] - half
    total = kept[...] + got[...]
    stay[:half, :] = total[:half, :wide]
    sent[:half, :] = total[:half, wide:]
    for out in (stay, sent):
        for j in range(2):
            out[half + j * tall : half + (j + 1) * tall, :] = total[half:, j * wide : (j + 1) * wide]


def gram_kernel(samples, sizes, alpha, *refs):
    *sums, solved, left, out, solved_out, left_out, full, sems = refs
    copies = fetch(
        [
            pltpu.make_async_copy(solved, solved_out, sems.at[0]),
            pltpu.make_async_copy(left, left_out, sems.at[1]),
        ]
    )
    me = lax.axis_index("samp")
    count = out.shape[2]
    block = out.shape[1]
    half = GENE_MAX // 2
    rows = full.shape[0]
    total = sums[0][...]
    for ref in sums[1:]:
        total = total + ref[...]
    parts = count // LANES
    for j in range(parts):
        low = half + (j % 2 * (parts // 2) + j // 2) * rows
        full[:, j * LANES : (j + 1) * LANES] = total[low : low + rows, :] * alpha[:, :1]
    cross = jnp.concatenate([total[:half, :block], total[:half, block : 2 * block]], axis=0).T
    cross = jnp.concatenate([cross] * (-(-count // GENE_MAX)), axis=1)[:, :count]
    first = me * block
    window = max(block, LANES)
    base = pl.multiple_of(first // window * window, window)
    wide = lax.dot_general(
        full[:, pl.ds(base, window)],
        full[...],
        (((0,), (0,)), ((), ())),
        precision=lax.Precision.HIGHEST,
        preferred_element_type=F32,
    )
    correction = wide[:block]
    for step in range(1, window // block):
        correction = jnp.where(first - base == step * block, wide[step * block : (step + 1) * block], correction)
    low, high = gene_bounds(sizes, first + lax.broadcasted_iota(jnp.int32, (block, LANES), 0), count)
    column = lax.broadcasted_iota(jnp.int32, (block, count), 1)
    same = (column >= low[:, :1]) & (column < high[:, :1])
    out[0] = jnp.where(same, (cross - correction) / samples, 0.0)
    for copy in copies:
        copy.wait()


def cut_by(products, scores, count, stride):
    wide = products.shape[1] // 8
    low, high = products[:, : 4 * wide], products[:, 4 * wide :]
    cut = [jnp.concatenate([p[:, j * wide : (j + 1) * wide] for p in (low, high)], axis=1) for j in range(4)]
    kept = jnp.concatenate([cut[0], cut[2]], axis=1)
    kept = kept + swap(jnp.concatenate([cut[1], cut[3]], axis=1), count, stride)
    scores = scores + swap(scores, count, stride)
    products = kept[:, : 2 * wide] + swap(kept[:, 2 * wide :], count, 2 * stride)
    return products, scores + swap(scores, count, 2 * stride)


def merge_kernel(*refs):
    terms, outs = refs[:-4], refs[-4:]
    wide = outs[0].shape[1]
    for j, out in enumerate(outs):
        total = terms[0][:, j * wide : (j + 1) * wide]
        for ref in terms[1:]:
            total = total + ref[:, j * wide : (j + 1) * wide]
        out[...] = total


@dataclasses.dataclass(frozen=True)
class Plan:
    count: int
    radix: int
    stride: int
    rest: tuple
    width: int
    total: int
    markers: int


def tied(array, *others):
    return lax.optimization_barrier((array, *others))[0]


def body(genotypes, variants, weights, variance_ratio, panel, gene_sizes):
    count = lax.axis_size("samp")
    marks = lax.axis_size("mark")
    stages = stages_of(count)
    (radix, stride), later = stages[0], stages[1:]
    firsts = [digit * stride for digit in range(radix)]
    rest = offsets_of(later)
    local, samples = genotypes.shape
    width = up(-(-local // count), LANES)
    if count * width - local < 2:
        width += LANES
    plan = Plan(count, radix, stride, tuple(rest), width, local, local * marks)
    num_variants = variants.shape[0]
    rows = panel.shape[0]
    vmem = pl.BlockSpec(memory_space=VMEM)
    smem = pl.BlockSpec(memory_space=pltpu.SMEM)
    hbm = pl.BlockSpec(memory_space=pl.ANY)
    columns = len(rest) * width
    payload = VMEM((rows, columns), F32)

    lead = radix - 1
    sent = {}
    sent[lead], diag, right, start, start_bf, weighted, stats = pl.pallas_call(
        functools.partial(lead_kernel, plan, lead),
        out_shape=[
            payload,
            VMEM((8, samples), F32),
            VMEM((rows, samples), F32),
            VMEM((rows, samples), F32),
            VMEM((rows, samples), BF16),
            VMEM((2 * rows, samples), BF16),
            VMEM((rows, LANES), F32),
        ],
        in_specs=[hbm] * 4,
        out_specs=[vmem] * 7,
        scratch_shapes=[
            VMEM((columns, samples), BF16),
            VMEM((samples,), F32),
            pltpu.SMEM((1,), F32),
            pltpu.SemaphoreType.DMA((len(rest),)),
            pltpu.SemaphoreType.DMA((3,)),
        ],
        name="scores_lead",
    )(variance_ratio, weights, panel, genotypes)
    diag, right, start = in_vmem(diag), in_vmem(right), in_vmem(start)
    after = sent[lead]
    for digits in (tuple(range(1, lead)), (0,)):
        start_bf, after = lax.optimization_barrier((start_bf, after))
        found = pl.pallas_call(
            functools.partial(scores_kernel, plan, digits),
            out_shape=[payload] * len(digits),
            in_specs=[vmem] * 2 + [hbm],
            out_specs=[vmem] * len(digits),
            scratch_shapes=[
                VMEM((len(digits) * columns, samples), BF16),
                pltpu.SemaphoreType.DMA((len(digits) * len(rest),)),
            ],
            name="scores",
        )(in_vmem(start_bf), in_vmem(stats), genotypes)
        sent.update(zip(digits, found))
        after = found[0]

    assert radix == 4 and all(r == 4 for r, _ in later)
    block = num_variants // count
    quarter = block * len(rest)
    assert 4 * quarter == num_variants
    half = GENE_MAX // 2
    own_shape = VMEM((half, quarter), F32)
    pass_shape = VMEM((half + 2 * rows, quarter), F32)
    send_shape = VMEM((half + rows, 2 * quarter), F32)
    *parts, send_x, send_y = pl.pallas_call(
        functools.partial(cross_kernel, plan, block),
        out_shape=[own_shape] * 2 + [pass_shape] * 2 + [send_shape] * 2,
        in_specs=[smem] + [vmem] * 3,
        out_specs=[vmem] * 6,
        scratch_shapes=[VMEM((quarter, samples), BF16)],
        name="cross",
    )(gene_sizes, weights, tied(variants, sent[0]), in_vmem(weighted))

    terms = [sent[0]] + [swap(sent[d], count, firsts[d]) for d in range(1, radix)]
    wide = columns
    for level, (r, s) in enumerate(later):
        wide //= r
        pieces = pl.pallas_call(
            merge_kernel,
            out_shape=[VMEM((rows, wide), F32)] * r,
            in_specs=[vmem] * len(terms),
            out_specs=[vmem] * r,
            name="merge",
        )(*map(in_vmem, terms))
        piece = pieces[0]
        if level == 0:
            piece, send_x, send_y = lax.optimization_barrier((piece, send_x, send_y))
        terms = [piece] + [swap(pieces[d], count, d * s) for d in range(1, r)]
    got = terms[0]
    for one in terms[1:]:
        got = got + one
    for r, s in reversed(later):
        got = jnp.concatenate([got] + [swap(got, count, d * s) for d in range(1, r)], axis=1)
    arrays = [in_vmem(got)] + [in_vmem(swap(got, count, firsts[d])) for d in range(1, radix)]

    got_x = swap(send_x, count, firsts[1])
    got_y = swap(send_y, count, firsts[2])
    own_x, own_y, pass_x, pass_y = pl.pallas_call(
        halves_kernel,
        out_shape=[own_shape] * 2 + [pass_shape] * 2,
        in_specs=[vmem] * 6,
        out_specs=[vmem] * 4,
        input_output_aliases={2 + i: i for i in range(4)},
        name="halves",
    )(*map(in_vmem, (got_x, got_y, *parts)))
    got_x, got_y = swap(pass_x, count, firsts[2]), swap(pass_y, count, firsts[1])
    (r, s), deeper = later[0], later[1:]
    wide = quarter // 2
    tall = half + 4 * rows
    kept, moved = pl.pallas_call(
        split_kernel,
        out_shape=[VMEM((tall, quarter), F32)] * 2,
        in_specs=[vmem] * 6,
        out_specs=[vmem] * 2,
        name="split",
    )(*map(in_vmem, (own_x, own_y, pass_x, pass_y, got_x, got_y)))
    got_x = swap(moved, count, s)
    kept, moved = pl.pallas_call(
        functools.partial(pair_kernel, half),
        out_shape=[VMEM((tall + 4 * rows, wide), F32)] * 2,
        in_specs=[vmem] * 2,
        out_specs=[vmem] * 2,
        name="pair",
    )(in_vmem(kept), in_vmem(got_x))
    sums = [kept, swap(moved, count, 2 * s)]
    if deeper:
        products, scores = sums[0] + sums[1], None
        products, scores = products[:half], products[half:]
        for r, s in deeper:
            products, scores = cut_by(products, scores, count, s)
        products = jnp.pad(products, ((0, 0), (0, wide - products.shape[1])))
        sums = [jnp.concatenate([products, scores], axis=0)]

    own = ()
    for d in range(radix):
        whole = pl.pallas_call(
            functools.partial(terms_kernel, plan, d),
            out_shape=VMEM((rows, samples + LANES), F32),
            in_specs=[vmem] * (2 + len(own)) + [hbm],
            out_specs=vmem,
            scratch_shapes=[VMEM((columns, samples), BF16), pltpu.SemaphoreType.DMA((len(rest),))],
            name="terms",
        )(diag, arrays[d], *map(in_vmem, own), genotypes)
        own = (whole,)
    (held,) = own
    assert marks & (marks - 1) == 0
    other = None
    offset = 1
    while offset < marks:
        other = swap(held, marks, offset, "mark")
        offset *= 2
        if offset < marks:
            kept = held[:, samples : samples + 2]
            held = held + other
            held = jnp.concatenate([held[:, :samples], kept, held[:, samples + 2 :]], axis=1)
    held = in_vmem(held)
    flat = VMEM((rows, LANES), F32)
    full = jax.ShapeDtypeStruct((rows, samples), F32)
    solution, residual, norm, alpha = pl.pallas_call(
        update_kernel,
        out_shape=[VMEM((rows, samples), F32)] * 2 + [flat] * 2,
        in_specs=[vmem] * 5,
        out_specs=[vmem] * 4,
        name="update",
    )(diag, start, right, held, in_vmem(other))
    norms = [norm]
    for r, s in stages:
        total = norms[0]
        for one in norms[1:]:
            total = total + one
        norms = [total] + [swap(total, count, d * s) for d in range(1, r)]
    direction = pl.pallas_call(
        direction_kernel,
        out_shape=full,
        in_specs=[vmem] * (4 + len(norms)),
        out_specs=vmem,
        name="direction",
    )(diag, start, held, in_vmem(residual), *map(in_vmem, norms))

    gram, solution, residual = pl.pallas_call(
        functools.partial(gram_kernel, samples * count),
        out_shape=[jax.ShapeDtypeStruct((1, block, num_variants), F32), full, full],
        in_specs=[smem] + [vmem] * (3 + len(sums)),
        out_specs=[vmem, hbm, hbm],
        scratch_shapes=[VMEM((rows, num_variants), F32), pltpu.SemaphoreType.DMA((2,))],
        name="gram",
    )(gene_sizes, *map(in_vmem, (alpha, *sums, solution, residual)))
    return solution, residual, direction, gram


def solution(mesh):
    return jax.shard_map(
        body,
        mesh=mesh,
        in_specs=(
            P("mark", "samp"),
            P("mark", "samp"),
            P("samp"),
            P(),
            P(None, "samp"),
            P("mark", None),
        ),
        out_specs=(P(None, "samp"), P(None, "samp"), P(None, "samp"), P("mark", "samp", None)),
        check_vma=False,
    )
```

time: 82.5 us -> 79.1 us (0.959)
  waiting for transfers between devices: 20.2 us -> 16.1 us
  starting transfers between devices: 31.7 us -> 34.8 us
  local copies, waits for them, and re-layouts: 1.3 us -> 0 us
  Pallas kernels: 27.5 us -> 26.5 us
    ppermute x25, waiting for transfers between devices: 20.2 us -> 16.1 us  [swap(): return lax.ppermute(array, axis, [(i, i ^ offset) for i in range(count)])]
    ppermute x25, starting transfers between devices: 31.7 us -> 34.8 us  [swap(): return lax.ppermute(array, axis, [(i, i ^ offset) for i in range(count)])]
    unnamed x5 -> x0, local copies, waits for them, and re-layouts: 1.28 us -> none
    pallas_call x5 -> x6, Pallas kernels: 6.21 us -> 7.12 us  [the longest x1 4.21 us: body(): pl.pallas_call(functools.partial(cross_kernel, plan, block), out_shape=[o...]
    pallas_call x1, Pallas kernels: 1.19 us -> 0.31 us  [body(): pl.pallas_call(update_kernel, out_shape=[VMEM((rows, samples), F32)] * 2...]
  transfers between devices with their start and end apart: 25 -> 25, of which waited for: 10 -> 9; matrix products, arithmetic and copies ran while one was open for 2% -> 0% of each run, Pallas kernels for 21% -> 27%
where the time goes in v5:
time: 79.1 us; the launch traced here: 78.9 us
  starting transfers between devices  34.8 us (44%)
  Pallas kernels  26.5 us (34%)
  waiting for transfers between devices  16.1 us (20%)
  between operations  1.44 us (2%)
    ppermute x25, starting transfers between devices, swap(): return lax.ppermute(array, axis, [(i, i ^ offset) for i in range(count)])  34.8 us
    ppermute x25, waiting for transfers between devices, swap(): return lax.ppermute(array, axis, [(i, i ^ offset) for i in range(count)])  16.1 us
    pallas_call x4, Pallas kernels, body(): pl.pallas_call(functools.partial(terms_kernel, plan, d), out_shape=VMEM((...  8.64 us
    pallas_call x2, Pallas kernels, body(): pl.pallas_call(functools.partial(scores_kernel, plan, digits), out_shape=...  7.14 us
    pallas_call x1, Pallas kernels, body(): pl.pallas_call(functools.partial(cross_kernel, plan, block), out_shape=[o...  4.21 us
    pallas_call x1, Pallas kernels, body(): pl.pallas_call(functools.partial(lead_kernel, plan, lead), out_shape=[pay...  2.62 us
    pallas_call x1, Pallas kernels, body(): pl.pallas_call(functools.partial(gram_kernel, samples * count), out_shape...  2.46 us
  transfers between devices with their start and end apart: 25, of which 9 were waited for; matrix products, arithmetic and copies ran while one was open for 0% of the time, Pallas kernels for 27%

profile of v5, /device:TPU:0, one launch (start us, length us, event | category | flops | bytes accessed | tf_op | source)
XLA Modules:
  0.0 78.9 jit_solution(9747994802518909714)
XLA Ops:
  1.3 2.6 %scores_lead.1 = (f32[24,2048]{1,0:T(8,128)S(1)}, f32[8,768]{1,0:T(8,128)S(1)}, f32[24,768]{1,0:T(8,128)S(1)}, f32[24,768]{1,0:T(8,128)S(1)}, bf16[24,768]{1,0:T...) custom-call(f32[1]{0:T(128)S(6)} %copy.18.ratio, f32[768]{0:T(1024)} %weights.3, f32[24,768]{1,0:T(8,128)} %panel.1, ...), custom_call_target="tpu_custom_call" | custom-call | tf_op jit(solution)/shard_map/scores_lead/pallas_call | solution.py:379
  3.9 4.0 %collective-permute-start.2 = (f32[24,2048]{1,0:T(8,128)S(1)}, f32[24,2048]{1,0:T(8,128)S(1)}, u32[]{:S(2)}, u32[]{:S(2)}) collective-permute-start(f32[24,2048]{1,0:T(8,128)S(1)} %get-tuple-element.48), channel_id=1, source_target_pairs={{0,6},{2,4},{4,2},{6,0},{8,14},{10,12},{12,10},{14,8},{16,22},{18,... | collective-permute-start | bytes 589832 | tf_op jit(solution)/shard_map/ppermute | solution.py:41
  7.9 4.6 %scores.2 = (f32[24,2048]{1,0:T(8,128)S(1)}, f32[24,2048]{1,0:T(8,128)}) custom-call(bf16[24,768]{1,0:T(8,128)(2,1)S(1)} %get-tuple-element.52.start_bf, f32[24,128]{1,0:T(8,128)S(1)} %get-tuple-element.50.stats, bf16[8000,768]{1,0:T(8,128)(2,1)} %refs_1_.5), custom_call_target="tpu_custom_call" | custom-call | tf_op jit(solution)/shard_map/scores/pallas_call | solution.py:405
  13.2 2.5 %scores.3.refs_0_ = f32[24,2048]{1,0:T(8,128)S(1)} custom-call(bf16[24,768]{1,0:T(8,128)(2,1)S(1)} %get-tuple-element.52.start_bf, f32[24,128]{1,0:T(8,128)S(1)} %get-tuple-element.50.stats, bf16[8000,768]{1,0:T(8,128)(2,1)} %refs_1_.5), custom_call_target="tpu_custom_call" | custom-call | tf_op jit(solution)/shard_map/scores/pallas_call | solution.py:405
  15.7 4.2 %cross.1 = (f32[200,256]{1,0:T(8,128)S(1)}, f32[200,256]{1,0:T(8,128)S(1)}, f32[248,256]{1,0:T(8,128)S(1)}, f32[248,256]{1,0:T(8,128)S(1)}, f32[224,512]{1,0:T(8,128)S(1)}, /*index=5*/f32[224,512]{1,0:T(8,128)S(1)}) custom-call(s32[1,24]{1,0:T(1,128)} %sizes.3, f32[768]{0:T(1024)} %weights.3, bf16[1024,768]{1,0:T(8,128)(2,1)} %variants, ...), custom_call_target="tpu_custom_call" | custom-call | tf_op jit(solution)/shard_map/cross/pallas_call | solution.py:427
  20.0 2.0 %collective-permute-start.13 = (f32[224,512]{1,0:T(8,128)S(1)}, f32[224,512]{1,0:T(8,128)S(1)}, u32[]{:S(2)}, u32[]{:S(2)}) collective-permute-start(f32[224,512]{1,0:T(8,128)S(1)} %get-tuple-element.64), channel_id=1, source_target_pairs={{0,2},{2,0},{4,6},{6,4},{8,10},{10,8},{12,14},{14,12},{16,18},{18,... | collective-permute-start | bytes 1376264 | tf_op jit(solution)/shard_map/ppermute | solution.py:41
  22.0 1.5 %collective-permute-start.14 = (f32[224,512]{1,0:T(8,128)S(1)}, f32[224,512]{1,0:T(8,128)S(1)}, u32[]{:S(2)}, u32[]{:S(2)}) collective-permute-start(f32[224,512]{1,0:T(8,128)S(1)} %get-tuple-element.65), channel_id=1, source_target_pairs={{0,4},{2,6},{4,0},{6,2},{8,12},{10,14},{12,8},{14,10},{16,20},{18,... | collective-permute-start | bytes 1376264 | tf_op jit(solution)/shard_map/ppermute | solution.py:41
  23.5 1.6 %collective-permute-start.3 = (f32[24,512]{1,0:T(8,128)S(1)}, f32[24,512]{1,0:T(8,128)S(1)}, u32[]{:S(2)}, u32[]{:S(2)}) collective-permute-start(f32[24,512]{1,0:T(8,128)S(1)} %get-tuple-element.60), channel_id=1, source_target_pairs={{0,8},{2,10},{4,12},{6,14},{8,0},{10,2},{12,4},{14,6},{16,24},{18,... | collective-permute-start | bytes 147464 | tf_op jit(solution)/shard_map/ppermute | solution.py:41
  25.1 2.6 %collective-permute-start.4 = (f32[24,512]{1,0:T(8,128)S(1)}, f32[24,512]{1,0:T(8,128)S(1)}, u32[]{:S(2)}, u32[]{:S(2)}) collective-permute-start(f32[24,512]{1,0:T(8,128)S(1)} %get-tuple-element.61), channel_id=1, source_target_pairs={{0,16},{2,18},{4,20},{6,22},{8,24},{10,26},{12,28},{14,30},{16,0},... | collective-permute-start | bytes 147464 | tf_op jit(solution)/shard_map/ppermute | solution.py:41
  27.9 3.9 %collective-permute-done.13.got_x = f32[224,512]{1,0:T(8,128)S(1)} collective-permute-done((f32[224,512]{1,0:T(8,128)S(1)}, f32[224,512]{1,0:T(8,128)S(1)}, u32[]{:S(2)}, u32[]{:S(2)}) %collective-permute-start.13) | collective-permute-done | bytes 458784 | tf_op jit(solution)/shard_map/ppermute | solution.py:41
  31.8 1.4 %collective-permute-done.14.got_y = f32[224,512]{1,0:T(8,128)S(1)} collective-permute-done((f32[224,512]{1,0:T(8,128)S(1)}, f32[224,512]{1,0:T(8,128)S(1)}, u32[]{:S(2)}, u32[]{:S(2)}) %collective-permute-start.14) | collective-permute-done | bytes 458784 | tf_op jit(solution)/shard_map/ppermute | solution.py:41
  33.3 1.6 %collective-permute-start.15 = (f32[248,256]{1,0:T(8,128)S(1)}, f32[248,256]{1,0:T(8,128)S(1)}, u32[]{:S(2)}, u32[]{:S(2)}) collective-permute-start(f32[248,256]{1,0:T(8,128)S(1)} %get-tuple-element.72.pass_x), channel_id=1, source_target_pairs={{0,4},{2,6},{4,0},{6,2},{8,12},{10,14},{12,8},{14,10},{16,20},{18,... | collective-permute-start | bytes 761864 | tf_op jit(solution)/shard_map/ppermute | solution.py:41
  35.5 3.7 %collective-permute-start.8 = (f32[24,512]{1,0:T(8,128)S(1)}, f32[24,512]{1,0:T(8,128)S(1)}, u32[]{:S(2)}, u32[]{:S(2)}) collective-permute-start(f32[24,512]{1,0:T(8,128)S(1)} %add_add_fusion), channel_id=1, source_target_pairs={{0,24},{2,26},{4,28},{6,30},{8,16},{10,18},{12,20},{14,22},{16,8},... | collective-permute-start | bytes 147464 | tf_op jit(solution)/shard_map/ppermute | solution.py:41
  40.0 1.3 %collective-permute-done.16.got_y = f32[248,256]{1,0:T(8,128)S(1)} collective-permute-done((f32[248,256]{1,0:T(8,128)S(1)}, f32[248,256]{1,0:T(8,128)S(1)}, u32[]{:S(2)}, u32[]{:S(2)}) %collective-permute-start.16) | collective-permute-done | bytes 253984 | tf_op jit(solution)/shard_map/ppermute | solution.py:41
  41.4 1.6 %collective-permute-start.17 = (f32[296,256]{1,0:T(8,128)S(1)}, f32[296,256]{1,0:T(8,128)S(1)}, u32[]{:S(2)}, u32[]{:S(2)}) collective-permute-start(f32[296,256]{1,0:T(8,128)S(1)} %get-tuple-element.75), channel_id=1, source_target_pairs={{0,8},{2,10},{4,12},{6,14},{8,0},{10,2},{12,4},{14,6},{16,24},{18,... | collective-permute-start | bytes 909320 | tf_op jit(solution)/shard_map/ppermute | solution.py:41
  43.0 1.2 %collective-permute-done.7 = f32[24,512]{1,0:T(8,128)S(1)} collective-permute-done((f32[24,512]{1,0:T(8,128)S(1)}, f32[24,512]{1,0:T(8,128)S(1)}, u32[]{:S(2)}, u32[]{:S(2)}) %collective-permute-start.7) | collective-permute-done | bytes 49184 | tf_op jit(solution)/shard_map/ppermute | solution.py:41
  44.3 1.6 %collective-permute-start.11 = (f32[24,2048]{1,0:T(8,128)S(1)}, f32[24,2048]{1,0:T(8,128)S(1)}, u32[]{:S(2)}, u32[]{:S(2)}) collective-permute-start(f32[24,2048]{1,0:T(8,128)S(1)} %pad_maximum_fusion.scores), channel_id=1, source_target_pairs={{0,2},{2,0},{4,6},{6,4},{8,10},{10,8},{12,14},{14,12},{16,18},{18,... | collective-permute-start | bytes 589832 | tf_op jit(solution)/shard_map/ppermute | solution.py:41
  46.4 1.5 %collective-permute-start.9 = (f32[24,2048]{1,0:T(8,128)S(1)}, f32[24,2048]{1,0:T(8,128)S(1)}, u32[]{:S(2)}, u32[]{:S(2)}) collective-permute-start(f32[24,2048]{1,0:T(8,128)S(1)} %pad_maximum_fusion.scores), channel_id=1, source_target_pairs={{0,6},{2,4},{4,2},{6,0},{8,14},{10,12},{12,10},{14,8},{16,22},{18,... | collective-permute-start | bytes 589832 | tf_op jit(solution)/shard_map/ppermute | solution.py:41
  47.9 2.2 %terms.4.refs_0_ = f32[24,896]{1,0:T(8,128)S(1)} custom-call(f32[8,768]{1,0:T(8,128)S(1)} %get-tuple-element.44.diag, f32[24,2048]{1,0:T(8,128)S(1)} %pad_maximum_fusion.scores, bf16[8000,768]{1,0:T(8,128)(2,1)} %refs_1_.5), custom_call_target="tpu_custom_call" | custom-call | tf_op jit(solution)/shard_map/terms/pallas_call | solution.py:498
  50.1 2.2 %terms.5.refs_0_ = f32[24,896]{1,0:T(8,128)S(1)} custom-call(f32[8,768]{1,0:T(8,128)S(1)} %get-tuple-element.44.diag, f32[24,2048]{1,0:T(8,128)S(1)} %collective-permute-done.11.scores, f32[24,896]{1,0:T(8,128)S(1)} %terms.4.refs_0_, bf16[8000,768]{1,0:T(8,128)(2,1)} %refs_1_.5), custom_call_target="tpu_custom_call" | custom-call | tf_op jit(solution)/shard_map/terms/pallas_call | solution.py:498
  52.2 1.4 %collective-permute-done.10.scores = f32[24,2048]{1,0:T(8,128)S(1)} collective-permute-done((f32[24,2048]{1,0:T(8,128)S(1)}, f32[24,2048]{1,0:T(8,128)S(1)}, u32[]{:S(2)}, u32[]{:S(2)}) %collective-permute-start.10) | collective-permute-done | bytes 196640 | tf_op jit(solution)/shard_map/ppermute | solution.py:41
  53.7 2.2 %terms.6.refs_0_ = f32[24,896]{1,0:T(8,128)S(1)} custom-call(f32[8,768]{1,0:T(8,128)S(1)} %get-tuple-element.44.diag, f32[24,2048]{1,0:T(8,128)S(1)} %collective-permute-done.10.scores, f32[24,896]{1,0:T(8,128)S(1)} %terms.5.refs_0_, bf16[8000,768]{1,0:T(8,128)(2,1)} %refs_1_.5), custom_call_target="tpu_custom_call" | custom-call | tf_op jit(solution)/shard_map/terms/pallas_call | solution.py:498
  55.8 2.2 %terms.7.own = f32[24,896]{1,0:T(8,128)S(1)} custom-call(f32[8,768]{1,0:T(8,128)S(1)} %get-tuple-element.44.diag, f32[24,2048]{1,0:T(8,128)S(1)} %collective-permute-done.9.scores, f32[24,896]{1,0:T(8,128)S(1)} %terms.6.refs_0_, bf16[8000,768]{1,0:T(8,128)(2,1)} %refs_1_.5), custom_call_target="tpu_custom_call" | custom-call | tf_op jit(solution)/shard_map/terms/pallas_call | solution.py:498
  58.1 1.3 %collective-permute-done.12.other = f32[24,896]{1,0:T(8,128)S(1)} collective-permute-done((f32[24,896]{1,0:T(8,128)S(1)}, f32[24,896]{1,0:T(8,128)S(1)}, u32[]{:S(2)}, u32[]{:S(2)}) %collective-permute-start.12) | collective-permute-done | bytes 86048 | tf_op jit(solution)/shard_map/ppermute | solution.py:41
  59.7 2.0 %collective-permute-start.20 = (f32[24,128]{1,0:T(8,128)S(1)}, f32[24,128]{1,0:T(8,128)S(1)}, u32[]{:S(2)}, u32[]{:S(2)}) collective-permute-start(f32[24,128]{1,0:T(8,128)S(1)} %get-tuple-element.82), channel_id=1, source_target_pairs={{0,4},{2,6},{4,0},{6,2},{8,12},{10,14},{12,8},{14,10},{16,20},{18,... | collective-permute-start | bytes 36872 | tf_op jit(solution)/shard_map/ppermute | solution.py:41
  61.7 1.5 %collective-permute-start.19 = (f32[24,128]{1,0:T(8,128)S(1)}, f32[24,128]{1,0:T(8,128)S(1)}, u32[]{:S(2)}, u32[]{:S(2)}) collective-permute-start(f32[24,128]{1,0:T(8,128)S(1)} %get-tuple-element.82), channel_id=1, source_target_pairs={{0,2},{2,0},{4,6},{6,4},{8,10},{10,8},{12,14},{14,12},{16,18},{18,... | collective-permute-start | bytes 36872 | tf_op jit(solution)/shard_map/ppermute | solution.py:41
  63.2 2.5 %collective-permute-start.18 = (f32[392,128]{1,0:T(8,128)S(1)}, f32[392,128]{1,0:T(8,128)S(1)}, u32[]{:S(2)}, u32[]{:S(2)}) collective-permute-start(f32[392,128]{1,0:T(8,128)S(1)} %get-tuple-element.77), channel_id=1, source_target_pairs={{0,16},{2,18},{4,20},{6,22},{8,24},{10,26},{12,28},{14,30},{16,0},... | collective-permute-start | bytes 602120 | tf_op jit(solution)/shard_map/ppermute | solution.py:41
  65.7 1.8 %collective-permute-start.24 = (f32[24,128]{1,0:T(8,128)S(1)}, f32[24,128]{1,0:T(8,128)S(1)}, u32[]{:S(2)}, u32[]{:S(2)}) collective-permute-start(f32[24,128]{1,0:T(8,128)S(1)} %add_add_fusion.1.refs_0_), channel_id=1, source_target_pairs={{0,24},{2,26},{4,28},{6,30},{8,16},{10,18},{12,20},{14,22},{16,8},... | collective-permute-start | bytes 36872 | tf_op jit(solution)/shard_map/ppermute | solution.py:41
  68.4 1.7 %collective-permute-start.22 = (f32[24,128]{1,0:T(8,128)S(1)}, f32[24,128]{1,0:T(8,128)S(1)}, u32[]{:S(2)}, u32[]{:S(2)}) collective-permute-start(f32[24,128]{1,0:T(8,128)S(1)} %add_add_fusion.1.refs_0_), channel_id=1, source_target_pairs={{0,8},{2,10},{4,12},{6,14},{8,0},{10,2},{12,4},{14,6},{16,24},{18,... | collective-permute-start | bytes 36872 | tf_op jit(solution)/shard_map/ppermute | solution.py:41
  70.1 1.8 %collective-permute-done.24.refs_3_ = f32[24,128]{1,0:T(8,128)S(1)} collective-permute-done((f32[24,128]{1,0:T(8,128)S(1)}, f32[24,128]{1,0:T(8,128)S(1)}, u32[]{:S(2)}, u32[]{:S(2)}) %collective-permute-start.24) | collective-permute-done | bytes 12320 | tf_op jit(solution)/shard_map/ppermute | solution.py:41
  72.0 3.8 %collective-permute-done.23.refs_2_ = f32[24,128]{1,0:T(8,128)S(1)} collective-permute-done((f32[24,128]{1,0:T(8,128)S(1)}, f32[24,128]{1,0:T(8,128)S(1)}, u32[]{:S(2)}, u32[]{:S(2)}) %collective-permute-start.23) | collective-permute-done | bytes 12320 | tf_op jit(solution)/shard_map/ppermute | solution.py:41
  76.5 2.5 %gram.1 = (f32[1,64,1024]{2,1,0:T(8,128)}, f32[24,768]{1,0:T(8,128)}, f32[24,768]{1,0:T(8,128)}) custom-call(s32[1,24]{1,0:T(1,128)} %sizes.3, f32[24,128]{1,0:T(8,128)S(1)} %get-tuple-element.63.alpha, f32[392,128]{1,0:T(8,128)S(1)} %get-tuple-element.76.refs_0_, f32[392,128]{1,0:T(8,128)S(1)} %collective-permute-done.18.refs_1_, ...), custom_call_target="tpu_custom_call" | custom-call | tf_op jit(solution)/shard_map/gram/pallas_call | solution.py:542
  (36 shorter events, 5.4 us)
Async XLA Ops:
  3.9 16.0 %collective-permute-start.2 = (f32[24,2048]{1,0:T(8,128)S(1)}, f32[24,2048]{1,0:T(8,128)S(1)}, u32[]{:S(2)}, u32[]{:S(2)}) collective-permute-start(f32[24,2048]{1,0:T(8,128)S(1)} %get-tuple-element.48), channel_id=1, source_target_pairs={{0,6},{2,4},{4,2},{6,0},{8,14},{10,12},{12,10},{14,8},{16,22},{18,... | collective-permute-start | bytes 589832 | tf_op jit(solution)/shard_map/ppermute | solution.py:41
  12.5 7.5 %collective-permute-start.1 = (f32[24,2048]{1,0:T(8,128)}, f32[24,2048]{1,0:T(8,128)S(1)}, u32[]{:S(2)}, u32[]{:S(2)}) collective-permute-start(f32[24,2048]{1,0:T(8,128)} %get-tuple-element.53), channel_id=1, source_target_pairs={{0,4},{2,6},{4,0},{6,2},{8,12},{10,14},{12,8},{14,10},{16,20},{18,... | collective-permute-start | bytes 589832 | tf_op jit(solution)/shard_map/ppermute | solution.py:41
  13.1 6.9 %collective-permute-start = (f32[24,2048]{1,0:T(8,128)S(1)}, f32[24,2048]{1,0:T(8,128)S(1)}, u32[]{:S(2)}, u32[]{:S(2)}) collective-permute-start(f32[24,2048]{1,0:T(8,128)S(1)} %get-tuple-element.51), channel_id=1, source_target_pairs={{0,2},{2,0},{4,6},{6,4},{8,10},{10,8},{12,14},{14,12},{16,18},{18,... | collective-permute-start | bytes 589832 | tf_op jit(solution)/shard_map/ppermute | solution.py:41
  20.0 11.8 %collective-permute-start.13 = (f32[224,512]{1,0:T(8,128)S(1)}, f32[224,512]{1,0:T(8,128)S(1)}, u32[]{:S(2)}, u32[]{:S(2)}) collective-permute-start(f32[224,512]{1,0:T(8,128)S(1)} %get-tuple-element.64), channel_id=1, source_target_pairs={{0,2},{2,0},{4,6},{6,4},{8,10},{10,8},{12,14},{14,12},{16,18},{18,... | collective-permute-start | bytes 1376264 | tf_op jit(solution)/shard_map/ppermute | solution.py:41
  22.0 11.1 %collective-permute-start.14 = (f32[224,512]{1,0:T(8,128)S(1)}, f32[224,512]{1,0:T(8,128)S(1)}, u32[]{:S(2)}, u32[]{:S(2)}) collective-permute-start(f32[224,512]{1,0:T(8,128)S(1)} %get-tuple-element.65), channel_id=1, source_target_pairs={{0,4},{2,6},{4,0},{6,2},{8,12},{10,14},{12,8},{14,10},{16,20},{18,... | collective-permute-start | bytes 1376264 | tf_op jit(solution)/shard_map/ppermute | solution.py:41
  23.5 11.9 %collective-permute-start.3 = (f32[24,512]{1,0:T(8,128)S(1)}, f32[24,512]{1,0:T(8,128)S(1)}, u32[]{:S(2)}, u32[]{:S(2)}) collective-permute-start(f32[24,512]{1,0:T(8,128)S(1)} %get-tuple-element.60), channel_id=1, source_target_pairs={{0,8},{2,10},{4,12},{6,14},{8,0},{10,2},{12,4},{14,6},{16,24},{18,... | collective-permute-start | bytes 147464 | tf_op jit(solution)/shard_map/ppermute | solution.py:41
  25.1 10.3 %collective-permute-start.4 = (f32[24,512]{1,0:T(8,128)S(1)}, f32[24,512]{1,0:T(8,128)S(1)}, u32[]{:S(2)}, u32[]{:S(2)}) collective-permute-start(f32[24,512]{1,0:T(8,128)S(1)} %get-tuple-element.61), channel_id=1, source_target_pairs={{0,16},{2,18},{4,20},{6,22},{8,24},{10,26},{12,28},{14,30},{16,0},... | collective-permute-start | bytes 147464 | tf_op jit(solution)/shard_map/ppermute | solution.py:41
  27.7 7.8 %collective-permute-start.5 = (f32[24,512]{1,0:T(8,128)S(1)}, f32[24,512]{1,0:T(8,128)S(1)}, u32[]{:S(2)}, u32[]{:S(2)}) collective-permute-start(f32[24,512]{1,0:T(8,128)S(1)} %get-tuple-element.62), channel_id=1, source_target_pairs={{0,24},{2,26},{4,28},{6,30},{8,16},{10,18},{12,20},{14,22},{16,8},... | collective-permute-start | bytes 147464 | tf_op jit(solution)/shard_map/ppermute | solution.py:41
  33.3 6.6 %collective-permute-start.15 = (f32[248,256]{1,0:T(8,128)S(1)}, f32[248,256]{1,0:T(8,128)S(1)}, u32[]{:S(2)}, u32[]{:S(2)}) collective-permute-start(f32[248,256]{1,0:T(8,128)S(1)} %get-tuple-element.72.pass_x), channel_id=1, source_target_pairs={{0,4},{2,6},{4,0},{6,2},{8,12},{10,14},{12,8},{14,10},{16,20},{18,... | collective-permute-start | bytes 761864 | tf_op jit(solution)/shard_map/ppermute | solution.py:41
  34.9 6.3 %collective-permute-start.16 = (f32[248,256]{1,0:T(8,128)S(1)}, f32[248,256]{1,0:T(8,128)S(1)}, u32[]{:S(2)}, u32[]{:S(2)}) collective-permute-start(f32[248,256]{1,0:T(8,128)S(1)} %get-tuple-element.73.pass_y), channel_id=1, source_target_pairs={{0,2},{2,0},{4,6},{6,4},{8,10},{10,8},{12,14},{14,12},{16,18},{18,... | collective-permute-start | bytes 761864 | tf_op jit(solution)/shard_map/ppermute | solution.py:41
  35.5 7.5 %collective-permute-start.8 = (f32[24,512]{1,0:T(8,128)S(1)}, f32[24,512]{1,0:T(8,128)S(1)}, u32[]{:S(2)}, u32[]{:S(2)}) collective-permute-start(f32[24,512]{1,0:T(8,128)S(1)} %add_add_fusion), channel_id=1, source_target_pairs={{0,24},{2,26},{4,28},{6,30},{8,16},{10,18},{12,20},{14,22},{16,8},... | collective-permute-start | bytes 147464 | tf_op jit(solution)/shard_map/ppermute | solution.py:41
  39.2 5.1 %collective-permute-start.7 = (f32[24,512]{1,0:T(8,128)S(1)}, f32[24,512]{1,0:T(8,128)S(1)}, u32[]{:S(2)}, u32[]{:S(2)}) collective-permute-start(f32[24,512]{1,0:T(8,128)S(1)} %add_add_fusion), channel_id=1, source_target_pairs={{0,16},{2,18},{4,20},{6,22},{8,24},{10,26},{12,28},{14,30},{16,0},... | collective-permute-start | bytes 147464 | tf_op jit(solution)/shard_map/ppermute | solution.py:41
  39.2 5.1 %collective-permute-start.6 = (f32[24,512]{1,0:T(8,128)S(1)}, f32[24,512]{1,0:T(8,128)S(1)}, u32[]{:S(2)}, u32[]{:S(2)}) collective-permute-start(f32[24,512]{1,0:T(8,128)S(1)} %add_add_fusion), channel_id=1, source_target_pairs={{0,8},{2,10},{4,12},{6,14},{8,0},{10,2},{12,4},{14,6},{16,24},{18,... | collective-permute-start | bytes 147464 | tf_op jit(solution)/shard_map/ppermute | solution.py:41
  41.4 21.8 %collective-permute-start.17 = (f32[296,256]{1,0:T(8,128)S(1)}, f32[296,256]{1,0:T(8,128)S(1)}, u32[]{:S(2)}, u32[]{:S(2)}) collective-permute-start(f32[296,256]{1,0:T(8,128)S(1)} %get-tuple-element.75), channel_id=1, source_target_pairs={{0,8},{2,10},{4,12},{6,14},{8,0},{10,2},{12,4},{14,6},{16,24},{18,... | collective-permute-start | bytes 909320 | tf_op jit(solution)/shard_map/ppermute | solution.py:41
  44.3 5.7 %collective-permute-start.11 = (f32[24,2048]{1,0:T(8,128)S(1)}, f32[24,2048]{1,0:T(8,128)S(1)}, u32[]{:S(2)}, u32[]{:S(2)}) collective-permute-start(f32[24,2048]{1,0:T(8,128)S(1)} %pad_maximum_fusion.scores), channel_id=1, source_target_pairs={{0,2},{2,0},{4,6},{6,4},{8,10},{10,8},{12,14},{14,12},{16,18},{18,... | collective-permute-start | bytes 589832 | tf_op jit(solution)/shard_map/ppermute | solution.py:41
  45.9 7.8 %collective-permute-start.10 = (f32[24,2048]{1,0:T(8,128)S(1)}, f32[24,2048]{1,0:T(8,128)S(1)}, u32[]{:S(2)}, u32[]{:S(2)}) collective-permute-start(f32[24,2048]{1,0:T(8,128)S(1)} %pad_maximum_fusion.scores), channel_id=1, source_target_pairs={{0,4},{2,6},{4,0},{6,2},{8,12},{10,14},{12,8},{14,10},{16,20},{18,... | collective-permute-start | bytes 589832 | tf_op jit(solution)/shard_map/ppermute | solution.py:41
  46.4 9.4 %collective-permute-start.9 = (f32[24,2048]{1,0:T(8,128)S(1)}, f32[24,2048]{1,0:T(8,128)S(1)}, u32[]{:S(2)}, u32[]{:S(2)}) collective-permute-start(f32[24,2048]{1,0:T(8,128)S(1)} %pad_maximum_fusion.scores), channel_id=1, source_target_pairs={{0,6},{2,4},{4,2},{6,0},{8,14},{10,12},{12,10},{14,8},{16,22},{18,... | collective-permute-start | bytes 589832 | tf_op jit(solution)/shard_map/ppermute | solution.py:41
  58.0 1.3 %collective-permute-start.12 = (f32[24,896]{1,0:T(8,128)S(1)}, f32[24,896]{1,0:T(8,128)S(1)}, u32[]{:S(2)}, u32[]{:S(2)}) collective-permute-start(f32[24,896]{1,0:T(8,128)S(1)} %terms.7.own), channel_id=1, source_target_pairs={{0,1},{1,0},{2,3},{3,2},{4,5},{5,4},{6,7},{7,6},{8,9},{9,8},{10,11... | collective-permute-start | bytes 258056 | tf_op jit(solution)/shard_map/ppermute | solution.py:41
  59.7 6.0 %collective-permute-start.21 = (f32[24,128]{1,0:T(8,128)S(1)}, f32[24,128]{1,0:T(8,128)S(1)}, u32[]{:S(2)}, u32[]{:S(2)}) collective-permute-start(f32[24,128]{1,0:T(8,128)S(1)} %get-tuple-element.82), channel_id=1, source_target_pairs={{0,6},{2,4},{4,2},{6,0},{8,14},{10,12},{12,10},{14,8},{16,22},{18,... | collective-permute-start | bytes 36872 | tf_op jit(solution)/shard_map/ppermute | solution.py:41
  59.7 6.0 %collective-permute-start.20 = (f32[24,128]{1,0:T(8,128)S(1)}, f32[24,128]{1,0:T(8,128)S(1)}, u32[]{:S(2)}, u32[]{:S(2)}) collective-permute-start(f32[24,128]{1,0:T(8,128)S(1)} %get-tuple-element.82), channel_id=1, source_target_pairs={{0,4},{2,6},{4,0},{6,2},{8,12},{10,14},{12,8},{14,10},{16,20},{18,... | collective-permute-start | bytes 36872 | tf_op jit(solution)/shard_map/ppermute | solution.py:41
  61.7 4.0 %collective-permute-start.19 = (f32[24,128]{1,0:T(8,128)S(1)}, f32[24,128]{1,0:T(8,128)S(1)}, u32[]{:S(2)}, u32[]{:S(2)}) collective-permute-start(f32[24,128]{1,0:T(8,128)S(1)} %get-tuple-element.82), channel_id=1, source_target_pairs={{0,2},{2,0},{4,6},{6,4},{8,10},{10,8},{12,14},{14,12},{16,18},{18,... | collective-permute-start | bytes 36872 | tf_op jit(solution)/shard_map/ppermute | solution.py:41
  63.2 13.3 %collective-permute-start.18 = (f32[392,128]{1,0:T(8,128)S(1)}, f32[392,128]{1,0:T(8,128)S(1)}, u32[]{:S(2)}, u32[]{:S(2)}) collective-permute-start(f32[392,128]{1,0:T(8,128)S(1)} %get-tuple-element.77), channel_id=1, source_target_pairs={{0,16},{2,18},{4,20},{6,22},{8,24},{10,26},{12,28},{14,30},{16,0},... | collective-permute-start | bytes 602120 | tf_op jit(solution)/shard_map/ppermute | solution.py:41
  65.7 6.3 %collective-permute-start.24 = (f32[24,128]{1,0:T(8,128)S(1)}, f32[24,128]{1,0:T(8,128)S(1)}, u32[]{:S(2)}, u32[]{:S(2)}) collective-permute-start(f32[24,128]{1,0:T(8,128)S(1)} %add_add_fusion.1.refs_0_), channel_id=1, source_target_pairs={{0,24},{2,26},{4,28},{6,30},{8,16},{10,18},{12,20},{14,22},{16,8},... | collective-permute-start | bytes 36872 | tf_op jit(solution)/shard_map/ppermute | solution.py:41
  67.5 8.3 %collective-permute-start.23 = (f32[24,128]{1,0:T(8,128)S(1)}, f32[24,128]{1,0:T(8,128)S(1)}, u32[]{:S(2)}, u32[]{:S(2)}) collective-permute-start(f32[24,128]{1,0:T(8,128)S(1)} %add_add_fusion.1.refs_0_), channel_id=1, source_target_pairs={{0,16},{2,18},{4,20},{6,22},{8,24},{10,26},{12,28},{14,30},{16,0},... | collective-permute-start | bytes 36872 | tf_op jit(solution)/shard_map/ppermute | solution.py:41
  68.4 7.3 %collective-permute-start.22 = (f32[24,128]{1,0:T(8,128)S(1)}, f32[24,128]{1,0:T(8,128)S(1)}, u32[]{:S(2)}, u32[]{:S(2)}) collective-permute-start(f32[24,128]{1,0:T(8,128)S(1)} %add_add_fusion.1.refs_0_), channel_id=1, source_target_pairs={{0,8},{2,10},{4,12},{6,14},{8,0},{10,2},{12,4},{14,6},{16,24},{18,... | collective-permute-start | bytes 36872 | tf_op jit(solution)/shard_map/ppermute | solution.py:41

commit v6 on v5

--- a/solution.py
+++ b/solution.py
@@ -171,16 +171,6 @@
     alpha_out[...] = jnp.broadcast_to(alpha, alpha_out.shape)
 
 
-def direction_kernel(diag, start, own, residual, *refs):
-    *norms, out = refs
-    samples = start.shape[1]
-    total = norms[0][:, :1]
-    for ref in norms[1:]:
-        total = total + ref[:, :1]
-    start_norm = own[:, samples : samples + 1]
-    out[...] = residual[...] / diag[0:1, :] + (total / start_norm) * start[...]
-
-
 def gene_bounds(sizes, index, count):
     low = jnp.zeros(index.shape, jnp.int32)
     high = jnp.full(index.shape, count, jnp.int32)
@@ -192,10 +182,18 @@
     return low, high
 
 
-def cross_kernel(plan, block, sizes, weights, variants, weighted, *refs):
-    *outs, scaled = refs
+def cross_kernel(plan, block, digit, sizes, start_bf, stats, diag, weighted, geno, all_variants, *refs):
+    *outs, held, variants, scaled, sems, small = refs
+    me = lax.axis_index("samp")
+    (copy,) = fetch([pltpu.make_async_copy(all_variants, variants, small.at[0])])
+    begun = scores_begin(plan, (digit,), me, geno, held, sems)
+    copy.wait()
+    cross_products(plan, block, me, sizes, diag[1:2, :], variants, weighted, scaled, outs[1:])
+    scores_finish(plan, begun, start_bf[...], stats[...], held, outs[:1])
+
+
+def cross_products(plan, block, me, sizes, mu, variants, weighted, scaled, outs):
     own_x, own_y, pass_x, pass_y, send_x, send_y = outs
-    me = lax.axis_index("samp")
     count = variants.shape[0]
     half = GENE_MAX // 2
     quarter = block * len(plan.rest)
@@ -207,7 +205,6 @@
         for j in range(2):
             low = (2 * at + j) * quarter
             kept[half + j * rows : half + (j + 1) * rows, :] = beta[:, low : low + quarter]
-    mu = weights[...].reshape(1, weights.shape[0])
     lane = lax.broadcasted_iota(jnp.int32, (1, quarter), 1)
     column = lax.broadcasted_iota(jnp.int32, (count, quarter), 0)
     places = (
@@ -275,14 +272,22 @@
             out[half + j * tall : half + (j + 1) * tall, :] = total[half:, j * wide : (j + 1) * wide]
 
 
-def gram_kernel(samples, sizes, alpha, *refs):
-    *sums, solved, left, out, solved_out, left_out, full, sems = refs
+def last_kernel(samples, levels, sizes, diag, start, held, alpha, solved, left, *refs):
+    *ins, solved_out, left_out, way_out, gram_out, way, out, full, sems = refs
+    norms, sums = ins[:levels], ins[levels:]
     copies = fetch(
         [
             pltpu.make_async_copy(solved, solved_out, sems.at[0]),
             pltpu.make_async_copy(left, left_out, sems.at[1]),
         ]
     )
+    norm = norms[0][:, :1]
+    for ref in norms[1:]:
+        norm = norm + ref[:, :1]
+    wide = start.shape[1]
+    start_norm = held[:, wide : wide + 1]
+    way[...] = left[...] / diag[0:1, :] + (norm / start_norm) * start[...]
+    copies += fetch([pltpu.make_async_copy(way, way_out, sems.at[2])])
     me = lax.axis_index("samp")
     count = out.shape[2]
     block = out.shape[1]
@@ -314,6 +319,7 @@
     column = lax.broadcasted_iota(jnp.int32, (block, count), 1)
     same = (column >= low[:, :1]) & (column < high[:, :1])
     out[0] = jnp.where(same, (cross - correction) / samples, 0.0)
+    copies += fetch([pltpu.make_async_copy(out, gram_out, sems.at[3])])
     for copy in copies:
         copy.wait()
 
@@ -348,10 +354,6 @@
     width: int
     total: int
     markers: int
-
-
-def tied(array, *others):
-    return lax.optimization_barrier((array, *others))[0]
 
 
 def body(genotypes, variants, weights, variance_ratio, panel, gene_sizes):
@@ -370,7 +372,7 @@
     rows = panel.shape[0]
     vmem = pl.BlockSpec(memory_space=VMEM)
     smem = pl.BlockSpec(memory_space=pltpu.SMEM)
-    hbm = pl.BlockSpec(memory_space=pl.ANY)
+    hbm = pl.BlockSpec(memory_space=pltpu.MemorySpace.HBM)
     columns = len(rest) * width
     payload = VMEM((rows, columns), F32)
 
@@ -400,21 +402,21 @@
     )(variance_ratio, weights, panel, genotypes)
     diag, right, start = in_vmem(diag), in_vmem(right), in_vmem(start)
     after = sent[lead]
-    for digits in (tuple(range(1, lead)), (0,)):
-        start_bf, after = lax.optimization_barrier((start_bf, after))
-        found = pl.pallas_call(
-            functools.partial(scores_kernel, plan, digits),
-            out_shape=[payload] * len(digits),
-            in_specs=[vmem] * 2 + [hbm],
-            out_specs=[vmem] * len(digits),
-            scratch_shapes=[
-                VMEM((len(digits) * columns, samples), BF16),
-                pltpu.SemaphoreType.DMA((len(digits) * len(rest),)),
-            ],
-            name="scores",
-        )(in_vmem(start_bf), in_vmem(stats), genotypes)
-        sent.update(zip(digits, found))
-        after = found[0]
+    start_bf, after = lax.optimization_barrier((start_bf, after))
+    digits = tuple(range(1, lead))
+    found = pl.pallas_call(
+        functools.partial(scores_kernel, plan, digits),
+        out_shape=[payload] * len(digits),
+        in_specs=[vmem] * 2 + [hbm],
+        out_specs=[vmem] * len(digits),
+        scratch_shapes=[
+            VMEM((len(digits) * columns, samples), BF16),
+            pltpu.SemaphoreType.DMA((len(digits) * len(rest),)),
+        ],
+        name="scores",
+    )(in_vmem(start_bf), in_vmem(stats), genotypes)
+    sent.update(zip(digits, found))
+    start_bf, after = lax.optimization_barrier((start_bf, found[0]))
 
     assert radix == 4 and all(r == 4 for r, _ in later)
     block = num_variants // count
@@ -424,14 +426,20 @@
     own_shape = VMEM((half, quarter), F32)
     pass_shape = VMEM((half + 2 * rows, quarter), F32)
     send_shape = VMEM((half + rows, 2 * quarter), F32)
-    *parts, send_x, send_y = pl.pallas_call(
-        functools.partial(cross_kernel, plan, block),
-        out_shape=[own_shape] * 2 + [pass_shape] * 2 + [send_shape] * 2,
-        in_specs=[smem] + [vmem] * 3,
-        out_specs=[vmem] * 6,
-        scratch_shapes=[VMEM((quarter, samples), BF16)],
-        name="cross",
-    )(gene_sizes, weights, tied(variants, sent[0]), in_vmem(weighted))
+    sent[0], *parts, send_x, send_y = pl.pallas_call(
+        functools.partial(cross_kernel, plan, block, 0),
+        out_shape=[payload] + [own_shape] * 2 + [pass_shape] * 2 + [send_shape] * 2,
+        in_specs=[smem] + [vmem] * 4 + [hbm] * 2,
+        out_specs=[vmem] * 7,
+        scratch_shapes=[
+            VMEM((columns, samples), BF16),
+            VMEM((num_variants, samples), BF16),
+            VMEM((quarter, samples), BF16),
+            pltpu.SemaphoreType.DMA((len(rest),)),
+            pltpu.SemaphoreType.DMA((1,)),
+        ],
+        name="scores_cross",
+    )(gene_sizes, in_vmem(start_bf), in_vmem(stats), diag, in_vmem(weighted), genotypes, variants)
 
     terms = [sent[0]] + [swap(sent[d], count, firsts[d]) for d in range(1, radix)]
     wide = columns
@@ -531,22 +539,20 @@
         for one in norms[1:]:
             total = total + one
         norms = [total] + [swap(total, count, d * s) for d in range(1, r)]
-    direction = pl.pallas_call(
-        direction_kernel,
-        out_shape=full,
-        in_specs=[vmem] * (4 + len(norms)),
-        out_specs=vmem,
-        name="direction",
-    )(diag, start, held, in_vmem(residual), *map(in_vmem, norms))
-
-    gram, solution, residual = pl.pallas_call(
-        functools.partial(gram_kernel, samples * count),
-        out_shape=[jax.ShapeDtypeStruct((1, block, num_variants), F32), full, full],
-        in_specs=[smem] + [vmem] * (3 + len(sums)),
-        out_specs=[vmem, hbm, hbm],
-        scratch_shapes=[VMEM((rows, num_variants), F32), pltpu.SemaphoreType.DMA((2,))],
-        name="gram",
-    )(gene_sizes, *map(in_vmem, (alpha, *sums, solution, residual)))
+    gram_shape = (1, block, num_variants)
+    solution, residual, direction, gram = pl.pallas_call(
+        functools.partial(last_kernel, samples * count, len(norms)),
+        out_shape=[full] * 3 + [jax.ShapeDtypeStruct(gram_shape, F32)],
+        in_specs=[smem] + [vmem] * (6 + len(norms) + len(sums)),
+        out_specs=[hbm] * 4,
+        scratch_shapes=[
+            VMEM((rows, samples), F32),
+            VMEM(gram_shape, F32),
+            VMEM((rows, num_variants), F32),
+            pltpu.SemaphoreType.DMA((4,)),
+        ],
+        name="last",
+    )(gene_sizes, diag, start, held, *map(in_vmem, (alpha, solution, residual, *norms, *sums)))
     return solution, residual, direction, gram
 
 

time: 79.1 us -> 79.2 us (level)
  waiting for transfers between devices: 16.1 us -> 20.9 us
  starting transfers between devices: 34.8 us -> 30.3 us
  Pallas kernels: 26.5 us -> 25.7 us
    ppermute x25, waiting for transfers between devices: 16.1 us -> 20.9 us  [swap(): return lax.ppermute(array, axis, [(i, i ^ offset) for i in range(count)])]
    ppermute x25, starting transfers between devices: 34.8 us -> 30.3 us  [swap(): return lax.ppermute(array, axis, [(i, i ^ offset) for i in range(count)])]
    pallas_call x2 -> x1, Pallas kernels: 7.14 us -> 4.62 us  [body(): pl.pallas_call(functools.partial(scores_kernel, plan, digits), out_shape=...]
    pallas_call x3 -> x2, Pallas kernels: 7.39 us -> 8.41 us  [the longest x1 6.24 us: body(): pl.pallas_call(functools.partial(cross_kernel, plan, block, 0), out_shape...]
  transfers between devices with their start and end apart: 25 -> 25, of which waited for: 9 -> 12; matrix products, arithmetic and copies ran while one was open for 0% -> 0% of each run, Pallas kernels for 27% -> 21%
where the time goes in v6:
time: 79.2 us; the launch traced here: 79 us
  starting transfers between devices  30.3 us (38%)
  Pallas kernels  25.7 us (32%)
  waiting for transfers between devices  20.9 us (26%)
  between operations  1.43 us (2%)
    ppermute x25, starting transfers between devices, swap(): return lax.ppermute(array, axis, [(i, i ^ offset) for i in range(count)])  30.3 us
    ppermute x25, waiting for transfers between devices, swap(): return lax.ppermute(array, axis, [(i, i ^ offset) for i in range(count)])  20.9 us
    pallas_call x4, Pallas kernels, body(): pl.pallas_call(functools.partial(terms_kernel, plan, d), out_shape=VMEM((...  8.63 us
    pallas_call x1, Pallas kernels, body(): pl.pallas_call(functools.partial(cross_kernel, plan, block, 0), out_shape...  6.24 us
    pallas_call x1, Pallas kernels, body(): pl.pallas_call(functools.partial(scores_kernel, plan, digits), out_shape=...  4.62 us
    pallas_call x1, Pallas kernels, body(): pl.pallas_call(functools.partial(lead_kernel, plan, lead), out_shape=[pay...  2.62 us
    pallas_call x1, Pallas kernels, body(): pl.pallas_call(functools.partial(last_kernel, samples * count, len(norms)...  2.18 us
  transfers between devices with their start and end apart: 25, of which 12 were waited for; matrix products, arithmetic and copies ran while one was open for 0% of the time, Pallas kernels for 21%

profile of v6, /device:TPU:0, one launch (start us, length us, event | category | flops | bytes accessed | tf_op | source)
XLA Modules:
  0.0 79.0 jit_solution(12574215212485806275)
XLA Ops:
  1.3 2.6 %scores_lead.1 = (f32[24,2048]{1,0:T(8,128)S(1)}, f32[8,768]{1,0:T(8,128)S(1)}, f32[24,768]{1,0:T(8,128)S(1)}, f32[24,768]{1,0:T(8,128)S(1)}, bf16[24,768]{1,0:T...) custom-call(f32[1]{0:T(128)S(6)} %copy.18.ratio, f32[768]{0:T(1024)} %weights.1, f32[24,768]{1,0:T(8,128)} %panel.1, ...), custom_call_target="tpu_custom_call" | custom-call | tf_op jit(solution)/shard_map/scores_lead/pallas_call | solution.py:381
  3.9 4.6 %scores.1 = (f32[24,2048]{1,0:T(8,128)}, f32[24,2048]{1,0:T(8,128)}) custom-call(bf16[24,768]{1,0:T(8,128)(2,1)S(1)} %get-tuple-element.48.start_bf, f32[24,128]{1,0:T(8,128)S(1)} %get-tuple-element.46.stats, bf16[8000,768]{1,0:T(8,128)(2,1)} %refs_1_.5), custom_call_target="tpu_custom_call" | custom-call | tf_op jit(solution)/shard_map/scores/pallas_call | solution.py:407
  8.5 3.0 %collective-permute-start = (f32[24,2048]{1,0:T(8,128)}, f32[24,2048]{1,0:T(8,128)S(1)}, u32[]{:S(2)}, u32[]{:S(2)}) collective-permute-start(f32[24,2048]{1,0:T(8,128)} %get-tuple-element.47), channel_id=1, source_target_pairs={{0,2},{2,0},{4,6},{6,4},{8,10},{10,8},{12,14},{14,12},{16,18},{18,... | collective-permute-start | bytes 589832 | tf_op jit(solution)/shard_map/ppermute | solution.py:41
  11.6 1.5 %collective-permute-start.1 = (f32[24,2048]{1,0:T(8,128)}, f32[24,2048]{1,0:T(8,128)S(1)}, u32[]{:S(2)}, u32[]{:S(2)}) collective-permute-start(f32[24,2048]{1,0:T(8,128)} %get-tuple-element.51), channel_id=1, source_target_pairs={{0,4},{2,6},{4,0},{6,2},{8,12},{10,14},{12,8},{14,10},{16,20},{18,... | collective-permute-start | bytes 589832 | tf_op jit(solution)/shard_map/ppermute | solution.py:41
  13.1 6.2 %scores_cross.1 = (f32[24,2048]{1,0:T(8,128)S(1)}, f32[200,256]{1,0:T(8,128)S(1)}, f32[200,256]{1,0:T(8,128)S(1)}, f32[248,256]{1,0:T(8,128)S(1)}, f32[248,256]{...) custom-call(s32[1,24]{1,0:T(1,128)} %sizes.3, bf16[24,768]{1,0:T(8,128)(2,1)S(1)} %get-tuple-element.48.start_bf, ...), custom_call_target="tpu_custom_call" | custom-call | tf_op jit(solution)/shard_map/scores_cross/pallas_call | solution.py:429
  19.4 3.0 %collective-permute-done.1.refs_2_ = f32[24,2048]{1,0:T(8,128)S(1)} collective-permute-done((f32[24,2048]{1,0:T(8,128)}, f32[24,2048]{1,0:T(8,128)S(1)}, u32[]{:S(2)}, u32[]{:S(2)}) %collective-permute-start.1) | collective-permute-done | bytes 196640 | tf_op jit(solution)/shard_map/ppermute | solution.py:41
  23.0 1.2 %collective-permute-start.19 = (f32[224,512]{1,0:T(8,128)S(1)}, f32[224,512]{1,0:T(8,128)S(1)}, u32[]{:S(2)}, u32[]{:S(2)}) collective-permute-start(f32[224,512]{1,0:T(8,128)S(1)} %get-tuple-element.64), channel_id=1, source_target_pairs={{0,2},{2,0},{4,6},{6,4},{8,10},{10,8},{12,14},{14,12},{16,18},{18,... | collective-permute-start | bytes 1376264 | tf_op jit(solution)/shard_map/ppermute | solution.py:41
  25.1 1.6 %collective-permute-start.3 = (f32[24,512]{1,0:T(8,128)}, f32[24,512]{1,0:T(8,128)S(1)}, u32[]{:S(2)}, u32[]{:S(2)}) collective-permute-start(f32[24,512]{1,0:T(8,128)} %copy-done), channel_id=1, source_target_pairs={{0,8},{2,10},{4,12},{6,14},{8,0},{10,2},{12,4},{14,6},{16,24},{18,... | collective-permute-start | bytes 147464 | tf_op jit(solution)/shard_map/ppermute | solution.py:41
  26.7 2.6 %collective-permute-start.4 = (f32[24,512]{1,0:T(8,128)S(1)}, f32[24,512]{1,0:T(8,128)S(1)}, u32[]{:S(2)}, u32[]{:S(2)}) collective-permute-start(f32[24,512]{1,0:T(8,128)S(1)} %get-tuple-element.57), channel_id=1, source_target_pairs={{0,16},{2,18},{4,20},{6,22},{8,24},{10,26},{12,28},{14,30},{16,0},... | collective-permute-start | bytes 147464 | tf_op jit(solution)/shard_map/ppermute | solution.py:41
  29.5 4.7 %collective-permute-done.19.got_x = f32[224,512]{1,0:T(8,128)S(1)} collective-permute-done((f32[224,512]{1,0:T(8,128)S(1)}, f32[224,512]{1,0:T(8,128)S(1)}, u32[]{:S(2)}, u32[]{:S(2)}) %collective-permute-start.19) | collective-permute-done | bytes 458784 | tf_op jit(solution)/shard_map/ppermute | solution.py:41
  34.2 1.2 %collective-permute-done.20.got_y = f32[224,512]{1,0:T(8,128)S(1)} collective-permute-done((f32[224,512]{1,0:T(8,128)S(1)}, f32[224,512]{1,0:T(8,128)S(1)}, u32[]{:S(2)}, u32[]{:S(2)}) %collective-permute-start.20) | collective-permute-done | bytes 458784 | tf_op jit(solution)/shard_map/ppermute | solution.py:41
  36.8 1.6 %collective-permute-start.6 = (f32[24,512]{1,0:T(8,128)S(1)}, f32[24,512]{1,0:T(8,128)S(1)}, u32[]{:S(2)}, u32[]{:S(2)}) collective-permute-start(f32[24,512]{1,0:T(8,128)S(1)} %add_add_fusion), channel_id=1, source_target_pairs={{0,8},{2,10},{4,12},{6,14},{8,0},{10,2},{12,4},{14,6},{16,24},{18,... | collective-permute-start | bytes 147464 | tf_op jit(solution)/shard_map/ppermute | solution.py:41
  38.4 2.6 %collective-permute-start.7 = (f32[24,512]{1,0:T(8,128)S(1)}, f32[24,512]{1,0:T(8,128)S(1)}, u32[]{:S(2)}, u32[]{:S(2)}) collective-permute-start(f32[24,512]{1,0:T(8,128)S(1)} %add_add_fusion), channel_id=1, source_target_pairs={{0,16},{2,18},{4,20},{6,22},{8,24},{10,26},{12,28},{14,30},{16,0},... | collective-permute-start | bytes 147464 | tf_op jit(solution)/shard_map/ppermute | solution.py:41
  42.5 0.9 %split.1 = (f32[296,256]{1,0:T(8,128)S(1)}, f32[296,256]{1,0:T(8,128)}) custom-call(f32[200,256]{1,0:T(8,128)S(1)} %get-tuple-element.70.own_x, f32[200,256]{1,0:T(8,128)S(1)} %get-tuple-element.71.own_y, f32[248,256]{1,0:T(8,128)S(1)} %get-tuple-element.72.pass_x, f32[248,256]{1,0:T(8,128)S(1)} %get-tuple-element.73.pass_y, ...), custom_call_target="tpu_custom_call" | custom-call | tf_op jit(solution)/shard_map/split/pallas_call | solution.py:480
  43.3 1.6 %collective-permute-start.23 = (f32[296,256]{1,0:T(8,128)}, f32[296,256]{1,0:T(8,128)S(1)}, u32[]{:S(2)}, u32[]{:S(2)}) collective-permute-start(f32[296,256]{1,0:T(8,128)} %get-tuple-element.75), channel_id=1, source_target_pairs={{0,8},{2,10},{4,12},{6,14},{8,0},{10,2},{12,4},{14,6},{16,24},{18,... | collective-permute-start | bytes 909320 | tf_op jit(solution)/shard_map/ppermute | solution.py:41
  45.0 2.4 %collective-permute-done.8 = f32[24,512]{1,0:T(8,128)S(1)} collective-permute-done((f32[24,512]{1,0:T(8,128)S(1)}, f32[24,512]{1,0:T(8,128)S(1)}, u32[]{:S(2)}, u32[]{:S(2)}) %collective-permute-start.8) | collective-permute-done | bytes 49184 | tf_op jit(solution)/shard_map/ppermute | solution.py:41
  47.4 1.5 %collective-permute-start.11 = (f32[24,2048]{1,0:T(8,128)S(1)}, f32[24,2048]{1,0:T(8,128)S(1)}, u32[]{:S(2)}, u32[]{:S(2)}) collective-permute-start(f32[24,2048]{1,0:T(8,128)S(1)} %pad_maximum_fusion.scores), channel_id=1, source_target_pairs={{0,2},{2,0},{4,6},{6,4},{8,10},{10,8},{12,14},{14,12},{16,18},{18,... | collective-permute-start | bytes 589832 | tf_op jit(solution)/shard_map/ppermute | solution.py:41
  48.9 1.5 %collective-permute-start.10 = (f32[24,2048]{1,0:T(8,128)S(1)}, f32[24,2048]{1,0:T(8,128)S(1)}, u32[]{:S(2)}, u32[]{:S(2)}) collective-permute-start(f32[24,2048]{1,0:T(8,128)S(1)} %pad_maximum_fusion.scores), channel_id=1, source_target_pairs={{0,4},{2,6},{4,0},{6,2},{8,12},{10,14},{12,8},{14,10},{16,20},{18,... | collective-permute-start | bytes 589832 | tf_op jit(solution)/shard_map/ppermute | solution.py:41
  51.0 2.2 %terms.4.refs_0_ = f32[24,896]{1,0:T(8,128)S(1)} custom-call(f32[8,768]{1,0:T(8,128)S(1)} %get-tuple-element.41.diag, f32[24,2048]{1,0:T(8,128)S(1)} %pad_maximum_fusion.scores, bf16[8000,768]{1,0:T(8,128)(2,1)} %refs_1_.5), custom_call_target="tpu_custom_call" | custom-call | tf_op jit(solution)/shard_map/terms/pallas_call | solution.py:506
  53.1 2.2 %terms.5.refs_0_ = f32[24,896]{1,0:T(8,128)S(1)} custom-call(f32[8,768]{1,0:T(8,128)S(1)} %get-tuple-element.41.diag, f32[24,2048]{1,0:T(8,128)S(1)} %collective-permute-done.11.scores, f32[24,896]{1,0:T(8,128)S(1)} %terms.4.refs_0_, bf16[8000,768]{1,0:T(8,128)(2,1)} %refs_1_.5), custom_call_target="tpu_custom_call" | custom-call | tf_op jit(solution)/shard_map/terms/pallas_call | solution.py:506
  55.8 2.2 %terms.6.refs_0_ = f32[24,896]{1,0:T(8,128)S(1)} custom-call(f32[8,768]{1,0:T(8,128)S(1)} %get-tuple-element.41.diag, f32[24,2048]{1,0:T(8,128)S(1)} %collective-permute-done.10.scores, f32[24,896]{1,0:T(8,128)S(1)} %terms.5.refs_0_, bf16[8000,768]{1,0:T(8,128)(2,1)} %refs_1_.5), custom_call_target="tpu_custom_call" | custom-call | tf_op jit(solution)/shard_map/terms/pallas_call | solution.py:506
  57.9 2.2 %terms.7.own.held = f32[24,896]{1,0:T(8,128)S(1)} custom-call(f32[8,768]{1,0:T(8,128)S(1)} %get-tuple-element.41.diag, f32[24,2048]{1,0:T(8,128)S(1)} %collective-permute-done.9.scores, f32[24,896]{1,0:T(8,128)S(1)} %terms.6.refs_0_, bf16[8000,768]{1,0:T(8,128)(2,1)} %refs_1_.5), custom_call_target="tpu_custom_call" | custom-call | tf_op jit(solution)/shard_map/terms/pallas_call | solution.py:506
  60.2 1.3 %collective-permute-done.12.other = f32[24,896]{1,0:T(8,128)S(1)} collective-permute-done((f32[24,896]{1,0:T(8,128)S(1)}, f32[24,896]{1,0:T(8,128)S(1)}, u32[]{:S(2)}, u32[]{:S(2)}) %collective-permute-start.12) | collective-permute-done | bytes 86048 | tf_op jit(solution)/shard_map/ppermute | solution.py:41
  61.8 1.0 %collective-permute-start.13 = (f32[24,128]{1,0:T(8,128)S(1)}, f32[24,128]{1,0:T(8,128)S(1)}, u32[]{:S(2)}, u32[]{:S(2)}) collective-permute-start(f32[24,128]{1,0:T(8,128)S(1)} %get-tuple-element.63), channel_id=1, source_target_pairs={{0,2},{2,0},{4,6},{6,4},{8,10},{10,8},{12,14},{14,12},{16,18},{18,... | collective-permute-start | bytes 36872 | tf_op jit(solution)/shard_map/ppermute | solution.py:41
  62.8 2.0 %collective-permute-start.14 = (f32[24,128]{1,0:T(8,128)S(1)}, f32[24,128]{1,0:T(8,128)S(1)}, u32[]{:S(2)}, u32[]{:S(2)}) collective-permute-start(f32[24,128]{1,0:T(8,128)S(1)} %get-tuple-element.63), channel_id=1, source_target_pairs={{0,4},{2,6},{4,0},{6,2},{8,12},{10,14},{12,8},{14,10},{16,20},{18,... | collective-permute-start | bytes 36872 | tf_op jit(solution)/shard_map/ppermute | solution.py:41
  64.8 0.9 %collective-permute-start.15 = (f32[24,128]{1,0:T(8,128)S(1)}, f32[24,128]{1,0:T(8,128)S(1)}, u32[]{:S(2)}, u32[]{:S(2)}) collective-permute-start(f32[24,128]{1,0:T(8,128)S(1)} %get-tuple-element.63), channel_id=1, source_target_pairs={{0,6},{2,4},{4,2},{6,0},{8,14},{10,12},{12,10},{14,8},{16,22},{18,... | collective-permute-start | bytes 36872 | tf_op jit(solution)/shard_map/ppermute | solution.py:41
  66.5 2.9 %collective-permute-done.15 = f32[24,128]{1,0:T(8,128)S(1)} collective-permute-done((f32[24,128]{1,0:T(8,128)S(1)}, f32[24,128]{1,0:T(8,128)S(1)}, u32[]{:S(2)}, u32[]{:S(2)}) %collective-permute-start.15) | collective-permute-done | bytes 12320 | tf_op jit(solution)/shard_map/ppermute | solution.py:41
  69.4 1.6 %collective-permute-start.17 = (f32[24,128]{1,0:T(8,128)S(1)}, f32[24,128]{1,0:T(8,128)S(1)}, u32[]{:S(2)}, u32[]{:S(2)}) collective-permute-start(f32[24,128]{1,0:T(8,128)S(1)} %add_add_fusion.1.refs_0_), channel_id=1, source_target_pairs={{0,16},{2,18},{4,20},{6,22},{8,24},{10,26},{12,28},{14,30},{16,0},... | collective-permute-start | bytes 36872 | tf_op jit(solution)/shard_map/ppermute | solution.py:41
  71.0 2.8 %collective-permute-start.18 = (f32[24,128]{1,0:T(8,128)S(1)}, f32[24,128]{1,0:T(8,128)S(1)}, u32[]{:S(2)}, u32[]{:S(2)}) collective-permute-start(f32[24,128]{1,0:T(8,128)S(1)} %add_add_fusion.1.refs_0_), channel_id=1, source_target_pairs={{0,24},{2,26},{4,28},{6,30},{8,16},{10,18},{12,20},{14,22},{16,8},... | collective-permute-start | bytes 36872 | tf_op jit(solution)/shard_map/ppermute | solution.py:41
  73.8 1.7 %collective-permute-done.16.refs_1_ = f32[24,128]{1,0:T(8,128)S(1)} collective-permute-done((f32[24,128]{1,0:T(8,128)S(1)}, f32[24,128]{1,0:T(8,128)S(1)}, u32[]{:S(2)}, u32[]{:S(2)}) %collective-permute-start.16) | collective-permute-done | bytes 12320 | tf_op jit(solution)/shard_map/ppermute | solution.py:41
  75.5 1.3 %collective-permute-done.17.refs_2_ = f32[24,128]{1,0:T(8,128)S(1)} collective-permute-done((f32[24,128]{1,0:T(8,128)S(1)}, f32[24,128]{1,0:T(8,128)S(1)}, u32[]{:S(2)}, u32[]{:S(2)}) %collective-permute-start.17) | collective-permute-done | bytes 12320 | tf_op jit(solution)/shard_map/ppermute | solution.py:41
  76.8 2.2 %last.1 = (f32[24,768]{1,0:T(8,128)}, f32[24,768]{1,0:T(8,128)}, f32[24,768]{1,0:T(8,128)}, f32[1,64,1024]{2,1,0:T(8,128)}) custom-call(s32[1,24]{1,0:T(1,128)} %sizes.3, f32[8,768]{1,0:T(8,128)S(1)} %get-tuple-element.41.diag, f32[24,768]{1,0:T(8,128)S(1)} %get-tuple-element.42.start, f32[24,896]{1,0:T(8,128)S(1)} %terms.7.own.held, ...), custom_call_target="tpu_custom_call" | custom-call | tf_op jit(solution)/shard_map/last/pallas_call | solution.py:543
  (36 shorter events, 6.8 us)
Async XLA Ops:
  8.5 10.8 %collective-permute-start = (f32[24,2048]{1,0:T(8,128)}, f32[24,2048]{1,0:T(8,128)S(1)}, u32[]{:S(2)}, u32[]{:S(2)}) collective-permute-start(f32[24,2048]{1,0:T(8,128)} %get-tuple-element.47), channel_id=1, source_target_pairs={{0,2},{2,0},{4,6},{6,4},{8,10},{10,8},{12,14},{14,12},{16,18},{18,... | collective-permute-start | bytes 589832 | tf_op jit(solution)/shard_map/ppermute | solution.py:41
  11.6 10.8 %collective-permute-start.1 = (f32[24,2048]{1,0:T(8,128)}, f32[24,2048]{1,0:T(8,128)S(1)}, u32[]{:S(2)}, u32[]{:S(2)}) collective-permute-start(f32[24,2048]{1,0:T(8,128)} %get-tuple-element.51), channel_id=1, source_target_pairs={{0,4},{2,6},{4,0},{6,2},{8,12},{10,14},{12,8},{14,10},{16,20},{18,... | collective-permute-start | bytes 589832 | tf_op jit(solution)/shard_map/ppermute | solution.py:41
  13.1 9.3 %collective-permute-start.2 = (f32[24,2048]{1,0:T(8,128)S(1)}, f32[24,2048]{1,0:T(8,128)S(1)}, u32[]{:S(2)}, u32[]{:S(2)}) collective-permute-start(f32[24,2048]{1,0:T(8,128)S(1)} %get-tuple-element.44), channel_id=1, source_target_pairs={{0,6},{2,4},{4,2},{6,0},{8,14},{10,12},{12,10},{14,8},{16,22},{18,... | collective-permute-start | bytes 589832 | tf_op jit(solution)/shard_map/ppermute | solution.py:41
  22.4 0.6 copy-start
  23.0 11.2 %collective-permute-start.19 = (f32[224,512]{1,0:T(8,128)S(1)}, f32[224,512]{1,0:T(8,128)S(1)}, u32[]{:S(2)}, u32[]{:S(2)}) collective-permute-start(f32[224,512]{1,0:T(8,128)S(1)} %get-tuple-element.64), channel_id=1, source_target_pairs={{0,2},{2,0},{4,6},{6,4},{8,10},{10,8},{12,14},{14,12},{16,18},{18,... | collective-permute-start | bytes 1376264 | tf_op jit(solution)/shard_map/ppermute | solution.py:41
  24.3 11.1 %collective-permute-start.20 = (f32[224,512]{1,0:T(8,128)S(1)}, f32[224,512]{1,0:T(8,128)S(1)}, u32[]{:S(2)}, u32[]{:S(2)}) collective-permute-start(f32[224,512]{1,0:T(8,128)S(1)} %get-tuple-element.65), channel_id=1, source_target_pairs={{0,4},{2,6},{4,0},{6,2},{8,12},{10,14},{12,8},{14,10},{16,20},{18,... | collective-permute-start | bytes 1376264 | tf_op jit(solution)/shard_map/ppermute | solution.py:41
  25.1 11.7 %collective-permute-start.3 = (f32[24,512]{1,0:T(8,128)}, f32[24,512]{1,0:T(8,128)S(1)}, u32[]{:S(2)}, u32[]{:S(2)}) collective-permute-start(f32[24,512]{1,0:T(8,128)} %copy-done), channel_id=1, source_target_pairs={{0,8},{2,10},{4,12},{6,14},{8,0},{10,2},{12,4},{14,6},{16,24},{18,... | collective-permute-start | bytes 147464 | tf_op jit(solution)/shard_map/ppermute | solution.py:41
  26.7 10.1 %collective-permute-start.4 = (f32[24,512]{1,0:T(8,128)S(1)}, f32[24,512]{1,0:T(8,128)S(1)}, u32[]{:S(2)}, u32[]{:S(2)}) collective-permute-start(f32[24,512]{1,0:T(8,128)S(1)} %get-tuple-element.57), channel_id=1, source_target_pairs={{0,16},{2,18},{4,20},{6,22},{8,24},{10,26},{12,28},{14,30},{16,0},... | collective-permute-start | bytes 147464 | tf_op jit(solution)/shard_map/ppermute | solution.py:41
  29.2 7.5 %collective-permute-start.5 = (f32[24,512]{1,0:T(8,128)S(1)}, f32[24,512]{1,0:T(8,128)S(1)}, u32[]{:S(2)}, u32[]{:S(2)}) collective-permute-start(f32[24,512]{1,0:T(8,128)S(1)} %get-tuple-element.58), channel_id=1, source_target_pairs={{0,24},{2,26},{4,28},{6,30},{8,16},{10,18},{12,20},{14,22},{16,8},... | collective-permute-start | bytes 147464 | tf_op jit(solution)/shard_map/ppermute | solution.py:41
  35.5 6.3 %collective-permute-start.21 = (f32[248,256]{1,0:T(8,128)S(1)}, f32[248,256]{1,0:T(8,128)S(1)}, u32[]{:S(2)}, u32[]{:S(2)}) collective-permute-start(f32[248,256]{1,0:T(8,128)S(1)} %get-tuple-element.72.pass_x), channel_id=1, source_target_pairs={{0,4},{2,6},{4,0},{6,2},{8,12},{10,14},{12,8},{14,10},{16,20},{18,... | collective-permute-start | bytes 761864 | tf_op jit(solution)/shard_map/ppermute | solution.py:41
  36.2 6.3 %collective-permute-start.22 = (f32[248,256]{1,0:T(8,128)S(1)}, f32[248,256]{1,0:T(8,128)S(1)}, u32[]{:S(2)}, u32[]{:S(2)}) collective-permute-start(f32[248,256]{1,0:T(8,128)S(1)} %get-tuple-element.73.pass_y), channel_id=1, source_target_pairs={{0,2},{2,0},{4,6},{6,4},{8,10},{10,8},{12,14},{14,12},{16,18},{18,... | collective-permute-start | bytes 761864 | tf_op jit(solution)/shard_map/ppermute | solution.py:41
  36.8 8.2 %collective-permute-start.6 = (f32[24,512]{1,0:T(8,128)S(1)}, f32[24,512]{1,0:T(8,128)S(1)}, u32[]{:S(2)}, u32[]{:S(2)}) collective-permute-start(f32[24,512]{1,0:T(8,128)S(1)} %add_add_fusion), channel_id=1, source_target_pairs={{0,8},{2,10},{4,12},{6,14},{8,0},{10,2},{12,4},{14,6},{16,24},{18,... | collective-permute-start | bytes 147464 | tf_op jit(solution)/shard_map/ppermute | solution.py:41
  38.4 6.6 %collective-permute-start.7 = (f32[24,512]{1,0:T(8,128)S(1)}, f32[24,512]{1,0:T(8,128)S(1)}, u32[]{:S(2)}, u32[]{:S(2)}) collective-permute-start(f32[24,512]{1,0:T(8,128)S(1)} %add_add_fusion), channel_id=1, source_target_pairs={{0,16},{2,18},{4,20},{6,22},{8,24},{10,26},{12,28},{14,30},{16,0},... | collective-permute-start | bytes 147464 | tf_op jit(solution)/shard_map/ppermute | solution.py:41
  41.0 6.4 %collective-permute-start.8 = (f32[24,512]{1,0:T(8,128)S(1)}, f32[24,512]{1,0:T(8,128)S(1)}, u32[]{:S(2)}, u32[]{:S(2)}) collective-permute-start(f32[24,512]{1,0:T(8,128)S(1)} %add_add_fusion), channel_id=1, source_target_pairs={{0,24},{2,26},{4,28},{6,30},{8,16},{10,18},{12,20},{14,22},{16,8},... | collective-permute-start | bytes 147464 | tf_op jit(solution)/shard_map/ppermute | solution.py:41
  43.3 22.3 %collective-permute-start.23 = (f32[296,256]{1,0:T(8,128)}, f32[296,256]{1,0:T(8,128)S(1)}, u32[]{:S(2)}, u32[]{:S(2)}) collective-permute-start(f32[296,256]{1,0:T(8,128)} %get-tuple-element.75), channel_id=1, source_target_pairs={{0,8},{2,10},{4,12},{6,14},{8,0},{10,2},{12,4},{14,6},{16,24},{18,... | collective-permute-start | bytes 909320 | tf_op jit(solution)/shard_map/ppermute | solution.py:41
  47.4 5.7 %collective-permute-start.11 = (f32[24,2048]{1,0:T(8,128)S(1)}, f32[24,2048]{1,0:T(8,128)S(1)}, u32[]{:S(2)}, u32[]{:S(2)}) collective-permute-start(f32[24,2048]{1,0:T(8,128)S(1)} %pad_maximum_fusion.scores), channel_id=1, source_target_pairs={{0,2},{2,0},{4,6},{6,4},{8,10},{10,8},{12,14},{14,12},{16,18},{18,... | collective-permute-start | bytes 589832 | tf_op jit(solution)/shard_map/ppermute | solution.py:41
  48.9 6.8 %collective-permute-start.10 = (f32[24,2048]{1,0:T(8,128)S(1)}, f32[24,2048]{1,0:T(8,128)S(1)}, u32[]{:S(2)}, u32[]{:S(2)}) collective-permute-start(f32[24,2048]{1,0:T(8,128)S(1)} %pad_maximum_fusion.scores), channel_id=1, source_target_pairs={{0,4},{2,6},{4,0},{6,2},{8,12},{10,14},{12,8},{14,10},{16,20},{18,... | collective-permute-start | bytes 589832 | tf_op jit(solution)/shard_map/ppermute | solution.py:41
  50.4 7.5 %collective-permute-start.9 = (f32[24,2048]{1,0:T(8,128)S(1)}, f32[24,2048]{1,0:T(8,128)S(1)}, u32[]{:S(2)}, u32[]{:S(2)}) collective-permute-start(f32[24,2048]{1,0:T(8,128)S(1)} %pad_maximum_fusion.scores), channel_id=1, source_target_pairs={{0,6},{2,4},{4,2},{6,0},{8,14},{10,12},{12,10},{14,8},{16,22},{18,... | collective-permute-start | bytes 589832 | tf_op jit(solution)/shard_map/ppermute | solution.py:41
  60.1 1.3 %collective-permute-start.12 = (f32[24,896]{1,0:T(8,128)S(1)}, f32[24,896]{1,0:T(8,128)S(1)}, u32[]{:S(2)}, u32[]{:S(2)}) collective-permute-start(f32[24,896]{1,0:T(8,128)S(1)} %terms.7.own.held), channel_id=1, source_target_pairs={{0,1},{1,0},{2,3},{3,2},{4,5},{5,4},{6,7},{7,6},{8,9},{9,8},{10,11... | collective-permute-start | bytes 258056 | tf_op jit(solution)/shard_map/ppermute | solution.py:41
  61.8 4.0 %collective-permute-start.13 = (f32[24,128]{1,0:T(8,128)S(1)}, f32[24,128]{1,0:T(8,128)S(1)}, u32[]{:S(2)}, u32[]{:S(2)}) collective-permute-start(f32[24,128]{1,0:T(8,128)S(1)} %get-tuple-element.63), channel_id=1, source_target_pairs={{0,2},{2,0},{4,6},{6,4},{8,10},{10,8},{12,14},{14,12},{16,18},{18,... | collective-permute-start | bytes 36872 | tf_op jit(solution)/shard_map/ppermute | solution.py:41
  62.8 3.7 %collective-permute-start.14 = (f32[24,128]{1,0:T(8,128)S(1)}, f32[24,128]{1,0:T(8,128)S(1)}, u32[]{:S(2)}, u32[]{:S(2)}) collective-permute-start(f32[24,128]{1,0:T(8,128)S(1)} %get-tuple-element.63), channel_id=1, source_target_pairs={{0,4},{2,6},{4,0},{6,2},{8,12},{10,14},{12,8},{14,10},{16,20},{18,... | collective-permute-start | bytes 36872 | tf_op jit(solution)/shard_map/ppermute | solution.py:41
  64.8 4.6 %collective-permute-start.15 = (f32[24,128]{1,0:T(8,128)S(1)}, f32[24,128]{1,0:T(8,128)S(1)}, u32[]{:S(2)}, u32[]{:S(2)}) collective-permute-start(f32[24,128]{1,0:T(8,128)S(1)} %get-tuple-element.63), channel_id=1, source_target_pairs={{0,6},{2,4},{4,2},{6,0},{8,14},{10,12},{12,10},{14,8},{16,22},{18,... | collective-permute-start | bytes 36872 | tf_op jit(solution)/shard_map/ppermute | solution.py:41
  65.7 11.1 %collective-permute-start.24 = (f32[392,128]{1,0:T(8,128)S(1)}, f32[392,128]{1,0:T(8,128)S(1)}, u32[]{:S(2)}, u32[]{:S(2)}) collective-permute-start(f32[392,128]{1,0:T(8,128)S(1)} %get-tuple-element.77), channel_id=1, source_target_pairs={{0,16},{2,18},{4,20},{6,22},{8,24},{10,26},{12,28},{14,30},{16,0},... | collective-permute-start | bytes 602120 | tf_op jit(solution)/shard_map/ppermute | solution.py:41
  69.4 6.1 %collective-permute-start.16 = (f32[24,128]{1,0:T(8,128)S(1)}, f32[24,128]{1,0:T(8,128)S(1)}, u32[]{:S(2)}, u32[]{:S(2)}) collective-permute-start(f32[24,128]{1,0:T(8,128)S(1)} %add_add_fusion.1.refs_0_), channel_id=1, source_target_pairs={{0,8},{2,10},{4,12},{6,14},{8,0},{10,2},{12,4},{14,6},{16,24},{18,... | collective-permute-start | bytes 36872 | tf_op jit(solution)/shard_map/ppermute | solution.py:41
  69.4 7.4 %collective-permute-start.17 = (f32[24,128]{1,0:T(8,128)S(1)}, f32[24,128]{1,0:T(8,128)S(1)}, u32[]{:S(2)}, u32[]{:S(2)}) collective-permute-start(f32[24,128]{1,0:T(8,128)S(1)} %add_add_fusion.1.refs_0_), channel_id=1, source_target_pairs={{0,16},{2,18},{4,20},{6,22},{8,24},{10,26},{12,28},{14,30},{16,0},... | collective-permute-start | bytes 36872 | tf_op jit(solution)/shard_map/ppermute | solution.py:41
  71.0 5.8 %collective-permute-start.18 = (f32[24,128]{1,0:T(8,128)S(1)}, f32[24,128]{1,0:T(8,128)S(1)}, u32[]{:S(2)}, u32[]{:S(2)}) collective-permute-start(f32[24,128]{1,0:T(8,128)S(1)} %add_add_fusion.1.refs_0_), channel_id=1, source_target_pairs={{0,24},{2,26},{4,28},{6,30},{8,16},{10,18},{12,20},{14,22},{16,8},... | collective-permute-start | bytes 36872 | tf_op jit(solution)/shard_map/ppermute | solution.py:41

commit v7 on v6

--- a/solution.py
+++ b/solution.py
@@ -48,6 +48,10 @@
 def fresh_lanes(chunk, width, total, rows):
     lane = lax.broadcasted_iota(jnp.int32, (rows, width), 1)
     return lane + jnp.minimum(chunk * width, total - width) >= chunk * width
+
+
+def kernel(*args, grant=16 << 20, **kwargs):
+    return pl.pallas_call(*args, compiler_params=pltpu.CompilerParams(vmem_limit_bytes=grant), **kwargs)
 
 
 def in_vmem(array):
@@ -72,22 +76,20 @@
     ]
 
 
-def scores_begin(plan, digits, me, geno, held, sems):
+def scores_begin(plan, digits, me, geno, helds, sems):
     begun, per = [], len(plan.rest)
-    columns = held.shape[0] // len(digits)
-    for at, digit in enumerate(digits):
+    for at, (digit, held) in enumerate(zip(digits, helds)):
         chunks = [me ^ (digit * plan.stride) ^ r for r in plan.rest]
-        window = held.at[pl.ds(at * columns, columns), :]
-        begun.append((chunks, fetch(geno_copies(plan, chunks, geno, window, sems, at * per))))
+        begun.append((chunks, held, fetch(geno_copies(plan, chunks, geno, held, sems, at * per))))
     return begun
 
 
-def scores_finish(plan, begun, start_bf, stats, held, outs):
+def scores_finish(plan, begun, start_bf, stats, outs):
     width, total = plan.width, plan.total
-    for at, ((chunks, copies), out) in enumerate(zip(begun, outs)):
+    for (chunks, held, copies), out in zip(begun, outs):
         for j, copy in enumerate(copies):
             copy.wait()
-            low = (at * len(chunks) + j) * width
+            low = j * width
             part = lax.dot_general(start_bf, held[low : low + width, :], NT, preferred_element_type=F32)
             part = jnp.where(fresh_lanes(chunks[j], width, total, part.shape[0]), part, 0.0)
             out[:, j * width : (j + 1) * width] = part
@@ -96,8 +98,8 @@
             out[:, j * width : j * width + LANES] = head
 
 
-def lead_kernel(plan, digit, ratio, weights, panel, geno, out, diag, right, start, start_bf, weighted, stats, *scratch):
-    held, weights_held, ratio_held, sems, small = scratch
+def lead_kernel(plan, digit, ratio, weights, panel, geno, out, held, diag, right, start, start_bf, weighted, stats, *scratch):
+    weights_held, ratio_held, sems, small = scratch
     first = fetch(
         [
             pltpu.make_async_copy(panel, right, small.at[0]),
@@ -105,7 +107,7 @@
             pltpu.make_async_copy(ratio, ratio_held, small.at[2]),
         ]
     )
-    begun = scores_begin(plan, (digit,), lax.axis_index("samp"), geno, held, sems)
+    begun = scores_begin(plan, (digit,), lax.axis_index("samp"), geno, (held,), sems)
     for copy in first:
         copy.wait()
     mu = weights_held[...].reshape(1, weights_held.shape[0])
@@ -123,33 +125,32 @@
     own = jnp.sum(way * (way / mu), axis=1, keepdims=True)
     lane = lax.broadcasted_iota(jnp.int32, stats.shape, 1)
     stats[...] = jnp.where(lane == 0, norm, jnp.where(lane == 1, own, 0.0))
-    scores_finish(plan, begun, start_bf[...], stats[...], held, (out,))
+    scores_finish(plan, begun, start_bf[...], stats[...], (out,))
 
 
 def scores_kernel(plan, digits, start_bf, stats, geno, *refs):
-    *outs, held, sems = refs
-    begun = scores_begin(plan, digits, lax.axis_index("samp"), geno, held, sems)
-    scores_finish(plan, begun, start_bf[...], stats[...], held, outs)
-
-
-def terms_kernel(plan, digit, diag, scores, *refs):
-    *before, geno, out, held, sems = refs
+    *outs, sems = refs
+    outs, helds = outs[: len(digits)], outs[len(digits) :]
+    begun = scores_begin(plan, digits, lax.axis_index("samp"), geno, helds, sems)
+    scores_finish(plan, begun, start_bf[...], stats[...], outs)
+
+
+def terms_kernel(plan, digit, diag, scores, held, *refs):
+    *before, out = refs
     width, total = plan.width, plan.total
     me = lax.axis_index("samp")
-    samples = geno.shape[1]
+    samples = held.shape[1]
     chunks = [me ^ (digit * plan.stride) ^ r for r in plan.rest]
-    copies = fetch(geno_copies(plan, chunks, geno, held, sems))
     scale = diag[2:3, 0:1] / plan.markers
     terms = before[0][:, :samples] if before else jnp.zeros((out.shape[0], samples), F32)
     stats = before[0][:, samples:] if before else jnp.zeros((out.shape[0], LANES), F32)
     lane = lax.broadcasted_iota(jnp.int32, stats.shape, 1)
-    for j, copy in enumerate(copies):
+    for j in range(len(chunks)):
         raw = scores[:, j * width : (j + 1) * width]
         fresh = fresh_lanes(chunks[j], width, total, raw.shape[0])
         scaled = jnp.where(fresh, scale * raw, 0.0)
         square = jnp.sum(scaled * raw, axis=1, keepdims=True)
         stats = stats + jnp.where(lane == 2, square, jnp.where((lane < 2) & (chunks[j] == plan.count - 1), raw[:, :LANES], 0.0))
-        copy.wait()
         terms = terms + jnp.dot(
             scaled.astype(BF16), held[j * width : (j + 1) * width, :], preferred_element_type=F32
         )
@@ -183,13 +184,13 @@
 
 
 def cross_kernel(plan, block, digit, sizes, start_bf, stats, diag, weighted, geno, all_variants, *refs):
-    *outs, held, variants, scaled, sems, small = refs
+    out, held, *outs, variants, scaled, sems, small = refs
     me = lax.axis_index("samp")
     (copy,) = fetch([pltpu.make_async_copy(all_variants, variants, small.at[0])])
-    begun = scores_begin(plan, (digit,), me, geno, held, sems)
+    begun = scores_begin(plan, (digit,), me, geno, (held,), sems)
     copy.wait()
-    cross_products(plan, block, me, sizes, diag[1:2, :], variants, weighted, scaled, outs[1:])
-    scores_finish(plan, begun, start_bf[...], stats[...], held, outs[:1])
+    cross_products(plan, block, me, sizes, diag[1:2, :], variants, weighted, scaled, outs)
+    scores_finish(plan, begun, start_bf[...], stats[...], (out,))
 
 
 def cross_products(plan, block, me, sizes, mu, variants, weighted, scaled, outs):
@@ -375,13 +376,15 @@
     hbm = pl.BlockSpec(memory_space=pltpu.MemorySpace.HBM)
     columns = len(rest) * width
     payload = VMEM((rows, columns), F32)
+    window = VMEM((columns, samples), BF16)
 
     lead = radix - 1
-    sent = {}
-    sent[lead], diag, right, start, start_bf, weighted, stats = pl.pallas_call(
+    sent, genos = {}, {}
+    sent[lead], genos[lead], diag, right, start, start_bf, weighted, stats = kernel(
         functools.partial(lead_kernel, plan, lead),
         out_shape=[
             payload,
+            window,
             VMEM((8, samples), F32),
             VMEM((rows, samples), F32),
             VMEM((rows, samples), F32),
@@ -390,9 +393,8 @@
             VMEM((rows, LANES), F32),
         ],
         in_specs=[hbm] * 4,
-        out_specs=[vmem] * 7,
+        out_specs=[vmem] * 8,
         scratch_shapes=[
-            VMEM((columns, samples), BF16),
             VMEM((samples,), F32),
             pltpu.SMEM((1,), F32),
             pltpu.SemaphoreType.DMA((len(rest),)),
@@ -404,18 +406,18 @@
     after = sent[lead]
     start_bf, after = lax.optimization_barrier((start_bf, after))
     digits = tuple(range(1, lead))
-    found = pl.pallas_call(
+    found = kernel(
         functools.partial(scores_kernel, plan, digits),
-        out_shape=[payload] * len(digits),
+        out_shape=[payload] * len(digits) + [window] * len(digits),
         in_specs=[vmem] * 2 + [hbm],
-        out_specs=[vmem] * len(digits),
+        out_specs=[vmem] * (2 * len(digits)),
         scratch_shapes=[
-            VMEM((len(digits) * columns, samples), BF16),
             pltpu.SemaphoreType.DMA((len(digits) * len(rest),)),
         ],
         name="scores",
     )(in_vmem(start_bf), in_vmem(stats), genotypes)
     sent.update(zip(digits, found))
+    genos.update(zip(digits, found[len(digits) :]))
     start_bf, after = lax.optimization_barrier((start_bf, found[0]))
 
     assert radix == 4 and all(r == 4 for r, _ in later)
@@ -426,13 +428,12 @@
     own_shape = VMEM((half, quarter), F32)
     pass_shape = VMEM((half + 2 * rows, quarter), F32)
     send_shape = VMEM((half + rows, 2 * quarter), F32)
-    sent[0], *parts, send_x, send_y = pl.pallas_call(
+    sent[0], genos[0], *parts, send_x, send_y = kernel(
         functools.partial(cross_kernel, plan, block, 0),
-        out_shape=[payload] + [own_shape] * 2 + [pass_shape] * 2 + [send_shape] * 2,
+        out_shape=[payload, window] + [own_shape] * 2 + [pass_shape] * 2 + [send_shape] * 2,
         in_specs=[smem] + [vmem] * 4 + [hbm] * 2,
-        out_specs=[vmem] * 7,
+        out_specs=[vmem] * 8,
         scratch_shapes=[
-            VMEM((columns, samples), BF16),
             VMEM((num_variants, samples), BF16),
             VMEM((quarter, samples), BF16),
             pltpu.SemaphoreType.DMA((len(rest),)),
@@ -445,7 +446,7 @@
     wide = columns
     for level, (r, s) in enumerate(later):
         wide //= r
-        pieces = pl.pallas_call(
+        pieces = kernel(
             merge_kernel,
             out_shape=[VMEM((rows, wide), F32)] * r,
             in_specs=[vmem] * len(terms),
@@ -465,7 +466,7 @@
 
     got_x = swap(send_x, count, firsts[1])
     got_y = swap(send_y, count, firsts[2])
-    own_x, own_y, pass_x, pass_y = pl.pallas_call(
+    own_x, own_y, pass_x, pass_y = kernel(
         halves_kernel,
         out_shape=[own_shape] * 2 + [pass_shape] * 2,
         in_specs=[vmem] * 6,
@@ -477,7 +478,7 @@
     (r, s), deeper = later[0], later[1:]
     wide = quarter // 2
     tall = half + 4 * rows
-    kept, moved = pl.pallas_call(
+    kept, moved = kernel(
         split_kernel,
         out_shape=[VMEM((tall, quarter), F32)] * 2,
         in_specs=[vmem] * 6,
@@ -485,7 +486,7 @@
         name="split",
     )(*map(in_vmem, (own_x, own_y, pass_x, pass_y, got_x, got_y)))
     got_x = swap(moved, count, s)
-    kept, moved = pl.pallas_call(
+    kept, moved = kernel(
         functools.partial(pair_kernel, half),
         out_shape=[VMEM((tall + 4 * rows, wide), F32)] * 2,
         in_specs=[vmem] * 2,
@@ -503,14 +504,13 @@
 
     own = ()
     for d in range(radix):
-        whole = pl.pallas_call(
+        whole = kernel(
             functools.partial(terms_kernel, plan, d),
             out_shape=VMEM((rows, samples + LANES), F32),
-            in_specs=[vmem] * (2 + len(own)) + [hbm],
+            in_specs=[vmem] * (3 + len(own)),
             out_specs=vmem,
-            scratch_shapes=[VMEM((columns, samples), BF16), pltpu.SemaphoreType.DMA((len(rest),))],
             name="terms",
-        )(diag, arrays[d], *map(in_vmem, own), genotypes)
+        )(diag, arrays[d], in_vmem(genos[d]), *map(in_vmem, own))
         own = (whole,)
     (held,) = own
     assert marks & (marks - 1) == 0
@@ -526,7 +526,7 @@
     held = in_vmem(held)
     flat = VMEM((rows, LANES), F32)
     full = jax.ShapeDtypeStruct((rows, samples), F32)
-    solution, residual, norm, alpha = pl.pallas_call(
+    solution, residual, norm, alpha = kernel(
         update_kernel,
         out_shape=[VMEM((rows, samples), F32)] * 2 + [flat] * 2,
         in_specs=[vmem] * 5,
@@ -540,7 +540,7 @@
             total = total + one
         norms = [total] + [swap(total, count, d * s) for d in range(1, r)]
     gram_shape = (1, block, num_variants)
-    solution, residual, direction, gram = pl.pallas_call(
+    solution, residual, direction, gram = kernel(
         functools.partial(last_kernel, samples * count, len(norms)),
         out_shape=[full] * 3 + [jax.ShapeDtypeStruct(gram_shape, F32)],
         in_specs=[smem] + [vmem] * (6 + len(norms) + len(sums)),

time: 79.2 us -> 77.6 us (0.980)
  Pallas kernels: 25.7 us -> 16 us
  local copies, waits for them, and re-layouts: 0.61 us -> 6.07 us
  starting transfers between devices: 30.3 us -> 35 us
  waiting for transfers between devices: 20.9 us -> 18.8 us
    pallas_call x13, Pallas kernels: 25.7 us -> 16 us  [the longest x1 5.05 us: body(): kernel(functools.partial(cross_kernel, plan, block, 0), out_shape=[payloa...]
    unnamed x2 -> x12, local copies, waits for them, and re-layouts: 0.61 us -> 6.07 us
    ppermute x25, starting transfers between devices: 30.3 us -> 35 us  [swap(): return lax.ppermute(array, axis, [(i, i ^ offset) for i in range(count)])]
    ppermute x25, waiting for transfers between devices: 20.9 us -> 18.8 us  [swap(): return lax.ppermute(array, axis, [(i, i ^ offset) for i in range(count)])]
  transfers between devices with their start and end apart: 25 -> 25, of which waited for: 12 -> 12; matrix products, arithmetic and copies ran while one was open for 0% -> 0% of each run, Pallas kernels for 21% -> 15%
where the time goes in v7:
time: 77.6 us; the launch traced here: 77.3 us
  starting transfers between devices  35 us (45%)
  waiting for transfers between devices  18.8 us (24%)
  Pallas kernels  16 us (21%)
  local copies, waits for them, and re-layouts  6.07 us (8%)
  between operations  1.4 us (2%)
    ppermute x25, starting transfers between devices, swap(): return lax.ppermute(array, axis, [(i, i ^ offset) for i in range(count)])  35 us
    ppermute x25, waiting for transfers between devices, swap(): return lax.ppermute(array, axis, [(i, i ^ offset) for i in range(count)])  18.8 us
    unnamed x12, local copies, waits for them, and re-layouts  6.07 us
    pallas_call x1, Pallas kernels, body(): kernel(functools.partial(cross_kernel, plan, block, 0), out_shape=[payloa...  5.05 us
    pallas_call x1, Pallas kernels, body(): kernel(functools.partial(scores_kernel, plan, digits), out_shape=[payload...  3.24 us
    pallas_call x4, Pallas kernels, body(): kernel(functools.partial(terms_kernel, plan, d), out_shape=VMEM((rows, sa...  2.71 us
    pallas_call x1, Pallas kernels, body(): kernel(functools.partial(lead_kernel, plan, lead), out_shape=[payload, wi...  2.17 us
    pallas_call x1, Pallas kernels, body(): kernel(functools.partial(last_kernel, samples * count, len(norms)), out_s...  2.06 us
  transfers between devices with their start and end apart: 25, of which 12 were waited for; matrix products, arithmetic and copies ran while one was open for 0% of the time, Pallas kernels for 15%

profile of v7, /device:TPU:0, one launch (start us, length us, event | category | flops | bytes accessed | tf_op | source)
XLA Modules:
  0.0 77.3 jit_solution(3978423358442639487)
XLA Ops:
  1.3 4.5 %copy-done = bf16[8000,768]{1,0:T(8,128)(2,1)S(1)} copy-done((bf16[8000,768]{1,0:T(8,128)(2,1)S(1)}, bf16[8000,768]{1,0:T(8,128)(2,1)}, u32[]{:S(2)}) %copy-start) | copy-done | bytes 12288024
  5.8 0.9 %copy-done.3 = f32[24,768]{1,0:T(8,128)S(1)} copy-done((f32[24,768]{1,0:T(8,128)S(1)}, f32[24,768]{1,0:T(8,128)}, u32[]{:S(2)}) %copy-start.3) | copy-done | bytes 73752
  7.3 2.2 %scores_lead.1 = (f32[24,2048]{1,0:T(8,128)S(1)}, bf16[2048,768]{1,0:T(8,128)(2,1)S(1)}, f32[8,768]{1,0:T(8,128)S(1)}, f32[24,768]{1,0:T(8,128)S(1)}, f32[24,768...) custom-call(f32[1]{0:T(128)S(6)} %copy.18.ratio, ...), custom_call_target="tpu_custom_call" | custom-call | tf_op jit(solution)/shard_map/scores_lead/pallas_call | solution.py:383
  9.5 4.0 %collective-permute-start.2 = (f32[24,2048]{1,0:T(8,128)S(1)}, f32[24,2048]{1,0:T(8,128)S(1)}, u32[]{:S(2)}, u32[]{:S(2)}) collective-permute-start(f32[24,2048]{1,0:T(8,128)S(1)} %get-tuple-element.48), channel_id=1, source_target_pairs={{0,6},{2,4},{4,2},{6,0},{8,14},{10,12},{12,10},{14,8},{16,22},{18,... | collective-permute-start | bytes 589832 | tf_op jit(solution)/shard_map/ppermute | solution.py:41
  13.5 3.2 %scores.1 = (f32[24,2048]{1,0:T(8,128)S(1)}, f32[24,2048]{1,0:T(8,128)S(1)}, bf16[2048,768]{1,0:T(8,128)(2,1)S(1)}, bf16[2048,768]{1,0:T(8,128)(2,1)S(1)}) custom-call(bf16[24,768]{1,0:T(8,128)(2,1)S(1)} %get-tuple-element.52.start_bf, f32[24,128]{1,0:T(8,128)S(1)} %get-tuple-element.50.stats, bf16[8000,768]{1,0:T(8,128)(2,1)S(1)} %copy-done.1), custom_call_target="tpu_custom_call" | custom-call | tf_op jit(solution)/shard_map/scores/pallas_call | solution.py:409
  16.8 1.4 %collective-permute-start.1 = (f32[24,2048]{1,0:T(8,128)S(1)}, f32[24,2048]{1,0:T(8,128)S(1)}, u32[]{:S(2)}, u32[]{:S(2)}) collective-permute-start(f32[24,2048]{1,0:T(8,128)S(1)} %get-tuple-element.55), channel_id=1, source_target_pairs={{0,4},{2,6},{4,0},{6,2},{8,12},{10,14},{12,8},{14,10},{16,20},{18,... | collective-permute-start | bytes 589832 | tf_op jit(solution)/shard_map/ppermute | solution.py:41
  18.1 1.5 %collective-permute-start = (f32[24,2048]{1,0:T(8,128)S(1)}, f32[24,2048]{1,0:T(8,128)S(1)}, u32[]{:S(2)}, u32[]{:S(2)}) collective-permute-start(f32[24,2048]{1,0:T(8,128)S(1)} %get-tuple-element.51), channel_id=1, source_target_pairs={{0,2},{2,0},{4,6},{6,4},{8,10},{10,8},{12,14},{14,12},{16,18},{18,... | collective-permute-start | bytes 589832 | tf_op jit(solution)/shard_map/ppermute | solution.py:41
  19.6 5.0 %scores_cross.1 = (f32[24,2048]{1,0:T(8,128)S(1)}, bf16[2048,768]{1,0:T(8,128)(2,1)S(1)}, f32[200,256]{1,0:T(8,128)S(1)}, f32[200,256]{1,0:T(8,128)S(1)}, f32[24...) custom-call(s32[1,24]{1,0:T(1,128)S(1)} %copy-done.5, ...), custom_call_target="tpu_custom_call" | custom-call | tf_op jit(solution)/shard_map/scores_cross/pallas_call | solution.py:431
  24.8 1.3 %collective-permute-start.19 = (f32[224,512]{1,0:T(8,128)S(1)}, f32[224,512]{1,0:T(8,128)S(1)}, u32[]{:S(2)}, u32[]{:S(2)}) collective-permute-start(f32[224,512]{1,0:T(8,128)S(1)} %get-tuple-element.72), channel_id=1, source_target_pairs={{0,2},{2,0},{4,6},{6,4},{8,10},{10,8},{12,14},{14,12},{16,18},{18,... | collective-permute-start | bytes 1376264 | tf_op jit(solution)/shard_map/ppermute | solution.py:41
  26.6 1.6 %collective-permute-start.3 = (f32[24,512]{1,0:T(8,128)S(1)}, f32[24,512]{1,0:T(8,128)S(1)}, u32[]{:S(2)}, u32[]{:S(2)}) collective-permute-start(f32[24,512]{1,0:T(8,128)S(1)} %get-tuple-element.60), channel_id=1, source_target_pairs={{0,8},{2,10},{4,12},{6,14},{8,0},{10,2},{12,4},{14,6},{16,24},{18,... | collective-permute-start | bytes 147464 | tf_op jit(solution)/shard_map/ppermute | solution.py:41
  28.2 2.6 %collective-permute-start.4 = (f32[24,512]{1,0:T(8,128)S(1)}, f32[24,512]{1,0:T(8,128)S(1)}, u32[]{:S(2)}, u32[]{:S(2)}) collective-permute-start(f32[24,512]{1,0:T(8,128)S(1)} %get-tuple-element.61), channel_id=1, source_target_pairs={{0,16},{2,18},{4,20},{6,22},{8,24},{10,26},{12,28},{14,30},{16,0},... | collective-permute-start | bytes 147464 | tf_op jit(solution)/shard_map/ppermute | solution.py:41
  31.0 5.5 %collective-permute-done.19.got_x = f32[224,512]{1,0:T(8,128)S(1)} collective-permute-done((f32[224,512]{1,0:T(8,128)S(1)}, f32[224,512]{1,0:T(8,128)S(1)}, u32[]{:S(2)}, u32[]{:S(2)}) %collective-permute-start.19) | collective-permute-done | bytes 458784 | tf_op jit(solution)/shard_map/ppermute | solution.py:41
  37.8 1.3 %collective-permute-start.22 = (f32[248,256]{1,0:T(8,128)S(1)}, f32[248,256]{1,0:T(8,128)S(1)}, u32[]{:S(2)}, u32[]{:S(2)}) collective-permute-start(f32[248,256]{1,0:T(8,128)S(1)} %get-tuple-element.81.pass_y), channel_id=1, source_target_pairs={{0,2},{2,0},{4,6},{6,4},{8,10},{10,8},{12,14},{14,12},{16,18},{18,... | collective-permute-start | bytes 761864 | tf_op jit(solution)/shard_map/ppermute | solution.py:41
  39.1 3.7 %collective-permute-start.8 = (f32[24,512]{1,0:T(8,128)S(1)}, f32[24,512]{1,0:T(8,128)S(1)}, u32[]{:S(2)}, u32[]{:S(2)}) collective-permute-start(f32[24,512]{1,0:T(8,128)S(1)} %add_add_fusion), channel_id=1, source_target_pairs={{0,24},{2,26},{4,28},{6,30},{8,16},{10,18},{12,20},{14,22},{16,8},... | collective-permute-start | bytes 147464 | tf_op jit(solution)/shard_map/ppermute | solution.py:41
  42.8 0.8 %collective-permute-start.6 = (f32[24,512]{1,0:T(8,128)S(1)}, f32[24,512]{1,0:T(8,128)S(1)}, u32[]{:S(2)}, u32[]{:S(2)}) collective-permute-start(f32[24,512]{1,0:T(8,128)S(1)} %add_add_fusion), channel_id=1, source_target_pairs={{0,8},{2,10},{4,12},{6,14},{8,0},{10,2},{12,4},{14,6},{16,24},{18,... | collective-permute-start | bytes 147464 | tf_op jit(solution)/shard_map/ppermute | solution.py:41
  44.2 1.6 %collective-permute-start.23 = (f32[296,256]{1,0:T(8,128)S(1)}, f32[296,256]{1,0:T(8,128)S(1)}, u32[]{:S(2)}, u32[]{:S(2)}) collective-permute-start(f32[296,256]{1,0:T(8,128)S(1)} %get-tuple-element.83), channel_id=1, source_target_pairs={{0,8},{2,10},{4,12},{6,14},{8,0},{10,2},{12,4},{14,6},{16,24},{18,... | collective-permute-start | bytes 909320 | tf_op jit(solution)/shard_map/ppermute | solution.py:41
  45.9 2.0 %collective-permute-done.7 = f32[24,512]{1,0:T(8,128)S(1)} collective-permute-done((f32[24,512]{1,0:T(8,128)S(1)}, f32[24,512]{1,0:T(8,128)S(1)}, u32[]{:S(2)}, u32[]{:S(2)}) %collective-permute-start.7) | collective-permute-done | bytes 49184 | tf_op jit(solution)/shard_map/ppermute | solution.py:41
  47.9 0.8 %collective-permute-start.11 = (f32[24,2048]{1,0:T(8,128)S(1)}, f32[24,2048]{1,0:T(8,128)S(1)}, u32[]{:S(2)}, u32[]{:S(2)}) collective-permute-start(f32[24,2048]{1,0:T(8,128)S(1)} %pad_maximum_fusion.scores), channel_id=1, source_target_pairs={{0,2},{2,0},{4,6},{6,4},{8,10},{10,8},{12,14},{14,12},{16,18},{18,... | collective-permute-start | bytes 589832 | tf_op jit(solution)/shard_map/ppermute | solution.py:41
  48.7 1.5 %collective-permute-start.10 = (f32[24,2048]{1,0:T(8,128)S(1)}, f32[24,2048]{1,0:T(8,128)S(1)}, u32[]{:S(2)}, u32[]{:S(2)}) collective-permute-start(f32[24,2048]{1,0:T(8,128)S(1)} %pad_maximum_fusion.scores), channel_id=1, source_target_pairs={{0,4},{2,6},{4,0},{6,2},{8,12},{10,14},{12,8},{14,10},{16,20},{18,... | collective-permute-start | bytes 589832 | tf_op jit(solution)/shard_map/ppermute | solution.py:41
  50.2 1.3 %collective-permute-start.9 = (f32[24,2048]{1,0:T(8,128)S(1)}, f32[24,2048]{1,0:T(8,128)S(1)}, u32[]{:S(2)}, u32[]{:S(2)}) collective-permute-start(f32[24,2048]{1,0:T(8,128)S(1)} %pad_maximum_fusion.scores), channel_id=1, source_target_pairs={{0,6},{2,4},{4,2},{6,0},{8,14},{10,12},{12,10},{14,8},{16,22},{18,... | collective-permute-start | bytes 589832 | tf_op jit(solution)/shard_map/ppermute | solution.py:41
  52.1 1.5 %collective-permute-done.11.scores = f32[24,2048]{1,0:T(8,128)S(1)} collective-permute-done((f32[24,2048]{1,0:T(8,128)S(1)}, f32[24,2048]{1,0:T(8,128)S(1)}, u32[]{:S(2)}, u32[]{:S(2)}) %collective-permute-start.11) | collective-permute-done | bytes 196640 | tf_op jit(solution)/shard_map/ppermute | solution.py:41
  54.3 1.2 %collective-permute-done.10.scores = f32[24,2048]{1,0:T(8,128)S(1)} collective-permute-done((f32[24,2048]{1,0:T(8,128)S(1)}, f32[24,2048]{1,0:T(8,128)S(1)}, u32[]{:S(2)}, u32[]{:S(2)}) %collective-permute-start.10) | collective-permute-done | bytes 196640 | tf_op jit(solution)/shard_map/ppermute | solution.py:41
  57.5 1.3 %collective-permute-done.12.other = f32[24,896]{1,0:T(8,128)S(1)} collective-permute-done((f32[24,896]{1,0:T(8,128)S(1)}, f32[24,896]{1,0:T(8,128)S(1)}, u32[]{:S(2)}, u32[]{:S(2)}) %collective-permute-start.12) | collective-permute-done | bytes 86048 | tf_op jit(solution)/shard_map/ppermute | solution.py:41
  59.0 2.7 %collective-permute-start.15 = (f32[24,128]{1,0:T(8,128)S(1)}, f32[24,128]{1,0:T(8,128)S(1)}, u32[]{:S(2)}, u32[]{:S(2)}) collective-permute-start(f32[24,128]{1,0:T(8,128)S(1)} %get-tuple-element.71), channel_id=1, source_target_pairs={{0,6},{2,4},{4,2},{6,0},{8,14},{10,12},{12,10},{14,8},{16,22},{18,... | collective-permute-start | bytes 36872 | tf_op jit(solution)/shard_map/ppermute | solution.py:41
  61.8 0.7 collective-permute-start.13
  62.6 2.5 %collective-permute-start.24 = (f32[392,128]{1,0:T(8,128)S(1)}, f32[392,128]{1,0:T(8,128)S(1)}, u32[]{:S(2)}, u32[]{:S(2)}) collective-permute-start(f32[392,128]{1,0:T(8,128)S(1)} %get-tuple-element.85), channel_id=1, source_target_pairs={{0,16},{2,18},{4,20},{6,22},{8,24},{10,26},{12,28},{14,30},{16,0},... | collective-permute-start | bytes 602120 | tf_op jit(solution)/shard_map/ppermute | solution.py:41
  65.5 2.1 %collective-permute-start.18 = (f32[24,128]{1,0:T(8,128)S(1)}, f32[24,128]{1,0:T(8,128)S(1)}, u32[]{:S(2)}, u32[]{:S(2)}) collective-permute-start(f32[24,128]{1,0:T(8,128)S(1)} %add_add_fusion.1.refs_0_), channel_id=1, source_target_pairs={{0,24},{2,26},{4,28},{6,30},{8,16},{10,18},{12,20},{14,22},{16,8},... | collective-permute-start | bytes 36872 | tf_op jit(solution)/shard_map/ppermute | solution.py:41
  67.6 1.0 %collective-permute-start.17 = (f32[24,128]{1,0:T(8,128)S(1)}, f32[24,128]{1,0:T(8,128)S(1)}, u32[]{:S(2)}, u32[]{:S(2)}) collective-permute-start(f32[24,128]{1,0:T(8,128)S(1)} %add_add_fusion.1.refs_0_), channel_id=1, source_target_pairs={{0,16},{2,18},{4,20},{6,22},{8,24},{10,26},{12,28},{14,30},{16,0},... | collective-permute-start | bytes 36872 | tf_op jit(solution)/shard_map/ppermute | solution.py:41
  68.6 1.3 %collective-permute-start.16 = (f32[24,128]{1,0:T(8,128)S(1)}, f32[24,128]{1,0:T(8,128)S(1)}, u32[]{:S(2)}, u32[]{:S(2)}) collective-permute-start(f32[24,128]{1,0:T(8,128)S(1)} %add_add_fusion.1.refs_0_), channel_id=1, source_target_pairs={{0,8},{2,10},{4,12},{6,14},{8,0},{10,2},{12,4},{14,6},{16,24},{18,... | collective-permute-start | bytes 36872 | tf_op jit(solution)/shard_map/ppermute | solution.py:41
  69.9 1.6 %collective-permute-done.18.refs_3_ = f32[24,128]{1,0:T(8,128)S(1)} collective-permute-done((f32[24,128]{1,0:T(8,128)S(1)}, f32[24,128]{1,0:T(8,128)S(1)}, u32[]{:S(2)}, u32[]{:S(2)}) %collective-permute-start.18) | collective-permute-done | bytes 12320 | tf_op jit(solution)/shard_map/ppermute | solution.py:41
  71.5 3.8 %collective-permute-done.17.refs_2_ = f32[24,128]{1,0:T(8,128)S(1)} collective-permute-done((f32[24,128]{1,0:T(8,128)S(1)}, f32[24,128]{1,0:T(8,128)S(1)}, u32[]{:S(2)}, u32[]{:S(2)}) %collective-permute-start.17) | collective-permute-done | bytes 12320 | tf_op jit(solution)/shard_map/ppermute | solution.py:41
  75.3 2.1 %last.1 = (f32[24,768]{1,0:T(8,128)}, f32[24,768]{1,0:T(8,128)}, f32[24,768]{1,0:T(8,128)}, f32[1,64,1024]{2,1,0:T(8,128)}) custom-call(s32[1,24]{1,0:T(1,128)S(1)} %copy-done.5, f32[8,768]{1,0:T(8,128)S(1)} %get-tuple-element.45.diag, f32[24,768]{1,0:T(8,128)S(1)} %get-tuple-element.46.start, f32[24,896]{1,0:T(8,128)S(1)} %terms.7.own.held, ...), custom_call_target="tpu_custom_call" | custom-call | tf_op jit(solution)/shard_map/last/pallas_call | solution.py:543
  (46 shorter events, 7.7 us)
Async XLA Ops:
  1.3 4.5 %copy-start = (bf16[8000,768]{1,0:T(8,128)(2,1)S(1)}, bf16[8000,768]{1,0:T(8,128)(2,1)}, u32[]{:S(2)}) copy-start(bf16[8000,768]{1,0:T(8,128)(2,1)} %geno.5) | copy-start | bytes 36864004
  5.8 0.9 %copy-start.3 = (f32[24,768]{1,0:T(8,128)S(1)}, f32[24,768]{1,0:T(8,128)}, u32[]{:S(2)}) copy-start(f32[24,768]{1,0:T(8,128)} %panel.1) | copy-start | bytes 221188
  6.7 0.7 copy-start.4
  7.3 6.2 %copy-start.1 = (bf16[8000,768]{1,0:T(8,128)(2,1)S(1)}, bf16[8000,768]{1,0:T(8,128)(2,1)}, u32[]{:S(2)}) copy-start(bf16[8000,768]{1,0:T(8,128)(2,1)} %geno.5) | copy-start | bytes 36864004
  9.5 15.2 %collective-permute-start.2 = (f32[24,2048]{1,0:T(8,128)S(1)}, f32[24,2048]{1,0:T(8,128)S(1)}, u32[]{:S(2)}, u32[]{:S(2)}) collective-permute-start(f32[24,2048]{1,0:T(8,128)S(1)} %get-tuple-element.48), channel_id=1, source_target_pairs={{0,6},{2,4},{4,2},{6,0},{8,14},{10,12},{12,10},{14,8},{16,22},{18,... | collective-permute-start | bytes 589832 | tf_op jit(solution)/shard_map/ppermute | solution.py:41
  13.5 6.1 %copy-start.2 = (bf16[1024,768]{1,0:T(8,128)(2,1)S(1)}, bf16[1024,768]{1,0:T(8,128)(2,1)}, u32[]{:S(2)}) copy-start(bf16[1024,768]{1,0:T(8,128)(2,1)} %all_variants.1) | copy-start | bytes 4718596
  13.5 6.1 %copy-start.5 = (s32[1,24]{1,0:T(1,128)S(1)}, s32[1,24]{1,0:T(1,128)}, u32[]{:S(2)}) copy-start(s32[1,24]{1,0:T(1,128)} %sizes.3) | copy-start | bytes 292
  16.8 7.9 %collective-permute-start.1 = (f32[24,2048]{1,0:T(8,128)S(1)}, f32[24,2048]{1,0:T(8,128)S(1)}, u32[]{:S(2)}, u32[]{:S(2)}) collective-permute-start(f32[24,2048]{1,0:T(8,128)S(1)} %get-tuple-element.55), channel_id=1, source_target_pairs={{0,4},{2,6},{4,0},{6,2},{8,12},{10,14},{12,8},{14,10},{16,20},{18,... | collective-permute-start | bytes 589832 | tf_op jit(solution)/shard_map/ppermute | solution.py:41
  18.1 6.6 %collective-permute-start = (f32[24,2048]{1,0:T(8,128)S(1)}, f32[24,2048]{1,0:T(8,128)S(1)}, u32[]{:S(2)}, u32[]{:S(2)}) collective-permute-start(f32[24,2048]{1,0:T(8,128)S(1)} %get-tuple-element.51), channel_id=1, source_target_pairs={{0,2},{2,0},{4,6},{6,4},{8,10},{10,8},{12,14},{14,12},{16,18},{18,... | collective-permute-start | bytes 589832 | tf_op jit(solution)/shard_map/ppermute | solution.py:41
  24.8 11.8 %collective-permute-start.19 = (f32[224,512]{1,0:T(8,128)S(1)}, f32[224,512]{1,0:T(8,128)S(1)}, u32[]{:S(2)}, u32[]{:S(2)}) collective-permute-start(f32[224,512]{1,0:T(8,128)S(1)} %get-tuple-element.72), channel_id=1, source_target_pairs={{0,2},{2,0},{4,6},{6,4},{8,10},{10,8},{12,14},{14,12},{16,18},{18,... | collective-permute-start | bytes 1376264 | tf_op jit(solution)/shard_map/ppermute | solution.py:41
  26.1 10.8 %collective-permute-start.20 = (f32[224,512]{1,0:T(8,128)S(1)}, f32[224,512]{1,0:T(8,128)S(1)}, u32[]{:S(2)}, u32[]{:S(2)}) collective-permute-start(f32[224,512]{1,0:T(8,128)S(1)} %get-tuple-element.73), channel_id=1, source_target_pairs={{0,4},{2,6},{4,0},{6,2},{8,12},{10,14},{12,8},{14,10},{16,20},{18,... | collective-permute-start | bytes 1376264 | tf_op jit(solution)/shard_map/ppermute | solution.py:41
  26.6 12.4 %collective-permute-start.3 = (f32[24,512]{1,0:T(8,128)S(1)}, f32[24,512]{1,0:T(8,128)S(1)}, u32[]{:S(2)}, u32[]{:S(2)}) collective-permute-start(f32[24,512]{1,0:T(8,128)S(1)} %get-tuple-element.60), channel_id=1, source_target_pairs={{0,8},{2,10},{4,12},{6,14},{8,0},{10,2},{12,4},{14,6},{16,24},{18,... | collective-permute-start | bytes 147464 | tf_op jit(solution)/shard_map/ppermute | solution.py:41
  28.2 10.9 %collective-permute-start.4 = (f32[24,512]{1,0:T(8,128)S(1)}, f32[24,512]{1,0:T(8,128)S(1)}, u32[]{:S(2)}, u32[]{:S(2)}) collective-permute-start(f32[24,512]{1,0:T(8,128)S(1)} %get-tuple-element.61), channel_id=1, source_target_pairs={{0,16},{2,18},{4,20},{6,22},{8,24},{10,26},{12,28},{14,30},{16,0},... | collective-permute-start | bytes 147464 | tf_op jit(solution)/shard_map/ppermute | solution.py:41
  30.8 8.3 %collective-permute-start.5 = (f32[24,512]{1,0:T(8,128)S(1)}, f32[24,512]{1,0:T(8,128)S(1)}, u32[]{:S(2)}, u32[]{:S(2)}) collective-permute-start(f32[24,512]{1,0:T(8,128)S(1)} %get-tuple-element.62), channel_id=1, source_target_pairs={{0,24},{2,26},{4,28},{6,30},{8,16},{10,18},{12,20},{14,22},{16,8},... | collective-permute-start | bytes 147464 | tf_op jit(solution)/shard_map/ppermute | solution.py:41
  37.1 6.4 %collective-permute-start.21 = (f32[248,256]{1,0:T(8,128)S(1)}, f32[248,256]{1,0:T(8,128)S(1)}, u32[]{:S(2)}, u32[]{:S(2)}) collective-permute-start(f32[248,256]{1,0:T(8,128)S(1)} %get-tuple-element.80.pass_x), channel_id=1, source_target_pairs={{0,4},{2,6},{4,0},{6,2},{8,12},{10,14},{12,8},{14,10},{16,20},{18,... | collective-permute-start | bytes 761864 | tf_op jit(solution)/shard_map/ppermute | solution.py:41
  37.8 6.3 %collective-permute-start.22 = (f32[248,256]{1,0:T(8,128)S(1)}, f32[248,256]{1,0:T(8,128)S(1)}, u32[]{:S(2)}, u32[]{:S(2)}) collective-permute-start(f32[248,256]{1,0:T(8,128)S(1)} %get-tuple-element.81.pass_y), channel_id=1, source_target_pairs={{0,2},{2,0},{4,6},{6,4},{8,10},{10,8},{12,14},{14,12},{16,18},{18,... | collective-permute-start | bytes 761864 | tf_op jit(solution)/shard_map/ppermute | solution.py:41
  39.1 6.8 %collective-permute-start.8 = (f32[24,512]{1,0:T(8,128)S(1)}, f32[24,512]{1,0:T(8,128)S(1)}, u32[]{:S(2)}, u32[]{:S(2)}) collective-permute-start(f32[24,512]{1,0:T(8,128)S(1)} %add_add_fusion), channel_id=1, source_target_pairs={{0,24},{2,26},{4,28},{6,30},{8,16},{10,18},{12,20},{14,22},{16,8},... | collective-permute-start | bytes 147464 | tf_op jit(solution)/shard_map/ppermute | solution.py:41
  42.8 5.1 %collective-permute-start.7 = (f32[24,512]{1,0:T(8,128)S(1)}, f32[24,512]{1,0:T(8,128)S(1)}, u32[]{:S(2)}, u32[]{:S(2)}) collective-permute-start(f32[24,512]{1,0:T(8,128)S(1)} %add_add_fusion), channel_id=1, source_target_pairs={{0,16},{2,18},{4,20},{6,22},{8,24},{10,26},{12,28},{14,30},{16,0},... | collective-permute-start | bytes 147464 | tf_op jit(solution)/shard_map/ppermute | solution.py:41
  42.8 5.1 %collective-permute-start.6 = (f32[24,512]{1,0:T(8,128)S(1)}, f32[24,512]{1,0:T(8,128)S(1)}, u32[]{:S(2)}, u32[]{:S(2)}) collective-permute-start(f32[24,512]{1,0:T(8,128)S(1)} %add_add_fusion), channel_id=1, source_target_pairs={{0,8},{2,10},{4,12},{6,14},{8,0},{10,2},{12,4},{14,6},{16,24},{18,... | collective-permute-start | bytes 147464 | tf_op jit(solution)/shard_map/ppermute | solution.py:41
  44.2 18.3 %collective-permute-start.23 = (f32[296,256]{1,0:T(8,128)S(1)}, f32[296,256]{1,0:T(8,128)S(1)}, u32[]{:S(2)}, u32[]{:S(2)}) collective-permute-start(f32[296,256]{1,0:T(8,128)S(1)} %get-tuple-element.83), channel_id=1, source_target_pairs={{0,8},{2,10},{4,12},{6,14},{8,0},{10,2},{12,4},{14,6},{16,24},{18,... | collective-permute-start | bytes 909320 | tf_op jit(solution)/shard_map/ppermute | solution.py:41
  47.9 5.7 %collective-permute-start.11 = (f32[24,2048]{1,0:T(8,128)S(1)}, f32[24,2048]{1,0:T(8,128)S(1)}, u32[]{:S(2)}, u32[]{:S(2)}) collective-permute-start(f32[24,2048]{1,0:T(8,128)S(1)} %pad_maximum_fusion.scores), channel_id=1, source_target_pairs={{0,2},{2,0},{4,6},{6,4},{8,10},{10,8},{12,14},{14,12},{16,18},{18,... | collective-permute-start | bytes 589832 | tf_op jit(solution)/shard_map/ppermute | solution.py:41
  48.7 6.8 %collective-permute-start.10 = (f32[24,2048]{1,0:T(8,128)S(1)}, f32[24,2048]{1,0:T(8,128)S(1)}, u32[]{:S(2)}, u32[]{:S(2)}) collective-permute-start(f32[24,2048]{1,0:T(8,128)S(1)} %pad_maximum_fusion.scores), channel_id=1, source_target_pairs={{0,4},{2,6},{4,0},{6,2},{8,12},{10,14},{12,8},{14,10},{16,20},{18,... | collective-permute-start | bytes 589832 | tf_op jit(solution)/shard_map/ppermute | solution.py:41
  50.2 6.6 %collective-permute-start.9 = (f32[24,2048]{1,0:T(8,128)S(1)}, f32[24,2048]{1,0:T(8,128)S(1)}, u32[]{:S(2)}, u32[]{:S(2)}) collective-permute-start(f32[24,2048]{1,0:T(8,128)S(1)} %pad_maximum_fusion.scores), channel_id=1, source_target_pairs={{0,6},{2,4},{4,2},{6,0},{8,14},{10,12},{12,10},{14,8},{16,22},{18,... | collective-permute-start | bytes 589832 | tf_op jit(solution)/shard_map/ppermute | solution.py:41
  57.4 1.3 %collective-permute-start.12 = (f32[24,896]{1,0:T(8,128)S(1)}, f32[24,896]{1,0:T(8,128)S(1)}, u32[]{:S(2)}, u32[]{:S(2)}) collective-permute-start(f32[24,896]{1,0:T(8,128)S(1)} %terms.7.own.held), channel_id=1, source_target_pairs={{0,1},{1,0},{2,3},{3,2},{4,5},{5,4},{6,7},{7,6},{8,9},{9,8},{10,11... | collective-permute-start | bytes 258056 | tf_op jit(solution)/shard_map/ppermute | solution.py:41
  59.0 6.0 %collective-permute-start.15 = (f32[24,128]{1,0:T(8,128)S(1)}, f32[24,128]{1,0:T(8,128)S(1)}, u32[]{:S(2)}, u32[]{:S(2)}) collective-permute-start(f32[24,128]{1,0:T(8,128)S(1)} %get-tuple-element.71), channel_id=1, source_target_pairs={{0,6},{2,4},{4,2},{6,0},{8,14},{10,12},{12,10},{14,8},{16,22},{18,... | collective-permute-start | bytes 36872 | tf_op jit(solution)/shard_map/ppermute | solution.py:41
  61.7 3.7 %collective-permute-start.14 = (f32[24,128]{1,0:T(8,128)S(1)}, f32[24,128]{1,0:T(8,128)S(1)}, u32[]{:S(2)}, u32[]{:S(2)}) collective-permute-start(f32[24,128]{1,0:T(8,128)S(1)} %get-tuple-element.71), channel_id=1, source_target_pairs={{0,4},{2,6},{4,0},{6,2},{8,12},{10,14},{12,8},{14,10},{16,20},{18,... | collective-permute-start | bytes 36872 | tf_op jit(solution)/shard_map/ppermute | solution.py:41
  61.8 3.7 %collective-permute-start.13 = (f32[24,128]{1,0:T(8,128)S(1)}, f32[24,128]{1,0:T(8,128)S(1)}, u32[]{:S(2)}, u32[]{:S(2)}) collective-permute-start(f32[24,128]{1,0:T(8,128)S(1)} %get-tuple-element.71), channel_id=1, source_target_pairs={{0,2},{2,0},{4,6},{6,4},{8,10},{10,8},{12,14},{14,12},{16,18},{18,... | collective-permute-start | bytes 36872 | tf_op jit(solution)/shard_map/ppermute | solution.py:41
  62.6 12.7 %collective-permute-start.24 = (f32[392,128]{1,0:T(8,128)S(1)}, f32[392,128]{1,0:T(8,128)S(1)}, u32[]{:S(2)}, u32[]{:S(2)}) collective-permute-start(f32[392,128]{1,0:T(8,128)S(1)} %get-tuple-element.85), channel_id=1, source_target_pairs={{0,16},{2,18},{4,20},{6,22},{8,24},{10,26},{12,28},{14,30},{16,0},... | collective-permute-start | bytes 602120 | tf_op jit(solution)/shard_map/ppermute | solution.py:41
  65.5 6.0 %collective-permute-start.18 = (f32[24,128]{1,0:T(8,128)S(1)}, f32[24,128]{1,0:T(8,128)S(1)}, u32[]{:S(2)}, u32[]{:S(2)}) collective-permute-start(f32[24,128]{1,0:T(8,128)S(1)} %add_add_fusion.1.refs_0_), channel_id=1, source_target_pairs={{0,24},{2,26},{4,28},{6,30},{8,16},{10,18},{12,20},{14,22},{16,8},... | collective-permute-start | bytes 36872 | tf_op jit(solution)/shard_map/ppermute | solution.py:41
  67.6 7.6 %collective-permute-start.17 = (f32[24,128]{1,0:T(8,128)S(1)}, f32[24,128]{1,0:T(8,128)S(1)}, u32[]{:S(2)}, u32[]{:S(2)}) collective-permute-start(f32[24,128]{1,0:T(8,128)S(1)} %add_add_fusion.1.refs_0_), channel_id=1, source_target_pairs={{0,16},{2,18},{4,20},{6,22},{8,24},{10,26},{12,28},{14,30},{16,0},... | collective-permute-start | bytes 36872 | tf_op jit(solution)/shard_map/ppermute | solution.py:41
  68.6 6.7 %collective-permute-start.16 = (f32[24,128]{1,0:T(8,128)S(1)}, f32[24,128]{1,0:T(8,128)S(1)}, u32[]{:S(2)}, u32[]{:S(2)}) collective-permute-start(f32[24,128]{1,0:T(8,128)S(1)} %add_add_fusion.1.refs_0_), channel_id=1, source_target_pairs={{0,8},{2,10},{4,12},{6,14},{8,0},{10,2},{12,4},{14,6},{16,24},{18,... | collective-permute-start | bytes 36872 | tf_op jit(solution)/shard_map/ppermute | solution.py:41

commit v8 on v7

--- a/solution.py
+++ b/solution.py
@@ -56,6 +56,10 @@
 
 def in_vmem(array):
     return pltpu.with_memory_space_constraint(array, pltpu.VMEM)
+
+
+def in_hbm(array):
+    return pltpu.with_memory_space_constraint(array, pltpu.MemorySpace.HBM)
 
 
 def fetch(copies):
@@ -183,12 +187,10 @@
     return low, high
 
 
-def cross_kernel(plan, block, digit, sizes, start_bf, stats, diag, weighted, geno, all_variants, *refs):
-    out, held, *outs, variants, scaled, sems, small = refs
+def cross_kernel(plan, block, digit, sizes, start_bf, stats, diag, weighted, geno, variants, *refs):
+    out, held, *outs, scaled, sems = refs
     me = lax.axis_index("samp")
-    (copy,) = fetch([pltpu.make_async_copy(all_variants, variants, small.at[0])])
     begun = scores_begin(plan, (digit,), me, geno, (held,), sems)
-    copy.wait()
     cross_products(plan, block, me, sizes, diag[1:2, :], variants, weighted, scaled, outs)
     scores_finish(plan, begun, start_bf[...], stats[...], (out,))
 
@@ -374,6 +376,7 @@
     vmem = pl.BlockSpec(memory_space=VMEM)
     smem = pl.BlockSpec(memory_space=pltpu.SMEM)
     hbm = pl.BlockSpec(memory_space=pltpu.MemorySpace.HBM)
+    genotypes, panel, weights = map(in_hbm, (genotypes, panel, weights))
     columns = len(rest) * width
     payload = VMEM((rows, columns), F32)
     window = VMEM((columns, samples), BF16)
@@ -431,16 +434,14 @@
     sent[0], genos[0], *parts, send_x, send_y = kernel(
         functools.partial(cross_kernel, plan, block, 0),
         out_shape=[payload, window] + [own_shape] * 2 + [pass_shape] * 2 + [send_shape] * 2,
-        in_specs=[smem] + [vmem] * 4 + [hbm] * 2,
+        in_specs=[smem] + [vmem] * 4 + [hbm, vmem],
         out_specs=[vmem] * 8,
         scratch_shapes=[
-            VMEM((num_variants, samples), BF16),
             VMEM((quarter, samples), BF16),
             pltpu.SemaphoreType.DMA((len(rest),)),
-            pltpu.SemaphoreType.DMA((1,)),
         ],
         name="scores_cross",
-    )(gene_sizes, in_vmem(start_bf), in_vmem(stats), diag, in_vmem(weighted), genotypes, variants)
+    )(gene_sizes, in_vmem(start_bf), in_vmem(stats), diag, in_vmem(weighted), genotypes, in_vmem(variants))
 
     terms = [sent[0]] + [swap(sent[d], count, firsts[d]) for d in range(1, radix)]
     wide = columns

time: 77.6 us -> 73.4 us (0.946)
  local copies, waits for them, and re-layouts: 6.07 us -> 0.01 us
  Pallas kernels: 16 us -> 18 us
    unnamed x12 -> x4, local copies, waits for them, and re-layouts: 6.07 us -> 0.01 us
    pallas_call x1, Pallas kernels: 3.24 us -> 4.05 us  [body(): kernel(functools.partial(scores_kernel, plan, digits), out_shape=[payload...]
  transfers between devices with their start and end apart: 25 -> 25, of which waited for: 12 -> 11; matrix products, arithmetic and copies ran while one was open for 0% -> 0% of each run, Pallas kernels for 15% -> 18%
where the time goes in v8:
time: 73.4 us; the launch traced here: 73.2 us
  starting transfers between devices  34.6 us (47%)
  waiting for transfers between devices  19.2 us (26%)
  Pallas kernels  18 us (25%)
  between operations  1.4 us (2%)
    ppermute x25, starting transfers between devices, swap(): return lax.ppermute(array, axis, [(i, i ^ offset) for i in range(count)])  34.6 us
    ppermute x25, waiting for transfers between devices, swap(): return lax.ppermute(array, axis, [(i, i ^ offset) for i in range(count)])  19.2 us
    pallas_call x1, Pallas kernels, body(): kernel(functools.partial(cross_kernel, plan, block, 0), out_shape=[payloa...  5.76 us
    pallas_call x1, Pallas kernels, body(): kernel(functools.partial(scores_kernel, plan, digits), out_shape=[payload...  4.05 us
    pallas_call x4, Pallas kernels, body(): kernel(functools.partial(terms_kernel, plan, d), out_shape=VMEM((rows, sa...  2.73 us
    pallas_call x1, Pallas kernels, body(): kernel(functools.partial(lead_kernel, plan, lead), out_shape=[payload, wi...  2.62 us
    pallas_call x1, Pallas kernels, body(): kernel(functools.partial(last_kernel, samples * count, len(norms)), out_s...  2.06 us
  transfers between devices with their start and end apart: 25, of which 11 were waited for; matrix products, arithmetic and copies ran while one was open for 0% of the time, Pallas kernels for 18%

profile of v8, /device:TPU:0, one launch (start us, length us, event | category | flops | bytes accessed | tf_op | source)
XLA Modules:
  0.0 73.2 jit_solution(17683166165982117496)
XLA Ops:
  1.3 2.6 %scores_lead.1 = (f32[24,2048]{1,0:T(8,128)S(1)}, bf16[2048,768]{1,0:T(8,128)(2,1)S(1)}, f32[8,768]{1,0:T(8,128)S(1)}, f32[24,768]{1,0:T(8,128)S(1)}, f32[24,768...) custom-call(f32[1]{0:T(128)S(6)} %copy.18.ratio, ...), custom_call_target="tpu_custom_call" | custom-call | tf_op jit(solution)/shard_map/scores_lead/pallas_call | solution.py:386
  3.9 4.0 %collective-permute-start.2 = (f32[24,2048]{1,0:T(8,128)S(1)}, f32[24,2048]{1,0:T(8,128)S(1)}, u32[]{:S(2)}, u32[]{:S(2)}) collective-permute-start(f32[24,2048]{1,0:T(8,128)S(1)} %get-tuple-element.48), channel_id=1, source_target_pairs={{0,6},{2,4},{4,2},{6,0},{8,14},{10,12},{12,10},{14,8},{16,22},{18,... | collective-permute-start | bytes 589832 | tf_op jit(solution)/shard_map/ppermute | solution.py:41
  7.9 4.1 %scores.1 = (f32[24,2048]{1,0:T(8,128)S(1)}, f32[24,2048]{1,0:T(8,128)S(1)}, bf16[2048,768]{1,0:T(8,128)(2,1)S(1)}, bf16[2048,768]{1,0:T(8,128)(2,1)S(1)}) custom-call(bf16[24,768]{1,0:T(8,128)(2,1)S(1)} %get-tuple-element.52.start_bf, f32[24,128]{1,0:T(8,128)S(1)} %get-tuple-element.50.stats, bf16[8000,768]{1,0:T(8,128)(2,1)} %geno.5), custom_call_target="tpu_custom_call" | custom-call | tf_op jit(solution)/shard_map/scores/pallas_call | solution.py:412
  12.6 5.8 %scores_cross.1 = (f32[24,2048]{1,0:T(8,128)S(1)}, bf16[2048,768]{1,0:T(8,128)(2,1)S(1)}, f32[200,256]{1,0:T(8,128)S(1)}, f32[200,256]{1,0:T(8,128)S(1)}, f32[24...) custom-call(s32[1,24]{1,0:T(1,128)S(1)} %copy-done.1, ...), custom_call_target="tpu_custom_call" | custom-call | tf_op jit(solution)/shard_map/scores_cross/pallas_call | solution.py:434
  18.7 1.8 %collective-permute-start.19 = (f32[224,512]{1,0:T(8,128)S(1)}, f32[224,512]{1,0:T(8,128)S(1)}, u32[]{:S(2)}, u32[]{:S(2)}) collective-permute-start(f32[224,512]{1,0:T(8,128)S(1)} %get-tuple-element.72), channel_id=1, source_target_pairs={{0,2},{2,0},{4,6},{6,4},{8,10},{10,8},{12,14},{14,12},{16,18},{18,... | collective-permute-start | bytes 1376264 | tf_op jit(solution)/shard_map/ppermute | solution.py:41
  20.5 1.5 %collective-permute-start.20 = (f32[224,512]{1,0:T(8,128)S(1)}, f32[224,512]{1,0:T(8,128)S(1)}, u32[]{:S(2)}, u32[]{:S(2)}) collective-permute-start(f32[224,512]{1,0:T(8,128)S(1)} %get-tuple-element.73), channel_id=1, source_target_pairs={{0,4},{2,6},{4,0},{6,2},{8,12},{10,14},{12,8},{14,10},{16,20},{18,... | collective-permute-start | bytes 1376264 | tf_op jit(solution)/shard_map/ppermute | solution.py:41
  22.0 1.6 %collective-permute-start.3 = (f32[24,512]{1,0:T(8,128)S(1)}, f32[24,512]{1,0:T(8,128)S(1)}, u32[]{:S(2)}, u32[]{:S(2)}) collective-permute-start(f32[24,512]{1,0:T(8,128)S(1)} %get-tuple-element.60), channel_id=1, source_target_pairs={{0,8},{2,10},{4,12},{6,14},{8,0},{10,2},{12,4},{14,6},{16,24},{18,... | collective-permute-start | bytes 147464 | tf_op jit(solution)/shard_map/ppermute | solution.py:41
  23.6 2.6 %collective-permute-start.4 = (f32[24,512]{1,0:T(8,128)S(1)}, f32[24,512]{1,0:T(8,128)S(1)}, u32[]{:S(2)}, u32[]{:S(2)}) collective-permute-start(f32[24,512]{1,0:T(8,128)S(1)} %get-tuple-element.61), channel_id=1, source_target_pairs={{0,16},{2,18},{4,20},{6,22},{8,24},{10,26},{12,28},{14,30},{16,0},... | collective-permute-start | bytes 147464 | tf_op jit(solution)/shard_map/ppermute | solution.py:41
  26.4 3.9 %collective-permute-done.19.got_x = f32[224,512]{1,0:T(8,128)S(1)} collective-permute-done((f32[224,512]{1,0:T(8,128)S(1)}, f32[224,512]{1,0:T(8,128)S(1)}, u32[]{:S(2)}, u32[]{:S(2)}) %collective-permute-start.19) | collective-permute-done | bytes 458784 | tf_op jit(solution)/shard_map/ppermute | solution.py:41
  30.3 1.4 %collective-permute-done.20.got_y = f32[224,512]{1,0:T(8,128)S(1)} collective-permute-done((f32[224,512]{1,0:T(8,128)S(1)}, f32[224,512]{1,0:T(8,128)S(1)}, u32[]{:S(2)}, u32[]{:S(2)}) %collective-permute-start.20) | collective-permute-done | bytes 458784 | tf_op jit(solution)/shard_map/ppermute | solution.py:41
  31.8 1.6 %collective-permute-start.21 = (f32[248,256]{1,0:T(8,128)S(1)}, f32[248,256]{1,0:T(8,128)S(1)}, u32[]{:S(2)}, u32[]{:S(2)}) collective-permute-start(f32[248,256]{1,0:T(8,128)S(1)} %get-tuple-element.80.pass_x), channel_id=1, source_target_pairs={{0,4},{2,6},{4,0},{6,2},{8,12},{10,14},{12,8},{14,10},{16,20},{18,... | collective-permute-start | bytes 761864 | tf_op jit(solution)/shard_map/ppermute | solution.py:41
  33.9 3.7 %collective-permute-start.8 = (f32[24,512]{1,0:T(8,128)S(1)}, f32[24,512]{1,0:T(8,128)S(1)}, u32[]{:S(2)}, u32[]{:S(2)}) collective-permute-start(f32[24,512]{1,0:T(8,128)S(1)} %add_add_fusion), channel_id=1, source_target_pairs={{0,24},{2,26},{4,28},{6,30},{8,16},{10,18},{12,20},{14,22},{16,8},... | collective-permute-start | bytes 147464 | tf_op jit(solution)/shard_map/ppermute | solution.py:41
  37.6 0.8 %collective-permute-start.6 = (f32[24,512]{1,0:T(8,128)S(1)}, f32[24,512]{1,0:T(8,128)S(1)}, u32[]{:S(2)}, u32[]{:S(2)}) collective-permute-start(f32[24,512]{1,0:T(8,128)S(1)} %add_add_fusion), channel_id=1, source_target_pairs={{0,8},{2,10},{4,12},{6,14},{8,0},{10,2},{12,4},{14,6},{16,24},{18,... | collective-permute-start | bytes 147464 | tf_op jit(solution)/shard_map/ppermute | solution.py:41
  38.4 1.3 %collective-permute-done.22.got_y = f32[248,256]{1,0:T(8,128)S(1)} collective-permute-done((f32[248,256]{1,0:T(8,128)S(1)}, f32[248,256]{1,0:T(8,128)S(1)}, u32[]{:S(2)}, u32[]{:S(2)}) %collective-permute-start.22) | collective-permute-done | bytes 253984 | tf_op jit(solution)/shard_map/ppermute | solution.py:41
  39.8 1.6 %collective-permute-start.23 = (f32[296,256]{1,0:T(8,128)S(1)}, f32[296,256]{1,0:T(8,128)S(1)}, u32[]{:S(2)}, u32[]{:S(2)}) collective-permute-start(f32[296,256]{1,0:T(8,128)S(1)} %get-tuple-element.83), channel_id=1, source_target_pairs={{0,8},{2,10},{4,12},{6,14},{8,0},{10,2},{12,4},{14,6},{16,24},{18,... | collective-permute-start | bytes 909320 | tf_op jit(solution)/shard_map/ppermute | solution.py:41
  41.5 1.2 %collective-permute-done.7 = f32[24,512]{1,0:T(8,128)S(1)} collective-permute-done((f32[24,512]{1,0:T(8,128)S(1)}, f32[24,512]{1,0:T(8,128)S(1)}, u32[]{:S(2)}, u32[]{:S(2)}) %collective-permute-start.7) | collective-permute-done | bytes 49184 | tf_op jit(solution)/shard_map/ppermute | solution.py:41
  42.8 1.6 %collective-permute-start.11 = (f32[24,2048]{1,0:T(8,128)S(1)}, f32[24,2048]{1,0:T(8,128)S(1)}, u32[]{:S(2)}, u32[]{:S(2)}) collective-permute-start(f32[24,2048]{1,0:T(8,128)S(1)} %pad_maximum_fusion.scores), channel_id=1, source_target_pairs={{0,2},{2,0},{4,6},{6,4},{8,10},{10,8},{12,14},{14,12},{16,18},{18,... | collective-permute-start | bytes 589832 | tf_op jit(solution)/shard_map/ppermute | solution.py:41
  44.8 1.5 %collective-permute-start.9 = (f32[24,2048]{1,0:T(8,128)S(1)}, f32[24,2048]{1,0:T(8,128)S(1)}, u32[]{:S(2)}, u32[]{:S(2)}) collective-permute-start(f32[24,2048]{1,0:T(8,128)S(1)} %pad_maximum_fusion.scores), channel_id=1, source_target_pairs={{0,6},{2,4},{4,2},{6,0},{8,14},{10,12},{12,10},{14,8},{16,22},{18,... | collective-permute-start | bytes 589832 | tf_op jit(solution)/shard_map/ppermute | solution.py:41
  47.0 1.5 %collective-permute-done.11.scores = f32[24,2048]{1,0:T(8,128)S(1)} collective-permute-done((f32[24,2048]{1,0:T(8,128)S(1)}, f32[24,2048]{1,0:T(8,128)S(1)}, u32[]{:S(2)}, u32[]{:S(2)}) %collective-permute-start.11) | collective-permute-done | bytes 196640 | tf_op jit(solution)/shard_map/ppermute | solution.py:41
  49.2 2.9 %collective-permute-done.10.scores = f32[24,2048]{1,0:T(8,128)S(1)} collective-permute-done((f32[24,2048]{1,0:T(8,128)S(1)}, f32[24,2048]{1,0:T(8,128)S(1)}, u32[]{:S(2)}, u32[]{:S(2)}) %collective-permute-start.10) | collective-permute-done | bytes 196640 | tf_op jit(solution)/shard_map/ppermute | solution.py:41
  52.1 0.7 terms.6.refs_0_
  52.8 0.7 terms.7.own.held
  53.5 1.3 %collective-permute-done.12.other = f32[24,896]{1,0:T(8,128)S(1)} collective-permute-done((f32[24,896]{1,0:T(8,128)S(1)}, f32[24,896]{1,0:T(8,128)S(1)}, u32[]{:S(2)}, u32[]{:S(2)}) %collective-permute-start.12) | collective-permute-done | bytes 86048 | tf_op jit(solution)/shard_map/ppermute | solution.py:41
  55.3 1.8 %collective-permute-start.14 = (f32[24,128]{1,0:T(8,128)S(1)}, f32[24,128]{1,0:T(8,128)S(1)}, u32[]{:S(2)}, u32[]{:S(2)}) collective-permute-start(f32[24,128]{1,0:T(8,128)S(1)} %get-tuple-element.71), channel_id=1, source_target_pairs={{0,4},{2,6},{4,0},{6,2},{8,12},{10,14},{12,8},{14,10},{16,20},{18,... | collective-permute-start | bytes 36872 | tf_op jit(solution)/shard_map/ppermute | solution.py:41
  57.1 1.5 %collective-permute-start.13 = (f32[24,128]{1,0:T(8,128)S(1)}, f32[24,128]{1,0:T(8,128)S(1)}, u32[]{:S(2)}, u32[]{:S(2)}) collective-permute-start(f32[24,128]{1,0:T(8,128)S(1)} %get-tuple-element.71), channel_id=1, source_target_pairs={{0,2},{2,0},{4,6},{6,4},{8,10},{10,8},{12,14},{14,12},{16,18},{18,... | collective-permute-start | bytes 36872 | tf_op jit(solution)/shard_map/ppermute | solution.py:41
  58.6 2.5 %collective-permute-start.24 = (f32[392,128]{1,0:T(8,128)S(1)}, f32[392,128]{1,0:T(8,128)S(1)}, u32[]{:S(2)}, u32[]{:S(2)}) collective-permute-start(f32[392,128]{1,0:T(8,128)S(1)} %get-tuple-element.85), channel_id=1, source_target_pairs={{0,16},{2,18},{4,20},{6,22},{8,24},{10,26},{12,28},{14,30},{16,0},... | collective-permute-start | bytes 602120 | tf_op jit(solution)/shard_map/ppermute | solution.py:41
  61.1 1.7 %collective-permute-start.18 = (f32[24,128]{1,0:T(8,128)S(1)}, f32[24,128]{1,0:T(8,128)S(1)}, u32[]{:S(2)}, u32[]{:S(2)}) collective-permute-start(f32[24,128]{1,0:T(8,128)S(1)} %add_add_fusion.1.refs_0_), channel_id=1, source_target_pairs={{0,24},{2,26},{4,28},{6,30},{8,16},{10,18},{12,20},{14,22},{16,8},... | collective-permute-start | bytes 36872 | tf_op jit(solution)/shard_map/ppermute | solution.py:41
  62.9 1.0 %collective-permute-start.17 = (f32[24,128]{1,0:T(8,128)S(1)}, f32[24,128]{1,0:T(8,128)S(1)}, u32[]{:S(2)}, u32[]{:S(2)}) collective-permute-start(f32[24,128]{1,0:T(8,128)S(1)} %add_add_fusion.1.refs_0_), channel_id=1, source_target_pairs={{0,16},{2,18},{4,20},{6,22},{8,24},{10,26},{12,28},{14,30},{16,0},... | collective-permute-start | bytes 36872 | tf_op jit(solution)/shard_map/ppermute | solution.py:41
  63.8 1.8 %collective-permute-start.16 = (f32[24,128]{1,0:T(8,128)S(1)}, f32[24,128]{1,0:T(8,128)S(1)}, u32[]{:S(2)}, u32[]{:S(2)}) collective-permute-start(f32[24,128]{1,0:T(8,128)S(1)} %add_add_fusion.1.refs_0_), channel_id=1, source_target_pairs={{0,8},{2,10},{4,12},{6,14},{8,0},{10,2},{12,4},{14,6},{16,24},{18,... | collective-permute-start | bytes 36872 | tf_op jit(solution)/shard_map/ppermute | solution.py:41
  65.6 1.8 %collective-permute-done.18.refs_3_ = f32[24,128]{1,0:T(8,128)S(1)} collective-permute-done((f32[24,128]{1,0:T(8,128)S(1)}, f32[24,128]{1,0:T(8,128)S(1)}, u32[]{:S(2)}, u32[]{:S(2)}) %collective-permute-start.18) | collective-permute-done | bytes 12320 | tf_op jit(solution)/shard_map/ppermute | solution.py:41
  67.4 3.8 %collective-permute-done.17.refs_2_ = f32[24,128]{1,0:T(8,128)S(1)} collective-permute-done((f32[24,128]{1,0:T(8,128)S(1)}, f32[24,128]{1,0:T(8,128)S(1)}, u32[]{:S(2)}, u32[]{:S(2)}) %collective-permute-start.17) | collective-permute-done | bytes 12320 | tf_op jit(solution)/shard_map/ppermute | solution.py:41
  71.2 2.1 %last.1 = (f32[24,768]{1,0:T(8,128)}, f32[24,768]{1,0:T(8,128)}, f32[24,768]{1,0:T(8,128)}, f32[1,64,1024]{2,1,0:T(8,128)}) custom-call(s32[1,24]{1,0:T(1,128)S(1)} %copy-done.1, f32[8,768]{1,0:T(8,128)S(1)} %get-tuple-element.45.diag, f32[24,768]{1,0:T(8,128)S(1)} %get-tuple-element.46.start, f32[24,896]{1,0:T(8,128)S(1)} %terms.7.own.held, ...), custom_call_target="tpu_custom_call" | custom-call | tf_op jit(solution)/shard_map/last/pallas_call | solution.py:544
  (38 shorter events, 4.6 us)
Async XLA Ops:
  3.9 14.5 %collective-permute-start.2 = (f32[24,2048]{1,0:T(8,128)S(1)}, f32[24,2048]{1,0:T(8,128)S(1)}, u32[]{:S(2)}, u32[]{:S(2)}) collective-permute-start(f32[24,2048]{1,0:T(8,128)S(1)} %get-tuple-element.48), channel_id=1, source_target_pairs={{0,6},{2,4},{4,2},{6,0},{8,14},{10,12},{12,10},{14,8},{16,22},{18,... | collective-permute-start | bytes 589832 | tf_op jit(solution)/shard_map/ppermute | solution.py:41
  7.9 4.7 %copy-start = (bf16[1024,768]{1,0:T(8,128)(2,1)S(1)}, bf16[1024,768]{1,0:T(8,128)(2,1)}, u32[]{:S(2)}) copy-start(bf16[1024,768]{1,0:T(8,128)(2,1)} %variants.1) | copy-start | bytes 4718596
  7.9 4.7 %copy-start.1 = (s32[1,24]{1,0:T(1,128)S(1)}, s32[1,24]{1,0:T(1,128)}, u32[]{:S(2)}) copy-start(s32[1,24]{1,0:T(1,128)} %sizes.3) | copy-start | bytes 292
  12.0 6.5 %collective-permute-start.1 = (f32[24,2048]{1,0:T(8,128)S(1)}, f32[24,2048]{1,0:T(8,128)S(1)}, u32[]{:S(2)}, u32[]{:S(2)}) collective-permute-start(f32[24,2048]{1,0:T(8,128)S(1)} %get-tuple-element.55), channel_id=1, source_target_pairs={{0,4},{2,6},{4,0},{6,2},{8,12},{10,14},{12,8},{14,10},{16,20},{18,... | collective-permute-start | bytes 589832 | tf_op jit(solution)/shard_map/ppermute | solution.py:41
  12.5 6.1 %collective-permute-start = (f32[24,2048]{1,0:T(8,128)S(1)}, f32[24,2048]{1,0:T(8,128)S(1)}, u32[]{:S(2)}, u32[]{:S(2)}) collective-permute-start(f32[24,2048]{1,0:T(8,128)S(1)} %get-tuple-element.51), channel_id=1, source_target_pairs={{0,2},{2,0},{4,6},{6,4},{8,10},{10,8},{12,14},{14,12},{16,18},{18,... | collective-permute-start | bytes 589832 | tf_op jit(solution)/shard_map/ppermute | solution.py:41
  18.7 11.6 %collective-permute-start.19 = (f32[224,512]{1,0:T(8,128)S(1)}, f32[224,512]{1,0:T(8,128)S(1)}, u32[]{:S(2)}, u32[]{:S(2)}) collective-permute-start(f32[224,512]{1,0:T(8,128)S(1)} %get-tuple-element.72), channel_id=1, source_target_pairs={{0,2},{2,0},{4,6},{6,4},{8,10},{10,8},{12,14},{14,12},{16,18},{18,... | collective-permute-start | bytes 1376264 | tf_op jit(solution)/shard_map/ppermute | solution.py:41
  20.5 11.1 %collective-permute-start.20 = (f32[224,512]{1,0:T(8,128)S(1)}, f32[224,512]{1,0:T(8,128)S(1)}, u32[]{:S(2)}, u32[]{:S(2)}) collective-permute-start(f32[224,512]{1,0:T(8,128)S(1)} %get-tuple-element.73), channel_id=1, source_target_pairs={{0,4},{2,6},{4,0},{6,2},{8,12},{10,14},{12,8},{14,10},{16,20},{18,... | collective-permute-start | bytes 1376264 | tf_op jit(solution)/shard_map/ppermute | solution.py:41
  22.0 11.9 %collective-permute-start.3 = (f32[24,512]{1,0:T(8,128)S(1)}, f32[24,512]{1,0:T(8,128)S(1)}, u32[]{:S(2)}, u32[]{:S(2)}) collective-permute-start(f32[24,512]{1,0:T(8,128)S(1)} %get-tuple-element.60), channel_id=1, source_target_pairs={{0,8},{2,10},{4,12},{6,14},{8,0},{10,2},{12,4},{14,6},{16,24},{18,... | collective-permute-start | bytes 147464 | tf_op jit(solution)/shard_map/ppermute | solution.py:41
  23.6 10.3 %collective-permute-start.4 = (f32[24,512]{1,0:T(8,128)S(1)}, f32[24,512]{1,0:T(8,128)S(1)}, u32[]{:S(2)}, u32[]{:S(2)}) collective-permute-start(f32[24,512]{1,0:T(8,128)S(1)} %get-tuple-element.61), channel_id=1, source_target_pairs={{0,16},{2,18},{4,20},{6,22},{8,24},{10,26},{12,28},{14,30},{16,0},... | collective-permute-start | bytes 147464 | tf_op jit(solution)/shard_map/ppermute | solution.py:41
  26.2 7.8 %collective-permute-start.5 = (f32[24,512]{1,0:T(8,128)S(1)}, f32[24,512]{1,0:T(8,128)S(1)}, u32[]{:S(2)}, u32[]{:S(2)}) collective-permute-start(f32[24,512]{1,0:T(8,128)S(1)} %get-tuple-element.62), channel_id=1, source_target_pairs={{0,24},{2,26},{4,28},{6,30},{8,16},{10,18},{12,20},{14,22},{16,8},... | collective-permute-start | bytes 147464 | tf_op jit(solution)/shard_map/ppermute | solution.py:41
  31.8 6.6 %collective-permute-start.21 = (f32[248,256]{1,0:T(8,128)S(1)}, f32[248,256]{1,0:T(8,128)S(1)}, u32[]{:S(2)}, u32[]{:S(2)}) collective-permute-start(f32[248,256]{1,0:T(8,128)S(1)} %get-tuple-element.80.pass_x), channel_id=1, source_target_pairs={{0,4},{2,6},{4,0},{6,2},{8,12},{10,14},{12,8},{14,10},{16,20},{18,... | collective-permute-start | bytes 761864 | tf_op jit(solution)/shard_map/ppermute | solution.py:41
  33.4 6.3 %collective-permute-start.22 = (f32[248,256]{1,0:T(8,128)S(1)}, f32[248,256]{1,0:T(8,128)S(1)}, u32[]{:S(2)}, u32[]{:S(2)}) collective-permute-start(f32[248,256]{1,0:T(8,128)S(1)} %get-tuple-element.81.pass_y), channel_id=1, source_target_pairs={{0,2},{2,0},{4,6},{6,4},{8,10},{10,8},{12,14},{14,12},{16,18},{18,... | collective-permute-start | bytes 761864 | tf_op jit(solution)/shard_map/ppermute | solution.py:41
  33.9 7.5 %collective-permute-start.8 = (f32[24,512]{1,0:T(8,128)S(1)}, f32[24,512]{1,0:T(8,128)S(1)}, u32[]{:S(2)}, u32[]{:S(2)}) collective-permute-start(f32[24,512]{1,0:T(8,128)S(1)} %add_add_fusion), channel_id=1, source_target_pairs={{0,24},{2,26},{4,28},{6,30},{8,16},{10,18},{12,20},{14,22},{16,8},... | collective-permute-start | bytes 147464 | tf_op jit(solution)/shard_map/ppermute | solution.py:41
  37.6 5.1 %collective-permute-start.7 = (f32[24,512]{1,0:T(8,128)S(1)}, f32[24,512]{1,0:T(8,128)S(1)}, u32[]{:S(2)}, u32[]{:S(2)}) collective-permute-start(f32[24,512]{1,0:T(8,128)S(1)} %add_add_fusion), channel_id=1, source_target_pairs={{0,16},{2,18},{4,20},{6,22},{8,24},{10,26},{12,28},{14,30},{16,0},... | collective-permute-start | bytes 147464 | tf_op jit(solution)/shard_map/ppermute | solution.py:41
  37.6 5.1 %collective-permute-start.6 = (f32[24,512]{1,0:T(8,128)S(1)}, f32[24,512]{1,0:T(8,128)S(1)}, u32[]{:S(2)}, u32[]{:S(2)}) collective-permute-start(f32[24,512]{1,0:T(8,128)S(1)} %add_add_fusion), channel_id=1, source_target_pairs={{0,8},{2,10},{4,12},{6,14},{8,0},{10,2},{12,4},{14,6},{16,24},{18,... | collective-permute-start | bytes 147464 | tf_op jit(solution)/shard_map/ppermute | solution.py:41
  39.8 18.8 %collective-permute-start.23 = (f32[296,256]{1,0:T(8,128)S(1)}, f32[296,256]{1,0:T(8,128)S(1)}, u32[]{:S(2)}, u32[]{:S(2)}) collective-permute-start(f32[296,256]{1,0:T(8,128)S(1)} %get-tuple-element.83), channel_id=1, source_target_pairs={{0,8},{2,10},{4,12},{6,14},{8,0},{10,2},{12,4},{14,6},{16,24},{18,... | collective-permute-start | bytes 909320 | tf_op jit(solution)/shard_map/ppermute | solution.py:41
  42.8 5.7 %collective-permute-start.11 = (f32[24,2048]{1,0:T(8,128)S(1)}, f32[24,2048]{1,0:T(8,128)S(1)}, u32[]{:S(2)}, u32[]{:S(2)}) collective-permute-start(f32[24,2048]{1,0:T(8,128)S(1)} %pad_maximum_fusion.scores), channel_id=1, source_target_pairs={{0,2},{2,0},{4,6},{6,4},{8,10},{10,8},{12,14},{14,12},{16,18},{18,... | collective-permute-start | bytes 589832 | tf_op jit(solution)/shard_map/ppermute | solution.py:41
  44.3 7.8 %collective-permute-start.10 = (f32[24,2048]{1,0:T(8,128)S(1)}, f32[24,2048]{1,0:T(8,128)S(1)}, u32[]{:S(2)}, u32[]{:S(2)}) collective-permute-start(f32[24,2048]{1,0:T(8,128)S(1)} %pad_maximum_fusion.scores), channel_id=1, source_target_pairs={{0,4},{2,6},{4,0},{6,2},{8,12},{10,14},{12,8},{14,10},{16,20},{18,... | collective-permute-start | bytes 589832 | tf_op jit(solution)/shard_map/ppermute | solution.py:41
  44.8 8.0 %collective-permute-start.9 = (f32[24,2048]{1,0:T(8,128)S(1)}, f32[24,2048]{1,0:T(8,128)S(1)}, u32[]{:S(2)}, u32[]{:S(2)}) collective-permute-start(f32[24,2048]{1,0:T(8,128)S(1)} %pad_maximum_fusion.scores), channel_id=1, source_target_pairs={{0,6},{2,4},{4,2},{6,0},{8,14},{10,12},{12,10},{14,8},{16,22},{18,... | collective-permute-start | bytes 589832 | tf_op jit(solution)/shard_map/ppermute | solution.py:41
  53.5 1.3 %collective-permute-start.12 = (f32[24,896]{1,0:T(8,128)S(1)}, f32[24,896]{1,0:T(8,128)S(1)}, u32[]{:S(2)}, u32[]{:S(2)}) collective-permute-start(f32[24,896]{1,0:T(8,128)S(1)} %terms.7.own.held), channel_id=1, source_target_pairs={{0,1},{1,0},{2,3},{3,2},{4,5},{5,4},{6,7},{7,6},{8,9},{9,8},{10,11... | collective-permute-start | bytes 258056 | tf_op jit(solution)/shard_map/ppermute | solution.py:41
  55.1 6.0 %collective-permute-start.15 = (f32[24,128]{1,0:T(8,128)S(1)}, f32[24,128]{1,0:T(8,128)S(1)}, u32[]{:S(2)}, u32[]{:S(2)}) collective-permute-start(f32[24,128]{1,0:T(8,128)S(1)} %get-tuple-element.71), channel_id=1, source_target_pairs={{0,6},{2,4},{4,2},{6,0},{8,14},{10,12},{12,10},{14,8},{16,22},{18,... | collective-permute-start | bytes 36872 | tf_op jit(solution)/shard_map/ppermute | solution.py:41
  55.3 5.8 %collective-permute-start.14 = (f32[24,128]{1,0:T(8,128)S(1)}, f32[24,128]{1,0:T(8,128)S(1)}, u32[]{:S(2)}, u32[]{:S(2)}) collective-permute-start(f32[24,128]{1,0:T(8,128)S(1)} %get-tuple-element.71), channel_id=1, source_target_pairs={{0,4},{2,6},{4,0},{6,2},{8,12},{10,14},{12,8},{14,10},{16,20},{18,... | collective-permute-start | bytes 36872 | tf_op jit(solution)/shard_map/ppermute | solution.py:41
  57.1 4.0 %collective-permute-start.13 = (f32[24,128]{1,0:T(8,128)S(1)}, f32[24,128]{1,0:T(8,128)S(1)}, u32[]{:S(2)}, u32[]{:S(2)}) collective-permute-start(f32[24,128]{1,0:T(8,128)S(1)} %get-tuple-element.71), channel_id=1, source_target_pairs={{0,2},{2,0},{4,6},{6,4},{8,10},{10,8},{12,14},{14,12},{16,18},{18,... | collective-permute-start | bytes 36872 | tf_op jit(solution)/shard_map/ppermute | solution.py:41
  58.6 12.5 %collective-permute-start.24 = (f32[392,128]{1,0:T(8,128)S(1)}, f32[392,128]{1,0:T(8,128)S(1)}, u32[]{:S(2)}, u32[]{:S(2)}) collective-permute-start(f32[392,128]{1,0:T(8,128)S(1)} %get-tuple-element.85), channel_id=1, source_target_pairs={{0,16},{2,18},{4,20},{6,22},{8,24},{10,26},{12,28},{14,30},{16,0},... | collective-permute-start | bytes 602120 | tf_op jit(solution)/shard_map/ppermute | solution.py:41
  61.1 6.3 %collective-permute-start.18 = (f32[24,128]{1,0:T(8,128)S(1)}, f32[24,128]{1,0:T(8,128)S(1)}, u32[]{:S(2)}, u32[]{:S(2)}) collective-permute-start(f32[24,128]{1,0:T(8,128)S(1)} %add_add_fusion.1.refs_0_), channel_id=1, source_target_pairs={{0,24},{2,26},{4,28},{6,30},{8,16},{10,18},{12,20},{14,22},{16,8},... | collective-permute-start | bytes 36872 | tf_op jit(solution)/shard_map/ppermute | solution.py:41
  62.9 8.3 %collective-permute-start.17 = (f32[24,128]{1,0:T(8,128)S(1)}, f32[24,128]{1,0:T(8,128)S(1)}, u32[]{:S(2)}, u32[]{:S(2)}) collective-permute-start(f32[24,128]{1,0:T(8,128)S(1)} %add_add_fusion.1.refs_0_), channel_id=1, source_target_pairs={{0,16},{2,18},{4,20},{6,22},{8,24},{10,26},{12,28},{14,30},{16,0},... | collective-permute-start | bytes 36872 | tf_op jit(solution)/shard_map/ppermute | solution.py:41
  63.8 7.3 %collective-permute-start.16 = (f32[24,128]{1,0:T(8,128)S(1)}, f32[24,128]{1,0:T(8,128)S(1)}, u32[]{:S(2)}, u32[]{:S(2)}) collective-permute-start(f32[24,128]{1,0:T(8,128)S(1)} %add_add_fusion.1.refs_0_), channel_id=1, source_target_pairs={{0,8},{2,10},{4,12},{6,14},{8,0},{10,2},{12,4},{14,6},{16,24},{18,... | collective-permute-start | bytes 36872 | tf_op jit(solution)/shard_map/ppermute | solution.py:41

commit v9 on v8

--- a/solution.py
+++ b/solution.py
@@ -445,7 +445,7 @@
 
     terms = [sent[0]] + [swap(sent[d], count, firsts[d]) for d in range(1, radix)]
     wide = columns
-    for level, (r, s) in enumerate(later):
+    for r, s in later:
         wide //= r
         pieces = kernel(
             merge_kernel,
@@ -454,10 +454,7 @@
             out_specs=[vmem] * r,
             name="merge",
         )(*map(in_vmem, terms))
-        piece = pieces[0]
-        if level == 0:
-            piece, send_x, send_y = lax.optimization_barrier((piece, send_x, send_y))
-        terms = [piece] + [swap(pieces[d], count, d * s) for d in range(1, r)]
+        terms = [pieces[0]] + [swap(pieces[d], count, d * s) for d in range(1, r)]
     got = terms[0]
     for one in terms[1:]:
         got = got + one

time: 73.4 us -> 84.3 us (1.15)
  waiting for transfers between devices: 19.2 us -> 32.5 us
  starting transfers between devices: 34.6 us -> 32.2 us
    ppermute x25, waiting for transfers between devices: 19.2 us -> 32.5 us  [swap(): return lax.ppermute(array, axis, [(i, i ^ offset) for i in range(count)])]
    ppermute x25, starting transfers between devices: 34.6 us -> 32.2 us  [swap(): return lax.ppermute(array, axis, [(i, i ^ offset) for i in range(count)])]
  transfers between devices with their start and end apart: 25 -> 25, of which waited for: 11 -> 14; matrix products, arithmetic and copies ran while one was open for 0% -> 0% of each run, Pallas kernels for 18% -> 4%
where the time goes in v9:
time: 84.3 us; the launch traced here: 84.1 us
  waiting for transfers between devices  32.5 us (39%)
  starting transfers between devices  32.2 us (38%)
  Pallas kernels  18 us (21%)
  between operations  1.4 us (2%)
    ppermute x25, waiting for transfers between devices, swap(): return lax.ppermute(array, axis, [(i, i ^ offset) for i in range(count)])  32.5 us
    ppermute x25, starting transfers between devices, swap(): return lax.ppermute(array, axis, [(i, i ^ offset) for i in range(count)])  32.2 us
    pallas_call x1, Pallas kernels, body(): kernel(functools.partial(cross_kernel, plan, block, 0), out_shape=[payloa...  5.76 us
    pallas_call x1, Pallas kernels, body(): kernel(functools.partial(scores_kernel, plan, digits), out_shape=[payload...  4.06 us
    pallas_call x4, Pallas kernels, body(): kernel(functools.partial(terms_kernel, plan, d), out_shape=VMEM((rows, sa...  2.73 us
    pallas_call x1, Pallas kernels, body(): kernel(functools.partial(lead_kernel, plan, lead), out_shape=[payload, wi...  2.62 us
    pallas_call x1, Pallas kernels, body(): kernel(functools.partial(last_kernel, samples * count, len(norms)), out_s...  2.06 us
  transfers between devices with their start and end apart: 25, of which 14 were waited for; matrix products, arithmetic and copies ran while one was open for 0% of the time, Pallas kernels for 4%

profile of v9, /device:TPU:0, one launch (start us, length us, event | category | flops | bytes accessed | tf_op | source)
XLA Modules:
  0.0 84.1 jit_solution(12856575515916950361)
XLA Ops:
  1.3 2.6 %scores_lead.1 = (f32[24,2048]{1,0:T(8,128)S(1)}, bf16[2048,768]{1,0:T(8,128)(2,1)S(1)}, f32[8,768]{1,0:T(8,128)S(1)}, f32[24,768]{1,0:T(8,128)S(1)}, f32[24,768...) custom-call(f32[1]{0:T(128)S(6)} %copy.18.ratio, ...), custom_call_target="tpu_custom_call" | custom-call | tf_op jit(solution)/shard_map/scores_lead/pallas_call | solution.py:386
  3.9 4.1 %scores.1 = (f32[24,2048]{1,0:T(8,128)S(1)}, f32[24,2048]{1,0:T(8,128)S(1)}, bf16[2048,768]{1,0:T(8,128)(2,1)S(1)}, bf16[2048,768]{1,0:T(8,128)(2,1)S(1)}) custom-call(bf16[24,768]{1,0:T(8,128)(2,1)S(1)} %get-tuple-element.49.start_bf, f32[24,128]{1,0:T(8,128)S(1)} %get-tuple-element.47.stats, bf16[8000,768]{1,0:T(8,128)(2,1)} %geno.5), custom_call_target="tpu_custom_call" | custom-call | tf_op jit(solution)/shard_map/scores/pallas_call | solution.py:412
  8.0 5.8 %scores_cross.1 = (f32[24,2048]{1,0:T(8,128)S(1)}, bf16[2048,768]{1,0:T(8,128)(2,1)S(1)}, f32[200,256]{1,0:T(8,128)S(1)}, f32[200,256]{1,0:T(8,128)S(1)}, f32[24...) custom-call(s32[1,24]{1,0:T(1,128)S(1)} %copy-done.1, ...), custom_call_target="tpu_custom_call" | custom-call | tf_op jit(solution)/shard_map/scores_cross/pallas_call | solution.py:434
  13.8 3.0 %collective-permute-start.19 = (f32[224,512]{1,0:T(8,128)S(1)}, f32[224,512]{1,0:T(8,128)S(1)}, u32[]{:S(2)}, u32[]{:S(2)}) collective-permute-start(f32[224,512]{1,0:T(8,128)S(1)} %get-tuple-element.66), channel_id=1, source_target_pairs={{0,2},{2,0},{4,6},{6,4},{8,10},{10,8},{12,14},{14,12},{16,18},{18,... | collective-permute-start | bytes 1376264 | tf_op jit(solution)/shard_map/ppermute | solution.py:41
  16.8 1.5 %collective-permute-start.20 = (f32[224,512]{1,0:T(8,128)S(1)}, f32[224,512]{1,0:T(8,128)S(1)}, u32[]{:S(2)}, u32[]{:S(2)}) collective-permute-start(f32[224,512]{1,0:T(8,128)S(1)} %get-tuple-element.67), channel_id=1, source_target_pairs={{0,4},{2,6},{4,0},{6,2},{8,12},{10,14},{12,8},{14,10},{16,20},{18,... | collective-permute-start | bytes 1376264 | tf_op jit(solution)/shard_map/ppermute | solution.py:41
  18.4 2.0 %collective-permute-start.1 = (f32[24,2048]{1,0:T(8,128)S(1)}, f32[24,2048]{1,0:T(8,128)S(1)}, u32[]{:S(2)}, u32[]{:S(2)}) collective-permute-start(f32[24,2048]{1,0:T(8,128)S(1)} %get-tuple-element.52), channel_id=1, source_target_pairs={{0,4},{2,6},{4,0},{6,2},{8,12},{10,14},{12,8},{14,10},{16,20},{18,... | collective-permute-start | bytes 589832 | tf_op jit(solution)/shard_map/ppermute | solution.py:41
  20.3 1.5 %collective-permute-start = (f32[24,2048]{1,0:T(8,128)S(1)}, f32[24,2048]{1,0:T(8,128)S(1)}, u32[]{:S(2)}, u32[]{:S(2)}) collective-permute-start(f32[24,2048]{1,0:T(8,128)S(1)} %get-tuple-element.48), channel_id=1, source_target_pairs={{0,2},{2,0},{4,6},{6,4},{8,10},{10,8},{12,14},{14,12},{16,18},{18,... | collective-permute-start | bytes 589832 | tf_op jit(solution)/shard_map/ppermute | solution.py:41
  21.8 12.1 %collective-permute-done.2.refs_3_ = f32[24,2048]{1,0:T(8,128)S(1)} collective-permute-done((f32[24,2048]{1,0:T(8,128)S(1)}, f32[24,2048]{1,0:T(8,128)S(1)}, u32[]{:S(2)}, u32[]{:S(2)}) %collective-permute-start.2) | collective-permute-done | bytes 196640 | tf_op jit(solution)/shard_map/ppermute | solution.py:41
  33.9 3.3 %collective-permute-done.1.refs_2_ = f32[24,2048]{1,0:T(8,128)S(1)} collective-permute-done((f32[24,2048]{1,0:T(8,128)S(1)}, f32[24,2048]{1,0:T(8,128)S(1)}, u32[]{:S(2)}, u32[]{:S(2)}) %collective-permute-start.1) | collective-permute-done | bytes 196640 | tf_op jit(solution)/shard_map/ppermute | solution.py:41
  37.3 1.6 %collective-permute-start.3 = (f32[24,512]{1,0:T(8,128)S(1)}, f32[24,512]{1,0:T(8,128)S(1)}, u32[]{:S(2)}, u32[]{:S(2)}) collective-permute-start(f32[24,512]{1,0:T(8,128)S(1)} %get-tuple-element.54), channel_id=1, source_target_pairs={{0,8},{2,10},{4,12},{6,14},{8,0},{10,2},{12,4},{14,6},{16,24},{18,... | collective-permute-start | bytes 147464 | tf_op jit(solution)/shard_map/ppermute | solution.py:41
  38.9 2.6 %collective-permute-start.4 = (f32[24,512]{1,0:T(8,128)S(1)}, f32[24,512]{1,0:T(8,128)S(1)}, u32[]{:S(2)}, u32[]{:S(2)}) collective-permute-start(f32[24,512]{1,0:T(8,128)S(1)} %get-tuple-element.55), channel_id=1, source_target_pairs={{0,16},{2,18},{4,20},{6,22},{8,24},{10,26},{12,28},{14,30},{16,0},... | collective-permute-start | bytes 147464 | tf_op jit(solution)/shard_map/ppermute | solution.py:41
  41.9 1.6 %collective-permute-start.21 = (f32[248,256]{1,0:T(8,128)S(1)}, f32[248,256]{1,0:T(8,128)S(1)}, u32[]{:S(2)}, u32[]{:S(2)}) collective-permute-start(f32[248,256]{1,0:T(8,128)S(1)} %get-tuple-element.74.pass_x), channel_id=1, source_target_pairs={{0,4},{2,6},{4,0},{6,2},{8,12},{10,14},{12,8},{14,10},{16,20},{18,... | collective-permute-start | bytes 761864 | tf_op jit(solution)/shard_map/ppermute | solution.py:41
  44.0 0.9 %collective-permute-done.4 = f32[24,512]{1,0:T(8,128)S(1)} collective-permute-done((f32[24,512]{1,0:T(8,128)S(1)}, f32[24,512]{1,0:T(8,128)S(1)}, u32[]{:S(2)}, u32[]{:S(2)}) %collective-permute-start.4) | collective-permute-done | bytes 49184 | tf_op jit(solution)/shard_map/ppermute | solution.py:41
  45.0 2.4 %collective-permute-done.5 = f32[24,512]{1,0:T(8,128)S(1)} collective-permute-done((f32[24,512]{1,0:T(8,128)S(1)}, f32[24,512]{1,0:T(8,128)S(1)}, u32[]{:S(2)}, u32[]{:S(2)}) %collective-permute-start.5) | collective-permute-done | bytes 49184 | tf_op jit(solution)/shard_map/ppermute | solution.py:41
  48.1 3.8 %collective-permute-start.6 = (f32[24,512]{1,0:T(8,128)S(1)}, f32[24,512]{1,0:T(8,128)S(1)}, u32[]{:S(2)}, u32[]{:S(2)}) collective-permute-start(f32[24,512]{1,0:T(8,128)S(1)} %add_add_fusion), channel_id=1, source_target_pairs={{0,8},{2,10},{4,12},{6,14},{8,0},{10,2},{12,4},{14,6},{16,24},{18,... | collective-permute-start | bytes 147464 | tf_op jit(solution)/shard_map/ppermute | solution.py:41
  52.1 1.8 %collective-permute-done.8 = f32[24,512]{1,0:T(8,128)S(1)} collective-permute-done((f32[24,512]{1,0:T(8,128)S(1)}, f32[24,512]{1,0:T(8,128)S(1)}, u32[]{:S(2)}, u32[]{:S(2)}) %collective-permute-start.8) | collective-permute-done | bytes 49184 | tf_op jit(solution)/shard_map/ppermute | solution.py:41
  53.9 0.8 collective-permute-done.6
  54.7 1.1 %collective-permute-start.11 = (f32[24,2048]{1,0:T(8,128)S(1)}, f32[24,2048]{1,0:T(8,128)S(1)}, u32[]{:S(2)}, u32[]{:S(2)}) collective-permute-start(f32[24,2048]{1,0:T(8,128)S(1)} %pad_maximum_fusion.scores), channel_id=1, source_target_pairs={{0,2},{2,0},{4,6},{6,4},{8,10},{10,8},{12,14},{14,12},{16,18},{18,... | collective-permute-start | bytes 589832 | tf_op jit(solution)/shard_map/ppermute | solution.py:41
  55.8 1.0 %collective-permute-start.10 = (f32[24,2048]{1,0:T(8,128)S(1)}, f32[24,2048]{1,0:T(8,128)S(1)}, u32[]{:S(2)}, u32[]{:S(2)}) collective-permute-start(f32[24,2048]{1,0:T(8,128)S(1)} %pad_maximum_fusion.scores), channel_id=1, source_target_pairs={{0,4},{2,6},{4,0},{6,2},{8,12},{10,14},{12,8},{14,10},{16,20},{18,... | collective-permute-start | bytes 589832 | tf_op jit(solution)/shard_map/ppermute | solution.py:41
  56.9 1.4 %collective-permute-start.9 = (f32[24,2048]{1,0:T(8,128)S(1)}, f32[24,2048]{1,0:T(8,128)S(1)}, u32[]{:S(2)}, u32[]{:S(2)}) collective-permute-start(f32[24,2048]{1,0:T(8,128)S(1)} %pad_maximum_fusion.scores), channel_id=1, source_target_pairs={{0,6},{2,4},{4,2},{6,0},{8,14},{10,12},{12,10},{14,8},{16,22},{18,... | collective-permute-start | bytes 589832 | tf_op jit(solution)/shard_map/ppermute | solution.py:41
  59.0 1.5 %collective-permute-done.11.scores = f32[24,2048]{1,0:T(8,128)S(1)} collective-permute-done((f32[24,2048]{1,0:T(8,128)S(1)}, f32[24,2048]{1,0:T(8,128)S(1)}, u32[]{:S(2)}, u32[]{:S(2)}) %collective-permute-start.11) | collective-permute-done | bytes 196640 | tf_op jit(solution)/shard_map/ppermute | solution.py:41
  62.2 1.4 %collective-permute-done.9.scores = f32[24,2048]{1,0:T(8,128)S(1)} collective-permute-done((f32[24,2048]{1,0:T(8,128)S(1)}, f32[24,2048]{1,0:T(8,128)S(1)}, u32[]{:S(2)}, u32[]{:S(2)}) %collective-permute-start.9) | collective-permute-done | bytes 196640 | tf_op jit(solution)/shard_map/ppermute | solution.py:41
  64.3 1.3 %collective-permute-done.12.other = f32[24,896]{1,0:T(8,128)S(1)} collective-permute-done((f32[24,896]{1,0:T(8,128)S(1)}, f32[24,896]{1,0:T(8,128)S(1)}, u32[]{:S(2)}, u32[]{:S(2)}) %collective-permute-start.12) | collective-permute-done | bytes 86048 | tf_op jit(solution)/shard_map/ppermute | solution.py:41
  65.9 2.7 %collective-permute-start.15 = (f32[24,128]{1,0:T(8,128)S(1)}, f32[24,128]{1,0:T(8,128)S(1)}, u32[]{:S(2)}, u32[]{:S(2)}) collective-permute-start(f32[24,128]{1,0:T(8,128)S(1)} %get-tuple-element.65), channel_id=1, source_target_pairs={{0,6},{2,4},{4,2},{6,0},{8,14},{10,12},{12,10},{14,8},{16,22},{18,... | collective-permute-start | bytes 36872 | tf_op jit(solution)/shard_map/ppermute | solution.py:41
  69.4 1.6 %collective-permute-start.24 = (f32[392,128]{1,0:T(8,128)S(1)}, f32[392,128]{1,0:T(8,128)S(1)}, u32[]{:S(2)}, u32[]{:S(2)}) collective-permute-start(f32[392,128]{1,0:T(8,128)S(1)} %get-tuple-element.79), channel_id=1, source_target_pairs={{0,16},{2,18},{4,20},{6,22},{8,24},{10,26},{12,28},{14,30},{16,0},... | collective-permute-start | bytes 602120 | tf_op jit(solution)/shard_map/ppermute | solution.py:41
  71.0 1.2 %collective-permute-done.14 = f32[24,128]{1,0:T(8,128)S(1)} collective-permute-done((f32[24,128]{1,0:T(8,128)S(1)}, f32[24,128]{1,0:T(8,128)S(1)}, u32[]{:S(2)}, u32[]{:S(2)}) %collective-permute-start.14) | collective-permute-done | bytes 12320 | tf_op jit(solution)/shard_map/ppermute | solution.py:41
  72.4 1.7 %collective-permute-start.18 = (f32[24,128]{1,0:T(8,128)S(1)}, f32[24,128]{1,0:T(8,128)S(1)}, u32[]{:S(2)}, u32[]{:S(2)}) collective-permute-start(f32[24,128]{1,0:T(8,128)S(1)} %add_add_fusion.1.refs_0_), channel_id=1, source_target_pairs={{0,24},{2,26},{4,28},{6,30},{8,16},{10,18},{12,20},{14,22},{16,8},... | collective-permute-start | bytes 36872 | tf_op jit(solution)/shard_map/ppermute | solution.py:41
  74.1 1.3 %collective-permute-start.17 = (f32[24,128]{1,0:T(8,128)S(1)}, f32[24,128]{1,0:T(8,128)S(1)}, u32[]{:S(2)}, u32[]{:S(2)}) collective-permute-start(f32[24,128]{1,0:T(8,128)S(1)} %add_add_fusion.1.refs_0_), channel_id=1, source_target_pairs={{0,16},{2,18},{4,20},{6,22},{8,24},{10,26},{12,28},{14,30},{16,0},... | collective-permute-start | bytes 36872 | tf_op jit(solution)/shard_map/ppermute | solution.py:41
  75.4 1.4 %collective-permute-start.16 = (f32[24,128]{1,0:T(8,128)S(1)}, f32[24,128]{1,0:T(8,128)S(1)}, u32[]{:S(2)}, u32[]{:S(2)}) collective-permute-start(f32[24,128]{1,0:T(8,128)S(1)} %add_add_fusion.1.refs_0_), channel_id=1, source_target_pairs={{0,8},{2,10},{4,12},{6,14},{8,0},{10,2},{12,4},{14,6},{16,24},{18,... | collective-permute-start | bytes 36872 | tf_op jit(solution)/shard_map/ppermute | solution.py:41
  76.8 1.5 %collective-permute-done.18.refs_3_ = f32[24,128]{1,0:T(8,128)S(1)} collective-permute-done((f32[24,128]{1,0:T(8,128)S(1)}, f32[24,128]{1,0:T(8,128)S(1)}, u32[]{:S(2)}, u32[]{:S(2)}) %collective-permute-start.18) | collective-permute-done | bytes 12320 | tf_op jit(solution)/shard_map/ppermute | solution.py:41
  78.3 3.8 %collective-permute-done.17.refs_2_ = f32[24,128]{1,0:T(8,128)S(1)} collective-permute-done((f32[24,128]{1,0:T(8,128)S(1)}, f32[24,128]{1,0:T(8,128)S(1)}, u32[]{:S(2)}, u32[]{:S(2)}) %collective-permute-start.17) | collective-permute-done | bytes 12320 | tf_op jit(solution)/shard_map/ppermute | solution.py:41
  82.1 2.1 %last.1 = (f32[24,768]{1,0:T(8,128)}, f32[24,768]{1,0:T(8,128)}, f32[24,768]{1,0:T(8,128)}, f32[1,64,1024]{2,1,0:T(8,128)}) custom-call(s32[1,24]{1,0:T(1,128)S(1)} %copy-done.1, f32[8,768]{1,0:T(8,128)S(1)} %get-tuple-element.42.diag, f32[24,768]{1,0:T(8,128)S(1)} %get-tuple-element.43.start, f32[24,896]{1,0:T(8,128)S(1)} %terms.7.own.held, ...), custom_call_target="tpu_custom_call" | custom-call | tf_op jit(solution)/shard_map/last/pallas_call | solution.py:541
  (38 shorter events, 6.3 us)
Async XLA Ops:
  3.9 4.1 %copy-start = (bf16[1024,768]{1,0:T(8,128)(2,1)S(1)}, bf16[1024,768]{1,0:T(8,128)(2,1)}, u32[]{:S(2)}) copy-start(bf16[1024,768]{1,0:T(8,128)(2,1)} %variants.1) | copy-start | bytes 4718596
  3.9 4.1 %copy-start.1 = (s32[1,24]{1,0:T(1,128)S(1)}, s32[1,24]{1,0:T(1,128)}, u32[]{:S(2)}) copy-start(s32[1,24]{1,0:T(1,128)} %sizes.3) | copy-start | bytes 292
  13.8 27.9 %collective-permute-start.19 = (f32[224,512]{1,0:T(8,128)S(1)}, f32[224,512]{1,0:T(8,128)S(1)}, u32[]{:S(2)}, u32[]{:S(2)}) collective-permute-start(f32[224,512]{1,0:T(8,128)S(1)} %get-tuple-element.66), channel_id=1, source_target_pairs={{0,2},{2,0},{4,6},{6,4},{8,10},{10,8},{12,14},{14,12},{16,18},{18,... | collective-permute-start | bytes 1376264 | tf_op jit(solution)/shard_map/ppermute | solution.py:41
  16.8 24.9 %collective-permute-start.20 = (f32[224,512]{1,0:T(8,128)S(1)}, f32[224,512]{1,0:T(8,128)S(1)}, u32[]{:S(2)}, u32[]{:S(2)}) collective-permute-start(f32[224,512]{1,0:T(8,128)S(1)} %get-tuple-element.67), channel_id=1, source_target_pairs={{0,4},{2,6},{4,0},{6,2},{8,12},{10,14},{12,8},{14,10},{16,20},{18,... | collective-permute-start | bytes 1376264 | tf_op jit(solution)/shard_map/ppermute | solution.py:41
  18.3 15.6 %collective-permute-start.2 = (f32[24,2048]{1,0:T(8,128)S(1)}, f32[24,2048]{1,0:T(8,128)S(1)}, u32[]{:S(2)}, u32[]{:S(2)}) collective-permute-start(f32[24,2048]{1,0:T(8,128)S(1)} %get-tuple-element.45), channel_id=1, source_target_pairs={{0,6},{2,4},{4,2},{6,0},{8,14},{10,12},{12,10},{14,8},{16,22},{18,... | collective-permute-start | bytes 589832 | tf_op jit(solution)/shard_map/ppermute | solution.py:41
  18.4 18.9 %collective-permute-start.1 = (f32[24,2048]{1,0:T(8,128)S(1)}, f32[24,2048]{1,0:T(8,128)S(1)}, u32[]{:S(2)}, u32[]{:S(2)}) collective-permute-start(f32[24,2048]{1,0:T(8,128)S(1)} %get-tuple-element.52), channel_id=1, source_target_pairs={{0,4},{2,6},{4,0},{6,2},{8,12},{10,14},{12,8},{14,10},{16,20},{18,... | collective-permute-start | bytes 589832 | tf_op jit(solution)/shard_map/ppermute | solution.py:41
  20.3 16.9 %collective-permute-start = (f32[24,2048]{1,0:T(8,128)S(1)}, f32[24,2048]{1,0:T(8,128)S(1)}, u32[]{:S(2)}, u32[]{:S(2)}) collective-permute-start(f32[24,2048]{1,0:T(8,128)S(1)} %get-tuple-element.48), channel_id=1, source_target_pairs={{0,2},{2,0},{4,6},{6,4},{8,10},{10,8},{12,14},{14,12},{16,18},{18,... | collective-permute-start | bytes 589832 | tf_op jit(solution)/shard_map/ppermute | solution.py:41
  37.3 6.8 %collective-permute-start.3 = (f32[24,512]{1,0:T(8,128)S(1)}, f32[24,512]{1,0:T(8,128)S(1)}, u32[]{:S(2)}, u32[]{:S(2)}) collective-permute-start(f32[24,512]{1,0:T(8,128)S(1)} %get-tuple-element.54), channel_id=1, source_target_pairs={{0,8},{2,10},{4,12},{6,14},{8,0},{10,2},{12,4},{14,6},{16,24},{18,... | collective-permute-start | bytes 147464 | tf_op jit(solution)/shard_map/ppermute | solution.py:41
  38.9 6.0 %collective-permute-start.4 = (f32[24,512]{1,0:T(8,128)S(1)}, f32[24,512]{1,0:T(8,128)S(1)}, u32[]{:S(2)}, u32[]{:S(2)}) collective-permute-start(f32[24,512]{1,0:T(8,128)S(1)} %get-tuple-element.55), channel_id=1, source_target_pairs={{0,16},{2,18},{4,20},{6,22},{8,24},{10,26},{12,28},{14,30},{16,0},... | collective-permute-start | bytes 147464 | tf_op jit(solution)/shard_map/ppermute | solution.py:41
  41.5 5.9 %collective-permute-start.5 = (f32[24,512]{1,0:T(8,128)S(1)}, f32[24,512]{1,0:T(8,128)S(1)}, u32[]{:S(2)}, u32[]{:S(2)}) collective-permute-start(f32[24,512]{1,0:T(8,128)S(1)} %get-tuple-element.56), channel_id=1, source_target_pairs={{0,24},{2,26},{4,28},{6,30},{8,16},{10,18},{12,20},{14,22},{16,8},... | collective-permute-start | bytes 147464 | tf_op jit(solution)/shard_map/ppermute | solution.py:41
  41.9 10.0 %collective-permute-start.21 = (f32[248,256]{1,0:T(8,128)S(1)}, f32[248,256]{1,0:T(8,128)S(1)}, u32[]{:S(2)}, u32[]{:S(2)}) collective-permute-start(f32[248,256]{1,0:T(8,128)S(1)} %get-tuple-element.74.pass_x), channel_id=1, source_target_pairs={{0,4},{2,6},{4,0},{6,2},{8,12},{10,14},{12,8},{14,10},{16,20},{18,... | collective-permute-start | bytes 761864 | tf_op jit(solution)/shard_map/ppermute | solution.py:41
  43.5 8.4 %collective-permute-start.22 = (f32[248,256]{1,0:T(8,128)S(1)}, f32[248,256]{1,0:T(8,128)S(1)}, u32[]{:S(2)}, u32[]{:S(2)}) collective-permute-start(f32[248,256]{1,0:T(8,128)S(1)} %get-tuple-element.75.pass_y), channel_id=1, source_target_pairs={{0,2},{2,0},{4,6},{6,4},{8,10},{10,8},{12,14},{14,12},{16,18},{18,... | collective-permute-start | bytes 761864 | tf_op jit(solution)/shard_map/ppermute | solution.py:41
  47.4 6.5 %collective-permute-start.8 = (f32[24,512]{1,0:T(8,128)S(1)}, f32[24,512]{1,0:T(8,128)S(1)}, u32[]{:S(2)}, u32[]{:S(2)}) collective-permute-start(f32[24,512]{1,0:T(8,128)S(1)} %add_add_fusion), channel_id=1, source_target_pairs={{0,24},{2,26},{4,28},{6,30},{8,16},{10,18},{12,20},{14,22},{16,8},... | collective-permute-start | bytes 147464 | tf_op jit(solution)/shard_map/ppermute | solution.py:41
  48.1 5.8 %collective-permute-start.7 = (f32[24,512]{1,0:T(8,128)S(1)}, f32[24,512]{1,0:T(8,128)S(1)}, u32[]{:S(2)}, u32[]{:S(2)}) collective-permute-start(f32[24,512]{1,0:T(8,128)S(1)} %add_add_fusion), channel_id=1, source_target_pairs={{0,16},{2,18},{4,20},{6,22},{8,24},{10,26},{12,28},{14,30},{16,0},... | collective-permute-start | bytes 147464 | tf_op jit(solution)/shard_map/ppermute | solution.py:41
  48.1 6.7 %collective-permute-start.6 = (f32[24,512]{1,0:T(8,128)S(1)}, f32[24,512]{1,0:T(8,128)S(1)}, u32[]{:S(2)}, u32[]{:S(2)}) collective-permute-start(f32[24,512]{1,0:T(8,128)S(1)} %add_add_fusion), channel_id=1, source_target_pairs={{0,8},{2,10},{4,12},{6,14},{8,0},{10,2},{12,4},{14,6},{16,24},{18,... | collective-permute-start | bytes 147464 | tf_op jit(solution)/shard_map/ppermute | solution.py:41
  52.1 17.3 %collective-permute-start.23 = (f32[296,256]{1,0:T(8,128)S(1)}, f32[296,256]{1,0:T(8,128)S(1)}, u32[]{:S(2)}, u32[]{:S(2)}) collective-permute-start(f32[296,256]{1,0:T(8,128)S(1)} %get-tuple-element.77), channel_id=1, source_target_pairs={{0,8},{2,10},{4,12},{6,14},{8,0},{10,2},{12,4},{14,6},{16,24},{18,... | collective-permute-start | bytes 909320 | tf_op jit(solution)/shard_map/ppermute | solution.py:41
  54.7 5.7 %collective-permute-start.11 = (f32[24,2048]{1,0:T(8,128)S(1)}, f32[24,2048]{1,0:T(8,128)S(1)}, u32[]{:S(2)}, u32[]{:S(2)}) collective-permute-start(f32[24,2048]{1,0:T(8,128)S(1)} %pad_maximum_fusion.scores), channel_id=1, source_target_pairs={{0,2},{2,0},{4,6},{6,4},{8,10},{10,8},{12,14},{14,12},{16,18},{18,... | collective-permute-start | bytes 589832 | tf_op jit(solution)/shard_map/ppermute | solution.py:41
  55.8 5.7 %collective-permute-start.10 = (f32[24,2048]{1,0:T(8,128)S(1)}, f32[24,2048]{1,0:T(8,128)S(1)}, u32[]{:S(2)}, u32[]{:S(2)}) collective-permute-start(f32[24,2048]{1,0:T(8,128)S(1)} %pad_maximum_fusion.scores), channel_id=1, source_target_pairs={{0,4},{2,6},{4,0},{6,2},{8,12},{10,14},{12,8},{14,10},{16,20},{18,... | collective-permute-start | bytes 589832 | tf_op jit(solution)/shard_map/ppermute | solution.py:41
  56.9 6.7 %collective-permute-start.9 = (f32[24,2048]{1,0:T(8,128)S(1)}, f32[24,2048]{1,0:T(8,128)S(1)}, u32[]{:S(2)}, u32[]{:S(2)}) collective-permute-start(f32[24,2048]{1,0:T(8,128)S(1)} %pad_maximum_fusion.scores), channel_id=1, source_target_pairs={{0,6},{2,4},{4,2},{6,0},{8,14},{10,12},{12,10},{14,8},{16,22},{18,... | collective-permute-start | bytes 589832 | tf_op jit(solution)/shard_map/ppermute | solution.py:41
  64.3 1.3 %collective-permute-start.12 = (f32[24,896]{1,0:T(8,128)S(1)}, f32[24,896]{1,0:T(8,128)S(1)}, u32[]{:S(2)}, u32[]{:S(2)}) collective-permute-start(f32[24,896]{1,0:T(8,128)S(1)} %terms.7.own.held), channel_id=1, source_target_pairs={{0,1},{1,0},{2,3},{3,2},{4,5},{5,4},{6,7},{7,6},{8,9},{9,8},{10,11... | collective-permute-start | bytes 258056 | tf_op jit(solution)/shard_map/ppermute | solution.py:41
  65.9 5.1 %collective-permute-start.15 = (f32[24,128]{1,0:T(8,128)S(1)}, f32[24,128]{1,0:T(8,128)S(1)}, u32[]{:S(2)}, u32[]{:S(2)}) collective-permute-start(f32[24,128]{1,0:T(8,128)S(1)} %get-tuple-element.65), channel_id=1, source_target_pairs={{0,6},{2,4},{4,2},{6,0},{8,14},{10,12},{12,10},{14,8},{16,22},{18,... | collective-permute-start | bytes 36872 | tf_op jit(solution)/shard_map/ppermute | solution.py:41
  68.6 3.7 %collective-permute-start.14 = (f32[24,128]{1,0:T(8,128)S(1)}, f32[24,128]{1,0:T(8,128)S(1)}, u32[]{:S(2)}, u32[]{:S(2)}) collective-permute-start(f32[24,128]{1,0:T(8,128)S(1)} %get-tuple-element.65), channel_id=1, source_target_pairs={{0,4},{2,6},{4,0},{6,2},{8,12},{10,14},{12,8},{14,10},{16,20},{18,... | collective-permute-start | bytes 36872 | tf_op jit(solution)/shard_map/ppermute | solution.py:41
  68.7 3.7 %collective-permute-start.13 = (f32[24,128]{1,0:T(8,128)S(1)}, f32[24,128]{1,0:T(8,128)S(1)}, u32[]{:S(2)}, u32[]{:S(2)}) collective-permute-start(f32[24,128]{1,0:T(8,128)S(1)} %get-tuple-element.65), channel_id=1, source_target_pairs={{0,2},{2,0},{4,6},{6,4},{8,10},{10,8},{12,14},{14,12},{16,18},{18,... | collective-permute-start | bytes 36872 | tf_op jit(solution)/shard_map/ppermute | solution.py:41
  69.4 12.6 %collective-permute-start.24 = (f32[392,128]{1,0:T(8,128)S(1)}, f32[392,128]{1,0:T(8,128)S(1)}, u32[]{:S(2)}, u32[]{:S(2)}) collective-permute-start(f32[392,128]{1,0:T(8,128)S(1)} %get-tuple-element.79), channel_id=1, source_target_pairs={{0,16},{2,18},{4,20},{6,22},{8,24},{10,26},{12,28},{14,30},{16,0},... | collective-permute-start | bytes 602120 | tf_op jit(solution)/shard_map/ppermute | solution.py:41
  72.4 5.9 %collective-permute-start.18 = (f32[24,128]{1,0:T(8,128)S(1)}, f32[24,128]{1,0:T(8,128)S(1)}, u32[]{:S(2)}, u32[]{:S(2)}) collective-permute-start(f32[24,128]{1,0:T(8,128)S(1)} %add_add_fusion.1.refs_0_), channel_id=1, source_target_pairs={{0,24},{2,26},{4,28},{6,30},{8,16},{10,18},{12,20},{14,22},{16,8},... | collective-permute-start | bytes 36872 | tf_op jit(solution)/shard_map/ppermute | solution.py:41
  74.1 8.0 %collective-permute-start.17 = (f32[24,128]{1,0:T(8,128)S(1)}, f32[24,128]{1,0:T(8,128)S(1)}, u32[]{:S(2)}, u32[]{:S(2)}) collective-permute-start(f32[24,128]{1,0:T(8,128)S(1)} %add_add_fusion.1.refs_0_), channel_id=1, source_target_pairs={{0,16},{2,18},{4,20},{6,22},{8,24},{10,26},{12,28},{14,30},{16,0},... | collective-permute-start | bytes 36872 | tf_op jit(solution)/shard_map/ppermute | solution.py:41
  75.4 6.7 %collective-permute-start.16 = (f32[24,128]{1,0:T(8,128)S(1)}, f32[24,128]{1,0:T(8,128)S(1)}, u32[]{:S(2)}, u32[]{:S(2)}) collective-permute-start(f32[24,128]{1,0:T(8,128)S(1)} %add_add_fusion.1.refs_0_), channel_id=1, source_target_pairs={{0,8},{2,10},{4,12},{6,14},{8,0},{10,2},{12,4},{14,6},{16,24},{18,... | collective-permute-start | bytes 36872 | tf_op jit(solution)/shard_map/ppermute | solution.py:41

commit v10 on v9

--- a/solution.py
+++ b/solution.py
@@ -88,18 +88,22 @@
     return begun
 
 
-def scores_finish(plan, begun, start_bf, stats, outs):
+def scores_finish(plan, begun, start_bf, stats, outs, group=1):
     width, total = plan.width, plan.total
     for (chunks, held, copies), out in zip(begun, outs):
-        for j, copy in enumerate(copies):
-            copy.wait()
-            low = j * width
-            part = lax.dot_general(start_bf, held[low : low + width, :], NT, preferred_element_type=F32)
-            part = jnp.where(fresh_lanes(chunks[j], width, total, part.shape[0]), part, 0.0)
-            out[:, j * width : (j + 1) * width] = part
-            lane = lax.broadcasted_iota(jnp.int32, stats.shape, 1)
-            head = jnp.where((lane < 2) & (chunks[j] == plan.count - 1), stats, part[:, :LANES])
-            out[:, j * width : j * width + LANES] = head
+        for base in range(0, len(copies), group):
+            near = range(base, min(base + group, len(copies)))
+            for j in near:
+                copies[j].wait()
+            low, high = near[0] * width, (near[-1] + 1) * width
+            parts = lax.dot_general(start_bf, held[low:high, :], NT, preferred_element_type=F32)
+            for j in near:
+                part = parts[:, j * width - low : (j + 1) * width - low]
+                part = jnp.where(fresh_lanes(chunks[j], width, total, part.shape[0]), part, 0.0)
+                out[:, j * width : (j + 1) * width] = part
+                lane = lax.broadcasted_iota(jnp.int32, stats.shape, 1)
+                head = jnp.where((lane < 2) & (chunks[j] == plan.count - 1), stats, part[:, :LANES])
+                out[:, j * width : j * width + LANES] = head
 
 
 def lead_kernel(plan, digit, ratio, weights, panel, geno, out, held, diag, right, start, start_bf, weighted, stats, *scratch):
@@ -136,7 +140,7 @@
     *outs, sems = refs
     outs, helds = outs[: len(digits)], outs[len(digits) :]
     begun = scores_begin(plan, digits, lax.axis_index("samp"), geno, helds, sems)
-    scores_finish(plan, begun, start_bf[...], stats[...], outs)
+    scores_finish(plan, begun, start_bf[...], stats[...], outs, 2)
 
 
 def terms_kernel(plan, digit, diag, scores, held, *refs):
@@ -192,7 +196,7 @@
     me = lax.axis_index("samp")
     begun = scores_begin(plan, (digit,), me, geno, (held,), sems)
     cross_products(plan, block, me, sizes, diag[1:2, :], variants, weighted, scaled, outs)
-    scores_finish(plan, begun, start_bf[...], stats[...], (out,))
+    scores_finish(plan, begun, start_bf[...], stats[...], (out,), 4)
 
 
 def cross_products(plan, block, me, sizes, mu, variants, weighted, scaled, outs):
@@ -275,22 +279,24 @@
             out[half + j * tall : half + (j + 1) * tall, :] = total[half:, j * wide : (j + 1) * wide]
 
 
-def last_kernel(samples, levels, sizes, diag, start, held, alpha, solved, left, *refs):
-    *ins, solved_out, left_out, way_out, gram_out, way, out, full, sems = refs
-    norms, sums = ins[:levels], ins[levels:]
+def direction_kernel(diag, start, held, left, *refs):
+    *norms, out = refs
+    norm = norms[0][:, :1]
+    for ref in norms[1:]:
+        norm = norm + ref[:, :1]
+    wide = start.shape[1]
+    start_norm = held[:, wide : wide + 1]
+    out[...] = left[...] / diag[0:1, :] + (norm / start_norm) * start[...]
+
+
+def gram_kernel(samples, sizes, alpha, solved, left, *refs):
+    *sums, solved_out, left_out, gram_out, out, full, sems = refs
     copies = fetch(
         [
             pltpu.make_async_copy(solved, solved_out, sems.at[0]),
             pltpu.make_async_copy(left, left_out, sems.at[1]),
         ]
     )
-    norm = norms[0][:, :1]
-    for ref in norms[1:]:
-        norm = norm + ref[:, :1]
-    wide = start.shape[1]
-    start_norm = held[:, wide : wide + 1]
-    way[...] = left[...] / diag[0:1, :] + (norm / start_norm) * start[...]
-    copies += fetch([pltpu.make_async_copy(way, way_out, sems.at[2])])
     me = lax.axis_index("samp")
     count = out.shape[2]
     block = out.shape[1]
@@ -322,7 +328,7 @@
     column = lax.broadcasted_iota(jnp.int32, (block, count), 1)
     same = (column >= low[:, :1]) & (column < high[:, :1])
     out[0] = jnp.where(same, (cross - correction) / samples, 0.0)
-    copies += fetch([pltpu.make_async_copy(out, gram_out, sems.at[3])])
+    copies += fetch([pltpu.make_async_copy(out, gram_out, sems.at[2])])
     for copy in copies:
         copy.wait()
 
@@ -537,20 +543,26 @@
         for one in norms[1:]:
             total = total + one
         norms = [total] + [swap(total, count, d * s) for d in range(1, r)]
+    direction = kernel(
+        direction_kernel,
+        out_shape=full,
+        in_specs=[vmem] * (4 + len(norms)),
+        out_specs=vmem,
+        name="direction",
+    )(diag, start, held, *map(in_vmem, (residual, *norms)))
     gram_shape = (1, block, num_variants)
-    solution, residual, direction, gram = kernel(
-        functools.partial(last_kernel, samples * count, len(norms)),
-        out_shape=[full] * 3 + [jax.ShapeDtypeStruct(gram_shape, F32)],
-        in_specs=[smem] + [vmem] * (6 + len(norms) + len(sums)),
-        out_specs=[hbm] * 4,
+    solution, residual, gram = kernel(
+        functools.partial(gram_kernel, samples * count),
+        out_shape=[full] * 2 + [jax.ShapeDtypeStruct(gram_shape, F32)],
+        in_specs=[smem] + [vmem] * (3 + len(sums)),
+        out_specs=[hbm] * 3,
         scratch_shapes=[
-            VMEM((rows, samples), F32),
             VMEM(gram_shape, F32),
             VMEM((rows, num_variants), F32),
-            pltpu.SemaphoreType.DMA((4,)),
+            pltpu.SemaphoreType.DMA((3,)),
         ],
-        name="last",
-    )(gene_sizes, diag, start, held, *map(in_vmem, (alpha, solution, residual, *norms, *sums)))
+        name="gram",
+    )(gene_sizes, *map(in_vmem, (alpha, solution, residual, *sums)))
     return solution, residual, direction, gram
 
 

time: 84.3 us -> 85.1 us (level)
    pallas_call x1 -> x2, Pallas kernels: 2.06 us -> 2.75 us  [the longest x1 2.03 us: body(): kernel(functools.partial(gram_kernel, samples * count), out_shape=[full]...]
  transfers between devices with their start and end apart: 25 -> 25, of which waited for: 14 -> 14; matrix products, arithmetic and copies ran while one was open for 0% -> 0% of each run, Pallas kernels for 4% -> 5%
where the time goes in v10:
time: 85.1 us; the launch traced here: 85 us
  waiting for transfers between devices  32.5 us (38%)
  starting transfers between devices  32.2 us (38%)
  Pallas kernels  18.8 us (22%)
  between operations  1.4 us (2%)
    ppermute x25, waiting for transfers between devices, swap(): return lax.ppermute(array, axis, [(i, i ^ offset) for i in range(count)])  32.5 us
    ppermute x25, starting transfers between devices, swap(): return lax.ppermute(array, axis, [(i, i ^ offset) for i in range(count)])  32.2 us
    pallas_call x1, Pallas kernels, body(): kernel(functools.partial(cross_kernel, plan, block, 0), out_shape=[payloa...  6.14 us
    pallas_call x1, Pallas kernels, body(): kernel(functools.partial(scores_kernel, plan, digits), out_shape=[payload...  3.85 us
    pallas_call x4, Pallas kernels, body(): kernel(functools.partial(terms_kernel, plan, d), out_shape=VMEM((rows, sa...  2.72 us
    pallas_call x1, Pallas kernels, body(): kernel(functools.partial(lead_kernel, plan, lead), out_shape=[payload, wi...  2.62 us
    pallas_call x1, Pallas kernels, body(): kernel(functools.partial(gram_kernel, samples * count), out_shape=[full]...  2.03 us
  transfers between devices with their start and end apart: 25, of which 14 were waited for; matrix products, arithmetic and copies ran while one was open for 0% of the time, Pallas kernels for 5%

profile of v10, /device:TPU:0, one launch (start us, length us, event | category | flops | bytes accessed | tf_op | source)
XLA Modules:
  0.0 85.0 jit_solution(172858595060857912)
XLA Ops:
  1.3 2.6 %scores_lead.1 = (f32[24,2048]{1,0:T(8,128)S(1)}, bf16[2048,768]{1,0:T(8,128)(2,1)S(1)}, f32[8,768]{1,0:T(8,128)S(1)}, f32[24,768]{1,0:T(8,128)S(1)}, f32[24,768...) custom-call(f32[1]{0:T(128)S(6)} %copy.18.ratio, ...), custom_call_target="tpu_custom_call" | custom-call | tf_op jit(solution)/shard_map/scores_lead/pallas_call | solution.py:392
  3.9 3.8 %scores.1 = (f32[24,2048]{1,0:T(8,128)S(1)}, f32[24,2048]{1,0:T(8,128)S(1)}, bf16[2048,768]{1,0:T(8,128)(2,1)S(1)}, bf16[2048,768]{1,0:T(8,128)(2,1)S(1)}) custom-call(bf16[24,768]{1,0:T(8,128)(2,1)S(1)} %get-tuple-element.53.start_bf, f32[24,128]{1,0:T(8,128)S(1)} %get-tuple-element.51.stats, bf16[8000,768]{1,0:T(8,128)(2,1)} %geno.5), custom_call_target="tpu_custom_call" | custom-call | tf_op jit(solution)/shard_map/scores/pallas_call | solution.py:418
  7.8 6.1 %scores_cross.1 = (f32[24,2048]{1,0:T(8,128)S(1)}, bf16[2048,768]{1,0:T(8,128)(2,1)S(1)}, f32[200,256]{1,0:T(8,128)S(1)}, f32[200,256]{1,0:T(8,128)S(1)}, f32[24...) custom-call(s32[1,24]{1,0:T(1,128)S(1)} %copy-done.1, ...), custom_call_target="tpu_custom_call" | custom-call | tf_op jit(solution)/shard_map/scores_cross/pallas_call | solution.py:440
  14.0 3.0 %collective-permute-start.13 = (f32[224,512]{1,0:T(8,128)S(1)}, f32[224,512]{1,0:T(8,128)S(1)}, u32[]{:S(2)}, u32[]{:S(2)}) collective-permute-start(f32[224,512]{1,0:T(8,128)S(1)} %get-tuple-element.68), channel_id=1, source_target_pairs={{0,2},{2,0},{4,6},{6,4},{8,10},{10,8},{12,14},{14,12},{16,18},{18,... | collective-permute-start | bytes 1376264 | tf_op jit(solution)/shard_map/ppermute | solution.py:41
  17.0 1.5 %collective-permute-start.14 = (f32[224,512]{1,0:T(8,128)S(1)}, f32[224,512]{1,0:T(8,128)S(1)}, u32[]{:S(2)}, u32[]{:S(2)}) collective-permute-start(f32[224,512]{1,0:T(8,128)S(1)} %get-tuple-element.69), channel_id=1, source_target_pairs={{0,4},{2,6},{4,0},{6,2},{8,12},{10,14},{12,8},{14,10},{16,20},{18,... | collective-permute-start | bytes 1376264 | tf_op jit(solution)/shard_map/ppermute | solution.py:41
  18.5 2.0 %collective-permute-start.1 = (f32[24,2048]{1,0:T(8,128)S(1)}, f32[24,2048]{1,0:T(8,128)S(1)}, u32[]{:S(2)}, u32[]{:S(2)}) collective-permute-start(f32[24,2048]{1,0:T(8,128)S(1)} %get-tuple-element.56), channel_id=1, source_target_pairs={{0,4},{2,6},{4,0},{6,2},{8,12},{10,14},{12,8},{14,10},{16,20},{18,... | collective-permute-start | bytes 589832 | tf_op jit(solution)/shard_map/ppermute | solution.py:41
  20.5 1.5 %collective-permute-start = (f32[24,2048]{1,0:T(8,128)S(1)}, f32[24,2048]{1,0:T(8,128)S(1)}, u32[]{:S(2)}, u32[]{:S(2)}) collective-permute-start(f32[24,2048]{1,0:T(8,128)S(1)} %get-tuple-element.52), channel_id=1, source_target_pairs={{0,2},{2,0},{4,6},{6,4},{8,10},{10,8},{12,14},{14,12},{16,18},{18,... | collective-permute-start | bytes 589832 | tf_op jit(solution)/shard_map/ppermute | solution.py:41
  22.0 12.1 %collective-permute-done.2.refs_3_ = f32[24,2048]{1,0:T(8,128)S(1)} collective-permute-done((f32[24,2048]{1,0:T(8,128)S(1)}, f32[24,2048]{1,0:T(8,128)S(1)}, u32[]{:S(2)}, u32[]{:S(2)}) %collective-permute-start.2) | collective-permute-done | bytes 196640 | tf_op jit(solution)/shard_map/ppermute | solution.py:41
  34.1 3.3 %collective-permute-done.1.refs_2_ = f32[24,2048]{1,0:T(8,128)S(1)} collective-permute-done((f32[24,2048]{1,0:T(8,128)S(1)}, f32[24,2048]{1,0:T(8,128)S(1)}, u32[]{:S(2)}, u32[]{:S(2)}) %collective-permute-start.1) | collective-permute-done | bytes 196640 | tf_op jit(solution)/shard_map/ppermute | solution.py:41
  37.4 1.6 %collective-permute-start.3 = (f32[24,512]{1,0:T(8,128)S(1)}, f32[24,512]{1,0:T(8,128)S(1)}, u32[]{:S(2)}, u32[]{:S(2)}) collective-permute-start(f32[24,512]{1,0:T(8,128)S(1)} %get-tuple-element.58), channel_id=1, source_target_pairs={{0,8},{2,10},{4,12},{6,14},{8,0},{10,2},{12,4},{14,6},{16,24},{18,... | collective-permute-start | bytes 147464 | tf_op jit(solution)/shard_map/ppermute | solution.py:41
  39.1 2.6 %collective-permute-start.4 = (f32[24,512]{1,0:T(8,128)S(1)}, f32[24,512]{1,0:T(8,128)S(1)}, u32[]{:S(2)}, u32[]{:S(2)}) collective-permute-start(f32[24,512]{1,0:T(8,128)S(1)} %get-tuple-element.59), channel_id=1, source_target_pairs={{0,16},{2,18},{4,20},{6,22},{8,24},{10,26},{12,28},{14,30},{16,0},... | collective-permute-start | bytes 147464 | tf_op jit(solution)/shard_map/ppermute | solution.py:41
  42.1 1.6 %collective-permute-start.15 = (f32[248,256]{1,0:T(8,128)S(1)}, f32[248,256]{1,0:T(8,128)S(1)}, u32[]{:S(2)}, u32[]{:S(2)}) collective-permute-start(f32[248,256]{1,0:T(8,128)S(1)} %get-tuple-element.76.pass_x), channel_id=1, source_target_pairs={{0,4},{2,6},{4,0},{6,2},{8,12},{10,14},{12,8},{14,10},{16,20},{18,... | collective-permute-start | bytes 761864 | tf_op jit(solution)/shard_map/ppermute | solution.py:41
  44.2 0.9 %collective-permute-done.4 = f32[24,512]{1,0:T(8,128)S(1)} collective-permute-done((f32[24,512]{1,0:T(8,128)S(1)}, f32[24,512]{1,0:T(8,128)S(1)}, u32[]{:S(2)}, u32[]{:S(2)}) %collective-permute-start.4) | collective-permute-done | bytes 49184 | tf_op jit(solution)/shard_map/ppermute | solution.py:41
  45.1 2.4 %collective-permute-done.5 = f32[24,512]{1,0:T(8,128)S(1)} collective-permute-done((f32[24,512]{1,0:T(8,128)S(1)}, f32[24,512]{1,0:T(8,128)S(1)}, u32[]{:S(2)}, u32[]{:S(2)}) %collective-permute-start.5) | collective-permute-done | bytes 49184 | tf_op jit(solution)/shard_map/ppermute | solution.py:41
  48.2 3.8 %collective-permute-start.6 = (f32[24,512]{1,0:T(8,128)S(1)}, f32[24,512]{1,0:T(8,128)S(1)}, u32[]{:S(2)}, u32[]{:S(2)}) collective-permute-start(f32[24,512]{1,0:T(8,128)S(1)} %add_add_fusion), channel_id=1, source_target_pairs={{0,8},{2,10},{4,12},{6,14},{8,0},{10,2},{12,4},{14,6},{16,24},{18,... | collective-permute-start | bytes 147464 | tf_op jit(solution)/shard_map/ppermute | solution.py:41
  52.3 1.8 %collective-permute-done.8 = f32[24,512]{1,0:T(8,128)S(1)} collective-permute-done((f32[24,512]{1,0:T(8,128)S(1)}, f32[24,512]{1,0:T(8,128)S(1)}, u32[]{:S(2)}, u32[]{:S(2)}) %collective-permute-start.8) | collective-permute-done | bytes 49184 | tf_op jit(solution)/shard_map/ppermute | solution.py:41
  54.1 0.8 collective-permute-done.6
  54.9 1.1 %collective-permute-start.11 = (f32[24,2048]{1,0:T(8,128)S(1)}, f32[24,2048]{1,0:T(8,128)S(1)}, u32[]{:S(2)}, u32[]{:S(2)}) collective-permute-start(f32[24,2048]{1,0:T(8,128)S(1)} %pad_maximum_fusion.scores), channel_id=1, source_target_pairs={{0,2},{2,0},{4,6},{6,4},{8,10},{10,8},{12,14},{14,12},{16,18},{18,... | collective-permute-start | bytes 589832 | tf_op jit(solution)/shard_map/ppermute | solution.py:41
  56.0 1.0 %collective-permute-start.10 = (f32[24,2048]{1,0:T(8,128)S(1)}, f32[24,2048]{1,0:T(8,128)S(1)}, u32[]{:S(2)}, u32[]{:S(2)}) collective-permute-start(f32[24,2048]{1,0:T(8,128)S(1)} %pad_maximum_fusion.scores), channel_id=1, source_target_pairs={{0,4},{2,6},{4,0},{6,2},{8,12},{10,14},{12,8},{14,10},{16,20},{18,... | collective-permute-start | bytes 589832 | tf_op jit(solution)/shard_map/ppermute | solution.py:41
  57.0 1.4 %collective-permute-start.9 = (f32[24,2048]{1,0:T(8,128)S(1)}, f32[24,2048]{1,0:T(8,128)S(1)}, u32[]{:S(2)}, u32[]{:S(2)}) collective-permute-start(f32[24,2048]{1,0:T(8,128)S(1)} %pad_maximum_fusion.scores), channel_id=1, source_target_pairs={{0,6},{2,4},{4,2},{6,0},{8,14},{10,12},{12,10},{14,8},{16,22},{18,... | collective-permute-start | bytes 589832 | tf_op jit(solution)/shard_map/ppermute | solution.py:41
  59.1 1.5 %collective-permute-done.11.scores = f32[24,2048]{1,0:T(8,128)S(1)} collective-permute-done((f32[24,2048]{1,0:T(8,128)S(1)}, f32[24,2048]{1,0:T(8,128)S(1)}, u32[]{:S(2)}, u32[]{:S(2)}) %collective-permute-start.11) | collective-permute-done | bytes 196640 | tf_op jit(solution)/shard_map/ppermute | solution.py:41
  62.3 1.4 %collective-permute-done.9.scores = f32[24,2048]{1,0:T(8,128)S(1)} collective-permute-done((f32[24,2048]{1,0:T(8,128)S(1)}, f32[24,2048]{1,0:T(8,128)S(1)}, u32[]{:S(2)}, u32[]{:S(2)}) %collective-permute-start.9) | collective-permute-done | bytes 196640 | tf_op jit(solution)/shard_map/ppermute | solution.py:41
  64.5 1.3 %collective-permute-done.12.other = f32[24,896]{1,0:T(8,128)S(1)} collective-permute-done((f32[24,896]{1,0:T(8,128)S(1)}, f32[24,896]{1,0:T(8,128)S(1)}, u32[]{:S(2)}, u32[]{:S(2)}) %collective-permute-start.12) | collective-permute-done | bytes 86048 | tf_op jit(solution)/shard_map/ppermute | solution.py:41
  66.0 2.7 %collective-permute-start.21 = (f32[24,128]{1,0:T(8,128)S(1)}, f32[24,128]{1,0:T(8,128)S(1)}, u32[]{:S(2)}, u32[]{:S(2)}) collective-permute-start(f32[24,128]{1,0:T(8,128)S(1)} %get-tuple-element.84), channel_id=1, source_target_pairs={{0,6},{2,4},{4,2},{6,0},{8,14},{10,12},{12,10},{14,8},{16,22},{18,... | collective-permute-start | bytes 36872 | tf_op jit(solution)/shard_map/ppermute | solution.py:41
  69.6 1.6 %collective-permute-start.18 = (f32[392,128]{1,0:T(8,128)S(1)}, f32[392,128]{1,0:T(8,128)S(1)}, u32[]{:S(2)}, u32[]{:S(2)}) collective-permute-start(f32[392,128]{1,0:T(8,128)S(1)} %get-tuple-element.81), channel_id=1, source_target_pairs={{0,16},{2,18},{4,20},{6,22},{8,24},{10,26},{12,28},{14,30},{16,0},... | collective-permute-start | bytes 602120 | tf_op jit(solution)/shard_map/ppermute | solution.py:41
  71.2 1.2 %collective-permute-done.20 = f32[24,128]{1,0:T(8,128)S(1)} collective-permute-done((f32[24,128]{1,0:T(8,128)S(1)}, f32[24,128]{1,0:T(8,128)S(1)}, u32[]{:S(2)}, u32[]{:S(2)}) %collective-permute-start.20) | collective-permute-done | bytes 12320 | tf_op jit(solution)/shard_map/ppermute | solution.py:41
  72.5 1.7 %collective-permute-start.24 = (f32[24,128]{1,0:T(8,128)S(1)}, f32[24,128]{1,0:T(8,128)S(1)}, u32[]{:S(2)}, u32[]{:S(2)}) collective-permute-start(f32[24,128]{1,0:T(8,128)S(1)} %add_add_fusion.1.refs_0_), channel_id=1, source_target_pairs={{0,24},{2,26},{4,28},{6,30},{8,16},{10,18},{12,20},{14,22},{16,8},... | collective-permute-start | bytes 36872 | tf_op jit(solution)/shard_map/ppermute | solution.py:41
  74.3 1.3 %collective-permute-start.23 = (f32[24,128]{1,0:T(8,128)S(1)}, f32[24,128]{1,0:T(8,128)S(1)}, u32[]{:S(2)}, u32[]{:S(2)}) collective-permute-start(f32[24,128]{1,0:T(8,128)S(1)} %add_add_fusion.1.refs_0_), channel_id=1, source_target_pairs={{0,16},{2,18},{4,20},{6,22},{8,24},{10,26},{12,28},{14,30},{16,0},... | collective-permute-start | bytes 36872 | tf_op jit(solution)/shard_map/ppermute | solution.py:41
  75.6 1.4 %collective-permute-start.22 = (f32[24,128]{1,0:T(8,128)S(1)}, f32[24,128]{1,0:T(8,128)S(1)}, u32[]{:S(2)}, u32[]{:S(2)}) collective-permute-start(f32[24,128]{1,0:T(8,128)S(1)} %add_add_fusion.1.refs_0_), channel_id=1, source_target_pairs={{0,8},{2,10},{4,12},{6,14},{8,0},{10,2},{12,4},{14,6},{16,24},{18,... | collective-permute-start | bytes 36872 | tf_op jit(solution)/shard_map/ppermute | solution.py:41
  76.9 1.5 %collective-permute-done.24.refs_3_ = f32[24,128]{1,0:T(8,128)S(1)} collective-permute-done((f32[24,128]{1,0:T(8,128)S(1)}, f32[24,128]{1,0:T(8,128)S(1)}, u32[]{:S(2)}, u32[]{:S(2)}) %collective-permute-start.24) | collective-permute-done | bytes 12320 | tf_op jit(solution)/shard_map/ppermute | solution.py:41
  78.4 3.8 %collective-permute-done.23.refs_2_ = f32[24,128]{1,0:T(8,128)S(1)} collective-permute-done((f32[24,128]{1,0:T(8,128)S(1)}, f32[24,128]{1,0:T(8,128)S(1)}, u32[]{:S(2)}, u32[]{:S(2)}) %collective-permute-start.23) | collective-permute-done | bytes 12320 | tf_op jit(solution)/shard_map/ppermute | solution.py:41
  82.9 2.0 %gram.1 = (f32[24,768]{1,0:T(8,128)}, f32[24,768]{1,0:T(8,128)}, f32[1,64,1024]{2,1,0:T(8,128)}) custom-call(s32[1,24]{1,0:T(1,128)S(1)} %copy-done.1, f32[24,128]{1,0:T(8,128)S(1)} %get-tuple-element.65.alpha, f32[24,768]{1,0:T(8,128)S(1)} %get-tuple-element.66.solved, f32[24,768]{1,0:T(8,128)S(1)} %get-tuple-element.67.left, ...), custom_call_target="tpu_custom_call" | custom-call | tf_op jit(solution)/shard_map/gram/pallas_call | solution.py:554
  (39 shorter events, 7.1 us)
Async XLA Ops:
  3.9 3.9 %copy-start = (bf16[1024,768]{1,0:T(8,128)(2,1)S(1)}, bf16[1024,768]{1,0:T(8,128)(2,1)}, u32[]{:S(2)}) copy-start(bf16[1024,768]{1,0:T(8,128)(2,1)} %variants.1) | copy-start | bytes 4718596
  3.9 3.9 %copy-start.1 = (s32[1,24]{1,0:T(1,128)S(1)}, s32[1,24]{1,0:T(1,128)}, u32[]{:S(2)}) copy-start(s32[1,24]{1,0:T(1,128)} %sizes.3) | copy-start | bytes 292
  14.0 27.9 %collective-permute-start.13 = (f32[224,512]{1,0:T(8,128)S(1)}, f32[224,512]{1,0:T(8,128)S(1)}, u32[]{:S(2)}, u32[]{:S(2)}) collective-permute-start(f32[224,512]{1,0:T(8,128)S(1)} %get-tuple-element.68), channel_id=1, source_target_pairs={{0,2},{2,0},{4,6},{6,4},{8,10},{10,8},{12,14},{14,12},{16,18},{18,... | collective-permute-start | bytes 1376264 | tf_op jit(solution)/shard_map/ppermute | solution.py:41
  17.0 24.9 %collective-permute-start.14 = (f32[224,512]{1,0:T(8,128)S(1)}, f32[224,512]{1,0:T(8,128)S(1)}, u32[]{:S(2)}, u32[]{:S(2)}) collective-permute-start(f32[224,512]{1,0:T(8,128)S(1)} %get-tuple-element.69), channel_id=1, source_target_pairs={{0,4},{2,6},{4,0},{6,2},{8,12},{10,14},{12,8},{14,10},{16,20},{18,... | collective-permute-start | bytes 1376264 | tf_op jit(solution)/shard_map/ppermute | solution.py:41
  18.5 15.6 %collective-permute-start.2 = (f32[24,2048]{1,0:T(8,128)S(1)}, f32[24,2048]{1,0:T(8,128)S(1)}, u32[]{:S(2)}, u32[]{:S(2)}) collective-permute-start(f32[24,2048]{1,0:T(8,128)S(1)} %get-tuple-element.49), channel_id=1, source_target_pairs={{0,6},{2,4},{4,2},{6,0},{8,14},{10,12},{12,10},{14,8},{16,22},{18,... | collective-permute-start | bytes 589832 | tf_op jit(solution)/shard_map/ppermute | solution.py:41
  18.5 18.9 %collective-permute-start.1 = (f32[24,2048]{1,0:T(8,128)S(1)}, f32[24,2048]{1,0:T(8,128)S(1)}, u32[]{:S(2)}, u32[]{:S(2)}) collective-permute-start(f32[24,2048]{1,0:T(8,128)S(1)} %get-tuple-element.56), channel_id=1, source_target_pairs={{0,4},{2,6},{4,0},{6,2},{8,12},{10,14},{12,8},{14,10},{16,20},{18,... | collective-permute-start | bytes 589832 | tf_op jit(solution)/shard_map/ppermute | solution.py:41
  20.5 16.9 %collective-permute-start = (f32[24,2048]{1,0:T(8,128)S(1)}, f32[24,2048]{1,0:T(8,128)S(1)}, u32[]{:S(2)}, u32[]{:S(2)}) collective-permute-start(f32[24,2048]{1,0:T(8,128)S(1)} %get-tuple-element.52), channel_id=1, source_target_pairs={{0,2},{2,0},{4,6},{6,4},{8,10},{10,8},{12,14},{14,12},{16,18},{18,... | collective-permute-start | bytes 589832 | tf_op jit(solution)/shard_map/ppermute | solution.py:41
  37.4 6.8 %collective-permute-start.3 = (f32[24,512]{1,0:T(8,128)S(1)}, f32[24,512]{1,0:T(8,128)S(1)}, u32[]{:S(2)}, u32[]{:S(2)}) collective-permute-start(f32[24,512]{1,0:T(8,128)S(1)} %get-tuple-element.58), channel_id=1, source_target_pairs={{0,8},{2,10},{4,12},{6,14},{8,0},{10,2},{12,4},{14,6},{16,24},{18,... | collective-permute-start | bytes 147464 | tf_op jit(solution)/shard_map/ppermute | solution.py:41
  39.1 6.0 %collective-permute-start.4 = (f32[24,512]{1,0:T(8,128)S(1)}, f32[24,512]{1,0:T(8,128)S(1)}, u32[]{:S(2)}, u32[]{:S(2)}) collective-permute-start(f32[24,512]{1,0:T(8,128)S(1)} %get-tuple-element.59), channel_id=1, source_target_pairs={{0,16},{2,18},{4,20},{6,22},{8,24},{10,26},{12,28},{14,30},{16,0},... | collective-permute-start | bytes 147464 | tf_op jit(solution)/shard_map/ppermute | solution.py:41
  41.7 5.9 %collective-permute-start.5 = (f32[24,512]{1,0:T(8,128)S(1)}, f32[24,512]{1,0:T(8,128)S(1)}, u32[]{:S(2)}, u32[]{:S(2)}) collective-permute-start(f32[24,512]{1,0:T(8,128)S(1)} %get-tuple-element.60), channel_id=1, source_target_pairs={{0,24},{2,26},{4,28},{6,30},{8,16},{10,18},{12,20},{14,22},{16,8},... | collective-permute-start | bytes 147464 | tf_op jit(solution)/shard_map/ppermute | solution.py:41
  42.1 10.0 %collective-permute-start.15 = (f32[248,256]{1,0:T(8,128)S(1)}, f32[248,256]{1,0:T(8,128)S(1)}, u32[]{:S(2)}, u32[]{:S(2)}) collective-permute-start(f32[248,256]{1,0:T(8,128)S(1)} %get-tuple-element.76.pass_x), channel_id=1, source_target_pairs={{0,4},{2,6},{4,0},{6,2},{8,12},{10,14},{12,8},{14,10},{16,20},{18,... | collective-permute-start | bytes 761864 | tf_op jit(solution)/shard_map/ppermute | solution.py:41
  43.7 8.4 %collective-permute-start.16 = (f32[248,256]{1,0:T(8,128)S(1)}, f32[248,256]{1,0:T(8,128)S(1)}, u32[]{:S(2)}, u32[]{:S(2)}) collective-permute-start(f32[248,256]{1,0:T(8,128)S(1)} %get-tuple-element.77.pass_y), channel_id=1, source_target_pairs={{0,2},{2,0},{4,6},{6,4},{8,10},{10,8},{12,14},{14,12},{16,18},{18,... | collective-permute-start | bytes 761864 | tf_op jit(solution)/shard_map/ppermute | solution.py:41
  47.6 6.5 %collective-permute-start.8 = (f32[24,512]{1,0:T(8,128)S(1)}, f32[24,512]{1,0:T(8,128)S(1)}, u32[]{:S(2)}, u32[]{:S(2)}) collective-permute-start(f32[24,512]{1,0:T(8,128)S(1)} %add_add_fusion), channel_id=1, source_target_pairs={{0,24},{2,26},{4,28},{6,30},{8,16},{10,18},{12,20},{14,22},{16,8},... | collective-permute-start | bytes 147464 | tf_op jit(solution)/shard_map/ppermute | solution.py:41
  48.2 5.8 %collective-permute-start.7 = (f32[24,512]{1,0:T(8,128)S(1)}, f32[24,512]{1,0:T(8,128)S(1)}, u32[]{:S(2)}, u32[]{:S(2)}) collective-permute-start(f32[24,512]{1,0:T(8,128)S(1)} %add_add_fusion), channel_id=1, source_target_pairs={{0,16},{2,18},{4,20},{6,22},{8,24},{10,26},{12,28},{14,30},{16,0},... | collective-permute-start | bytes 147464 | tf_op jit(solution)/shard_map/ppermute | solution.py:41
  48.2 6.7 %collective-permute-start.6 = (f32[24,512]{1,0:T(8,128)S(1)}, f32[24,512]{1,0:T(8,128)S(1)}, u32[]{:S(2)}, u32[]{:S(2)}) collective-permute-start(f32[24,512]{1,0:T(8,128)S(1)} %add_add_fusion), channel_id=1, source_target_pairs={{0,8},{2,10},{4,12},{6,14},{8,0},{10,2},{12,4},{14,6},{16,24},{18,... | collective-permute-start | bytes 147464 | tf_op jit(solution)/shard_map/ppermute | solution.py:41
  52.2 17.3 %collective-permute-start.17 = (f32[296,256]{1,0:T(8,128)S(1)}, f32[296,256]{1,0:T(8,128)S(1)}, u32[]{:S(2)}, u32[]{:S(2)}) collective-permute-start(f32[296,256]{1,0:T(8,128)S(1)} %get-tuple-element.79), channel_id=1, source_target_pairs={{0,8},{2,10},{4,12},{6,14},{8,0},{10,2},{12,4},{14,6},{16,24},{18,... | collective-permute-start | bytes 909320 | tf_op jit(solution)/shard_map/ppermute | solution.py:41
  54.9 5.7 %collective-permute-start.11 = (f32[24,2048]{1,0:T(8,128)S(1)}, f32[24,2048]{1,0:T(8,128)S(1)}, u32[]{:S(2)}, u32[]{:S(2)}) collective-permute-start(f32[24,2048]{1,0:T(8,128)S(1)} %pad_maximum_fusion.scores), channel_id=1, source_target_pairs={{0,2},{2,0},{4,6},{6,4},{8,10},{10,8},{12,14},{14,12},{16,18},{18,... | collective-permute-start | bytes 589832 | tf_op jit(solution)/shard_map/ppermute | solution.py:41
  56.0 5.7 %collective-permute-start.10 = (f32[24,2048]{1,0:T(8,128)S(1)}, f32[24,2048]{1,0:T(8,128)S(1)}, u32[]{:S(2)}, u32[]{:S(2)}) collective-permute-start(f32[24,2048]{1,0:T(8,128)S(1)} %pad_maximum_fusion.scores), channel_id=1, source_target_pairs={{0,4},{2,6},{4,0},{6,2},{8,12},{10,14},{12,8},{14,10},{16,20},{18,... | collective-permute-start | bytes 589832 | tf_op jit(solution)/shard_map/ppermute | solution.py:41
  57.0 6.7 %collective-permute-start.9 = (f32[24,2048]{1,0:T(8,128)S(1)}, f32[24,2048]{1,0:T(8,128)S(1)}, u32[]{:S(2)}, u32[]{:S(2)}) collective-permute-start(f32[24,2048]{1,0:T(8,128)S(1)} %pad_maximum_fusion.scores), channel_id=1, source_target_pairs={{0,6},{2,4},{4,2},{6,0},{8,14},{10,12},{12,10},{14,8},{16,22},{18,... | collective-permute-start | bytes 589832 | tf_op jit(solution)/shard_map/ppermute | solution.py:41
  64.4 1.3 %collective-permute-start.12 = (f32[24,896]{1,0:T(8,128)S(1)}, f32[24,896]{1,0:T(8,128)S(1)}, u32[]{:S(2)}, u32[]{:S(2)}) collective-permute-start(f32[24,896]{1,0:T(8,128)S(1)} %terms.7.own.held), channel_id=1, source_target_pairs={{0,1},{1,0},{2,3},{3,2},{4,5},{5,4},{6,7},{7,6},{8,9},{9,8},{10,11... | collective-permute-start | bytes 258056 | tf_op jit(solution)/shard_map/ppermute | solution.py:41
  66.0 5.1 %collective-permute-start.21 = (f32[24,128]{1,0:T(8,128)S(1)}, f32[24,128]{1,0:T(8,128)S(1)}, u32[]{:S(2)}, u32[]{:S(2)}) collective-permute-start(f32[24,128]{1,0:T(8,128)S(1)} %get-tuple-element.84), channel_id=1, source_target_pairs={{0,6},{2,4},{4,2},{6,0},{8,14},{10,12},{12,10},{14,8},{16,22},{18,... | collective-permute-start | bytes 36872 | tf_op jit(solution)/shard_map/ppermute | solution.py:41
  68.7 3.7 %collective-permute-start.20 = (f32[24,128]{1,0:T(8,128)S(1)}, f32[24,128]{1,0:T(8,128)S(1)}, u32[]{:S(2)}, u32[]{:S(2)}) collective-permute-start(f32[24,128]{1,0:T(8,128)S(1)} %get-tuple-element.84), channel_id=1, source_target_pairs={{0,4},{2,6},{4,0},{6,2},{8,12},{10,14},{12,8},{14,10},{16,20},{18,... | collective-permute-start | bytes 36872 | tf_op jit(solution)/shard_map/ppermute | solution.py:41
  68.8 3.7 %collective-permute-start.19 = (f32[24,128]{1,0:T(8,128)S(1)}, f32[24,128]{1,0:T(8,128)S(1)}, u32[]{:S(2)}, u32[]{:S(2)}) collective-permute-start(f32[24,128]{1,0:T(8,128)S(1)} %get-tuple-element.84), channel_id=1, source_target_pairs={{0,2},{2,0},{4,6},{6,4},{8,10},{10,8},{12,14},{14,12},{16,18},{18,... | collective-permute-start | bytes 36872 | tf_op jit(solution)/shard_map/ppermute | solution.py:41
  69.6 13.3 %collective-permute-start.18 = (f32[392,128]{1,0:T(8,128)S(1)}, f32[392,128]{1,0:T(8,128)S(1)}, u32[]{:S(2)}, u32[]{:S(2)}) collective-permute-start(f32[392,128]{1,0:T(8,128)S(1)} %get-tuple-element.81), channel_id=1, source_target_pairs={{0,16},{2,18},{4,20},{6,22},{8,24},{10,26},{12,28},{14,30},{16,0},... | collective-permute-start | bytes 602120 | tf_op jit(solution)/shard_map/ppermute | solution.py:41
  72.5 5.9 %collective-permute-start.24 = (f32[24,128]{1,0:T(8,128)S(1)}, f32[24,128]{1,0:T(8,128)S(1)}, u32[]{:S(2)}, u32[]{:S(2)}) collective-permute-start(f32[24,128]{1,0:T(8,128)S(1)} %add_add_fusion.1.refs_0_), channel_id=1, source_target_pairs={{0,24},{2,26},{4,28},{6,30},{8,16},{10,18},{12,20},{14,22},{16,8},... | collective-permute-start | bytes 36872 | tf_op jit(solution)/shard_map/ppermute | solution.py:41
  74.3 8.0 %collective-permute-start.23 = (f32[24,128]{1,0:T(8,128)S(1)}, f32[24,128]{1,0:T(8,128)S(1)}, u32[]{:S(2)}, u32[]{:S(2)}) collective-permute-start(f32[24,128]{1,0:T(8,128)S(1)} %add_add_fusion.1.refs_0_), channel_id=1, source_target_pairs={{0,16},{2,18},{4,20},{6,22},{8,24},{10,26},{12,28},{14,30},{16,0},... | collective-permute-start | bytes 36872 | tf_op jit(solution)/shard_map/ppermute | solution.py:41
  75.6 6.6 %collective-permute-start.22 = (f32[24,128]{1,0:T(8,128)S(1)}, f32[24,128]{1,0:T(8,128)S(1)}, u32[]{:S(2)}, u32[]{:S(2)}) collective-permute-start(f32[24,128]{1,0:T(8,128)S(1)} %add_add_fusion.1.refs_0_), channel_id=1, source_target_pairs={{0,8},{2,10},{4,12},{6,14},{8,0},{10,2},{12,4},{14,6},{16,24},{18,... | collective-permute-start | bytes 36872 | tf_op jit(solution)/shard_map/ppermute | solution.py:41

commit v11 on v10

--- a/solution.py
+++ b/solution.py
@@ -195,32 +195,37 @@
     out, held, *outs, scaled, sems = refs
     me = lax.axis_index("samp")
     begun = scores_begin(plan, (digit,), me, geno, (held,), sems)
-    cross_products(plan, block, me, sizes, diag[1:2, :], variants, weighted, scaled, outs)
-    scores_finish(plan, begun, start_bf[...], stats[...], (out,), 4)
-
-
-def cross_products(plan, block, me, sizes, mu, variants, weighted, scaled, outs):
-    own_x, own_y, pass_x, pass_y, send_x, send_y = outs
-    count = variants.shape[0]
-    half = GENE_MAX // 2
-    quarter = block * len(plan.rest)
+    share_scores(variants, weighted, *outs)
+    pass_x, pass_y, send_x, send_y = outs
+    places = {
+        1: ((send_x, 0), (pass_y, 0)),
+        2: ((pass_x, 0), (send_y, 0)),
+        3: ((send_x, 1), (send_y, 1)),
+    }
+    cross_products(plan, block, me, sizes, diag[1:2, :], variants, scaled, places)
+    scores_finish(plan, begun, start_bf[...], stats[...], (out,))
+
+
+def share_scores(variants, weighted, pass_x, pass_y, send_x, send_y):
     both = lax.dot_general(weighted[...], variants[...], NT, preferred_element_type=F32)
     rows = both.shape[0] // 2
+    quarter = pass_x.shape[1]
+    half = pass_x.shape[0] - 2 * rows
     beta = both[:rows] + both[rows:]
     for at, (sent, kept) in enumerate(((send_x, pass_x), (send_y, pass_y))):
         sent[half:, :] = beta[:, 2 * at * quarter : 2 * (at + 1) * quarter]
         for j in range(2):
             low = (2 * at + j) * quarter
             kept[half + j * rows : half + (j + 1) * rows, :] = beta[:, low : low + quarter]
+
+
+def cross_products(plan, block, me, sizes, mu, variants, scaled, places):
+    count = variants.shape[0]
+    half = GENE_MAX // 2
+    quarter = block * len(plan.rest)
     lane = lax.broadcasted_iota(jnp.int32, (1, quarter), 1)
     column = lax.broadcasted_iota(jnp.int32, (count, quarter), 0)
-    places = (
-        ((own_x, 0), (own_y, 0)),
-        ((send_x, 0), (pass_y, 0)),
-        ((pass_x, 0), (send_y, 0)),
-        ((send_x, 1), (send_y, 1)),
-    )
-    for digit in range(plan.radix):
+    for digit, homes in places.items():
         index = lane
         for j, r in enumerate(plan.rest):
             first = pl.multiple_of((me ^ (digit * plan.stride) ^ r) * block, block)
@@ -230,7 +235,7 @@
         cross = lax.dot_general(variants[...], scaled[...], NT, preferred_element_type=F32)
         low, high = gene_bounds(sizes, index, count)
         cross = jnp.where((column >= low) & (column < high), cross, 0.0)
-        for part, (out, at) in enumerate(places[digit]):
+        for part, (out, at) in enumerate(homes):
             folded = None
             for base in range(part * half, count, GENE_MAX):
                 piece = cross[base : min(base + half, count)]
@@ -238,6 +243,11 @@
                     piece = jnp.concatenate([piece, jnp.zeros((half - piece.shape[0], quarter), F32)], axis=0)
                 folded = piece if folded is None else folded + piece
             out[:half, at * quarter : (at + 1) * quarter] = folded
+
+
+def own_kernel(plan, block, sizes, diag, variants, own_x, own_y, scaled):
+    places = {0: ((own_x, 0), (own_y, 0))}
+    cross_products(plan, block, lax.axis_index("samp"), sizes, diag[1:2, :], variants, scaled, places)
 
 
 def halves_kernel(got_x, got_y, *refs):
@@ -437,17 +447,25 @@
     own_shape = VMEM((half, quarter), F32)
     pass_shape = VMEM((half + 2 * rows, quarter), F32)
     send_shape = VMEM((half + rows, 2 * quarter), F32)
-    sent[0], genos[0], *parts, send_x, send_y = kernel(
+    sent[0], genos[0], pass_x, pass_y, send_x, send_y = kernel(
         functools.partial(cross_kernel, plan, block, 0),
-        out_shape=[payload, window] + [own_shape] * 2 + [pass_shape] * 2 + [send_shape] * 2,
+        out_shape=[payload, window] + [pass_shape] * 2 + [send_shape] * 2,
         in_specs=[smem] + [vmem] * 4 + [hbm, vmem],
-        out_specs=[vmem] * 8,
+        out_specs=[vmem] * 6,
         scratch_shapes=[
             VMEM((quarter, samples), BF16),
             pltpu.SemaphoreType.DMA((len(rest),)),
         ],
         name="scores_cross",
     )(gene_sizes, in_vmem(start_bf), in_vmem(stats), diag, in_vmem(weighted), genotypes, in_vmem(variants))
+    own_x, own_y = kernel(
+        functools.partial(own_kernel, plan, block),
+        out_shape=[own_shape] * 2,
+        in_specs=[smem] + [vmem] * 2,
+        out_specs=[vmem] * 2,
+        scratch_shapes=[VMEM((quarter, samples), BF16)],
+        name="cross_own",
+    )(gene_sizes, diag, in_vmem(variants))
 
     terms = [sent[0]] + [swap(sent[d], count, firsts[d]) for d in range(1, radix)]
     wide = columns
@@ -477,7 +495,7 @@
         out_specs=[vmem] * 4,
         input_output_aliases={2 + i: i for i in range(4)},
         name="halves",
-    )(*map(in_vmem, (got_x, got_y, *parts)))
+    )(*map(in_vmem, (got_x, got_y, own_x, own_y, pass_x, pass_y)))
     got_x, got_y = swap(pass_x, count, firsts[2]), swap(pass_y, count, firsts[1])
     (r, s), deeper = later[0], later[1:]
     wide = quarter // 2

time: 85.1 us -> 86.7 us (1.019)
  waiting for transfers between devices: 32.5 us -> 34.5 us
  starting transfers between devices: 32.2 us -> 30.6 us
  Pallas kernels: 18.8 us -> 19.9 us
    ppermute x25, waiting for transfers between devices: 32.5 us -> 34.5 us  [swap(): return lax.ppermute(array, axis, [(i, i ^ offset) for i in range(count)])]
    ppermute x25, starting transfers between devices: 32.2 us -> 30.6 us  [swap(): return lax.ppermute(array, axis, [(i, i ^ offset) for i in range(count)])]
    pallas_call x0 -> x1, Pallas kernels: none -> 1.21 us  [body(): kernel(functools.partial(own_kernel, plan, block), out_shape=[own_shape]...]
  transfers between devices with their start and end apart: 25 -> 25, of which waited for: 14 -> 12; matrix products, arithmetic and copies ran while one was open for 0% -> 0% of each run, Pallas kernels for 5% -> 6%
where the time goes in v11:
time: 86.7 us; the launch traced here: 86.5 us
  waiting for transfers between devices  34.5 us (40%)
  starting transfers between devices  30.6 us (35%)
  Pallas kernels  19.9 us (23%)
  between operations  1.44 us (2%)
    ppermute x25, waiting for transfers between devices, swap(): return lax.ppermute(array, axis, [(i, i ^ offset) for i in range(count)])  34.5 us
    ppermute x25, starting transfers between devices, swap(): return lax.ppermute(array, axis, [(i, i ^ offset) for i in range(count)])  30.6 us
    pallas_call x1, Pallas kernels, body(): kernel(functools.partial(cross_kernel, plan, block, 0), out_shape=[payloa...  5.96 us
    pallas_call x1, Pallas kernels, body(): kernel(functools.partial(scores_kernel, plan, digits), out_shape=[payload...  3.85 us
    pallas_call x4, Pallas kernels, body(): kernel(functools.partial(terms_kernel, plan, d), out_shape=VMEM((rows, sa...  2.71 us
    pallas_call x1, Pallas kernels, body(): kernel(functools.partial(lead_kernel, plan, lead), out_shape=[payload, wi...  2.62 us
    pallas_call x1, Pallas kernels, body(): kernel(functools.partial(gram_kernel, samples * count), out_shape=[full]...  2.04 us
  transfers between devices with their start and end apart: 25, of which 12 were waited for; matrix products, arithmetic and copies ran while one was open for 0% of the time, Pallas kernels for 6%

profile of v11, /device:TPU:0, one launch (start us, length us, event | category | flops | bytes accessed | tf_op | source)
XLA Modules:
  0.0 86.5 jit_solution(4920175998294973292)
XLA Ops:
  1.3 2.6 %scores_lead.1 = (f32[24,2048]{1,0:T(8,128)S(1)}, bf16[2048,768]{1,0:T(8,128)(2,1)S(1)}, f32[8,768]{1,0:T(8,128)S(1)}, f32[24,768]{1,0:T(8,128)S(1)}, f32[24,768...) custom-call(f32[1]{0:T(128)S(6)} %copy.18.ratio, ...), custom_call_target="tpu_custom_call" | custom-call | tf_op jit(solution)/shard_map/scores_lead/pallas_call | solution.py:402
  3.9 3.8 %scores.1 = (f32[24,2048]{1,0:T(8,128)S(1)}, f32[24,2048]{1,0:T(8,128)S(1)}, bf16[2048,768]{1,0:T(8,128)(2,1)S(1)}, bf16[2048,768]{1,0:T(8,128)(2,1)S(1)}) custom-call(bf16[24,768]{1,0:T(8,128)(2,1)S(1)} %get-tuple-element.53.start_bf, f32[24,128]{1,0:T(8,128)S(1)} %get-tuple-element.51.stats, bf16[8000,768]{1,0:T(8,128)(2,1)} %geno.5), custom_call_target="tpu_custom_call" | custom-call | tf_op jit(solution)/shard_map/scores/pallas_call | solution.py:428
  7.8 6.0 %scores_cross.1 = (f32[24,2048]{1,0:T(8,128)S(1)}, bf16[2048,768]{1,0:T(8,128)(2,1)S(1)}, f32[248,256]{1,0:T(8,128)S(1)}, f32[248,256]{1,0:T(8,128)S(1)}, f32[22...) custom-call(s32[1,24]{1,0:T(1,128)S(1)} %copy-done.1, bf16[24,768]{1,0:T(8,128)(2,1)S(1)} %get-tuple-element.53.start_bf, ...), custom_call_target="tpu_custom_call" | custom-call | tf_op jit(solution)/shard_map/scores_cross/pallas_call | solution.py:450
  13.8 3.0 %collective-permute-start.13 = (f32[224,512]{1,0:T(8,128)S(1)}, f32[224,512]{1,0:T(8,128)S(1)}, u32[]{:S(2)}, u32[]{:S(2)}) collective-permute-start(f32[224,512]{1,0:T(8,128)S(1)} %get-tuple-element.68), channel_id=1, source_target_pairs={{0,2},{2,0},{4,6},{6,4},{8,10},{10,8},{12,14},{14,12},{16,18},{18,... | collective-permute-start | bytes 1376264 | tf_op jit(solution)/shard_map/ppermute | solution.py:41
  16.8 1.5 %collective-permute-start.14 = (f32[224,512]{1,0:T(8,128)S(1)}, f32[224,512]{1,0:T(8,128)S(1)}, u32[]{:S(2)}, u32[]{:S(2)}) collective-permute-start(f32[224,512]{1,0:T(8,128)S(1)} %get-tuple-element.69), channel_id=1, source_target_pairs={{0,4},{2,6},{4,0},{6,2},{8,12},{10,14},{12,8},{14,10},{16,20},{18,... | collective-permute-start | bytes 1376264 | tf_op jit(solution)/shard_map/ppermute | solution.py:41
  18.9 2.9 %collective-permute-start.2 = (f32[24,2048]{1,0:T(8,128)S(1)}, f32[24,2048]{1,0:T(8,128)S(1)}, u32[]{:S(2)}, u32[]{:S(2)}) collective-permute-start(f32[24,2048]{1,0:T(8,128)S(1)} %get-tuple-element.49), channel_id=1, source_target_pairs={{0,6},{2,4},{4,2},{6,0},{8,14},{10,12},{12,10},{14,8},{16,22},{18,... | collective-permute-start | bytes 589832 | tf_op jit(solution)/shard_map/ppermute | solution.py:41
  21.8 10.6 %collective-permute-done.refs_1_ = f32[24,2048]{1,0:T(8,128)S(1)} collective-permute-done((f32[24,2048]{1,0:T(8,128)S(1)}, f32[24,2048]{1,0:T(8,128)S(1)}, u32[]{:S(2)}, u32[]{:S(2)}) %collective-permute-start) | collective-permute-done | bytes 196640 | tf_op jit(solution)/shard_map/ppermute | solution.py:41
  32.4 4.8 %collective-permute-done.1.refs_2_ = f32[24,2048]{1,0:T(8,128)S(1)} collective-permute-done((f32[24,2048]{1,0:T(8,128)S(1)}, f32[24,2048]{1,0:T(8,128)S(1)}, u32[]{:S(2)}, u32[]{:S(2)}) %collective-permute-start.1) | collective-permute-done | bytes 196640 | tf_op jit(solution)/shard_map/ppermute | solution.py:41
  37.3 1.6 %collective-permute-start.3 = (f32[24,512]{1,0:T(8,128)S(1)}, f32[24,512]{1,0:T(8,128)S(1)}, u32[]{:S(2)}, u32[]{:S(2)}) collective-permute-start(f32[24,512]{1,0:T(8,128)S(1)} %get-tuple-element.58), channel_id=1, source_target_pairs={{0,8},{2,10},{4,12},{6,14},{8,0},{10,2},{12,4},{14,6},{16,24},{18,... | collective-permute-start | bytes 147464 | tf_op jit(solution)/shard_map/ppermute | solution.py:41
  38.9 2.6 %collective-permute-start.4 = (f32[24,512]{1,0:T(8,128)S(1)}, f32[24,512]{1,0:T(8,128)S(1)}, u32[]{:S(2)}, u32[]{:S(2)}) collective-permute-start(f32[24,512]{1,0:T(8,128)S(1)} %get-tuple-element.59), channel_id=1, source_target_pairs={{0,16},{2,18},{4,20},{6,22},{8,24},{10,26},{12,28},{14,30},{16,0},... | collective-permute-start | bytes 147464 | tf_op jit(solution)/shard_map/ppermute | solution.py:41
  41.7 1.2 %cross_own.1 = (f32[200,256]{1,0:T(8,128)S(1)}, f32[200,256]{1,0:T(8,128)S(1)}) custom-call(s32[1,24]{1,0:T(1,128)S(1)} %copy-done.1, f32[8,768]{1,0:T(8,128)S(1)} %get-tuple-element.45.diag, bf16[1024,768]{1,0:T(8,128)(2,1)S(1)} %copy-done), custom_call_target="tpu_custom_call" | custom-call | tf_op jit(solution)/shard_map/cross_own/pallas_call | solution.py:461
  43.1 1.6 %collective-permute-start.15 = (f32[248,256]{1,0:T(8,128)S(1)}, f32[248,256]{1,0:T(8,128)S(1)}, u32[]{:S(2)}, u32[]{:S(2)}) collective-permute-start(f32[248,256]{1,0:T(8,128)S(1)} %get-tuple-element.76.pass_x), channel_id=1, source_target_pairs={{0,4},{2,6},{4,0},{6,2},{8,12},{10,14},{12,8},{14,10},{16,20},{18,... | collective-permute-start | bytes 761864 | tf_op jit(solution)/shard_map/ppermute | solution.py:41
  45.3 2.4 %collective-permute-done.5 = f32[24,512]{1,0:T(8,128)S(1)} collective-permute-done((f32[24,512]{1,0:T(8,128)S(1)}, f32[24,512]{1,0:T(8,128)S(1)}, u32[]{:S(2)}, u32[]{:S(2)}) %collective-permute-start.5) | collective-permute-done | bytes 49184 | tf_op jit(solution)/shard_map/ppermute | solution.py:41
  47.8 1.8 %collective-permute-start.7 = (f32[24,512]{1,0:T(8,128)S(1)}, f32[24,512]{1,0:T(8,128)S(1)}, u32[]{:S(2)}, u32[]{:S(2)}) collective-permute-start(f32[24,512]{1,0:T(8,128)S(1)} %add_add_fusion), channel_id=1, source_target_pairs={{0,16},{2,18},{4,20},{6,22},{8,24},{10,26},{12,28},{14,30},{16,0},... | collective-permute-start | bytes 147464 | tf_op jit(solution)/shard_map/ppermute | solution.py:41
  49.5 2.6 %collective-permute-start.8 = (f32[24,512]{1,0:T(8,128)S(1)}, f32[24,512]{1,0:T(8,128)S(1)}, u32[]{:S(2)}, u32[]{:S(2)}) collective-permute-start(f32[24,512]{1,0:T(8,128)S(1)} %add_add_fusion), channel_id=1, source_target_pairs={{0,24},{2,26},{4,28},{6,30},{8,16},{10,18},{12,20},{14,22},{16,8},... | collective-permute-start | bytes 147464 | tf_op jit(solution)/shard_map/ppermute | solution.py:41
  52.4 0.7 collective-permute-done.6
  53.1 2.9 %collective-permute-done.8 = f32[24,512]{1,0:T(8,128)S(1)} collective-permute-done((f32[24,512]{1,0:T(8,128)S(1)}, f32[24,512]{1,0:T(8,128)S(1)}, u32[]{:S(2)}, u32[]{:S(2)}) %collective-permute-start.8) | collective-permute-done | bytes 49184 | tf_op jit(solution)/shard_map/ppermute | solution.py:41
  56.0 1.4 %collective-permute-start.11 = (f32[24,2048]{1,0:T(8,128)S(1)}, f32[24,2048]{1,0:T(8,128)S(1)}, u32[]{:S(2)}, u32[]{:S(2)}) collective-permute-start(f32[24,2048]{1,0:T(8,128)S(1)} %pad_maximum_fusion.scores), channel_id=1, source_target_pairs={{0,2},{2,0},{4,6},{6,4},{8,10},{10,8},{12,14},{14,12},{16,18},{18,... | collective-permute-start | bytes 589832 | tf_op jit(solution)/shard_map/ppermute | solution.py:41
  58.0 1.5 %collective-permute-start.9 = (f32[24,2048]{1,0:T(8,128)S(1)}, f32[24,2048]{1,0:T(8,128)S(1)}, u32[]{:S(2)}, u32[]{:S(2)}) collective-permute-start(f32[24,2048]{1,0:T(8,128)S(1)} %pad_maximum_fusion.scores), channel_id=1, source_target_pairs={{0,6},{2,4},{4,2},{6,0},{8,14},{10,12},{12,10},{14,8},{16,22},{18,... | collective-permute-start | bytes 589832 | tf_op jit(solution)/shard_map/ppermute | solution.py:41
  59.5 0.7 terms.4.refs_0_
  60.2 1.5 %collective-permute-done.11.scores = f32[24,2048]{1,0:T(8,128)S(1)} collective-permute-done((f32[24,2048]{1,0:T(8,128)S(1)}, f32[24,2048]{1,0:T(8,128)S(1)}, u32[]{:S(2)}, u32[]{:S(2)}) %collective-permute-start.11) | collective-permute-done | bytes 196640 | tf_op jit(solution)/shard_map/ppermute | solution.py:41
  62.4 2.7 %collective-permute-done.10.scores = f32[24,2048]{1,0:T(8,128)S(1)} collective-permute-done((f32[24,2048]{1,0:T(8,128)S(1)}, f32[24,2048]{1,0:T(8,128)S(1)}, u32[]{:S(2)}, u32[]{:S(2)}) %collective-permute-start.10) | collective-permute-done | bytes 196640 | tf_op jit(solution)/shard_map/ppermute | solution.py:41
  65.8 0.7 terms.7.own.held
  66.5 1.3 %collective-permute-done.12.other = f32[24,896]{1,0:T(8,128)S(1)} collective-permute-done((f32[24,896]{1,0:T(8,128)S(1)}, f32[24,896]{1,0:T(8,128)S(1)}, u32[]{:S(2)}, u32[]{:S(2)}) %collective-permute-start.12) | collective-permute-done | bytes 86048 | tf_op jit(solution)/shard_map/ppermute | solution.py:41
  68.1 1.9 %collective-permute-start.20 = (f32[24,128]{1,0:T(8,128)S(1)}, f32[24,128]{1,0:T(8,128)S(1)}, u32[]{:S(2)}, u32[]{:S(2)}) collective-permute-start(f32[24,128]{1,0:T(8,128)S(1)} %get-tuple-element.84), channel_id=1, source_target_pairs={{0,4},{2,6},{4,0},{6,2},{8,12},{10,14},{12,8},{14,10},{16,20},{18,... | collective-permute-start | bytes 36872 | tf_op jit(solution)/shard_map/ppermute | solution.py:41
  70.0 1.6 %collective-permute-start.21 = (f32[24,128]{1,0:T(8,128)S(1)}, f32[24,128]{1,0:T(8,128)S(1)}, u32[]{:S(2)}, u32[]{:S(2)}) collective-permute-start(f32[24,128]{1,0:T(8,128)S(1)} %get-tuple-element.84), channel_id=1, source_target_pairs={{0,6},{2,4},{4,2},{6,0},{8,14},{10,12},{12,10},{14,8},{16,22},{18,... | collective-permute-start | bytes 36872 | tf_op jit(solution)/shard_map/ppermute | solution.py:41
  71.9 2.7 %collective-permute-done.21 = f32[24,128]{1,0:T(8,128)S(1)} collective-permute-done((f32[24,128]{1,0:T(8,128)S(1)}, f32[24,128]{1,0:T(8,128)S(1)}, u32[]{:S(2)}, u32[]{:S(2)}) %collective-permute-start.21) | collective-permute-done | bytes 12320 | tf_op jit(solution)/shard_map/ppermute | solution.py:41
  74.8 3.0 %collective-permute-start.23 = (f32[24,128]{1,0:T(8,128)S(1)}, f32[24,128]{1,0:T(8,128)S(1)}, u32[]{:S(2)}, u32[]{:S(2)}) collective-permute-start(f32[24,128]{1,0:T(8,128)S(1)} %add_add_fusion.1.refs_0_), channel_id=1, source_target_pairs={{0,16},{2,18},{4,20},{6,22},{8,24},{10,26},{12,28},{14,30},{16,0},... | collective-permute-start | bytes 36872 | tf_op jit(solution)/shard_map/ppermute | solution.py:41
  77.7 1.3 %collective-permute-start.24 = (f32[24,128]{1,0:T(8,128)S(1)}, f32[24,128]{1,0:T(8,128)S(1)}, u32[]{:S(2)}, u32[]{:S(2)}) collective-permute-start(f32[24,128]{1,0:T(8,128)S(1)} %add_add_fusion.1.refs_0_), channel_id=1, source_target_pairs={{0,24},{2,26},{4,28},{6,30},{8,16},{10,18},{12,20},{14,22},{16,8},... | collective-permute-start | bytes 36872 | tf_op jit(solution)/shard_map/ppermute | solution.py:41
  79.0 4.7 %collective-permute-done.23.refs_2_ = f32[24,128]{1,0:T(8,128)S(1)} collective-permute-done((f32[24,128]{1,0:T(8,128)S(1)}, f32[24,128]{1,0:T(8,128)S(1)}, u32[]{:S(2)}, u32[]{:S(2)}) %collective-permute-start.23) | collective-permute-done | bytes 12320 | tf_op jit(solution)/shard_map/ppermute | solution.py:41
  83.8 0.7 direction.1
  84.5 2.0 %gram.1 = (f32[24,768]{1,0:T(8,128)}, f32[24,768]{1,0:T(8,128)}, f32[1,64,1024]{2,1,0:T(8,128)}) custom-call(s32[1,24]{1,0:T(1,128)S(1)} %copy-done.1, f32[24,128]{1,0:T(8,128)S(1)} %get-tuple-element.65.alpha, f32[24,768]{1,0:T(8,128)S(1)} %get-tuple-element.66.solved, f32[24,768]{1,0:T(8,128)S(1)} %get-tuple-element.67.left, ...), custom_call_target="tpu_custom_call" | custom-call | tf_op jit(solution)/shard_map/gram/pallas_call | solution.py:572
  (40 shorter events, 4.7 us)
Async XLA Ops:
  3.9 3.9 %copy-start = (bf16[1024,768]{1,0:T(8,128)(2,1)S(1)}, bf16[1024,768]{1,0:T(8,128)(2,1)}, u32[]{:S(2)}) copy-start(bf16[1024,768]{1,0:T(8,128)(2,1)} %variants.3) | copy-start | bytes 4718596
  3.9 3.9 %copy-start.1 = (s32[1,24]{1,0:T(1,128)S(1)}, s32[1,24]{1,0:T(1,128)}, u32[]{:S(2)}) copy-start(s32[1,24]{1,0:T(1,128)} %sizes.5) | copy-start | bytes 292
  13.8 29.2 %collective-permute-start.13 = (f32[224,512]{1,0:T(8,128)S(1)}, f32[224,512]{1,0:T(8,128)S(1)}, u32[]{:S(2)}, u32[]{:S(2)}) collective-permute-start(f32[224,512]{1,0:T(8,128)S(1)} %get-tuple-element.68), channel_id=1, source_target_pairs={{0,2},{2,0},{4,6},{6,4},{8,10},{10,8},{12,14},{14,12},{16,18},{18,... | collective-permute-start | bytes 1376264 | tf_op jit(solution)/shard_map/ppermute | solution.py:41
  16.8 26.2 %collective-permute-start.14 = (f32[224,512]{1,0:T(8,128)S(1)}, f32[224,512]{1,0:T(8,128)S(1)}, u32[]{:S(2)}, u32[]{:S(2)}) collective-permute-start(f32[224,512]{1,0:T(8,128)S(1)} %get-tuple-element.69), channel_id=1, source_target_pairs={{0,4},{2,6},{4,0},{6,2},{8,12},{10,14},{12,8},{14,10},{16,20},{18,... | collective-permute-start | bytes 1376264 | tf_op jit(solution)/shard_map/ppermute | solution.py:41
  18.3 14.1 %collective-permute-start = (f32[24,2048]{1,0:T(8,128)S(1)}, f32[24,2048]{1,0:T(8,128)S(1)}, u32[]{:S(2)}, u32[]{:S(2)}) collective-permute-start(f32[24,2048]{1,0:T(8,128)S(1)} %get-tuple-element.52), channel_id=1, source_target_pairs={{0,2},{2,0},{4,6},{6,4},{8,10},{10,8},{12,14},{14,12},{16,18},{18,... | collective-permute-start | bytes 589832 | tf_op jit(solution)/shard_map/ppermute | solution.py:41
  18.9 18.4 %collective-permute-start.1 = (f32[24,2048]{1,0:T(8,128)S(1)}, f32[24,2048]{1,0:T(8,128)S(1)}, u32[]{:S(2)}, u32[]{:S(2)}) collective-permute-start(f32[24,2048]{1,0:T(8,128)S(1)} %get-tuple-element.56), channel_id=1, source_target_pairs={{0,4},{2,6},{4,0},{6,2},{8,12},{10,14},{12,8},{14,10},{16,20},{18,... | collective-permute-start | bytes 589832 | tf_op jit(solution)/shard_map/ppermute | solution.py:41
  18.9 18.3 %collective-permute-start.2 = (f32[24,2048]{1,0:T(8,128)S(1)}, f32[24,2048]{1,0:T(8,128)S(1)}, u32[]{:S(2)}, u32[]{:S(2)}) collective-permute-start(f32[24,2048]{1,0:T(8,128)S(1)} %get-tuple-element.49), channel_id=1, source_target_pairs={{0,6},{2,4},{4,2},{6,0},{8,14},{10,12},{12,10},{14,8},{16,22},{18,... | collective-permute-start | bytes 589832 | tf_op jit(solution)/shard_map/ppermute | solution.py:41
  37.3 8.0 %collective-permute-start.3 = (f32[24,512]{1,0:T(8,128)S(1)}, f32[24,512]{1,0:T(8,128)S(1)}, u32[]{:S(2)}, u32[]{:S(2)}) collective-permute-start(f32[24,512]{1,0:T(8,128)S(1)} %get-tuple-element.58), channel_id=1, source_target_pairs={{0,8},{2,10},{4,12},{6,14},{8,0},{10,2},{12,4},{14,6},{16,24},{18,... | collective-permute-start | bytes 147464 | tf_op jit(solution)/shard_map/ppermute | solution.py:41
  38.9 6.4 %collective-permute-start.4 = (f32[24,512]{1,0:T(8,128)S(1)}, f32[24,512]{1,0:T(8,128)S(1)}, u32[]{:S(2)}, u32[]{:S(2)}) collective-permute-start(f32[24,512]{1,0:T(8,128)S(1)} %get-tuple-element.59), channel_id=1, source_target_pairs={{0,16},{2,18},{4,20},{6,22},{8,24},{10,26},{12,28},{14,30},{16,0},... | collective-permute-start | bytes 147464 | tf_op jit(solution)/shard_map/ppermute | solution.py:41
  41.5 6.2 %collective-permute-start.5 = (f32[24,512]{1,0:T(8,128)S(1)}, f32[24,512]{1,0:T(8,128)S(1)}, u32[]{:S(2)}, u32[]{:S(2)}) collective-permute-start(f32[24,512]{1,0:T(8,128)S(1)} %get-tuple-element.60), channel_id=1, source_target_pairs={{0,24},{2,26},{4,28},{6,30},{8,16},{10,18},{12,20},{14,22},{16,8},... | collective-permute-start | bytes 147464 | tf_op jit(solution)/shard_map/ppermute | solution.py:41
  43.1 9.0 %collective-permute-start.15 = (f32[248,256]{1,0:T(8,128)S(1)}, f32[248,256]{1,0:T(8,128)S(1)}, u32[]{:S(2)}, u32[]{:S(2)}) collective-permute-start(f32[248,256]{1,0:T(8,128)S(1)} %get-tuple-element.76.pass_x), channel_id=1, source_target_pairs={{0,4},{2,6},{4,0},{6,2},{8,12},{10,14},{12,8},{14,10},{16,20},{18,... | collective-permute-start | bytes 761864 | tf_op jit(solution)/shard_map/ppermute | solution.py:41
  44.7 7.4 %collective-permute-start.16 = (f32[248,256]{1,0:T(8,128)S(1)}, f32[248,256]{1,0:T(8,128)S(1)}, u32[]{:S(2)}, u32[]{:S(2)}) collective-permute-start(f32[248,256]{1,0:T(8,128)S(1)} %get-tuple-element.77.pass_y), channel_id=1, source_target_pairs={{0,2},{2,0},{4,6},{6,4},{8,10},{10,8},{12,14},{14,12},{16,18},{18,... | collective-permute-start | bytes 761864 | tf_op jit(solution)/shard_map/ppermute | solution.py:41
  47.7 5.4 %collective-permute-start.6 = (f32[24,512]{1,0:T(8,128)S(1)}, f32[24,512]{1,0:T(8,128)S(1)}, u32[]{:S(2)}, u32[]{:S(2)}) collective-permute-start(f32[24,512]{1,0:T(8,128)S(1)} %add_add_fusion), channel_id=1, source_target_pairs={{0,8},{2,10},{4,12},{6,14},{8,0},{10,2},{12,4},{14,6},{16,24},{18,... | collective-permute-start | bytes 147464 | tf_op jit(solution)/shard_map/ppermute | solution.py:41
  47.8 5.3 %collective-permute-start.7 = (f32[24,512]{1,0:T(8,128)S(1)}, f32[24,512]{1,0:T(8,128)S(1)}, u32[]{:S(2)}, u32[]{:S(2)}) collective-permute-start(f32[24,512]{1,0:T(8,128)S(1)} %add_add_fusion), channel_id=1, source_target_pairs={{0,16},{2,18},{4,20},{6,22},{8,24},{10,26},{12,28},{14,30},{16,0},... | collective-permute-start | bytes 147464 | tf_op jit(solution)/shard_map/ppermute | solution.py:41
  49.5 6.4 %collective-permute-start.8 = (f32[24,512]{1,0:T(8,128)S(1)}, f32[24,512]{1,0:T(8,128)S(1)}, u32[]{:S(2)}, u32[]{:S(2)}) collective-permute-start(f32[24,512]{1,0:T(8,128)S(1)} %add_add_fusion), channel_id=1, source_target_pairs={{0,24},{2,26},{4,28},{6,30},{8,16},{10,18},{12,20},{14,22},{16,8},... | collective-permute-start | bytes 147464 | tf_op jit(solution)/shard_map/ppermute | solution.py:41
  52.3 19.3 %collective-permute-start.17 = (f32[296,256]{1,0:T(8,128)S(1)}, f32[296,256]{1,0:T(8,128)S(1)}, u32[]{:S(2)}, u32[]{:S(2)}) collective-permute-start(f32[296,256]{1,0:T(8,128)S(1)} %get-tuple-element.79), channel_id=1, source_target_pairs={{0,8},{2,10},{4,12},{6,14},{8,0},{10,2},{12,4},{14,6},{16,24},{18,... | collective-permute-start | bytes 909320 | tf_op jit(solution)/shard_map/ppermute | solution.py:41
  56.0 5.7 %collective-permute-start.11 = (f32[24,2048]{1,0:T(8,128)S(1)}, f32[24,2048]{1,0:T(8,128)S(1)}, u32[]{:S(2)}, u32[]{:S(2)}) collective-permute-start(f32[24,2048]{1,0:T(8,128)S(1)} %pad_maximum_fusion.scores), channel_id=1, source_target_pairs={{0,2},{2,0},{4,6},{6,4},{8,10},{10,8},{12,14},{14,12},{16,18},{18,... | collective-permute-start | bytes 589832 | tf_op jit(solution)/shard_map/ppermute | solution.py:41
  57.4 7.8 %collective-permute-start.10 = (f32[24,2048]{1,0:T(8,128)S(1)}, f32[24,2048]{1,0:T(8,128)S(1)}, u32[]{:S(2)}, u32[]{:S(2)}) collective-permute-start(f32[24,2048]{1,0:T(8,128)S(1)} %pad_maximum_fusion.scores), channel_id=1, source_target_pairs={{0,4},{2,6},{4,0},{6,2},{8,12},{10,14},{12,8},{14,10},{16,20},{18,... | collective-permute-start | bytes 589832 | tf_op jit(solution)/shard_map/ppermute | solution.py:41
  58.0 7.8 %collective-permute-start.9 = (f32[24,2048]{1,0:T(8,128)S(1)}, f32[24,2048]{1,0:T(8,128)S(1)}, u32[]{:S(2)}, u32[]{:S(2)}) collective-permute-start(f32[24,2048]{1,0:T(8,128)S(1)} %pad_maximum_fusion.scores), channel_id=1, source_target_pairs={{0,6},{2,4},{4,2},{6,0},{8,14},{10,12},{12,10},{14,8},{16,22},{18,... | collective-permute-start | bytes 589832 | tf_op jit(solution)/shard_map/ppermute | solution.py:41
  66.5 1.3 %collective-permute-start.12 = (f32[24,896]{1,0:T(8,128)S(1)}, f32[24,896]{1,0:T(8,128)S(1)}, u32[]{:S(2)}, u32[]{:S(2)}) collective-permute-start(f32[24,896]{1,0:T(8,128)S(1)} %terms.7.own.held), channel_id=1, source_target_pairs={{0,1},{1,0},{2,3},{3,2},{4,5},{5,4},{6,7},{7,6},{8,9},{9,8},{10,11... | collective-permute-start | bytes 258056 | tf_op jit(solution)/shard_map/ppermute | solution.py:41
  68.1 3.7 %collective-permute-start.19 = (f32[24,128]{1,0:T(8,128)S(1)}, f32[24,128]{1,0:T(8,128)S(1)}, u32[]{:S(2)}, u32[]{:S(2)}) collective-permute-start(f32[24,128]{1,0:T(8,128)S(1)} %get-tuple-element.84), channel_id=1, source_target_pairs={{0,2},{2,0},{4,6},{6,4},{8,10},{10,8},{12,14},{14,12},{16,18},{18,... | collective-permute-start | bytes 36872 | tf_op jit(solution)/shard_map/ppermute | solution.py:41
  68.1 3.8 %collective-permute-start.20 = (f32[24,128]{1,0:T(8,128)S(1)}, f32[24,128]{1,0:T(8,128)S(1)}, u32[]{:S(2)}, u32[]{:S(2)}) collective-permute-start(f32[24,128]{1,0:T(8,128)S(1)} %get-tuple-element.84), channel_id=1, source_target_pairs={{0,4},{2,6},{4,0},{6,2},{8,12},{10,14},{12,8},{14,10},{16,20},{18,... | collective-permute-start | bytes 36872 | tf_op jit(solution)/shard_map/ppermute | solution.py:41
  70.0 4.6 %collective-permute-start.21 = (f32[24,128]{1,0:T(8,128)S(1)}, f32[24,128]{1,0:T(8,128)S(1)}, u32[]{:S(2)}, u32[]{:S(2)}) collective-permute-start(f32[24,128]{1,0:T(8,128)S(1)} %get-tuple-element.84), channel_id=1, source_target_pairs={{0,6},{2,4},{4,2},{6,0},{8,14},{10,12},{12,10},{14,8},{16,22},{18,... | collective-permute-start | bytes 36872 | tf_op jit(solution)/shard_map/ppermute | solution.py:41
  71.7 12.8 %collective-permute-start.18 = (f32[392,128]{1,0:T(8,128)S(1)}, f32[392,128]{1,0:T(8,128)S(1)}, u32[]{:S(2)}, u32[]{:S(2)}) collective-permute-start(f32[392,128]{1,0:T(8,128)S(1)} %get-tuple-element.81), channel_id=1, source_target_pairs={{0,16},{2,18},{4,20},{6,22},{8,24},{10,26},{12,28},{14,30},{16,0},... | collective-permute-start | bytes 602120 | tf_op jit(solution)/shard_map/ppermute | solution.py:41
  74.6 4.4 %collective-permute-start.22 = (f32[24,128]{1,0:T(8,128)S(1)}, f32[24,128]{1,0:T(8,128)S(1)}, u32[]{:S(2)}, u32[]{:S(2)}) collective-permute-start(f32[24,128]{1,0:T(8,128)S(1)} %add_add_fusion.1.refs_0_), channel_id=1, source_target_pairs={{0,8},{2,10},{4,12},{6,14},{8,0},{10,2},{12,4},{14,6},{16,24},{18,... | collective-permute-start | bytes 36872 | tf_op jit(solution)/shard_map/ppermute | solution.py:41
  74.8 9.0 %collective-permute-start.23 = (f32[24,128]{1,0:T(8,128)S(1)}, f32[24,128]{1,0:T(8,128)S(1)}, u32[]{:S(2)}, u32[]{:S(2)}) collective-permute-start(f32[24,128]{1,0:T(8,128)S(1)} %add_add_fusion.1.refs_0_), channel_id=1, source_target_pairs={{0,16},{2,18},{4,20},{6,22},{8,24},{10,26},{12,28},{14,30},{16,0},... | collective-permute-start | bytes 36872 | tf_op jit(solution)/shard_map/ppermute | solution.py:41
  77.7 6.0 %collective-permute-start.24 = (f32[24,128]{1,0:T(8,128)S(1)}, f32[24,128]{1,0:T(8,128)S(1)}, u32[]{:S(2)}, u32[]{:S(2)}) collective-permute-start(f32[24,128]{1,0:T(8,128)S(1)} %add_add_fusion.1.refs_0_), channel_id=1, source_target_pairs={{0,24},{2,26},{4,28},{6,30},{8,16},{10,18},{12,20},{14,22},{16,8},... | collective-permute-start | bytes 36872 | tf_op jit(solution)/shard_map/ppermute | solution.py:41

commit v12 on v11

--- a/solution.py
+++ b/solution.py
@@ -324,21 +324,25 @@
     first = me * block
     window = max(block, LANES)
     base = pl.multiple_of(first // window * window, window)
-    wide = lax.dot_general(
-        full[:, pl.ds(base, window)],
-        full[...],
-        (((0,), (0,)), ((), ())),
-        precision=lax.Precision.HIGHEST,
-        preferred_element_type=F32,
-    )
-    correction = wide[:block]
+    near = full[:, pl.ds(base, window)]
+    mine = near[:, :block]
     for step in range(1, window // block):
-        correction = jnp.where(first - base == step * block, wide[step * block : (step + 1) * block], correction)
+        mine = jnp.where(first - base == step * block, near[:, step * block : (step + 1) * block], mine)
     low, high = gene_bounds(sizes, first + lax.broadcasted_iota(jnp.int32, (block, LANES), 0), count)
-    column = lax.broadcasted_iota(jnp.int32, (block, count), 1)
-    same = (column >= low[:, :1]) & (column < high[:, :1])
-    out[0] = jnp.where(same, (cross - correction) / samples, 0.0)
-    copies += fetch([pltpu.make_async_copy(out, gram_out, sems.at[2])])
+    wide = count // 2
+    for at in range(2):
+        here = slice(at * wide, (at + 1) * wide)
+        correction = lax.dot_general(
+            mine,
+            full[:, here],
+            (((0,), (0,)), ((), ())),
+            precision=lax.Precision.HIGHEST,
+            preferred_element_type=F32,
+        )
+        column = lax.broadcasted_iota(jnp.int32, (block, wide), 1) + at * wide
+        same = (column >= low[:, :1]) & (column < high[:, :1])
+        out[0, :, here] = jnp.where(same, (cross[:, here] - correction) / samples, 0.0)
+        copies += fetch([pltpu.make_async_copy(out.at[:, :, here], gram_out.at[:, :, here], sems.at[2 + at])])
     for copy in copies:
         copy.wait()
 
@@ -577,7 +581,7 @@
         scratch_shapes=[
             VMEM(gram_shape, F32),
             VMEM((rows, num_variants), F32),
-            pltpu.SemaphoreType.DMA((3,)),
+            pltpu.SemaphoreType.DMA((4,)),
         ],
         name="gram",
     )(gene_sizes, *map(in_vmem, (alpha, solution, residual, *sums)))

time: 86.7 us -> 86.6 us (level)
  no operation moved by 1% of the time
where the time goes in v12:
time: 86.6 us; the launch traced here: 86.4 us
  waiting for transfers between devices  34.5 us (40%)
  starting transfers between devices  30.6 us (35%)
  Pallas kernels  19.8 us (23%)
  between operations  1.44 us (2%)
    ppermute x25, waiting for transfers between devices, swap(): return lax.ppermute(array, axis, [(i, i ^ offset) for i in range(count)])  34.5 us
    ppermute x25, starting transfers between devices, swap(): return lax.ppermute(array, axis, [(i, i ^ offset) for i in range(count)])  30.6 us
    pallas_call x1, Pallas kernels, body(): kernel(functools.partial(cross_kernel, plan, block, 0), out_shape=[payloa...  5.96 us
    pallas_call x1, Pallas kernels, body(): kernel(functools.partial(scores_kernel, plan, digits), out_shape=[payload...  3.85 us
    pallas_call x4, Pallas kernels, body(): kernel(functools.partial(terms_kernel, plan, d), out_shape=VMEM((rows, sa...  2.71 us
    pallas_call x1, Pallas kernels, body(): kernel(functools.partial(lead_kernel, plan, lead), out_shape=[payload, wi...  2.62 us
    pallas_call x1, Pallas kernels, body(): kernel(functools.partial(gram_kernel, samples * count), out_shape=[full]...  1.94 us
  transfers between devices with their start and end apart: 25, of which 12 were waited for; matrix products, arithmetic and copies ran while one was open for 0% of the time, Pallas kernels for 6%

profile of v12, /device:TPU:0, one launch (start us, length us, event | category | flops | bytes accessed | tf_op | source)
XLA Modules:
  0.0 86.4 jit_solution(15598948136395805669)
XLA Ops:
  1.3 2.6 %scores_lead.1 = (f32[24,2048]{1,0:T(8,128)S(1)}, bf16[2048,768]{1,0:T(8,128)(2,1)S(1)}, f32[8,768]{1,0:T(8,128)S(1)}, f32[24,768]{1,0:T(8,128)S(1)}, f32[24,768...) custom-call(f32[1]{0:T(128)S(6)} %copy.18.ratio, ...), custom_call_target="tpu_custom_call" | custom-call | tf_op jit(solution)/shard_map/scores_lead/pallas_call | solution.py:406
  3.9 3.8 %scores.1 = (f32[24,2048]{1,0:T(8,128)S(1)}, f32[24,2048]{1,0:T(8,128)S(1)}, bf16[2048,768]{1,0:T(8,128)(2,1)S(1)}, bf16[2048,768]{1,0:T(8,128)(2,1)S(1)}) custom-call(bf16[24,768]{1,0:T(8,128)(2,1)S(1)} %get-tuple-element.53.start_bf, f32[24,128]{1,0:T(8,128)S(1)} %get-tuple-element.51.stats, bf16[8000,768]{1,0:T(8,128)(2,1)} %geno.5), custom_call_target="tpu_custom_call" | custom-call | tf_op jit(solution)/shard_map/scores/pallas_call | solution.py:432
  7.8 6.0 %scores_cross.1 = (f32[24,2048]{1,0:T(8,128)S(1)}, bf16[2048,768]{1,0:T(8,128)(2,1)S(1)}, f32[248,256]{1,0:T(8,128)S(1)}, f32[248,256]{1,0:T(8,128)S(1)}, f32[22...) custom-call(s32[1,24]{1,0:T(1,128)S(1)} %copy-done.1, bf16[24,768]{1,0:T(8,128)(2,1)S(1)} %get-tuple-element.53.start_bf, ...), custom_call_target="tpu_custom_call" | custom-call | tf_op jit(solution)/shard_map/scores_cross/pallas_call | solution.py:454
  13.8 3.0 %collective-permute-start.13 = (f32[224,512]{1,0:T(8,128)S(1)}, f32[224,512]{1,0:T(8,128)S(1)}, u32[]{:S(2)}, u32[]{:S(2)}) collective-permute-start(f32[224,512]{1,0:T(8,128)S(1)} %get-tuple-element.68), channel_id=1, source_target_pairs={{0,2},{2,0},{4,6},{6,4},{8,10},{10,8},{12,14},{14,12},{16,18},{18,... | collective-permute-start | bytes 1376264 | tf_op jit(solution)/shard_map/ppermute | solution.py:41
  16.8 1.5 %collective-permute-start.14 = (f32[224,512]{1,0:T(8,128)S(1)}, f32[224,512]{1,0:T(8,128)S(1)}, u32[]{:S(2)}, u32[]{:S(2)}) collective-permute-start(f32[224,512]{1,0:T(8,128)S(1)} %get-tuple-element.69), channel_id=1, source_target_pairs={{0,4},{2,6},{4,0},{6,2},{8,12},{10,14},{12,8},{14,10},{16,20},{18,... | collective-permute-start | bytes 1376264 | tf_op jit(solution)/shard_map/ppermute | solution.py:41
  18.9 2.9 %collective-permute-start.2 = (f32[24,2048]{1,0:T(8,128)S(1)}, f32[24,2048]{1,0:T(8,128)S(1)}, u32[]{:S(2)}, u32[]{:S(2)}) collective-permute-start(f32[24,2048]{1,0:T(8,128)S(1)} %get-tuple-element.49), channel_id=1, source_target_pairs={{0,6},{2,4},{4,2},{6,0},{8,14},{10,12},{12,10},{14,8},{16,22},{18,... | collective-permute-start | bytes 589832 | tf_op jit(solution)/shard_map/ppermute | solution.py:41
  21.8 10.6 %collective-permute-done.refs_1_ = f32[24,2048]{1,0:T(8,128)S(1)} collective-permute-done((f32[24,2048]{1,0:T(8,128)S(1)}, f32[24,2048]{1,0:T(8,128)S(1)}, u32[]{:S(2)}, u32[]{:S(2)}) %collective-permute-start) | collective-permute-done | bytes 196640 | tf_op jit(solution)/shard_map/ppermute | solution.py:41
  32.4 4.8 %collective-permute-done.1.refs_2_ = f32[24,2048]{1,0:T(8,128)S(1)} collective-permute-done((f32[24,2048]{1,0:T(8,128)S(1)}, f32[24,2048]{1,0:T(8,128)S(1)}, u32[]{:S(2)}, u32[]{:S(2)}) %collective-permute-start.1) | collective-permute-done | bytes 196640 | tf_op jit(solution)/shard_map/ppermute | solution.py:41
  37.3 1.6 %collective-permute-start.3 = (f32[24,512]{1,0:T(8,128)S(1)}, f32[24,512]{1,0:T(8,128)S(1)}, u32[]{:S(2)}, u32[]{:S(2)}) collective-permute-start(f32[24,512]{1,0:T(8,128)S(1)} %get-tuple-element.58), channel_id=1, source_target_pairs={{0,8},{2,10},{4,12},{6,14},{8,0},{10,2},{12,4},{14,6},{16,24},{18,... | collective-permute-start | bytes 147464 | tf_op jit(solution)/shard_map/ppermute | solution.py:41
  38.9 2.6 %collective-permute-start.4 = (f32[24,512]{1,0:T(8,128)S(1)}, f32[24,512]{1,0:T(8,128)S(1)}, u32[]{:S(2)}, u32[]{:S(2)}) collective-permute-start(f32[24,512]{1,0:T(8,128)S(1)} %get-tuple-element.59), channel_id=1, source_target_pairs={{0,16},{2,18},{4,20},{6,22},{8,24},{10,26},{12,28},{14,30},{16,0},... | collective-permute-start | bytes 147464 | tf_op jit(solution)/shard_map/ppermute | solution.py:41
  41.7 1.2 %cross_own.1 = (f32[200,256]{1,0:T(8,128)S(1)}, f32[200,256]{1,0:T(8,128)S(1)}) custom-call(s32[1,24]{1,0:T(1,128)S(1)} %copy-done.1, f32[8,768]{1,0:T(8,128)S(1)} %get-tuple-element.45.diag, bf16[1024,768]{1,0:T(8,128)(2,1)S(1)} %copy-done), custom_call_target="tpu_custom_call" | custom-call | tf_op jit(solution)/shard_map/cross_own/pallas_call | solution.py:465
  43.1 1.6 %collective-permute-start.15 = (f32[248,256]{1,0:T(8,128)S(1)}, f32[248,256]{1,0:T(8,128)S(1)}, u32[]{:S(2)}, u32[]{:S(2)}) collective-permute-start(f32[248,256]{1,0:T(8,128)S(1)} %get-tuple-element.76.pass_x), channel_id=1, source_target_pairs={{0,4},{2,6},{4,0},{6,2},{8,12},{10,14},{12,8},{14,10},{16,20},{18,... | collective-permute-start | bytes 761864 | tf_op jit(solution)/shard_map/ppermute | solution.py:41
  45.3 2.4 %collective-permute-done.5 = f32[24,512]{1,0:T(8,128)S(1)} collective-permute-done((f32[24,512]{1,0:T(8,128)S(1)}, f32[24,512]{1,0:T(8,128)S(1)}, u32[]{:S(2)}, u32[]{:S(2)}) %collective-permute-start.5) | collective-permute-done | bytes 49184 | tf_op jit(solution)/shard_map/ppermute | solution.py:41
  47.8 1.8 %collective-permute-start.7 = (f32[24,512]{1,0:T(8,128)S(1)}, f32[24,512]{1,0:T(8,128)S(1)}, u32[]{:S(2)}, u32[]{:S(2)}) collective-permute-start(f32[24,512]{1,0:T(8,128)S(1)} %add_add_fusion), channel_id=1, source_target_pairs={{0,16},{2,18},{4,20},{6,22},{8,24},{10,26},{12,28},{14,30},{16,0},... | collective-permute-start | bytes 147464 | tf_op jit(solution)/shard_map/ppermute | solution.py:41
  49.5 2.6 %collective-permute-start.8 = (f32[24,512]{1,0:T(8,128)S(1)}, f32[24,512]{1,0:T(8,128)S(1)}, u32[]{:S(2)}, u32[]{:S(2)}) collective-permute-start(f32[24,512]{1,0:T(8,128)S(1)} %add_add_fusion), channel_id=1, source_target_pairs={{0,24},{2,26},{4,28},{6,30},{8,16},{10,18},{12,20},{14,22},{16,8},... | collective-permute-start | bytes 147464 | tf_op jit(solution)/shard_map/ppermute | solution.py:41
  52.4 0.7 collective-permute-done.6
  53.1 2.9 %collective-permute-done.8 = f32[24,512]{1,0:T(8,128)S(1)} collective-permute-done((f32[24,512]{1,0:T(8,128)S(1)}, f32[24,512]{1,0:T(8,128)S(1)}, u32[]{:S(2)}, u32[]{:S(2)}) %collective-permute-start.8) | collective-permute-done | bytes 49184 | tf_op jit(solution)/shard_map/ppermute | solution.py:41
  56.0 1.4 %collective-permute-start.11 = (f32[24,2048]{1,0:T(8,128)S(1)}, f32[24,2048]{1,0:T(8,128)S(1)}, u32[]{:S(2)}, u32[]{:S(2)}) collective-permute-start(f32[24,2048]{1,0:T(8,128)S(1)} %pad_maximum_fusion.scores), channel_id=1, source_target_pairs={{0,2},{2,0},{4,6},{6,4},{8,10},{10,8},{12,14},{14,12},{16,18},{18,... | collective-permute-start | bytes 589832 | tf_op jit(solution)/shard_map/ppermute | solution.py:41
  58.0 1.5 %collective-permute-start.9 = (f32[24,2048]{1,0:T(8,128)S(1)}, f32[24,2048]{1,0:T(8,128)S(1)}, u32[]{:S(2)}, u32[]{:S(2)}) collective-permute-start(f32[24,2048]{1,0:T(8,128)S(1)} %pad_maximum_fusion.scores), channel_id=1, source_target_pairs={{0,6},{2,4},{4,2},{6,0},{8,14},{10,12},{12,10},{14,8},{16,22},{18,... | collective-permute-start | bytes 589832 | tf_op jit(solution)/shard_map/ppermute | solution.py:41
  59.5 0.7 terms.4.refs_0_
  60.2 1.5 %collective-permute-done.11.scores = f32[24,2048]{1,0:T(8,128)S(1)} collective-permute-done((f32[24,2048]{1,0:T(8,128)S(1)}, f32[24,2048]{1,0:T(8,128)S(1)}, u32[]{:S(2)}, u32[]{:S(2)}) %collective-permute-start.11) | collective-permute-done | bytes 196640 | tf_op jit(solution)/shard_map/ppermute | solution.py:41
  62.4 2.7 %collective-permute-done.10.scores = f32[24,2048]{1,0:T(8,128)S(1)} collective-permute-done((f32[24,2048]{1,0:T(8,128)S(1)}, f32[24,2048]{1,0:T(8,128)S(1)}, u32[]{:S(2)}, u32[]{:S(2)}) %collective-permute-start.10) | collective-permute-done | bytes 196640 | tf_op jit(solution)/shard_map/ppermute | solution.py:41
  65.8 0.7 terms.7.own.held
  66.5 1.3 %collective-permute-done.12.other = f32[24,896]{1,0:T(8,128)S(1)} collective-permute-done((f32[24,896]{1,0:T(8,128)S(1)}, f32[24,896]{1,0:T(8,128)S(1)}, u32[]{:S(2)}, u32[]{:S(2)}) %collective-permute-start.12) | collective-permute-done | bytes 86048 | tf_op jit(solution)/shard_map/ppermute | solution.py:41
  68.1 1.9 %collective-permute-start.20 = (f32[24,128]{1,0:T(8,128)S(1)}, f32[24,128]{1,0:T(8,128)S(1)}, u32[]{:S(2)}, u32[]{:S(2)}) collective-permute-start(f32[24,128]{1,0:T(8,128)S(1)} %get-tuple-element.84), channel_id=1, source_target_pairs={{0,4},{2,6},{4,0},{6,2},{8,12},{10,14},{12,8},{14,10},{16,20},{18,... | collective-permute-start | bytes 36872 | tf_op jit(solution)/shard_map/ppermute | solution.py:41
  70.0 1.6 %collective-permute-start.21 = (f32[24,128]{1,0:T(8,128)S(1)}, f32[24,128]{1,0:T(8,128)S(1)}, u32[]{:S(2)}, u32[]{:S(2)}) collective-permute-start(f32[24,128]{1,0:T(8,128)S(1)} %get-tuple-element.84), channel_id=1, source_target_pairs={{0,6},{2,4},{4,2},{6,0},{8,14},{10,12},{12,10},{14,8},{16,22},{18,... | collective-permute-start | bytes 36872 | tf_op jit(solution)/shard_map/ppermute | solution.py:41
  71.9 2.7 %collective-permute-done.21 = f32[24,128]{1,0:T(8,128)S(1)} collective-permute-done((f32[24,128]{1,0:T(8,128)S(1)}, f32[24,128]{1,0:T(8,128)S(1)}, u32[]{:S(2)}, u32[]{:S(2)}) %collective-permute-start.21) | collective-permute-done | bytes 12320 | tf_op jit(solution)/shard_map/ppermute | solution.py:41
  74.8 3.0 %collective-permute-start.23 = (f32[24,128]{1,0:T(8,128)S(1)}, f32[24,128]{1,0:T(8,128)S(1)}, u32[]{:S(2)}, u32[]{:S(2)}) collective-permute-start(f32[24,128]{1,0:T(8,128)S(1)} %add_add_fusion.1.refs_0_), channel_id=1, source_target_pairs={{0,16},{2,18},{4,20},{6,22},{8,24},{10,26},{12,28},{14,30},{16,0},... | collective-permute-start | bytes 36872 | tf_op jit(solution)/shard_map/ppermute | solution.py:41
  77.7 1.3 %collective-permute-start.24 = (f32[24,128]{1,0:T(8,128)S(1)}, f32[24,128]{1,0:T(8,128)S(1)}, u32[]{:S(2)}, u32[]{:S(2)}) collective-permute-start(f32[24,128]{1,0:T(8,128)S(1)} %add_add_fusion.1.refs_0_), channel_id=1, source_target_pairs={{0,24},{2,26},{4,28},{6,30},{8,16},{10,18},{12,20},{14,22},{16,8},... | collective-permute-start | bytes 36872 | tf_op jit(solution)/shard_map/ppermute | solution.py:41
  79.0 4.7 %collective-permute-done.23.refs_2_ = f32[24,128]{1,0:T(8,128)S(1)} collective-permute-done((f32[24,128]{1,0:T(8,128)S(1)}, f32[24,128]{1,0:T(8,128)S(1)}, u32[]{:S(2)}, u32[]{:S(2)}) %collective-permute-start.23) | collective-permute-done | bytes 12320 | tf_op jit(solution)/shard_map/ppermute | solution.py:41
  83.8 0.7 direction.1
  84.5 1.9 %gram.1 = (f32[24,768]{1,0:T(8,128)}, f32[24,768]{1,0:T(8,128)}, f32[1,64,1024]{2,1,0:T(8,128)}) custom-call(s32[1,24]{1,0:T(1,128)S(1)} %copy-done.1, f32[24,128]{1,0:T(8,128)S(1)} %get-tuple-element.65.alpha, f32[24,768]{1,0:T(8,128)S(1)} %get-tuple-element.66.solved, f32[24,768]{1,0:T(8,128)S(1)} %get-tuple-element.67.left, ...), custom_call_target="tpu_custom_call" | custom-call | tf_op jit(solution)/shard_map/gram/pallas_call | solution.py:576
  (40 shorter events, 4.7 us)
Async XLA Ops:
  3.9 3.9 %copy-start = (bf16[1024,768]{1,0:T(8,128)(2,1)S(1)}, bf16[1024,768]{1,0:T(8,128)(2,1)}, u32[]{:S(2)}) copy-start(bf16[1024,768]{1,0:T(8,128)(2,1)} %variants.3) | copy-start | bytes 4718596
  3.9 3.9 %copy-start.1 = (s32[1,24]{1,0:T(1,128)S(1)}, s32[1,24]{1,0:T(1,128)}, u32[]{:S(2)}) copy-start(s32[1,24]{1,0:T(1,128)} %sizes.5) | copy-start | bytes 292
  13.8 29.2 %collective-permute-start.13 = (f32[224,512]{1,0:T(8,128)S(1)}, f32[224,512]{1,0:T(8,128)S(1)}, u32[]{:S(2)}, u32[]{:S(2)}) collective-permute-start(f32[224,512]{1,0:T(8,128)S(1)} %get-tuple-element.68), channel_id=1, source_target_pairs={{0,2},{2,0},{4,6},{6,4},{8,10},{10,8},{12,14},{14,12},{16,18},{18,... | collective-permute-start | bytes 1376264 | tf_op jit(solution)/shard_map/ppermute | solution.py:41
  16.8 26.2 %collective-permute-start.14 = (f32[224,512]{1,0:T(8,128)S(1)}, f32[224,512]{1,0:T(8,128)S(1)}, u32[]{:S(2)}, u32[]{:S(2)}) collective-permute-start(f32[224,512]{1,0:T(8,128)S(1)} %get-tuple-element.69), channel_id=1, source_target_pairs={{0,4},{2,6},{4,0},{6,2},{8,12},{10,14},{12,8},{14,10},{16,20},{18,... | collective-permute-start | bytes 1376264 | tf_op jit(solution)/shard_map/ppermute | solution.py:41
  18.3 14.1 %collective-permute-start = (f32[24,2048]{1,0:T(8,128)S(1)}, f32[24,2048]{1,0:T(8,128)S(1)}, u32[]{:S(2)}, u32[]{:S(2)}) collective-permute-start(f32[24,2048]{1,0:T(8,128)S(1)} %get-tuple-element.52), channel_id=1, source_target_pairs={{0,2},{2,0},{4,6},{6,4},{8,10},{10,8},{12,14},{14,12},{16,18},{18,... | collective-permute-start | bytes 589832 | tf_op jit(solution)/shard_map/ppermute | solution.py:41
  18.9 18.4 %collective-permute-start.1 = (f32[24,2048]{1,0:T(8,128)S(1)}, f32[24,2048]{1,0:T(8,128)S(1)}, u32[]{:S(2)}, u32[]{:S(2)}) collective-permute-start(f32[24,2048]{1,0:T(8,128)S(1)} %get-tuple-element.56), channel_id=1, source_target_pairs={{0,4},{2,6},{4,0},{6,2},{8,12},{10,14},{12,8},{14,10},{16,20},{18,... | collective-permute-start | bytes 589832 | tf_op jit(solution)/shard_map/ppermute | solution.py:41
  18.9 18.3 %collective-permute-start.2 = (f32[24,2048]{1,0:T(8,128)S(1)}, f32[24,2048]{1,0:T(8,128)S(1)}, u32[]{:S(2)}, u32[]{:S(2)}) collective-permute-start(f32[24,2048]{1,0:T(8,128)S(1)} %get-tuple-element.49), channel_id=1, source_target_pairs={{0,6},{2,4},{4,2},{6,0},{8,14},{10,12},{12,10},{14,8},{16,22},{18,... | collective-permute-start | bytes 589832 | tf_op jit(solution)/shard_map/ppermute | solution.py:41
  37.3 8.0 %collective-permute-start.3 = (f32[24,512]{1,0:T(8,128)S(1)}, f32[24,512]{1,0:T(8,128)S(1)}, u32[]{:S(2)}, u32[]{:S(2)}) collective-permute-start(f32[24,512]{1,0:T(8,128)S(1)} %get-tuple-element.58), channel_id=1, source_target_pairs={{0,8},{2,10},{4,12},{6,14},{8,0},{10,2},{12,4},{14,6},{16,24},{18,... | collective-permute-start | bytes 147464 | tf_op jit(solution)/shard_map/ppermute | solution.py:41
  38.9 6.4 %collective-permute-start.4 = (f32[24,512]{1,0:T(8,128)S(1)}, f32[24,512]{1,0:T(8,128)S(1)}, u32[]{:S(2)}, u32[]{:S(2)}) collective-permute-start(f32[24,512]{1,0:T(8,128)S(1)} %get-tuple-element.59), channel_id=1, source_target_pairs={{0,16},{2,18},{4,20},{6,22},{8,24},{10,26},{12,28},{14,30},{16,0},... | collective-permute-start | bytes 147464 | tf_op jit(solution)/shard_map/ppermute | solution.py:41
  41.5 6.2 %collective-permute-start.5 = (f32[24,512]{1,0:T(8,128)S(1)}, f32[24,512]{1,0:T(8,128)S(1)}, u32[]{:S(2)}, u32[]{:S(2)}) collective-permute-start(f32[24,512]{1,0:T(8,128)S(1)} %get-tuple-element.60), channel_id=1, source_target_pairs={{0,24},{2,26},{4,28},{6,30},{8,16},{10,18},{12,20},{14,22},{16,8},... | collective-permute-start | bytes 147464 | tf_op jit(solution)/shard_map/ppermute | solution.py:41
  43.1 9.0 %collective-permute-start.15 = (f32[248,256]{1,0:T(8,128)S(1)}, f32[248,256]{1,0:T(8,128)S(1)}, u32[]{:S(2)}, u32[]{:S(2)}) collective-permute-start(f32[248,256]{1,0:T(8,128)S(1)} %get-tuple-element.76.pass_x), channel_id=1, source_target_pairs={{0,4},{2,6},{4,0},{6,2},{8,12},{10,14},{12,8},{14,10},{16,20},{18,... | collective-permute-start | bytes 761864 | tf_op jit(solution)/shard_map/ppermute | solution.py:41
  44.7 7.4 %collective-permute-start.16 = (f32[248,256]{1,0:T(8,128)S(1)}, f32[248,256]{1,0:T(8,128)S(1)}, u32[]{:S(2)}, u32[]{:S(2)}) collective-permute-start(f32[248,256]{1,0:T(8,128)S(1)} %get-tuple-element.77.pass_y), channel_id=1, source_target_pairs={{0,2},{2,0},{4,6},{6,4},{8,10},{10,8},{12,14},{14,12},{16,18},{18,... | collective-permute-start | bytes 761864 | tf_op jit(solution)/shard_map/ppermute | solution.py:41
  47.7 5.4 %collective-permute-start.6 = (f32[24,512]{1,0:T(8,128)S(1)}, f32[24,512]{1,0:T(8,128)S(1)}, u32[]{:S(2)}, u32[]{:S(2)}) collective-permute-start(f32[24,512]{1,0:T(8,128)S(1)} %add_add_fusion), channel_id=1, source_target_pairs={{0,8},{2,10},{4,12},{6,14},{8,0},{10,2},{12,4},{14,6},{16,24},{18,... | collective-permute-start | bytes 147464 | tf_op jit(solution)/shard_map/ppermute | solution.py:41
  47.8 5.3 %collective-permute-start.7 = (f32[24,512]{1,0:T(8,128)S(1)}, f32[24,512]{1,0:T(8,128)S(1)}, u32[]{:S(2)}, u32[]{:S(2)}) collective-permute-start(f32[24,512]{1,0:T(8,128)S(1)} %add_add_fusion), channel_id=1, source_target_pairs={{0,16},{2,18},{4,20},{6,22},{8,24},{10,26},{12,28},{14,30},{16,0},... | collective-permute-start | bytes 147464 | tf_op jit(solution)/shard_map/ppermute | solution.py:41
  49.5 6.4 %collective-permute-start.8 = (f32[24,512]{1,0:T(8,128)S(1)}, f32[24,512]{1,0:T(8,128)S(1)}, u32[]{:S(2)}, u32[]{:S(2)}) collective-permute-start(f32[24,512]{1,0:T(8,128)S(1)} %add_add_fusion), channel_id=1, source_target_pairs={{0,24},{2,26},{4,28},{6,30},{8,16},{10,18},{12,20},{14,22},{16,8},... | collective-permute-start | bytes 147464 | tf_op jit(solution)/shard_map/ppermute | solution.py:41
  52.3 19.3 %collective-permute-start.17 = (f32[296,256]{1,0:T(8,128)S(1)}, f32[296,256]{1,0:T(8,128)S(1)}, u32[]{:S(2)}, u32[]{:S(2)}) collective-permute-start(f32[296,256]{1,0:T(8,128)S(1)} %get-tuple-element.79), channel_id=1, source_target_pairs={{0,8},{2,10},{4,12},{6,14},{8,0},{10,2},{12,4},{14,6},{16,24},{18,... | collective-permute-start | bytes 909320 | tf_op jit(solution)/shard_map/ppermute | solution.py:41
  56.0 5.7 %collective-permute-start.11 = (f32[24,2048]{1,0:T(8,128)S(1)}, f32[24,2048]{1,0:T(8,128)S(1)}, u32[]{:S(2)}, u32[]{:S(2)}) collective-permute-start(f32[24,2048]{1,0:T(8,128)S(1)} %pad_maximum_fusion.scores), channel_id=1, source_target_pairs={{0,2},{2,0},{4,6},{6,4},{8,10},{10,8},{12,14},{14,12},{16,18},{18,... | collective-permute-start | bytes 589832 | tf_op jit(solution)/shard_map/ppermute | solution.py:41
  57.4 7.8 %collective-permute-start.10 = (f32[24,2048]{1,0:T(8,128)S(1)}, f32[24,2048]{1,0:T(8,128)S(1)}, u32[]{:S(2)}, u32[]{:S(2)}) collective-permute-start(f32[24,2048]{1,0:T(8,128)S(1)} %pad_maximum_fusion.scores), channel_id=1, source_target_pairs={{0,4},{2,6},{4,0},{6,2},{8,12},{10,14},{12,8},{14,10},{16,20},{18,... | collective-permute-start | bytes 589832 | tf_op jit(solution)/shard_map/ppermute | solution.py:41
  58.0 7.8 %collective-permute-start.9 = (f32[24,2048]{1,0:T(8,128)S(1)}, f32[24,2048]{1,0:T(8,128)S(1)}, u32[]{:S(2)}, u32[]{:S(2)}) collective-permute-start(f32[24,2048]{1,0:T(8,128)S(1)} %pad_maximum_fusion.scores), channel_id=1, source_target_pairs={{0,6},{2,4},{4,2},{6,0},{8,14},{10,12},{12,10},{14,8},{16,22},{18,... | collective-permute-start | bytes 589832 | tf_op jit(solution)/shard_map/ppermute | solution.py:41
  66.5 1.3 %collective-permute-start.12 = (f32[24,896]{1,0:T(8,128)S(1)}, f32[24,896]{1,0:T(8,128)S(1)}, u32[]{:S(2)}, u32[]{:S(2)}) collective-permute-start(f32[24,896]{1,0:T(8,128)S(1)} %terms.7.own.held), channel_id=1, source_target_pairs={{0,1},{1,0},{2,3},{3,2},{4,5},{5,4},{6,7},{7,6},{8,9},{9,8},{10,11... | collective-permute-start | bytes 258056 | tf_op jit(solution)/shard_map/ppermute | solution.py:41
  68.1 3.7 %collective-permute-start.19 = (f32[24,128]{1,0:T(8,128)S(1)}, f32[24,128]{1,0:T(8,128)S(1)}, u32[]{:S(2)}, u32[]{:S(2)}) collective-permute-start(f32[24,128]{1,0:T(8,128)S(1)} %get-tuple-element.84), channel_id=1, source_target_pairs={{0,2},{2,0},{4,6},{6,4},{8,10},{10,8},{12,14},{14,12},{16,18},{18,... | collective-permute-start | bytes 36872 | tf_op jit(solution)/shard_map/ppermute | solution.py:41
  68.1 3.8 %collective-permute-start.20 = (f32[24,128]{1,0:T(8,128)S(1)}, f32[24,128]{1,0:T(8,128)S(1)}, u32[]{:S(2)}, u32[]{:S(2)}) collective-permute-start(f32[24,128]{1,0:T(8,128)S(1)} %get-tuple-element.84), channel_id=1, source_target_pairs={{0,4},{2,6},{4,0},{6,2},{8,12},{10,14},{12,8},{14,10},{16,20},{18,... | collective-permute-start | bytes 36872 | tf_op jit(solution)/shard_map/ppermute | solution.py:41
  70.0 4.6 %collective-permute-start.21 = (f32[24,128]{1,0:T(8,128)S(1)}, f32[24,128]{1,0:T(8,128)S(1)}, u32[]{:S(2)}, u32[]{:S(2)}) collective-permute-start(f32[24,128]{1,0:T(8,128)S(1)} %get-tuple-element.84), channel_id=1, source_target_pairs={{0,6},{2,4},{4,2},{6,0},{8,14},{10,12},{12,10},{14,8},{16,22},{18,... | collective-permute-start | bytes 36872 | tf_op jit(solution)/shard_map/ppermute | solution.py:41
  71.7 12.8 %collective-permute-start.18 = (f32[392,128]{1,0:T(8,128)S(1)}, f32[392,128]{1,0:T(8,128)S(1)}, u32[]{:S(2)}, u32[]{:S(2)}) collective-permute-start(f32[392,128]{1,0:T(8,128)S(1)} %get-tuple-element.81), channel_id=1, source_target_pairs={{0,16},{2,18},{4,20},{6,22},{8,24},{10,26},{12,28},{14,30},{16,0},... | collective-permute-start | bytes 602120 | tf_op jit(solution)/shard_map/ppermute | solution.py:41
  74.6 4.4 %collective-permute-start.22 = (f32[24,128]{1,0:T(8,128)S(1)}, f32[24,128]{1,0:T(8,128)S(1)}, u32[]{:S(2)}, u32[]{:S(2)}) collective-permute-start(f32[24,128]{1,0:T(8,128)S(1)} %add_add_fusion.1.refs_0_), channel_id=1, source_target_pairs={{0,8},{2,10},{4,12},{6,14},{8,0},{10,2},{12,4},{14,6},{16,24},{18,... | collective-permute-start | bytes 36872 | tf_op jit(solution)/shard_map/ppermute | solution.py:41
  74.8 9.0 %collective-permute-start.23 = (f32[24,128]{1,0:T(8,128)S(1)}, f32[24,128]{1,0:T(8,128)S(1)}, u32[]{:S(2)}, u32[]{:S(2)}) collective-permute-start(f32[24,128]{1,0:T(8,128)S(1)} %add_add_fusion.1.refs_0_), channel_id=1, source_target_pairs={{0,16},{2,18},{4,20},{6,22},{8,24},{10,26},{12,28},{14,30},{16,0},... | collective-permute-start | bytes 36872 | tf_op jit(solution)/shard_map/ppermute | solution.py:41
  77.7 6.0 %collective-permute-start.24 = (f32[24,128]{1,0:T(8,128)S(1)}, f32[24,128]{1,0:T(8,128)S(1)}, u32[]{:S(2)}, u32[]{:S(2)}) collective-permute-start(f32[24,128]{1,0:T(8,128)S(1)} %add_add_fusion.1.refs_0_), channel_id=1, source_target_pairs={{0,24},{2,26},{4,28},{6,30},{8,16},{10,18},{12,20},{14,22},{16,8},... | collective-permute-start | bytes 36872 | tf_op jit(solution)/shard_map/ppermute | solution.py:41

commit v13 on v12

--- a/solution.py
+++ b/solution.py
@@ -104,6 +104,7 @@
                 lane = lax.broadcasted_iota(jnp.int32, stats.shape, 1)
                 head = jnp.where((lane < 2) & (chunks[j] == plan.count - 1), stats, part[:, :LANES])
                 out[:, j * width : j * width + LANES] = head
+        group = len(copies)
 
 
 def lead_kernel(plan, digit, ratio, weights, panel, geno, out, held, diag, right, start, start_bf, weighted, stats, *scratch):
@@ -191,10 +192,9 @@
     return low, high
 
 
-def cross_kernel(plan, block, digit, sizes, start_bf, stats, diag, weighted, geno, variants, *refs):
-    out, held, *outs, scaled, sems = refs
+def cross_kernel(plan, block, sizes, diag, weighted, variants, *refs):
+    *outs, scaled = refs
     me = lax.axis_index("samp")
-    begun = scores_begin(plan, (digit,), me, geno, (held,), sems)
     share_scores(variants, weighted, *outs)
     pass_x, pass_y, send_x, send_y = outs
     places = {
@@ -203,7 +203,6 @@
         3: ((send_x, 1), (send_y, 1)),
     }
     cross_products(plan, block, me, sizes, diag[1:2, :], variants, scaled, places)
-    scores_finish(plan, begun, start_bf[...], stats[...], (out,))
 
 
 def share_scores(variants, weighted, pass_x, pass_y, send_x, send_y):
@@ -428,7 +427,7 @@
     diag, right, start = in_vmem(diag), in_vmem(right), in_vmem(start)
     after = sent[lead]
     start_bf, after = lax.optimization_barrier((start_bf, after))
-    digits = tuple(range(1, lead))
+    digits = (*range(1, lead), 0)
     found = kernel(
         functools.partial(scores_kernel, plan, digits),
         out_shape=[payload] * len(digits) + [window] * len(digits),
@@ -441,7 +440,7 @@
     )(in_vmem(start_bf), in_vmem(stats), genotypes)
     sent.update(zip(digits, found))
     genos.update(zip(digits, found[len(digits) :]))
-    start_bf, after = lax.optimization_barrier((start_bf, found[0]))
+    weighted, after = lax.optimization_barrier((weighted, found[0]))
 
     assert radix == 4 and all(r == 4 for r, _ in later)
     block = num_variants // count
@@ -451,17 +450,14 @@
     own_shape = VMEM((half, quarter), F32)
     pass_shape = VMEM((half + 2 * rows, quarter), F32)
     send_shape = VMEM((half + rows, 2 * quarter), F32)
-    sent[0], genos[0], pass_x, pass_y, send_x, send_y = kernel(
-        functools.partial(cross_kernel, plan, block, 0),
-        out_shape=[payload, window] + [pass_shape] * 2 + [send_shape] * 2,
-        in_specs=[smem] + [vmem] * 4 + [hbm, vmem],
-        out_specs=[vmem] * 6,
-        scratch_shapes=[
-            VMEM((quarter, samples), BF16),
-            pltpu.SemaphoreType.DMA((len(rest),)),
-        ],
-        name="scores_cross",
-    )(gene_sizes, in_vmem(start_bf), in_vmem(stats), diag, in_vmem(weighted), genotypes, in_vmem(variants))
+    pass_x, pass_y, send_x, send_y = kernel(
+        functools.partial(cross_kernel, plan, block),
+        out_shape=[pass_shape] * 2 + [send_shape] * 2,
+        in_specs=[smem] + [vmem] * 3,
+        out_specs=[vmem] * 4,
+        scratch_shapes=[VMEM((quarter, samples), BF16)],
+        name="cross_sent",
+    )(gene_sizes, diag, in_vmem(weighted), in_vmem(variants))
     own_x, own_y = kernel(
         functools.partial(own_kernel, plan, block),
         out_shape=[own_shape] * 2,

time: 86.6 us -> 84.8 us (0.979)
  Pallas kernels: 19.8 us -> 18 us
    pallas_call x1, Pallas kernels: 5.96 us -> 2.96 us  [body(): kernel(functools.partial(cross_kernel, plan, block), out_shape=[pass_shap...]
    pallas_call x1, Pallas kernels: 3.85 us -> 5.07 us  [body(): kernel(functools.partial(scores_kernel, plan, digits), out_shape=[payload...]
where the time goes in v13:
time: 84.8 us; the launch traced here: 84.6 us
  waiting for transfers between devices  34.5 us (41%)
  starting transfers between devices  30.6 us (36%)
  Pallas kernels  18 us (21%)
  between operations  1.45 us (2%)
    ppermute x25, waiting for transfers between devices, swap(): return lax.ppermute(array, axis, [(i, i ^ offset) for i in range(count)])  34.5 us
    ppermute x25, starting transfers between devices, swap(): return lax.ppermute(array, axis, [(i, i ^ offset) for i in range(count)])  30.6 us
    pallas_call x1, Pallas kernels, body(): kernel(functools.partial(scores_kernel, plan, digits), out_shape=[payload...  5.07 us
    pallas_call x1, Pallas kernels, body(): kernel(functools.partial(cross_kernel, plan, block), out_shape=[pass_shap...  2.96 us
    pallas_call x4, Pallas kernels, body(): kernel(functools.partial(terms_kernel, plan, d), out_shape=VMEM((rows, sa...  2.72 us
    pallas_call x1, Pallas kernels, body(): kernel(functools.partial(lead_kernel, plan, lead), out_shape=[payload, wi...  2.62 us
    pallas_call x1, Pallas kernels, body(): kernel(functools.partial(gram_kernel, samples * count), out_shape=[full]...  1.94 us
  transfers between devices with their start and end apart: 25, of which 12 were waited for; matrix products, arithmetic and copies ran while one was open for 0% of the time, Pallas kernels for 6%

profile of v13, /device:TPU:0, one launch (start us, length us, event | category | flops | bytes accessed | tf_op | source)
XLA Modules:
  0.0 84.6 jit_solution(6138638852939182496)
XLA Ops:
  1.3 2.6 %scores_lead.1 = (f32[24,2048]{1,0:T(8,128)S(1)}, bf16[2048,768]{1,0:T(8,128)(2,1)S(1)}, f32[8,768]{1,0:T(8,128)S(1)}, f32[24,768]{1,0:T(8,128)S(1)}, f32[24,768...) custom-call(f32[1]{0:T(128)S(6)} %copy.18.ratio, ...), custom_call_target="tpu_custom_call" | custom-call | tf_op jit(solution)/shard_map/scores_lead/pallas_call | solution.py:405
  3.9 5.1 %scores.1 = (f32[24,2048]{1,0:T(8,128)S(1)}, f32[24,2048]{1,0:T(8,128)S(1)}, f32[24,2048]{1,0:T(8,128)S(1)}, bf16[2048,768]{1,0:T(8,128)(2,1)S(1)}, bf16[2048,76...) custom-call(bf16[24,768]{1,0:T(8,128)(2,1)S(1)} %get-tuple-element.50.start_bf, f32[24,128]{1,0:T(8,128)S(1)} %get-tuple-element.51.stats, ...), custom_call_target="tpu_custom_call" | custom-call | tf_op jit(solution)/shard_map/scores/pallas_call | solution.py:431
  9.0 3.0 %cross_sent.1 = (f32[248,256]{1,0:T(8,128)S(1)}, f32[248,256]{1,0:T(8,128)S(1)}, f32[224,512]{1,0:T(8,128)S(1)}, f32[224,512]{1,0:T(8,128)S(1)}) custom-call(s32[1,24]{1,0:T(1,128)S(1)} %copy-done.1, f32[8,768]{1,0:T(8,128)S(1)} %get-tuple-element.45.diag, bf16[48,768]{1,0:T(8,128)(2,1)S(1)} %get-tuple-element.67.weighted, bf16[1024,768]{1,0:T(8,128)(2,1)S(1)} %copy-done), custom_call_target="tpu_custom_call" | custom-call | tf_op jit(solution)/shard_map/cross_sent/pallas_call | solution.py:453
  12.0 3.0 %collective-permute-start.13 = (f32[224,512]{1,0:T(8,128)S(1)}, f32[224,512]{1,0:T(8,128)S(1)}, u32[]{:S(2)}, u32[]{:S(2)}) collective-permute-start(f32[224,512]{1,0:T(8,128)S(1)} %get-tuple-element.68), channel_id=1, source_target_pairs={{0,2},{2,0},{4,6},{6,4},{8,10},{10,8},{12,14},{14,12},{16,18},{18,... | collective-permute-start | bytes 1376264 | tf_op jit(solution)/shard_map/ppermute | solution.py:41
  15.0 1.5 %collective-permute-start.14 = (f32[224,512]{1,0:T(8,128)S(1)}, f32[224,512]{1,0:T(8,128)S(1)}, u32[]{:S(2)}, u32[]{:S(2)}) collective-permute-start(f32[224,512]{1,0:T(8,128)S(1)} %get-tuple-element.69), channel_id=1, source_target_pairs={{0,4},{2,6},{4,0},{6,2},{8,12},{10,14},{12,8},{14,10},{16,20},{18,... | collective-permute-start | bytes 1376264 | tf_op jit(solution)/shard_map/ppermute | solution.py:41
  17.1 2.9 %collective-permute-start.2 = (f32[24,2048]{1,0:T(8,128)S(1)}, f32[24,2048]{1,0:T(8,128)S(1)}, u32[]{:S(2)}, u32[]{:S(2)}) collective-permute-start(f32[24,2048]{1,0:T(8,128)S(1)} %get-tuple-element.49), channel_id=1, source_target_pairs={{0,6},{2,4},{4,2},{6,0},{8,14},{10,12},{12,10},{14,8},{16,22},{18,... | collective-permute-start | bytes 589832 | tf_op jit(solution)/shard_map/ppermute | solution.py:41
  20.0 10.6 %collective-permute-done.refs_1_ = f32[24,2048]{1,0:T(8,128)S(1)} collective-permute-done((f32[24,2048]{1,0:T(8,128)S(1)}, f32[24,2048]{1,0:T(8,128)S(1)}, u32[]{:S(2)}, u32[]{:S(2)}) %collective-permute-start) | collective-permute-done | bytes 196640 | tf_op jit(solution)/shard_map/ppermute | solution.py:41
  30.6 4.8 %collective-permute-done.1.refs_2_ = f32[24,2048]{1,0:T(8,128)S(1)} collective-permute-done((f32[24,2048]{1,0:T(8,128)S(1)}, f32[24,2048]{1,0:T(8,128)S(1)}, u32[]{:S(2)}, u32[]{:S(2)}) %collective-permute-start.1) | collective-permute-done | bytes 196640 | tf_op jit(solution)/shard_map/ppermute | solution.py:41
  35.5 1.6 %collective-permute-start.3 = (f32[24,512]{1,0:T(8,128)S(1)}, f32[24,512]{1,0:T(8,128)S(1)}, u32[]{:S(2)}, u32[]{:S(2)}) collective-permute-start(f32[24,512]{1,0:T(8,128)S(1)} %get-tuple-element.56), channel_id=1, source_target_pairs={{0,8},{2,10},{4,12},{6,14},{8,0},{10,2},{12,4},{14,6},{16,24},{18,... | collective-permute-start | bytes 147464 | tf_op jit(solution)/shard_map/ppermute | solution.py:41
  37.1 2.6 %collective-permute-start.4 = (f32[24,512]{1,0:T(8,128)S(1)}, f32[24,512]{1,0:T(8,128)S(1)}, u32[]{:S(2)}, u32[]{:S(2)}) collective-permute-start(f32[24,512]{1,0:T(8,128)S(1)} %get-tuple-element.57), channel_id=1, source_target_pairs={{0,16},{2,18},{4,20},{6,22},{8,24},{10,26},{12,28},{14,30},{16,0},... | collective-permute-start | bytes 147464 | tf_op jit(solution)/shard_map/ppermute | solution.py:41
  39.9 1.2 %cross_own.1 = (f32[200,256]{1,0:T(8,128)S(1)}, f32[200,256]{1,0:T(8,128)S(1)}) custom-call(s32[1,24]{1,0:T(1,128)S(1)} %copy-done.1, f32[8,768]{1,0:T(8,128)S(1)} %get-tuple-element.45.diag, bf16[1024,768]{1,0:T(8,128)(2,1)S(1)} %copy-done), custom_call_target="tpu_custom_call" | custom-call | tf_op jit(solution)/shard_map/cross_own/pallas_call | solution.py:461
  41.4 1.6 %collective-permute-start.15 = (f32[248,256]{1,0:T(8,128)S(1)}, f32[248,256]{1,0:T(8,128)S(1)}, u32[]{:S(2)}, u32[]{:S(2)}) collective-permute-start(f32[248,256]{1,0:T(8,128)S(1)} %get-tuple-element.76.pass_x), channel_id=1, source_target_pairs={{0,4},{2,6},{4,0},{6,2},{8,12},{10,14},{12,8},{14,10},{16,20},{18,... | collective-permute-start | bytes 761864 | tf_op jit(solution)/shard_map/ppermute | solution.py:41
  43.5 2.4 %collective-permute-done.5 = f32[24,512]{1,0:T(8,128)S(1)} collective-permute-done((f32[24,512]{1,0:T(8,128)S(1)}, f32[24,512]{1,0:T(8,128)S(1)}, u32[]{:S(2)}, u32[]{:S(2)}) %collective-permute-start.5) | collective-permute-done | bytes 49184 | tf_op jit(solution)/shard_map/ppermute | solution.py:41
  46.0 1.8 %collective-permute-start.7 = (f32[24,512]{1,0:T(8,128)S(1)}, f32[24,512]{1,0:T(8,128)S(1)}, u32[]{:S(2)}, u32[]{:S(2)}) collective-permute-start(f32[24,512]{1,0:T(8,128)S(1)} %add_add_fusion), channel_id=1, source_target_pairs={{0,16},{2,18},{4,20},{6,22},{8,24},{10,26},{12,28},{14,30},{16,0},... | collective-permute-start | bytes 147464 | tf_op jit(solution)/shard_map/ppermute | solution.py:41
  47.7 2.6 %collective-permute-start.8 = (f32[24,512]{1,0:T(8,128)S(1)}, f32[24,512]{1,0:T(8,128)S(1)}, u32[]{:S(2)}, u32[]{:S(2)}) collective-permute-start(f32[24,512]{1,0:T(8,128)S(1)} %add_add_fusion), channel_id=1, source_target_pairs={{0,24},{2,26},{4,28},{6,30},{8,16},{10,18},{12,20},{14,22},{16,8},... | collective-permute-start | bytes 147464 | tf_op jit(solution)/shard_map/ppermute | solution.py:41
  50.6 0.7 collective-permute-done.6
  51.3 2.9 %collective-permute-done.8 = f32[24,512]{1,0:T(8,128)S(1)} collective-permute-done((f32[24,512]{1,0:T(8,128)S(1)}, f32[24,512]{1,0:T(8,128)S(1)}, u32[]{:S(2)}, u32[]{:S(2)}) %collective-permute-start.8) | collective-permute-done | bytes 49184 | tf_op jit(solution)/shard_map/ppermute | solution.py:41
  54.2 1.4 %collective-permute-start.11 = (f32[24,2048]{1,0:T(8,128)S(1)}, f32[24,2048]{1,0:T(8,128)S(1)}, u32[]{:S(2)}, u32[]{:S(2)}) collective-permute-start(f32[24,2048]{1,0:T(8,128)S(1)} %pad_maximum_fusion.scores), channel_id=1, source_target_pairs={{0,2},{2,0},{4,6},{6,4},{8,10},{10,8},{12,14},{14,12},{16,18},{18,... | collective-permute-start | bytes 589832 | tf_op jit(solution)/shard_map/ppermute | solution.py:41
  56.2 1.5 %collective-permute-start.9 = (f32[24,2048]{1,0:T(8,128)S(1)}, f32[24,2048]{1,0:T(8,128)S(1)}, u32[]{:S(2)}, u32[]{:S(2)}) collective-permute-start(f32[24,2048]{1,0:T(8,128)S(1)} %pad_maximum_fusion.scores), channel_id=1, source_target_pairs={{0,6},{2,4},{4,2},{6,0},{8,14},{10,12},{12,10},{14,8},{16,22},{18,... | collective-permute-start | bytes 589832 | tf_op jit(solution)/shard_map/ppermute | solution.py:41
  58.4 1.5 %collective-permute-done.11.scores = f32[24,2048]{1,0:T(8,128)S(1)} collective-permute-done((f32[24,2048]{1,0:T(8,128)S(1)}, f32[24,2048]{1,0:T(8,128)S(1)}, u32[]{:S(2)}, u32[]{:S(2)}) %collective-permute-start.11) | collective-permute-done | bytes 196640 | tf_op jit(solution)/shard_map/ppermute | solution.py:41
  59.9 0.7 terms.5.refs_0_
  60.6 2.7 %collective-permute-done.10.scores = f32[24,2048]{1,0:T(8,128)S(1)} collective-permute-done((f32[24,2048]{1,0:T(8,128)S(1)}, f32[24,2048]{1,0:T(8,128)S(1)}, u32[]{:S(2)}, u32[]{:S(2)}) %collective-permute-start.10) | collective-permute-done | bytes 196640 | tf_op jit(solution)/shard_map/ppermute | solution.py:41
  64.1 0.7 terms.7.own.held
  64.8 1.3 %collective-permute-done.12.other = f32[24,896]{1,0:T(8,128)S(1)} collective-permute-done((f32[24,896]{1,0:T(8,128)S(1)}, f32[24,896]{1,0:T(8,128)S(1)}, u32[]{:S(2)}, u32[]{:S(2)}) %collective-permute-start.12) | collective-permute-done | bytes 86048 | tf_op jit(solution)/shard_map/ppermute | solution.py:41
  66.4 1.9 %collective-permute-start.20 = (f32[24,128]{1,0:T(8,128)S(1)}, f32[24,128]{1,0:T(8,128)S(1)}, u32[]{:S(2)}, u32[]{:S(2)}) collective-permute-start(f32[24,128]{1,0:T(8,128)S(1)} %get-tuple-element.84), channel_id=1, source_target_pairs={{0,4},{2,6},{4,0},{6,2},{8,12},{10,14},{12,8},{14,10},{16,20},{18,... | collective-permute-start | bytes 36872 | tf_op jit(solution)/shard_map/ppermute | solution.py:41
  68.3 1.6 %collective-permute-start.21 = (f32[24,128]{1,0:T(8,128)S(1)}, f32[24,128]{1,0:T(8,128)S(1)}, u32[]{:S(2)}, u32[]{:S(2)}) collective-permute-start(f32[24,128]{1,0:T(8,128)S(1)} %get-tuple-element.84), channel_id=1, source_target_pairs={{0,6},{2,4},{4,2},{6,0},{8,14},{10,12},{12,10},{14,8},{16,22},{18,... | collective-permute-start | bytes 36872 | tf_op jit(solution)/shard_map/ppermute | solution.py:41
  70.1 2.7 %collective-permute-done.21 = f32[24,128]{1,0:T(8,128)S(1)} collective-permute-done((f32[24,128]{1,0:T(8,128)S(1)}, f32[24,128]{1,0:T(8,128)S(1)}, u32[]{:S(2)}, u32[]{:S(2)}) %collective-permute-start.21) | collective-permute-done | bytes 12320 | tf_op jit(solution)/shard_map/ppermute | solution.py:41
  73.0 3.0 %collective-permute-start.23 = (f32[24,128]{1,0:T(8,128)S(1)}, f32[24,128]{1,0:T(8,128)S(1)}, u32[]{:S(2)}, u32[]{:S(2)}) collective-permute-start(f32[24,128]{1,0:T(8,128)S(1)} %add_add_fusion.1.refs_0_), channel_id=1, source_target_pairs={{0,16},{2,18},{4,20},{6,22},{8,24},{10,26},{12,28},{14,30},{16,0},... | collective-permute-start | bytes 36872 | tf_op jit(solution)/shard_map/ppermute | solution.py:41
  75.9 1.3 %collective-permute-start.24 = (f32[24,128]{1,0:T(8,128)S(1)}, f32[24,128]{1,0:T(8,128)S(1)}, u32[]{:S(2)}, u32[]{:S(2)}) collective-permute-start(f32[24,128]{1,0:T(8,128)S(1)} %add_add_fusion.1.refs_0_), channel_id=1, source_target_pairs={{0,24},{2,26},{4,28},{6,30},{8,16},{10,18},{12,20},{14,22},{16,8},... | collective-permute-start | bytes 36872 | tf_op jit(solution)/shard_map/ppermute | solution.py:41
  77.2 4.7 %collective-permute-done.23.refs_2_ = f32[24,128]{1,0:T(8,128)S(1)} collective-permute-done((f32[24,128]{1,0:T(8,128)S(1)}, f32[24,128]{1,0:T(8,128)S(1)}, u32[]{:S(2)}, u32[]{:S(2)}) %collective-permute-start.23) | collective-permute-done | bytes 12320 | tf_op jit(solution)/shard_map/ppermute | solution.py:41
  82.0 0.7 direction.1
  82.7 1.9 %gram.1 = (f32[24,768]{1,0:T(8,128)}, f32[24,768]{1,0:T(8,128)}, f32[1,64,1024]{2,1,0:T(8,128)}) custom-call(s32[1,24]{1,0:T(1,128)S(1)} %copy-done.1, f32[24,128]{1,0:T(8,128)S(1)} %get-tuple-element.63.alpha, f32[24,768]{1,0:T(8,128)S(1)} %get-tuple-element.64.solved, f32[24,768]{1,0:T(8,128)S(1)} %get-tuple-element.65.left, ...), custom_call_target="tpu_custom_call" | custom-call | tf_op jit(solution)/shard_map/gram/pallas_call | solution.py:572
  (40 shorter events, 4.7 us)
Async XLA Ops:
  3.9 5.1 %copy-start = (bf16[1024,768]{1,0:T(8,128)(2,1)S(1)}, bf16[1024,768]{1,0:T(8,128)(2,1)}, u32[]{:S(2)}) copy-start(bf16[1024,768]{1,0:T(8,128)(2,1)} %variants.3) | copy-start | bytes 4718596
  3.9 5.1 %copy-start.1 = (s32[1,24]{1,0:T(1,128)S(1)}, s32[1,24]{1,0:T(1,128)}, u32[]{:S(2)}) copy-start(s32[1,24]{1,0:T(1,128)} %sizes.5) | copy-start | bytes 292
  12.0 29.2 %collective-permute-start.13 = (f32[224,512]{1,0:T(8,128)S(1)}, f32[224,512]{1,0:T(8,128)S(1)}, u32[]{:S(2)}, u32[]{:S(2)}) collective-permute-start(f32[224,512]{1,0:T(8,128)S(1)} %get-tuple-element.68), channel_id=1, source_target_pairs={{0,2},{2,0},{4,6},{6,4},{8,10},{10,8},{12,14},{14,12},{16,18},{18,... | collective-permute-start | bytes 1376264 | tf_op jit(solution)/shard_map/ppermute | solution.py:41
  15.0 26.1 %collective-permute-start.14 = (f32[224,512]{1,0:T(8,128)S(1)}, f32[224,512]{1,0:T(8,128)S(1)}, u32[]{:S(2)}, u32[]{:S(2)}) collective-permute-start(f32[224,512]{1,0:T(8,128)S(1)} %get-tuple-element.69), channel_id=1, source_target_pairs={{0,4},{2,6},{4,0},{6,2},{8,12},{10,14},{12,8},{14,10},{16,20},{18,... | collective-permute-start | bytes 1376264 | tf_op jit(solution)/shard_map/ppermute | solution.py:41
  16.6 14.1 %collective-permute-start = (f32[24,2048]{1,0:T(8,128)S(1)}, f32[24,2048]{1,0:T(8,128)S(1)}, u32[]{:S(2)}, u32[]{:S(2)}) collective-permute-start(f32[24,2048]{1,0:T(8,128)S(1)} %get-tuple-element.53), channel_id=1, source_target_pairs={{0,2},{2,0},{4,6},{6,4},{8,10},{10,8},{12,14},{14,12},{16,18},{18,... | collective-permute-start | bytes 589832 | tf_op jit(solution)/shard_map/ppermute | solution.py:41
  17.1 18.4 %collective-permute-start.1 = (f32[24,2048]{1,0:T(8,128)S(1)}, f32[24,2048]{1,0:T(8,128)S(1)}, u32[]{:S(2)}, u32[]{:S(2)}) collective-permute-start(f32[24,2048]{1,0:T(8,128)S(1)} %get-tuple-element.54), channel_id=1, source_target_pairs={{0,4},{2,6},{4,0},{6,2},{8,12},{10,14},{12,8},{14,10},{16,20},{18,... | collective-permute-start | bytes 589832 | tf_op jit(solution)/shard_map/ppermute | solution.py:41
  17.1 18.3 %collective-permute-start.2 = (f32[24,2048]{1,0:T(8,128)S(1)}, f32[24,2048]{1,0:T(8,128)S(1)}, u32[]{:S(2)}, u32[]{:S(2)}) collective-permute-start(f32[24,2048]{1,0:T(8,128)S(1)} %get-tuple-element.49), channel_id=1, source_target_pairs={{0,6},{2,4},{4,2},{6,0},{8,14},{10,12},{12,10},{14,8},{16,22},{18,... | collective-permute-start | bytes 589832 | tf_op jit(solution)/shard_map/ppermute | solution.py:41
  35.5 8.0 %collective-permute-start.3 = (f32[24,512]{1,0:T(8,128)S(1)}, f32[24,512]{1,0:T(8,128)S(1)}, u32[]{:S(2)}, u32[]{:S(2)}) collective-permute-start(f32[24,512]{1,0:T(8,128)S(1)} %get-tuple-element.56), channel_id=1, source_target_pairs={{0,8},{2,10},{4,12},{6,14},{8,0},{10,2},{12,4},{14,6},{16,24},{18,... | collective-permute-start | bytes 147464 | tf_op jit(solution)/shard_map/ppermute | solution.py:41
  37.1 6.4 %collective-permute-start.4 = (f32[24,512]{1,0:T(8,128)S(1)}, f32[24,512]{1,0:T(8,128)S(1)}, u32[]{:S(2)}, u32[]{:S(2)}) collective-permute-start(f32[24,512]{1,0:T(8,128)S(1)} %get-tuple-element.57), channel_id=1, source_target_pairs={{0,16},{2,18},{4,20},{6,22},{8,24},{10,26},{12,28},{14,30},{16,0},... | collective-permute-start | bytes 147464 | tf_op jit(solution)/shard_map/ppermute | solution.py:41
  39.7 6.2 %collective-permute-start.5 = (f32[24,512]{1,0:T(8,128)S(1)}, f32[24,512]{1,0:T(8,128)S(1)}, u32[]{:S(2)}, u32[]{:S(2)}) collective-permute-start(f32[24,512]{1,0:T(8,128)S(1)} %get-tuple-element.58), channel_id=1, source_target_pairs={{0,24},{2,26},{4,28},{6,30},{8,16},{10,18},{12,20},{14,22},{16,8},... | collective-permute-start | bytes 147464 | tf_op jit(solution)/shard_map/ppermute | solution.py:41
  41.4 9.0 %collective-permute-start.15 = (f32[248,256]{1,0:T(8,128)S(1)}, f32[248,256]{1,0:T(8,128)S(1)}, u32[]{:S(2)}, u32[]{:S(2)}) collective-permute-start(f32[248,256]{1,0:T(8,128)S(1)} %get-tuple-element.76.pass_x), channel_id=1, source_target_pairs={{0,4},{2,6},{4,0},{6,2},{8,12},{10,14},{12,8},{14,10},{16,20},{18,... | collective-permute-start | bytes 761864 | tf_op jit(solution)/shard_map/ppermute | solution.py:41
  42.9 7.4 %collective-permute-start.16 = (f32[248,256]{1,0:T(8,128)S(1)}, f32[248,256]{1,0:T(8,128)S(1)}, u32[]{:S(2)}, u32[]{:S(2)}) collective-permute-start(f32[248,256]{1,0:T(8,128)S(1)} %get-tuple-element.77.pass_y), channel_id=1, source_target_pairs={{0,2},{2,0},{4,6},{6,4},{8,10},{10,8},{12,14},{14,12},{16,18},{18,... | collective-permute-start | bytes 761864 | tf_op jit(solution)/shard_map/ppermute | solution.py:41
  45.9 5.4 %collective-permute-start.6 = (f32[24,512]{1,0:T(8,128)S(1)}, f32[24,512]{1,0:T(8,128)S(1)}, u32[]{:S(2)}, u32[]{:S(2)}) collective-permute-start(f32[24,512]{1,0:T(8,128)S(1)} %add_add_fusion), channel_id=1, source_target_pairs={{0,8},{2,10},{4,12},{6,14},{8,0},{10,2},{12,4},{14,6},{16,24},{18,... | collective-permute-start | bytes 147464 | tf_op jit(solution)/shard_map/ppermute | solution.py:41
  46.0 5.3 %collective-permute-start.7 = (f32[24,512]{1,0:T(8,128)S(1)}, f32[24,512]{1,0:T(8,128)S(1)}, u32[]{:S(2)}, u32[]{:S(2)}) collective-permute-start(f32[24,512]{1,0:T(8,128)S(1)} %add_add_fusion), channel_id=1, source_target_pairs={{0,16},{2,18},{4,20},{6,22},{8,24},{10,26},{12,28},{14,30},{16,0},... | collective-permute-start | bytes 147464 | tf_op jit(solution)/shard_map/ppermute | solution.py:41
  47.7 6.4 %collective-permute-start.8 = (f32[24,512]{1,0:T(8,128)S(1)}, f32[24,512]{1,0:T(8,128)S(1)}, u32[]{:S(2)}, u32[]{:S(2)}) collective-permute-start(f32[24,512]{1,0:T(8,128)S(1)} %add_add_fusion), channel_id=1, source_target_pairs={{0,24},{2,26},{4,28},{6,30},{8,16},{10,18},{12,20},{14,22},{16,8},... | collective-permute-start | bytes 147464 | tf_op jit(solution)/shard_map/ppermute | solution.py:41
  50.5 19.3 %collective-permute-start.17 = (f32[296,256]{1,0:T(8,128)S(1)}, f32[296,256]{1,0:T(8,128)S(1)}, u32[]{:S(2)}, u32[]{:S(2)}) collective-permute-start(f32[296,256]{1,0:T(8,128)S(1)} %get-tuple-element.79), channel_id=1, source_target_pairs={{0,8},{2,10},{4,12},{6,14},{8,0},{10,2},{12,4},{14,6},{16,24},{18,... | collective-permute-start | bytes 909320 | tf_op jit(solution)/shard_map/ppermute | solution.py:41
  54.2 5.7 %collective-permute-start.11 = (f32[24,2048]{1,0:T(8,128)S(1)}, f32[24,2048]{1,0:T(8,128)S(1)}, u32[]{:S(2)}, u32[]{:S(2)}) collective-permute-start(f32[24,2048]{1,0:T(8,128)S(1)} %pad_maximum_fusion.scores), channel_id=1, source_target_pairs={{0,2},{2,0},{4,6},{6,4},{8,10},{10,8},{12,14},{14,12},{16,18},{18,... | collective-permute-start | bytes 589832 | tf_op jit(solution)/shard_map/ppermute | solution.py:41
  55.6 7.8 %collective-permute-start.10 = (f32[24,2048]{1,0:T(8,128)S(1)}, f32[24,2048]{1,0:T(8,128)S(1)}, u32[]{:S(2)}, u32[]{:S(2)}) collective-permute-start(f32[24,2048]{1,0:T(8,128)S(1)} %pad_maximum_fusion.scores), channel_id=1, source_target_pairs={{0,4},{2,6},{4,0},{6,2},{8,12},{10,14},{12,8},{14,10},{16,20},{18,... | collective-permute-start | bytes 589832 | tf_op jit(solution)/shard_map/ppermute | solution.py:41
  56.2 7.8 %collective-permute-start.9 = (f32[24,2048]{1,0:T(8,128)S(1)}, f32[24,2048]{1,0:T(8,128)S(1)}, u32[]{:S(2)}, u32[]{:S(2)}) collective-permute-start(f32[24,2048]{1,0:T(8,128)S(1)} %pad_maximum_fusion.scores), channel_id=1, source_target_pairs={{0,6},{2,4},{4,2},{6,0},{8,14},{10,12},{12,10},{14,8},{16,22},{18,... | collective-permute-start | bytes 589832 | tf_op jit(solution)/shard_map/ppermute | solution.py:41
  64.7 1.3 %collective-permute-start.12 = (f32[24,896]{1,0:T(8,128)S(1)}, f32[24,896]{1,0:T(8,128)S(1)}, u32[]{:S(2)}, u32[]{:S(2)}) collective-permute-start(f32[24,896]{1,0:T(8,128)S(1)} %terms.7.own.held), channel_id=1, source_target_pairs={{0,1},{1,0},{2,3},{3,2},{4,5},{5,4},{6,7},{7,6},{8,9},{9,8},{10,11... | collective-permute-start | bytes 258056 | tf_op jit(solution)/shard_map/ppermute | solution.py:41
  66.3 3.7 %collective-permute-start.19 = (f32[24,128]{1,0:T(8,128)S(1)}, f32[24,128]{1,0:T(8,128)S(1)}, u32[]{:S(2)}, u32[]{:S(2)}) collective-permute-start(f32[24,128]{1,0:T(8,128)S(1)} %get-tuple-element.84), channel_id=1, source_target_pairs={{0,2},{2,0},{4,6},{6,4},{8,10},{10,8},{12,14},{14,12},{16,18},{18,... | collective-permute-start | bytes 36872 | tf_op jit(solution)/shard_map/ppermute | solution.py:41
  66.4 3.8 %collective-permute-start.20 = (f32[24,128]{1,0:T(8,128)S(1)}, f32[24,128]{1,0:T(8,128)S(1)}, u32[]{:S(2)}, u32[]{:S(2)}) collective-permute-start(f32[24,128]{1,0:T(8,128)S(1)} %get-tuple-element.84), channel_id=1, source_target_pairs={{0,4},{2,6},{4,0},{6,2},{8,12},{10,14},{12,8},{14,10},{16,20},{18,... | collective-permute-start | bytes 36872 | tf_op jit(solution)/shard_map/ppermute | solution.py:41
  68.3 4.6 %collective-permute-start.21 = (f32[24,128]{1,0:T(8,128)S(1)}, f32[24,128]{1,0:T(8,128)S(1)}, u32[]{:S(2)}, u32[]{:S(2)}) collective-permute-start(f32[24,128]{1,0:T(8,128)S(1)} %get-tuple-element.84), channel_id=1, source_target_pairs={{0,6},{2,4},{4,2},{6,0},{8,14},{10,12},{12,10},{14,8},{16,22},{18,... | collective-permute-start | bytes 36872 | tf_op jit(solution)/shard_map/ppermute | solution.py:41
  69.9 12.8 %collective-permute-start.18 = (f32[392,128]{1,0:T(8,128)S(1)}, f32[392,128]{1,0:T(8,128)S(1)}, u32[]{:S(2)}, u32[]{:S(2)}) collective-permute-start(f32[392,128]{1,0:T(8,128)S(1)} %get-tuple-element.81), channel_id=1, source_target_pairs={{0,16},{2,18},{4,20},{6,22},{8,24},{10,26},{12,28},{14,30},{16,0},... | collective-permute-start | bytes 602120 | tf_op jit(solution)/shard_map/ppermute | solution.py:41
  72.9 4.4 %collective-permute-start.22 = (f32[24,128]{1,0:T(8,128)S(1)}, f32[24,128]{1,0:T(8,128)S(1)}, u32[]{:S(2)}, u32[]{:S(2)}) collective-permute-start(f32[24,128]{1,0:T(8,128)S(1)} %add_add_fusion.1.refs_0_), channel_id=1, source_target_pairs={{0,8},{2,10},{4,12},{6,14},{8,0},{10,2},{12,4},{14,6},{16,24},{18,... | collective-permute-start | bytes 36872 | tf_op jit(solution)/shard_map/ppermute | solution.py:41
  73.0 9.0 %collective-permute-start.23 = (f32[24,128]{1,0:T(8,128)S(1)}, f32[24,128]{1,0:T(8,128)S(1)}, u32[]{:S(2)}, u32[]{:S(2)}) collective-permute-start(f32[24,128]{1,0:T(8,128)S(1)} %add_add_fusion.1.refs_0_), channel_id=1, source_target_pairs={{0,16},{2,18},{4,20},{6,22},{8,24},{10,26},{12,28},{14,30},{16,0},... | collective-permute-start | bytes 36872 | tf_op jit(solution)/shard_map/ppermute | solution.py:41
  75.9 6.0 %collective-permute-start.24 = (f32[24,128]{1,0:T(8,128)S(1)}, f32[24,128]{1,0:T(8,128)S(1)}, u32[]{:S(2)}, u32[]{:S(2)}) collective-permute-start(f32[24,128]{1,0:T(8,128)S(1)} %add_add_fusion.1.refs_0_), channel_id=1, source_target_pairs={{0,24},{2,26},{4,28},{6,30},{8,16},{10,18},{12,20},{14,22},{16,8},... | collective-permute-start | bytes 36872 | tf_op jit(solution)/shard_map/ppermute | solution.py:41
